TPU v7x, 32 devices: a whole 2x2x4 slice. The times are simulated.
32 devices in a mesh: dp: 8 (over y, x, core), fsdp: 4 (over z).
Axes of the slice: x: 2, y: 2, z: 4, core: 2. Of those that a mesh axis runs over, the one named last changes fastest.
Arguments:
- tokens: bfloat16 [16384, 1024], P(('dp', 'fsdp')), may hold values from -6 to 6
- segment_ids: int32 [32, 512], P(('dp', 'fsdp')), may hold values from 0 to 3, never falling along the last dimension, each value on 1 to 256 neighbouring positions
- decay_rate: float32 [16], replicated, may hold values from 0.0005 to 0.03
- cotangent: bfloat16 [16384, 1024], P(('dp', 'fsdp')), may hold values from -6 to 6
- attn_master: float32 [5, 1024, 1024], P(None, ('dp', 'fsdp')), may hold values from -0.1875 to 0.1875
- ffn_master: float32 [3, 2816, 1024], P(None, ('dp', 'fsdp')), may hold values from -0.1875 to 0.1875
- gains: float32 [3, 1024], P(None, ('dp', 'fsdp')), may hold values from 0.5 to 1.5
- attn_moment: float32 [5, 1024, 1024], P(None, ('dp', 'fsdp')), may hold values from -24 to 24
- ffn_moment: float32 [3, 2816, 1024], P(None, ('dp', 'fsdp')), may hold values from -24 to 24
- gain_first: float32 [3, 1024], P(None, ('dp', 'fsdp')), may hold values from -96 to 96
- gain_second: float32 [3, 1024], P(None, ('dp', 'fsdp')), may hold values from 16 to 4096
Outputs:
- out: bfloat16 [16384, 1024], P(('dp', 'fsdp'))
- x_grad: float32 [16384, 1024], P(('dp', 'fsdp'))
- attn_grad: float32 [5, 1024, 1024], P(None, ('dp', 'fsdp'))
- ffn_grad: float32 [3, 2816, 1024], P(None, ('dp', 'fsdp'))
- gain_grad: float32 [3, 1024], P(None, ('dp', 'fsdp'))
- attn_moment_new: float32 [5, 1024, 1024], P(None, ('dp', 'fsdp'))
- ffn_moment_new: float32 [3, 2816, 1024], P(None, ('dp', 'fsdp'))
- attn_master_new: float32 [5, 1024, 1024], P(None, ('dp', 'fsdp'))
- ffn_master_new: float32 [3, 2816, 1024], P(None, ('dp', 'fsdp'))
- attn_copy: bfloat16 [5, 1024, 1024], P(None, ('dp', 'fsdp'))
- ffn_copy: bfloat16 [3, 2816, 1024], P(None, ('dp', 'fsdp'))
- gains_new: float32 [3, 1024], P(None, ('dp', 'fsdp'))
- gain_first_new: float32 [3, 1024], P(None, ('dp', 'fsdp'))
- gain_second_new: float32 [3, 1024], P(None, ('dp', 'fsdp'))
Inputs may be any that keep to these rules, and one draw needn't show every extreme that they name: `segment_ids`: within a pack the ids never fall; each pack holds 4 documents of 1 to 256 tokens, one of exactly 256.
All inputs are finite; a program needn't handle non-finite values.
Results may differ from a plain program's by a relative error of at most 0.012.
The roundings to bfloat16 on the way count: a program that leaves them out, or rounds other values in their place, can miss the bound.
Values may be sent and summed in bfloat16 or wider, within the bound.
No kernel may reach another device: no remote copies, remote signals or barrier semaphores. Data moves between devices by JAX's collectives and lax.ppermute only.
A program may use at most 256 MiB of HBM per device.

v0:
```python
import math

import jax
import jax.numpy as jnp
from jax import lax
from jax.sharding import PartitionSpec as P

D = 1024
FF = 2816
NS_STEPS = 5


HIGH = lax.Precision.HIGHEST
EPS = 1e-06
NS_EPS = 1e-07
NS_A = 3.4445
NS_B = -4.775
NS_C = 2.0315
LR_MUON = 0.3
LR_GAIN = 0.1
MOMENT_DECAY = 0.5
BETA_ONE = 0.9
BETA_TWO = 0.95
ADAM_EPS = 1e-08
F32 = jnp.float32
B16 = jnp.bfloat16
ROWS_BY_ROWS = (((1,), (1,)), ((), ()))
TOKENS_OUT = (((0,), (0,)), ((), ()))


def as_sent(shard):

    def short(part):
        return part.astype(jnp.bfloat16) if part.dtype == jnp.float32 else part

    return jax.tree.map(short, shard)


def rms_scale(series):
    return lax.rsqrt(jnp.mean(series * series, axis=-1, keepdims=True) + EPS)


def rms_back(series, factor, upstream):
    return factor * upstream - series * (factor * factor * factor) * jnp.mean(
        upstream * series, axis=-1, keepdims=True
    )


def decay_mask(segments, decay_rate):
    length = segments.shape[0]
    places = jnp.arange(length, dtype=jnp.int32)
    distance = places[:, None] - places[None, :]
    allowed = (segments[:, None] == segments[None, :]) & (distance >= 0)
    fading = jnp.exp(-decay_rate[:, None, None] * jnp.maximum(distance, 0).astype(F32)[None])
    return jnp.where(allowed[None], fading, 0.0)


def forward(tokens, segments, decay_rate, attn_full, ffn_full, gain_low):
    length, model_width = tokens.shape
    head_count = decay_rate.shape[0]
    head_size = model_width // head_count
    hidden = ffn_full.shape[1]
    gain_full = gain_low.astype(F32)
    inputs = tokens.astype(F32)
    first_scale = rms_scale(inputs)
    normed = (inputs * first_scale * gain_full[0]).astype(B16)
    projected = lax.dot_general(
        normed,
        attn_full[:4].reshape(4 * model_width, model_width),
        ROWS_BY_ROWS,
        preferred_element_type=F32,
    )
    query_act = jax.nn.relu(projected[:, :model_width]).astype(B16)
    key_act = jax.nn.relu(projected[:, model_width : 2 * model_width]).astype(B16)
    value_act = projected[:, 2 * model_width : 3 * model_width].astype(B16)
    gate_pre = projected[:, 3 * model_width :]
    fading_mask = decay_mask(segments, decay_rate)
    query_heads = query_act.reshape(length, head_count, head_size)
    key_heads = key_act.reshape(length, head_count, head_size)
    value_heads = value_act.reshape(length, head_count, head_size)
    scores = jnp.einsum("the,she->hts", query_heads, key_heads, preferred_element_type=F32)
    weights_low = (scores * fading_mask).astype(B16)
    attended = jnp.einsum(
        "hts,she->the", weights_low, value_heads, preferred_element_type=F32
    ).reshape(length, model_width)
    out_scale = rms_scale(attended)
    normal_out = attended * out_scale * gain_full[2]
    gate_sig = jax.nn.sigmoid(gate_pre)
    gated_out = (normal_out * gate_sig).astype(B16)
    branch = lax.dot_general(gated_out, attn_full[4], ROWS_BY_ROWS, preferred_element_type=F32)
    middle = inputs + branch
    second_scale = rms_scale(middle)
    normed_two = (middle * second_scale * gain_full[1]).astype(B16)
    up_pair = lax.dot_general(
        normed_two,
        ffn_full[:2].reshape(2 * hidden, model_width),
        ROWS_BY_ROWS,
        preferred_element_type=F32,
    )
    up_one = up_pair[:, :hidden]
    up_two = up_pair[:, hidden:]
    product = (up_one * up_two).astype(B16)
    result = middle + jnp.dot(product, ffn_full[2], preferred_element_type=F32)
    stored = (
        inputs,
        first_scale,
        normed,
        query_act,
        key_act,
        value_act,
        gate_pre,
        fading_mask,
        weights_low,
        attended,
        out_scale,
        normal_out,
        gate_sig,
        gated_out,
        middle,
        second_scale,
        normed_two,
        up_one,
        up_two,
        product,
    )
    return (result.astype(B16), stored)


def backward(stored, cotangent, attn_full, ffn_full, gain_low):
    (
        inputs,
        first_scale,
        normed,
        query_act,
        key_act,
        value_act,
        gate_pre,
        fading_mask,
        weights_low,
        attended,
        out_scale,
        normal_out,
        gate_sig,
        gated_out,
        middle,
        second_scale,
        normed_two,
        up_one,
        up_two,
        product,
    ) = stored
    length, model_width = inputs.shape
    head_count = fading_mask.shape[0]
    head_size = model_width // head_count
    hidden = ffn_full.shape[1]
    gain_full = gain_low.astype(F32)
    grad_out = cotangent.astype(F32)
    grad_product = lax.dot_general(cotangent, ffn_full[2], ROWS_BY_ROWS, preferred_element_type=F32)
    grad_down = lax.dot_general(product, cotangent, TOKENS_OUT, preferred_element_type=F32)
    grad_pair = jnp.concatenate([grad_product * up_two, grad_product * up_one], axis=1).astype(B16)
    grad_normed_two = jnp.dot(
        grad_pair, ffn_full[:2].reshape(2 * hidden, model_width), preferred_element_type=F32
    )
    grad_up = lax.dot_general(
        grad_pair, normed_two, TOKENS_OUT, preferred_element_type=F32
    ).reshape(2, hidden, model_width)
    gain_two = jnp.sum(grad_normed_two * middle * second_scale, axis=0)
    grad_middle = grad_out + rms_back(middle, second_scale, grad_normed_two * gain_full[1])
    middle_low = grad_middle.astype(B16)
    grad_gated = jnp.dot(middle_low, attn_full[4], preferred_element_type=F32)
    grad_outproj = lax.dot_general(middle_low, gated_out, TOKENS_OUT, preferred_element_type=F32)
    grad_normal = grad_gated * gate_sig
    grad_gate = grad_gated * normal_out * gate_sig * (1.0 - gate_sig)
    gain_three = jnp.sum(grad_normal * attended * out_scale, axis=0)
    grad_attended = (
        rms_back(attended, out_scale, grad_normal * gain_full[2])
        .astype(B16)
        .reshape(length, head_count, head_size)
    )
    query_heads = query_act.reshape(length, head_count, head_size)
    key_heads = key_act.reshape(length, head_count, head_size)
    value_heads = value_act.reshape(length, head_count, head_size)
    grad_weights = jnp.einsum(
        "the,she->hts", grad_attended, value_heads, preferred_element_type=F32
    )
    grad_values = jnp.einsum(
        "hts,the->she", weights_low, grad_attended, preferred_element_type=F32
    ).reshape(length, model_width)
    grad_scores = (grad_weights * fading_mask).astype(B16)
    grad_queries = jnp.einsum(
        "hts,she->the", grad_scores, key_heads, preferred_element_type=F32
    ).reshape(length, model_width)
    grad_keys = jnp.einsum(
        "hts,the->she", grad_scores, query_heads, preferred_element_type=F32
    ).reshape(length, model_width)
    grad_mixed = jnp.concatenate(
        [
            jnp.where(query_act > 0, grad_queries, 0.0),
            jnp.where(key_act > 0, grad_keys, 0.0),
            grad_values,
            grad_gate,
        ],
        axis=1,
    ).astype(B16)
    grad_normed = jnp.dot(
        grad_mixed, attn_full[:4].reshape(4 * model_width, model_width), preferred_element_type=F32
    )
    grad_inner = lax.dot_general(
        grad_mixed, normed, TOKENS_OUT, preferred_element_type=F32
    ).reshape(4, model_width, model_width)
    gain_one = jnp.sum(grad_normed * inputs * first_scale, axis=0)
    grad_inputs = grad_middle + rms_back(inputs, first_scale, grad_normed * gain_full[0])
    grad_attn = jnp.concatenate([grad_inner, grad_outproj[None]], axis=0)
    grad_ffn = jnp.concatenate([grad_up, grad_down[None]], axis=0)
    grad_gain = jnp.stack([gain_one, gain_two, gain_three])
    return (grad_inputs, grad_attn, grad_ffn, grad_gain)


def newton_schulz(received):
    results = []
    for member in range(received.shape[1]):
        current = received[:, member].reshape(-1, received.shape[3])
        for iteration in range(NS_STEPS):
            local_gram = lax.dot_general(
                current, current, TOKENS_OUT, precision=HIGH, preferred_element_type=F32
            )
            gram_sum = lax.psum(local_gram.astype(jnp.bfloat16), "dp").astype(jnp.float32)
            if iteration == 0:
                norm_value = jnp.sqrt(jnp.trace(gram_sum)) + NS_EPS
                current = current / norm_value
                gram_sum = gram_sum / (norm_value * norm_value)
            partial_prod = jnp.dot(current, gram_sum, precision=HIGH)
            current = (
                NS_A * current
                + NS_B * partial_prod
                + NS_C * jnp.dot(partial_prod, gram_sum, precision=HIGH)
            )
        results.append(current.reshape(received.shape[0], received.shape[2], received.shape[3]))
    return jnp.stack(results, axis=1)


def on_device(
    tokens,
    segment_ids,
    decay_rate,
    cotangent,
    attn_master,
    ffn_master,
    gains,
    attn_moment,
    ffn_moment,
    gain_first,
    gain_second,
):
    attn_low = attn_master.astype(B16)
    ffn_low = ffn_master.astype(B16)
    gain_low = gains.astype(B16)
    attn_full, ffn_full, gain_whole = (
        lax.all_gather(attn_low, ("dp", "fsdp"), axis=1, tiled=True),
        lax.all_gather(ffn_low, ("dp", "fsdp"), axis=1, tiled=True),
        lax.all_gather(gain_low, ("dp", "fsdp"), axis=1, tiled=True),
    )
    out, stored = forward(tokens, segment_ids[0], decay_rate, attn_full, ffn_full, gain_whole)
    attn_full, ffn_full, gain_whole = (
        lax.all_gather(attn_low, ("dp", "fsdp"), axis=1, tiled=True),
        lax.all_gather(ffn_low, ("dp", "fsdp"), axis=1, tiled=True),
        lax.all_gather(gain_low, ("dp", "fsdp"), axis=1, tiled=True),
    )
    redone, stored = forward(tokens, segment_ids[0], decay_rate, attn_full, ffn_full, gain_whole)
    x_grad, grad_attn, grad_ffn, grad_gain = backward(
        stored, cotangent, attn_full, ffn_full, gain_whole
    )
    attn_grad, ffn_grad, gain_grad = (
        lax.psum_scatter(grad_attn, ("dp", "fsdp"), scatter_dimension=1, tiled=True),
        lax.psum_scatter(grad_ffn, ("dp", "fsdp"), scatter_dimension=1, tiled=True),
        lax.psum_scatter(grad_gain, ("dp", "fsdp"), scatter_dimension=1, tiled=True),
    )
    attn_state = MOMENT_DECAY * attn_moment + (1.0 - MOMENT_DECAY) * attn_grad
    ffn_state = MOMENT_DECAY * ffn_moment + (1.0 - MOMENT_DECAY) * ffn_grad
    attn_count = attn_state.shape[0]
    attn_rows = attn_state.shape[1]
    slot_rows = ffn_state.shape[1]
    model_width = ffn_state.shape[2]
    padded = jnp.pad(attn_state, ((0, 0), (0, slot_rows - attn_rows), (0, 0)))
    stacked = jnp.concatenate([padded, ffn_state], axis=0)
    owners = lax.axis_size("fsdp")
    outgoing = stacked.reshape(owners, stacked.shape[0] // owners, slot_rows, model_width)
    orthogonal = newton_schulz(
        lax.all_to_all(
            outgoing.astype(jnp.bfloat16), "fsdp", split_axis=0, concat_axis=0, tiled=True
        ).astype(outgoing.dtype)
    )
    returned = (
        lax.all_to_all(as_sent(orthogonal), "fsdp", split_axis=0, concat_axis=0, tiled=True)
        .astype(orthogonal.dtype)
        .reshape(stacked.shape)
    )
    attn_new = attn_master - LR_MUON * returned[:attn_count, :attn_rows]
    ffn_new = ffn_master - LR_MUON * math.sqrt(FF / D) * returned[attn_count:]
    first_new = BETA_ONE * gain_first + (1.0 - BETA_ONE) * gain_grad
    second_new = BETA_TWO * gain_second + (1.0 - BETA_TWO) * gain_grad * gain_grad
    gains_new = gains - LR_GAIN * first_new / (jnp.sqrt(second_new) + ADAM_EPS)
    return (
        out,
        x_grad,
        attn_grad,
        ffn_grad,
        gain_grad,
        attn_state,
        ffn_state,
        attn_new,
        ffn_new,
        attn_new.astype(B16),
        ffn_new.astype(B16),
        gains_new,
        first_new,
        second_new,
    )


def solution(mesh):
    return jax.shard_map(
        on_device,
        mesh=mesh,
        in_specs=(
            P(("dp", "fsdp"), None),
            P(("dp", "fsdp"), None),
            P(),
            P(("dp", "fsdp"), None),
            P(None, ("dp", "fsdp"), None),
            P(None, ("dp", "fsdp"), None),
            P(None, ("dp", "fsdp")),
            P(None, ("dp", "fsdp"), None),
            P(None, ("dp", "fsdp"), None),
            P(None, ("dp", "fsdp")),
            P(None, ("dp", "fsdp")),
        ),
        out_specs=(
            P(("dp", "fsdp"), None),
            P(("dp", "fsdp"), None),
            P(None, ("dp", "fsdp"), None),
            P(None, ("dp", "fsdp"), None),
            P(None, ("dp", "fsdp")),
            P(None, ("dp", "fsdp"), None),
            P(None, ("dp", "fsdp"), None),
            P(None, ("dp", "fsdp"), None),
            P(None, ("dp", "fsdp"), None),
            P(None, ("dp", "fsdp"), None),
            P(None, ("dp", "fsdp"), None),
            P(None, ("dp", "fsdp")),
            P(None, ("dp", "fsdp")),
            P(None, ("dp", "fsdp")),
        ),
        check_vma=False,
    )
```

profile of v0, /device:TPU:0, one launch (start us, length us, event | category | flops | bytes accessed | tf_op | source)
XLA Modules:
  0.0 2270.2 jit_solution(9891593484620817852)
XLA Ops:
  11.5 71.5 %all-gather = bf16[32,32,3]{1,2,0:T(4,128)(2,1)S(1)} all-gather(bf16[1,32,3]{1,2,0:T(4,128)(2,1)S(1)} %convert_bitcast_fusion), channel_id=1, replica_groups=mesh['dp'=8,'fsdp'=4] {'dp','fsdp'}, dimensions={0}, use_global_device_ids=true | all-gather | bytes 6336 | tf_op jit(solution)/shard_map/all_gather | solution.py:261
  85.3 15.1 all-gather.4.cloned.1.call-done
  142.2 77.2 %all-gather.6.cloned.1.call-done = bf16[3,2816,1024]{2,1,0:T(8,128)(2,1)} async-done(((bf16[3,88,1024]{2,1,0:T(8,128)(2,1)}), bf16[3,2816,1024]{2,1,0:T(8,128)(2,1)}) %all-gather.6.cloned.1.call-update) | async-done | bytes 17301520 | tf_op jit(solution)/shard_map/all_gather | solution.py:260
  229.7 9.0 fusion.59
  238.7 9.7 multiply_convert_fusion.3
  248.4 11.8 multiply_reduce_fusion.1
  279.3 17.1 multiply_convert_fusion
  310.4 8.2 fusion.46
  332.5 13.8 fusion.4
  346.3 20.4 pad_maximum_fusion
  366.8 408.9 %reduce-scatter.6.cloned.1.call-done = f32[5,32,1024]{2,1,0:T(8,128)} async-done(((f32[5,1024,1024]{2,1,0:T(8,128)}), f32[5,32,1024]{2,1,0:T(8,128)}) %reduce-scatter.6.cloned.1.call-update) | async-done | bytes 655376 | tf_op jit(solution)/shard_map/reduce_scatter | solution.py:274
  777.8 732.7 %reduce-scatter.8.cloned.1.call-done = f32[3,88,1024]{2,1,0:T(8,128)} async-done(((f32[3,2816,1024]{2,1,0:T(8,128)}), f32[3,88,1024]{2,1,0:T(8,128)}) %reduce-scatter.8.cloned.1.call-update) | async-done | bytes 1081360 | tf_op jit(solution)/shard_map/reduce_scatter | solution.py:275
  1513.1 38.0 %all_to_all.10 = bf16[4,2,88,1024]{3,2,1,0:T(8,128)(2,1)S(1)} all-to-all(bf16[4,2,88,1024]{3,2,1,0:T(8,128)(2,1)S(1)} %bitcast.176), channel_id=1, replica_groups=mesh['dp'=8,'fsdp'=4] {'fsdp'}, dimensions={0} | all-to-all | bytes 2883584 | tf_op jit(solution)/shard_map/all_to_all | solution.py:289
  1558.6 77.0 %all-reduce.20.cloned.1.call-done = (bf16[1024,1024]{1,0:T(8,128)(2,1)}, bf16[1024,1024]{1,0:T(8,128)(2,1)}) async-done(((bf16[1024,1024]{1,0:T(8,128)(2,1)}, bf16[1024,1024]{1,0:T(8,128)(2,1)}), (bf16[1024,1024]{1,0:T(8,128)(2,1)}, bf16[1024,1024]{1,0:T(8,128)(2,1)})) %all-reduce.20.cloned.1.call-update) | async-done | bytes 4194320 | tf_op jit(solution)/shard_map/psum | solution.py:227
  1680.1 80.8 %all-reduce.18.cloned.1.call-done = (bf16[1024,1024]{1,0:T(8,128)(2,1)}, bf16[1024,1024]{1,0:T(8,128)(2,1)}) async-done(((bf16[1024,1024]{1,0:T(8,128)(2,1)}, bf16[1024,1024]{1,0:T(8,128)(2,1)}), (bf16[1024,1024]{1,0:T(8,128)(2,1)}, bf16[1024,1024]{1,0:T(8,128)(2,1)})) %all-reduce.18.cloned.1.call-update) | async-done | bytes 4194320 | tf_op jit(solution)/shard_map/psum | solution.py:227
  1772.9 8.5 convolution_convert_fusion.6
  1789.6 80.8 %all-reduce.16.cloned.1.call-done = (bf16[1024,1024]{1,0:T(8,128)(2,1)}, bf16[1024,1024]{1,0:T(8,128)(2,1)}) async-done(((bf16[1024,1024]{1,0:T(8,128)(2,1)}, bf16[1024,1024]{1,0:T(8,128)(2,1)}), (bf16[1024,1024]{1,0:T(8,128)(2,1)}, bf16[1024,1024]{1,0:T(8,128)(2,1)})) %all-reduce.16.cloned.1.call-update) | async-done | bytes 4194320 | tf_op jit(solution)/shard_map/psum | solution.py:227
  1882.5 8.4 convolution_convert_fusion.5
  1899.3 80.8 %all-reduce.14.cloned.1.call-done = (bf16[1024,1024]{1,0:T(8,128)(2,1)}, bf16[1024,1024]{1,0:T(8,128)(2,1)}) async-done(((bf16[1024,1024]{1,0:T(8,128)(2,1)}, bf16[1024,1024]{1,0:T(8,128)(2,1)}), (bf16[1024,1024]{1,0:T(8,128)(2,1)}, bf16[1024,1024]{1,0:T(8,128)(2,1)})) %all-reduce.14.cloned.1.call-update) | async-done | bytes 4194320 | tf_op jit(solution)/shard_map/psum | solution.py:227
  1992.1 8.6 convolution_convert_fusion.4
  2008.8 81.1 %all-reduce.12.cloned.1.call-done = (bf16[1024,1024]{1,0:T(8,128)(2,1)}, bf16[1024,1024]{1,0:T(8,128)(2,1)}) async-done(((bf16[1024,1024]{1,0:T(8,128)(2,1)}, bf16[1024,1024]{1,0:T(8,128)(2,1)}), (bf16[1024,1024]{1,0:T(8,128)(2,1)}, bf16[1024,1024]{1,0:T(8,128)(2,1)})) %all-reduce.12.cloned.1.call-update) | async-done | bytes 4194320 | tf_op jit(solution)/shard_map/psum | solution.py:227
  2107.8 10.7 fusion.19
  2120.3 8.4 add_convert_fusion
  2130.6 127.1 %reduce-scatter.10.cloned.1.call-done = f32[32,3]{1,0:T(8,128)} async-done(((f32[1024,3]{1,0:T(8,128)}), f32[32,3]{1,0:T(8,128)}) %reduce-scatter.10.cloned.1.call-update) | async-done | bytes 400
  (230 shorter events, 248.3 us)
Async XLA Ops:
  7.2 93.2 %all-gather.4.cloned.1.call-start = ((), (), s32[]{:S(2)}) async-start(), calls=%async_computation.5 | async-start | bytes 10813440 | tf_op jit(solution)/shard_map/all_gather | solution.py:259
  9.1 75.1 %copy-start.18 = (bf16[512,1024]{1,0:T(8,128)(2,1)S(1)}, bf16[512,1024]{1,0:T(8,128)(2,1)}, u32[]{:S(2)}) copy-start(bf16[512,1024]{1,0:T(8,128)(2,1)} %param.11) | copy-start | bytes 3145732
  9.1 75.9 %copy-start.46 = (s32[1,512]{1,0:T(1,128)S(1)}, s32[1,512]{1,0:T(1,128)}, u32[]{:S(2)}) copy-start(s32[1,512]{1,0:T(1,128)} %param.12) | copy-start | bytes 6148
  9.1 210.2 %all-gather.6.cloned.1.call-start = ((), (), s32[]{:S(2)}) async-start(), calls=%async_computation.6 | async-start | bytes 17842176 | tf_op jit(solution)/shard_map/all_gather | solution.py:260
  11.4 764.3 %reduce-scatter.6.cloned.1.call-start = ((), (), s32[]{:S(2)}) async-start(), calls=%async_computation.7 | async-start | bytes 21626880 | tf_op jit(solution)/shard_map/reduce_scatter | solution.py:274
  248.3 11.8 copy-start.58
  248.3 11.8 copy-start.39
  279.3 17.1 copy-start.13
  326.1 1184.4 %reduce-scatter.8.cloned.1.call-start = ((), (), s32[]{:S(2)}) async-start(), calls=%async_computation.8 | async-start | bytes 35684352 | tf_op jit(solution)/shard_map/reduce_scatter | solution.py:275
  366.7 409.0 %copy-start.45 = (f32[5,32,1024]{2,1,0:T(8,128)S(1)}, f32[5,32,1024]{2,1,0:T(8,128)}, u32[]{:S(2)}) copy-start(f32[5,32,1024]{2,1,0:T(8,128)} %param.18) | copy-start | bytes 1966084
  366.7 1143.8 %copy-start.37 = (f32[3,88,1024]{2,1,0:T(8,128)S(1)}, f32[3,88,1024]{2,1,0:T(8,128)}, u32[]{:S(2)}) copy-start(f32[3,88,1024]{2,1,0:T(8,128)} %param.19) | copy-start | bytes 3244036
  366.8 1268.9 %all-reduce.20.cloned.1.call-start = ((), (), s32[]{:S(2)}) async-start(), calls=%async_computation.14 | async-start | bytes 8388608 | tf_op jit(solution)/shard_map/psum | solution.py:227
  1556.5 204.4 %all-reduce.18.cloned.1.call-start = ((), (), s32[]{:S(2)}) async-start(), calls=%async_computation.13 | async-start | bytes 8388608 | tf_op jit(solution)/shard_map/psum | solution.py:227
  1679.8 190.7 %all-reduce.16.cloned.1.call-start = ((), (), s32[]{:S(2)}) async-start(), calls=%async_computation.12 | async-start | bytes 8388608 | tf_op jit(solution)/shard_map/psum | solution.py:227
  1789.4 190.6 %all-reduce.14.cloned.1.call-start = ((), (), s32[]{:S(2)}) async-start(), calls=%async_computation.11 | async-start | bytes 8388608 | tf_op jit(solution)/shard_map/psum | solution.py:227
  1877.3 13.5 copy-start.1
  1898.9 81.1 %copy-start.2 = (f32[352,1024]{1,0:T(8,128)S(1)}, f32[352,1024]{1,0:T(8,128)}, u32[]{:S(2)}) copy-start(f32[352,1024]{1,0:T(8,128)} %copy-done.1) | copy-start | bytes 4325380
  1899.0 190.9 %all-reduce.12.cloned.1.call-start = ((), (), s32[]{:S(2)}) async-start(), calls=%async_computation.10 | async-start | bytes 8388608 | tf_op jit(solution)/shard_map/psum | solution.py:227
  2103.0 156.0 %all-to-all-start.1 = ((bf16[4,2,88,1024]{3,2,1,0:T(8,128)(2,1)}), bf16[4,2,88,1024]{3,2,1,0:T(8,128)(2,1)S(1)}, u32[]{:S(2)}, u32[]{:S(2)}) async-start(bf16[4,2,88,1024]{3,2,1,0:T(8,128)(2,1)} %pad_maximum_fusion.6), calls=%async_computation.3 | async-start | bytes 2883584 | tf_op jit(solution)/shard_map/all_to_all | solution.py:294
  2107.8 10.8 copy-start.52
  2107.8 149.9 %reduce-scatter.10.cloned.1.call-start = ((), (), s32[]{:S(2)}) async-start(), calls=%async_computation.9 | async-start | bytes 540672
  2128.7 129.8 %copy-start.50 = (f32[3,32]{1,0:T(4,128)S(1)}, f32[3,32]{1,0:T(4,128)}, u32[]{:S(2)}) copy-start(f32[3,32]{1,0:T(4,128)} %param.17) | copy-start | bytes 1156
  2128.7 129.8 %copy-start.53 = (f32[3,32]{1,0:T(4,128)S(1)}, f32[3,32]{1,0:T(4,128)}, u32[]{:S(2)}) copy-start(f32[3,32]{1,0:T(4,128)} %param.20) | copy-start | bytes 1156
  2128.7 129.8 %copy-start.54 = (f32[3,32]{1,0:T(4,128)S(1)}, f32[3,32]{1,0:T(4,128)}, u32[]{:S(2)}) copy-start(f32[3,32]{1,0:T(4,128)} %param.21) | copy-start | bytes 1156
  (48 other events, 218.7 us)
Sparse Core Ops, SparseCore 0:
  11.6 88.7 all-gather.3
  104.0 115.3 all-gather.5
  326.2 449.4 reduce-scatter.5
  778.5 731.9 reduce-scatter.7
  1556.6 78.9 all-reduce.19
  1679.9 80.8 all-reduce.17
  1789.5 80.8 all-reduce.15
  1899.1 80.8 all-reduce.13
  2008.9 80.8 all-reduce.11
  2119.7 137.8 reduce-scatter.9
where the time goes:
time: 2270 us
  waiting for transfers between devices  1760 us (78%)
  matrix products  273 us (12%)
  blocking collectives  109 us (5%)
  other arithmetic  63 us (3%)
  local copies, waits for them, and re-layouts  40.4 us (2%)
    reduce_scatter x1, waiting for transfers between devices, on_device(): lax.psum_scatter(grad_ffn, ('dp', 'fsdp'), scatter_dimension=1, tiled=True)  733 us
    reduce_scatter x1, waiting for transfers between devices, on_device(): lax.psum_scatter(grad_attn, ('dp', 'fsdp'), scatter_dimension=1, tiled=True)  409 us
    psum x5, waiting for transfers between devices, newton_schulz(): lax.psum(local_gram.astype(jnp.bfloat16), 'dp').astype(jnp.float32)  400 us
    unnamed x11, waiting for transfers between devices  127 us
    all_gather x1, waiting for transfers between devices, on_device(): lax.all_gather(ffn_low, ('dp', 'fsdp'), axis=1, tiled=True)  77.2 us
    all_gather x1, blocking collectives, on_device(): lax.all_gather(gain_low, ('dp', 'fsdp'), axis=1, tiled=True)  71.5 us
    dot_general x10, matrix products, newton_schulz(): lax.dot_general(current, current, TOKENS_OUT, precision=HIGH, preferred_e...  71 us
  transfers between devices with their start and end apart: 11, of which 10 were waited for; matrix products, arithmetic and copies ran while one was open for 5% of the time, Pallas kernels for 0%

commit v1 on v0

--- a/solution.py
+++ b/solution.py
@@ -10,7 +10,6 @@
 NS_STEPS = 5
 
 
-HIGH = lax.Precision.HIGHEST
 EPS = 1e-06
 NS_EPS = 1e-07
 NS_A = 3.4445
@@ -26,14 +25,6 @@
 B16 = jnp.bfloat16
 ROWS_BY_ROWS = (((1,), (1,)), ((), ()))
 TOKENS_OUT = (((0,), (0,)), ((), ()))
-
-
-def as_sent(shard):
-
-    def short(part):
-        return part.astype(jnp.bfloat16) if part.dtype == jnp.float32 else part
-
-    return jax.tree.map(short, shard)
 
 
 def rms_scale(series):
@@ -210,33 +201,168 @@
     ).reshape(4, model_width, model_width)
     gain_one = jnp.sum(grad_normed * inputs * first_scale, axis=0)
     grad_inputs = grad_middle + rms_back(inputs, first_scale, grad_normed * gain_full[0])
-    grad_attn = jnp.concatenate([grad_inner, grad_outproj[None]], axis=0)
-    grad_ffn = jnp.concatenate([grad_up, grad_down[None]], axis=0)
     grad_gain = jnp.stack([gain_one, gain_two, gain_three])
-    return (grad_inputs, grad_attn, grad_ffn, grad_gain)
-
-
-def newton_schulz(received):
-    results = []
-    for member in range(received.shape[1]):
-        current = received[:, member].reshape(-1, received.shape[3])
-        for iteration in range(NS_STEPS):
-            local_gram = lax.dot_general(
-                current, current, TOKENS_OUT, precision=HIGH, preferred_element_type=F32
+    return (grad_inputs, (grad_inner, grad_outproj, grad_up, grad_down), grad_gain)
+
+
+def plane_bits():
+    return lax.axis_size("dp").bit_length() - 1
+
+
+def swap_bit(value, bit):
+    count = lax.axis_size("dp")
+    return lax.ppermute(value, "dp", [(i, i ^ (1 << bit)) for i in range(count)])
+
+
+def choose(term, dims, bit, other):
+    place = (lax.axis_index("dp") >> bit) & 1
+    index = 1 - place if other else place
+    axis = dims.index(bit)
+    return lax.dynamic_index_in_dim(term, index, axis, keepdims=False)
+
+
+def plane_sum(pieces, order):
+    bits = plane_bits()
+    terms = [(pieces, list(range(bits))[::-1])]
+    for bit in order:
+        sent = sum(choose(t, dims, bit, True).astype(F32) for t, dims in terms).astype(B16)
+        left = terms[-1][1]
+        kept = [(choose(t, dims, bit, False), [b for b in dims if b != bit]) for t, dims in terms]
+        received = swap_bit(sent, bit)
+        terms = kept + [(received, [b for b in left if b != bit])]
+    return sum(t.astype(F32) for t, _ in terms)
+
+
+def scatter_sum(grad):
+    count, rows, columns = grad.shape
+    planes, lines = lax.axis_size("dp"), lax.axis_size("fsdp")
+    bits = plane_bits()
+    own = rows // (planes * lines)
+    blocks = grad.astype(B16).reshape((count,) + (2,) * bits + (lines, own, columns))
+    blocks = jnp.moveaxis(blocks, 0, bits)
+    half = lines // 2
+    rest = list(range(1, bits))
+    core_first = [0] + rest
+    core_back = [0] + rest[::-1]
+    one = plane_sum(blocks[..., :half, :, :], core_first)
+    two = plane_sum(blocks[..., half:, :, :], core_back)
+    mine = jnp.concatenate([one, two], axis=1).astype(B16)
+    return lax.psum_scatter(mine, "fsdp", scatter_dimension=1, tiled=True).astype(F32).reshape(count, own, columns)
+
+
+def gain_sum(grad):
+    rows, columns = grad.shape
+    total = lax.axis_size("dp") * lax.axis_size("fsdp")
+    blocks = jnp.transpose(grad.reshape(rows, total, columns // total), (1, 0, 2))
+    return jnp.sum(lax.all_to_all(blocks, ("dp", "fsdp"), 0, 0, tiled=True), axis=0)
+
+
+def diagonal(size):
+    return lax.broadcasted_iota(jnp.int32, (size, size), 0) == lax.broadcasted_iota(jnp.int32, (size, size), 1)
+
+
+def low_dot(left, right):
+    return jnp.dot(left.astype(B16), right.astype(B16), preferred_element_type=F32)
+
+
+def gram_orthogonalize(rows, gram):
+    size = gram.shape[0]
+    eye = diagonal(size)
+    square = jnp.sum(jnp.where(eye, gram, 0.0))
+    norm = jnp.sqrt(square) + NS_EPS
+    gram = gram / (norm * norm)
+    current = rows.astype(F32) / norm
+    for iteration in range(NS_STEPS):
+        shift = jnp.sum(jnp.where(eye, gram, 0.0)) / size
+        rest = gram - jnp.where(eye, shift, 0.0)
+        squared = low_dot(rest, rest) + 2.0 * shift * rest + jnp.where(eye, shift * shift, 0.0)
+        factor = NS_A + NS_B * shift + NS_C * shift * shift
+        poly = NS_B * gram + NS_C * squared + jnp.where(eye, NS_A - factor, 0.0)
+        current = factor * current + low_dot(current, poly)
+        if iteration + 1 < NS_STEPS:
+            half_way = low_dot(rest, poly) + shift * poly + factor * rest
+            gram = (
+                low_dot(half_way, poly)
+                + (shift * factor) * poly
+                + factor * half_way
+                + jnp.where(eye, shift * factor * factor, 0.0)
             )
-            gram_sum = lax.psum(local_gram.astype(jnp.bfloat16), "dp").astype(jnp.float32)
-            if iteration == 0:
-                norm_value = jnp.sqrt(jnp.trace(gram_sum)) + NS_EPS
-                current = current / norm_value
-                gram_sum = gram_sum / (norm_value * norm_value)
-            partial_prod = jnp.dot(current, gram_sum, precision=HIGH)
-            current = (
-                NS_A * current
-                + NS_B * partial_prod
-                + NS_C * jnp.dot(partial_prod, gram_sum, precision=HIGH)
+    return current
+
+
+def one_way(value, bit, lower, both=True):
+    count = lax.axis_size("dp")
+    start = 1 if lower else 0
+    return lax.ppermute(
+        value, "dp", [(i, i ^ (1 << bit)) for i in range(count) if (i & 1) == start]
+    )
+
+
+def swap_large(value, bit):
+    count = lax.axis_size("dp")
+    return lax.ppermute(value, "dp", [(i, i ^ (1 << bit)) for i in range(count) if (i & 1) == 0])
+
+
+def orthogonal_rows(attn_state, ffn_state):
+    lines = lax.axis_size("fsdp")
+    attn_count, small, columns = attn_state.shape
+    ffn_count, large, _ = ffn_state.shape
+    attn_low = attn_state.astype(B16)
+    ffn_low = ffn_state.astype(B16)
+    at_one = min(lines, attn_count)
+    spare = attn_count - at_one
+    top = jnp.pad(
+        jnp.concatenate([ffn_low, jnp.pad(attn_low[at_one:], ((0, 0), (0, large - small), (0, 0)))]),
+        ((0, lines - ffn_count - spare), (0, 0), (0, 0)),
+    )
+    low_part = jnp.pad(attn_low[:at_one], ((0, lines - at_one), (0, 0), (0, 0)))
+    outgoing = jnp.concatenate([top, low_part], axis=1)
+    arrived = lax.all_to_all(outgoing, "fsdp", split_axis=0, concat_axis=0, tiled=True)
+    big, little = arrived[:, :large], arrived[:, large:]
+    big_other = one_way(big, 0, True)
+    little_other = one_way(little, 0, False)
+    at_core = lax.axis_index("dp") & 1
+    block, little_block = lines * large, lines * small
+    fill = ((0, block - little_block), (0, 0))
+    mine = jnp.stack(
+        [
+            jnp.where(at_core == 0, big.reshape(block, columns), jnp.pad(little.reshape(little_block, columns), fill)),
+            jnp.where(
+                at_core == 0,
+                big_other.reshape(block, columns),
+                jnp.pad(little_other.reshape(little_block, columns), fill),
+            ),
+        ]
+    )
+    rest = list(range(1, plane_bits()))
+    held = [mine[0:1], mine[1:2]]
+    for step in range(len(rest)):
+        for color in range(2):
+            bit = rest[step] if color == 0 else rest[::-1][step]
+            part = held[color]
+            came = jnp.concatenate(
+                [swap_bit(part[:, :little_block], bit), swap_large(part[:, little_block:], bit)], axis=1
             )
-        results.append(current.reshape(received.shape[0], received.shape[2], received.shape[3]))
-    return jnp.stack(results, axis=1)
+            held[color] = jnp.concatenate([part, came])
+    gram = sum(
+        lax.dot_general(
+            part.reshape(-1, columns), part.reshape(-1, columns), TOKENS_OUT, preferred_element_type=F32
+        )
+        for part in held
+    )
+    result = gram_orthogonalize(mine.reshape(2 * block, columns), gram).astype(B16).reshape(2, block, columns)
+    own, other = result[0], result[1]
+    back_big = one_way(other, 0, False)
+    back_little = one_way(other[:little_block], 0, True)
+    big_out = jnp.where(at_core == 0, own, back_big).reshape(lines, large, columns)
+    little_out = jnp.where(at_core == 0, back_little, own[:little_block]).reshape(lines, small, columns)
+    returned = lax.all_to_all(
+        jnp.concatenate([big_out, little_out], axis=1), "fsdp", split_axis=0, concat_axis=0, tiled=True
+    ).astype(F32)
+    attn_out = jnp.concatenate(
+        [returned[:at_one, large:], returned[ffn_count : ffn_count + spare, :small]], axis=0
+    )
+    return attn_out, returned[:ffn_count, :large]
 
 
 def on_device(
@@ -261,42 +387,20 @@
         lax.all_gather(gain_low, ("dp", "fsdp"), axis=1, tiled=True),
     )
     out, stored = forward(tokens, segment_ids[0], decay_rate, attn_full, ffn_full, gain_whole)
-    attn_full, ffn_full, gain_whole = (
-        lax.all_gather(attn_low, ("dp", "fsdp"), axis=1, tiled=True),
-        lax.all_gather(ffn_low, ("dp", "fsdp"), axis=1, tiled=True),
-        lax.all_gather(gain_low, ("dp", "fsdp"), axis=1, tiled=True),
-    )
-    redone, stored = forward(tokens, segment_ids[0], decay_rate, attn_full, ffn_full, gain_whole)
-    x_grad, grad_attn, grad_ffn, grad_gain = backward(
+    x_grad, grads, grad_gain = backward(
         stored, cotangent, attn_full, ffn_full, gain_whole
     )
-    attn_grad, ffn_grad, gain_grad = (
-        lax.psum_scatter(grad_attn, ("dp", "fsdp"), scatter_dimension=1, tiled=True),
-        lax.psum_scatter(grad_ffn, ("dp", "fsdp"), scatter_dimension=1, tiled=True),
-        lax.psum_scatter(grad_gain, ("dp", "fsdp"), scatter_dimension=1, tiled=True),
-    )
+    grad_inner, grad_outproj, grad_up, grad_down = grads
+    down_sum = scatter_sum(grad_down[None])
+    up_sum = scatter_sum(grad_up)
+    attn_grad = jnp.concatenate([scatter_sum(grad_inner), scatter_sum(grad_outproj[None])], axis=0)
+    ffn_grad = jnp.concatenate([up_sum, down_sum], axis=0)
+    gain_grad = gain_sum(grad_gain)
     attn_state = MOMENT_DECAY * attn_moment + (1.0 - MOMENT_DECAY) * attn_grad
     ffn_state = MOMENT_DECAY * ffn_moment + (1.0 - MOMENT_DECAY) * ffn_grad
-    attn_count = attn_state.shape[0]
-    attn_rows = attn_state.shape[1]
-    slot_rows = ffn_state.shape[1]
-    model_width = ffn_state.shape[2]
-    padded = jnp.pad(attn_state, ((0, 0), (0, slot_rows - attn_rows), (0, 0)))
-    stacked = jnp.concatenate([padded, ffn_state], axis=0)
-    owners = lax.axis_size("fsdp")
-    outgoing = stacked.reshape(owners, stacked.shape[0] // owners, slot_rows, model_width)
-    orthogonal = newton_schulz(
-        lax.all_to_all(
-            outgoing.astype(jnp.bfloat16), "fsdp", split_axis=0, concat_axis=0, tiled=True
-        ).astype(outgoing.dtype)
-    )
-    returned = (
-        lax.all_to_all(as_sent(orthogonal), "fsdp", split_axis=0, concat_axis=0, tiled=True)
-        .astype(orthogonal.dtype)
-        .reshape(stacked.shape)
-    )
-    attn_new = attn_master - LR_MUON * returned[:attn_count, :attn_rows]
-    ffn_new = ffn_master - LR_MUON * math.sqrt(FF / D) * returned[attn_count:]
+    attn_orth, ffn_orth = orthogonal_rows(attn_state, ffn_state)
+    attn_new = attn_master - LR_MUON * attn_orth
+    ffn_new = ffn_master - LR_MUON * math.sqrt(FF / D) * ffn_orth
     first_new = BETA_ONE * gain_first + (1.0 - BETA_ONE) * gain_grad
     second_new = BETA_TWO * gain_second + (1.0 - BETA_TWO) * gain_grad * gain_grad
     gains_new = gains - LR_GAIN * first_new / (jnp.sqrt(second_new) + ADAM_EPS)

time: 2270 us -> 843 us (0.37)
  waiting for transfers between devices: 1760 us -> 287 us
  matrix products: 273 us -> 216 us
  local copies, waits for them, and re-layouts: 40.4 us -> 89.6 us
  starting transfers between devices: 6.19 us -> 53.1 us
  blocking collectives: 109 us -> 71.3 us
  other arithmetic: 63 us -> 88.2 us
    reduce_scatter x2 -> x4, waiting for transfers between devices: 1140 us -> 30.8 us  [scatter_sum(): lax.psum_scatter(mine, 'fsdp', scatter_dimension=1, tiled=True).astype(F32)]
    psum x5 -> x0, waiting for transfers between devices: 400 us -> none  [newton_schulz(): lax.psum(local_gram.astype(jnp.bfloat16), 'dp').astype(jnp.float32)]
    unnamed x11 -> x6, waiting for transfers between devices: 127 us -> 0.1 us
    ppermute x0 -> x36, waiting for transfers between devices: none -> 125 us  [the longest x28 125 us: swap_bit(): return lax.ppermute(value, 'dp', [(i, i ^ 1 << bit) for i in range(count)])]
    all_to_all x1 -> x3, waiting for transfers between devices: 0.01 us -> 40.5 us  [the longest x1 24.2 us: orthogonal_rows(): lax.all_to_all(outgoing, 'fsdp', split_axis=0, concat_axis=0, tiled=True)]
    ppermute x0 -> x36, starting transfers between devices: none -> 40.4 us  [the longest x28 21.4 us: swap_bit(): return lax.ppermute(value, 'dp', [(i, i ^ 1 << bit) for i in range(count)])]
    dot_general x30 -> x19, matrix products: 139 us -> 98.8 us  [the longest x17 89.1 us: low_dot(): jnp.dot(left.astype(B16), right.astype(B16), preferred_element_type=F32)]
    all_to_all x1 -> x0, blocking collectives: 38 us -> none  [on_device(): lax.all_to_all(outgoing.astype(jnp.bfloat16), 'fsdp', split_axis=0, conca...]
  transfers between devices with their start and end apart: 11 -> 45, of which waited for: 10 -> 21; matrix products, arithmetic and copies ran while one was open for 5% -> 23% of each run, Pallas kernels for 0% -> 0%
where the time goes in v1:
time: 843 us; the launch traced here: 838 us
  waiting for transfers between devices  287 us (34%)
  matrix products  216 us (26%)
  local copies, waits for them, and re-layouts  89.6 us (11%)
  other arithmetic  88.2 us (10%)
  blocking collectives  71.3 us (8%)
  starting transfers between devices  53.1 us (6%)
  between operations  33.1 us (4%)
    ppermute x28, waiting for transfers between devices, swap_bit(): return lax.ppermute(value, 'dp', [(i, i ^ 1 << bit) for i in range(count)])  125 us
    dot_general x17, matrix products, low_dot(): jnp.dot(left.astype(B16), right.astype(B16), preferred_element_type=F32)  89.1 us
    all_gather x1, waiting for transfers between devices, on_device(): lax.all_gather(ffn_low, ('dp', 'fsdp'), axis=1, tiled=True)  77 us
    all_gather x1, blocking collectives, on_device(): lax.all_gather(gain_low, ('dp', 'fsdp'), axis=1, tiled=True)  71.3 us
    reduce_scatter x4, waiting for transfers between devices, scatter_sum(): lax.psum_scatter(mine, 'fsdp', scatter_dimension=1, tiled=True).astype(F32)  30.8 us
    convert_element_type x16, other arithmetic, plane_sum(): sum((choose(t, dims, bit, True).astype(F32) for t, dims in terms))  27.8 us
    all_to_all x1, waiting for transfers between devices, orthogonal_rows(): lax.all_to_all(outgoing, 'fsdp', split_axis=0, concat_axis=0, tiled=True)  24.2 us
    ppermute x28, starting transfers between devices, swap_bit(): return lax.ppermute(value, 'dp', [(i, i ^ 1 << bit) for i in range(count)])  21.4 us
  transfers between devices with their start and end apart: 45, of which 21 were waited for; matrix products, arithmetic and copies ran while one was open for 23% of the time, Pallas kernels for 0%

profile of v1, /device:TPU:0, one launch (start us, length us, event | category | flops | bytes accessed | tf_op | source)
XLA Modules:
  0.0 838.3 jit_solution(12954506692618599321)
XLA Ops:
  12.1 71.3 %all-gather = bf16[32,32,3]{1,2,0:T(4,128)(2,1)S(1)} all-gather(bf16[1,32,3]{1,2,0:T(4,128)(2,1)S(1)} %convert_bitcast_fusion), channel_id=1, replica_groups=mesh['dp'=8,'fsdp'=4] {'dp','fsdp'}, dimensions={0}, use_global_device_ids=true | all-gather | bytes 6336 | tf_op jit(solution)/shard_map/all_gather | solution.py:387
  86.4 13.9 %all-gather.4.cloned.1.call-done = bf16[5,1024,1024]{2,1,0:T(8,128)(2,1)} async-done(((bf16[5,32,1024]{2,1,0:T(8,128)(2,1)}), bf16[5,1024,1024]{2,1,0:T(8,128)(2,1)}) %all-gather.4.cloned.1.call-update) | async-done | bytes 10485776 | tf_op jit(solution)/shard_map/all_gather | solution.py:385
  142.3 77.0 %all-gather.6.cloned.1.call-done = bf16[3,2816,1024]{2,1,0:T(8,128)(2,1)} async-done(((bf16[3,88,1024]{2,1,0:T(8,128)(2,1)}), bf16[3,2816,1024]{2,1,0:T(8,128)(2,1)}) %all-gather.6.cloned.1.call-update) | async-done | bytes 17301520 | tf_op jit(solution)/shard_map/all_gather | solution.py:386
  229.7 8.9 %fusion.182 = f32[512,5632]{1,0:T(8,128)} fusion(bf16[5632,1024]{1,0:T(8,128)(2,1)S(1)} %bitcast.364, f32[512,1024]{1,0:T(8,128)S(1)} %copy-done.32, f32[1024]{0:T(1024)S(1)} %bitcast.403, f32[512]{0:T(512)S(1)} %get-tuple-element.61), kind=kOutput, calls=%fused_computation.327 | convolution fusion | flops 5907152896 | bytes 25171968 | tf_op jit(solution)/shard_map/dot_general | solution.py:85
  238.6 9.6 %multiply_convert_fusion.3 = (bf16[512,2816]{1,0:T(8,128)(2,1)S(1)}, bf16[512,2816]{1,0:T(8,128)(2,1)}, bf16[512,2816]{1,0:T(8,128)(2,1)}) fusion(f32[512,5632]{1,0:T(8,128)} %fusion.182, bf16[512,1024]{1,0:T(8,128)(2,1)S(1)} %copy-done.37, bf16[3,2816,1024]{2,1,0:T(8,128)(2,1)} %all-gather.6.cloned.1.call-done), kind=kOutput, calls=%fused_computation.10 | convolution fusion | flops 2961440768 | bytes 27000832 | tf_op jit(solution)/shard_map/dot_general | solution.py:149
  248.3 11.9 %multiply_reduce_fusion.1 = (f32[1024]{0:T(1024)}, f32[512]{0:T(512)S(1)}, f32[512,1024]{1,0:T(8,128)S(1)}) fusion(f32[512,1024]{1,0:T(8,128)S(1)} %copy-done.32, f32[512]{0:T(512)S(1)} %get-tuple-element.61, f32[1024]{0:T(1024)S(1)} %bitcast.404, bf16[5632,1024]{1,0:T(8,128)(2,1)} %bitcast.365, bf16[512,2816]{1,0:T(8,128)(2,1)} %get-tuple-element.36, ...), kind=kOutput, calls=%fused_computation.133 | convolution fusion | flops 5920258560 | bytes 21508096 | tf_op jit(solution)/shard_map/dot_general | solution.py:152
  298.3 9.0 %convolution_convert_fusion.1 = bf16[4096,1024]{1,0:T(8,128)(2,1)} fusion(bf16[512,1024]{1,0:T(8,128)(2,1)S(1)} %copy-done.49, bf16[512,1024]{1,0:T(8,128)(2,1)S(1)} %copy-done.40, bf16[512,1024]{1,0:T(8,128)(2,1)S(1)} %get-tuple-element.79, bf16[512,1024]{1,0:T(8,128)(2,1)S(1)} %get-tuple-element.80, bf16[512,1024]{1,0:T(8,128)(2,1)S(1)} %copy-done.19, ...), kind=kOutput, calls=%fused_computation.6 | convolution fusion | flops 4318035968 | bytes 13637632 | tf_op jit(solution)/shard_map/dot_general | solution.py:199
  307.3 8.5 %copy.155 = bf16[4,2,2,2,4,32,1024]{6,5,0,4,3,2,1:T(8,128)(2,1)} copy(bf16[4,2,2,2,4,32,1024]{6,5,4,3,2,1,0:T(8,128)(2,1)} %bitcast.369) | data formatting | bytes 16777216 | tf_op jit(solution)/shard_map/convert_element_type | solution.py:241
  324.8 9.4 %convolution_convert_fusion = bf16[5632,1024]{1,0:T(8,128)(2,1)S(1)} fusion(bf16[512,2816]{1,0:T(8,128)(2,1)} %get-tuple-element.36, bf16[512,2816]{1,0:T(8,128)(2,1)} %copy-done.73, f32[512,1024]{1,0:T(8,128)S(1)} %copy-done.33, f32[1024]{0:T(1024)S(1)} %bitcast.406, f32[512]{0:T(512)S(1)} %get-tuple-element.61), kind=kOutput, calls=%fused_computation.4 | convolution fusion | flops 5924454400 | bytes 19404800 | tf_op jit(solution)/shard_map/dot_general | solution.py:155
  344.6 11.0 %fusion.190 = (bf16[2,2,2,2,2,88,1024]{6,5,3,4,2,1,0:T(8,128)(2,1)}, bf16[2,2,2,2,2,88,1024]{6,5,3,4,2,1,0:T(8,128)(2,1)}) fusion(bf16[2,2,2,2,4,88,1024]{6,5,3,4,2,1,0:T(8,128)(2,1)} %bitcast.348), kind=kLoop, calls=%fused_computation.332 | loop fusion | bytes 23068672 | tf_op jit(solution)/shard_map/slice | solution.py:247
  375.4 13.7 %collective-permute-done.10 = bf16[2,1,2,32,1024]{4,3,2,1,0:T(8,128)(2,1)S(1)} collective-permute-done((bf16[2,1,2,32,1024]{4,3,2,1,0:T(8,128)(2,1)S(1)}, bf16[2,1,2,32,1024]{4,3,2,1,0:T(8,128)(2,1)S(1)}, u32[]{:S(2)}, u32[]{:S(2)}) %collective-permute-start.10) | collective-permute-done | bytes 262176 | tf_op jit(solution)/shard_map/ppermute | solution.py:214
  394.9 8.2 collective-permute-done.7
  456.9 33.2 %collective-permute-done.23 = bf16[1,2,88,1024]{3,2,1,0:T(8,128)(2,1)S(1)} collective-permute-done((bf16[1,2,88,1024]{3,2,1,0:T(8,128)(2,1)S(1)}, bf16[1,2,88,1024]{3,2,1,0:T(8,128)(2,1)S(1)}, u32[]{:S(2)}, u32[]{:S(2)}) %collective-permute-start.23) | collective-permute-done | bytes 360480 | tf_op jit(solution)/shard_map/ppermute | solution.py:214
  499.1 11.1 %collective-permute-done.17 = bf16[2,2,88,1024]{3,2,0,1:T(8,128)(2,1)S(1)} collective-permute-done((bf16[2,2,88,1024]{3,2,0,1:T(8,128)(2,1)S(1)}, bf16[2,2,88,1024]{3,2,0,1:T(8,128)(2,1)S(1)}, u32[]{:S(2)}, u32[]{:S(2)}) %collective-permute-start.17) | collective-permute-done | bytes 720928 | tf_op jit(solution)/shard_map/ppermute | solution.py:214
  518.2 30.8 %reduce-scatter.9.cloned.1.call-done = bf16[2,1,88,1024]{3,2,0,1:T(8,128)(2,1)} async-done(((bf16[2,4,88,1024]{3,2,0,1:T(8,128)(2,1)}), bf16[2,1,88,1024]{3,2,0,1:T(8,128)(2,1)}) %reduce-scatter.9.cloned.1.call-update) | async-done | bytes 360464 | tf_op jit(solution)/shard_map/reduce_scatter | solution.py:250
  556.4 24.2 %all-to-all-done.1 = bf16[4,120,1024]{2,1,0:T(8,128)(2,1)S(1)} async-done(((bf16[4,120,1024]{2,1,0:T(8,128)(2,1)}), bf16[4,120,1024]{2,1,0:T(8,128)(2,1)S(1)}, u32[]{:S(2)}, u32[]{:S(2)}) %all-to-all-start.1) | async-done | bytes 983072 | tf_op jit(solution)/shard_map/all_to_all | solution.py:320
  587.5 9.7 %collective-permute-done.24 = bf16[1,128,1024]{2,1,0:T(8,128)(2,1)S(1)} collective-permute-done((bf16[1,128,1024]{2,1,0:T(8,128)(2,1)S(1)}, bf16[1,128,1024]{2,1,0:T(8,128)(2,1)S(1)}, u32[]{:S(2)}, u32[]{:S(2)}) %collective-permute-start.24) | collective-permute-done | bytes 262176 | tf_op jit(solution)/shard_map/ppermute | solution.py:214
  605.8 16.3 %collective-permute-done.30 = bf16[1,128,1024]{2,1,0:T(8,128)(2,1)S(1)} collective-permute-done((bf16[1,128,1024]{2,1,0:T(8,128)(2,1)S(1)}, bf16[1,128,1024]{2,1,0:T(8,128)(2,1)S(1)}, u32[]{:S(2)}, u32[]{:S(2)}) %collective-permute-start.30) | collective-permute-done | bytes 262176 | tf_op jit(solution)/shard_map/ppermute | solution.py:214
  631.2 11.9 %collective-permute-done.32 = bf16[2,128,1024]{2,1,0:T(8,128)(2,1)S(1)} collective-permute-done((bf16[2,128,1024]{2,1,0:T(8,128)(2,1)S(1)}, bf16[2,128,1024]{2,1,0:T(8,128)(2,1)S(1)}, u32[]{:S(2)}, u32[]{:S(2)}) %collective-permute-start.32) | collective-permute-done | bytes 524320 | tf_op jit(solution)/shard_map/ppermute | solution.py:214
  663.4 7.7 select_add_fusion.7
  703.6 7.9 select_add_fusion.3
  755.9 10.9 %add_convert_fusion.1 = bf16[704,1024]{1,0:T(8,128)(2,1)S(1)} fusion(f32[704,1024]{1,0:T(8,128)} %multiply_add_fusion.4, f32[]{:T(128)S(6)} %add.1115, f32[1024,1024]{1,0:T(8,128)} %get-tuple-element.78, f32[]{:T(128)S(6)} %sub.150, f32[]{:T(128)S(6)} %mul.754, f32[]{:T(128)S(6)} %mul.751, f32[]{:T(128)S(6)} %div.67), kind=kOutput, calls=%fused_computation.76 | convolution fusion | flops 3644588032 | bytes 8519700 | tf_op jit(solution)/shard_map/dot_general | solution.py:265
  769.9 10.8 %fusion.38 = (f32[1024]{0:T(1024)}, f32[512]{0:T(512)}, f32[512,1024]{1,0:T(8,128)}) fusion(bf16[512,1024]{1,0:T(8,128)(2,1)S(1)} %copy-done.20, f32[512]{0:T(512)S(1)} %copy-done.58, f32[1024]{0:T(1024)S(1)} %bitcast.401, bf16[4096,1024]{1,0:T(8,128)(2,1)} %bitcast.368, bf16[512,1024]{1,0:T(8,128)(2,1)} %get-tuple-element.38, ...), kind=kOutput, calls=%fused_computation.91 | convolution fusion | flops 4315412992 | bytes 15740928 | tf_op jit(solution)/shard_map/dot_general | solution.py:196
  816.5 11.7 %all-to-all-done.2 = bf16[4,120,1024]{2,1,0:T(8,128)(2,1)S(1)} async-done(((bf16[4,120,1024]{2,1,0:T(8,128)(2,1)}), bf16[4,120,1024]{2,1,0:T(8,128)(2,1)S(1)}, u32[]{:S(2)}, u32[]{:S(2)}) %all-to-all-start.2) | async-done | bytes 983072 | tf_op jit(solution)/shard_map/all_to_all | solution.py:359
  (387 shorter events, 366.7 us)
Async XLA Ops:
  7.2 93.2 %all-gather.4.cloned.1.call-start = ((), (), s32[]{:S(2)}) async-start(), calls=%async_computation.7 | async-start | bytes 10813440 | tf_op jit(solution)/shard_map/all_gather | solution.py:385
  9.2 210.1 %all-gather.6.cloned.1.call-start = ((), (), s32[]{:S(2)}) async-start(), calls=%async_computation.8 | async-start | bytes 17842176 | tf_op jit(solution)/shard_map/all_gather | solution.py:386
  11.4 504.5 %reduce-scatter.7.cloned.1.call-start = ((), (), s32[]{:S(2)}) async-start(), calls=%async_computation.10 | async-start | bytes 327680 | tf_op jit(solution)/shard_map/reduce_scatter | solution.py:250
  295.9 70.2 %collective-permute-start.9 = (bf16[2,2,1,2,32,1024]{5,4,3,2,1,0:T(8,128)(2,1)}, bf16[2,2,1,2,32,1024]{5,4,3,2,1,0:T(8,128)(2,1)}, u32[]{:S(2)}, u32[]{:S(2)}) collective-permute-start(bf16[2,2,1,2,32,1024]{5,4,3,2,1,0:T(8,128)(2,1)} %dynamic-slice_bitcast_fusion.4), channel_id=1, source_target_pairs={{0,4},{4,0},{8,12},{12,8},{16,20},{20,16},{24,28},{28,24},{1,5},{5... | collective-permute-start | bytes 1572872 | tf_op jit(solution)/shard_map/ppermute | solution.py:214
  296.9 77.4 %collective-permute-start.6 = (bf16[2,2,1,2,32,1024]{5,4,3,2,1,0:T(8,128)(2,1)}, bf16[2,2,1,2,32,1024]{5,4,3,2,1,0:T(8,128)(2,1)}, u32[]{:S(2)}, u32[]{:S(2)}) collective-permute-start(bf16[2,2,1,2,32,1024]{5,4,3,2,1,0:T(8,128)(2,1)} %dynamic-slice_bitcast_fusion.5), channel_id=1, source_target_pairs={{0,4},{4,0},{8,12},{12,8},{16,20},{20,16},{24,28},{28,24},{1,5},{5... | collective-permute-start | bytes 1572872 | tf_op jit(solution)/shard_map/ppermute | solution.py:214
  321.4 34.3 %collective-permute-start.3 = (bf16[2,2,4,2,32,1024]{5,4,2,3,1,0:T(8,128)(2,1)}, bf16[2,2,4,2,32,1024]{5,4,2,3,1,0:T(8,128)(2,1)S(1)}, u32[]{:S(2)}, u32[]{:S(2)}) collective-permute-start(bf16[2,2,4,2,32,1024]{5,4,2,3,1,0:T(8,128)(2,1)} %dynamic-slice_bitcast_fusion.1), channel_id=1, source_target_pairs={{0,4},{4,0},{8,12},{12,8},{16,20},{20,16},{24,28},{28,24},{1,5},{5... | collective-permute-start | bytes 6291464 | tf_op jit(solution)/shard_map/ppermute | solution.py:214
  324.5 44.9 %collective-permute-start = (bf16[2,2,4,2,32,1024]{5,4,2,3,0,1:T(8,128)(2,1)}, bf16[2,2,4,2,32,1024]{5,4,2,3,0,1:T(8,128)(2,1)}, u32[]{:S(2)}, u32[]{:S(2)}) collective-permute-start(bf16[2,2,4,2,32,1024]{5,4,2,3,0,1:T(8,128)(2,1)} %copy_bitcast_fusion.3), channel_id=1, source_target_pairs={{0,4},{4,0},{8,12},{12,8},{16,20},{20,16},{24,28},{28,24},{1,5},{5... | collective-permute-start | bytes 6291464 | tf_op jit(solution)/shard_map/ppermute | solution.py:214
  358.1 34.1 %collective-permute-start.4 = (bf16[2,4,2,32,1024]{4,3,1,2,0:T(8,128)(2,1)S(1)}, bf16[2,4,2,32,1024]{4,3,1,2,0:T(8,128)(2,1)S(1)}, u32[]{:S(2)}, u32[]{:S(2)}) collective-permute-start(bf16[2,4,2,32,1024]{4,3,1,2,0:T(8,128)(2,1)S(1)} %fusion.44), channel_id=1, source_target_pairs={{0,16},{4,20},{8,24},{12,28},{16,0},{20,4},{24,8},{28,12},{1,17},{... | collective-permute-start | bytes 3145736 | tf_op jit(solution)/shard_map/ppermute | solution.py:214
  366.0 70.6 %collective-permute-start.15 = (bf16[2,2,2,2,88,1024]{5,4,2,3,1,0:T(8,128)(2,1)}, bf16[2,2,2,2,88,1024]{5,4,2,3,1,0:T(8,128)(2,1)}, u32[]{:S(2)}, u32[]{:S(2)}) collective-permute-start(bf16[2,2,2,2,88,1024]{5,4,2,3,1,0:T(8,128)(2,1)} %dynamic-slice_bitcast_fusion), channel_id=1, source_target_pairs={{0,4},{4,0},{8,12},{12,8},{16,20},{20,16},{24,28},{28,24},{1,5},{5... | collective-permute-start | bytes 8650760 | tf_op jit(solution)/shard_map/ppermute | solution.py:214
  371.3 40.5 %collective-permute-start.1 = (bf16[2,4,2,32,1024]{4,3,1,2,0:T(8,128)(2,1)S(1)}, bf16[2,4,2,32,1024]{4,3,1,2,0:T(8,128)(2,1)S(1)}, u32[]{:S(2)}, u32[]{:S(2)}) collective-permute-start(bf16[2,4,2,32,1024]{4,3,1,2,0:T(8,128)(2,1)S(1)} %fusion.45), channel_id=1, source_target_pairs={{0,8},{4,12},{8,0},{12,4},{16,24},{20,28},{24,16},{28,20},{1,9},{5... | collective-permute-start | bytes 3145736 | tf_op jit(solution)/shard_map/ppermute | solution.py:214
  374.4 66.8 %collective-permute-start.12 = (bf16[2,2,2,2,88,1024]{5,4,2,3,0,1:T(8,128)(2,1)}, bf16[2,2,2,2,88,1024]{5,4,2,3,0,1:T(8,128)(2,1)}, u32[]{:S(2)}, u32[]{:S(2)}) collective-permute-start(bf16[2,2,2,2,88,1024]{5,4,2,3,0,1:T(8,128)(2,1)} %copy_bitcast_fusion.2), channel_id=1, source_target_pairs={{0,4},{4,0},{8,12},{12,8},{16,20},{20,16},{24,28},{28,24},{1,5},{5... | collective-permute-start | bytes 8650760 | tf_op jit(solution)/shard_map/ppermute | solution.py:214
  411.8 22.8 %collective-permute-start.18 = (bf16[2,2,1,2,88,1024]{5,4,3,2,1,0:T(8,128)(2,1)}, bf16[2,2,1,2,88,1024]{5,4,3,2,1,0:T(8,128)(2,1)}, u32[]{:S(2)}, u32[]{:S(2)}) collective-permute-start(bf16[2,2,1,2,88,1024]{5,4,3,2,1,0:T(8,128)(2,1)} %dynamic-slice_bitcast_fusion.3), channel_id=1, source_target_pairs={{0,4},{4,0},{8,12},{12,8},{16,20},{20,16},{24,28},{28,24},{1,5},{5... | collective-permute-start | bytes 4325384 | tf_op jit(solution)/shard_map/ppermute | solution.py:214
  419.1 96.9 %reduce-scatter.5.cloned.1.call-start = ((), (), s32[]{:S(2)}) async-start(), calls=%async_computation.9 | async-start | bytes 1310720 | tf_op jit(solution)/shard_map/reduce_scatter | solution.py:250
  431.2 87.0 %reduce-scatter.11.cloned.1.call-start = ((), (), s32[]{:S(2)}) async-start(), calls=%async_computation.12 | async-start | bytes 901120 | tf_op jit(solution)/shard_map/reduce_scatter | solution.py:250
  440.2 53.4 %collective-permute-start.16 = (bf16[2,2,2,88,1024]{4,3,1,2,0:T(8,128)(2,1)}, bf16[2,2,2,88,1024]{4,3,1,2,0:T(8,128)(2,1)}, u32[]{:S(2)}, u32[]{:S(2)}) collective-permute-start(bf16[2,2,2,88,1024]{4,3,1,2,0:T(8,128)(2,1)} %fusion.24), channel_id=1, source_target_pairs={{0,16},{4,20},{8,24},{12,28},{16,0},{20,4},{24,8},{28,12},{1,17},{... | collective-permute-start | bytes 4325384 | tf_op jit(solution)/shard_map/ppermute | solution.py:214
  444.7 51.5 %collective-permute-start.13 = (bf16[2,2,2,88,1024]{4,3,1,2,0:T(8,128)(2,1)}, bf16[2,2,2,88,1024]{4,3,1,2,0:T(8,128)(2,1)}, u32[]{:S(2)}, u32[]{:S(2)}) collective-permute-start(bf16[2,2,2,88,1024]{4,3,1,2,0:T(8,128)(2,1)} %fusion.25), channel_id=1, source_target_pairs={{0,8},{4,12},{8,0},{12,4},{16,24},{20,28},{24,16},{28,20},{1,9},{5... | collective-permute-start | bytes 4325384 | tf_op jit(solution)/shard_map/ppermute | solution.py:214
  453.4 36.6 %collective-permute-start.23 = (bf16[1,2,88,1024]{3,2,1,0:T(8,128)(2,1)S(1)}, bf16[1,2,88,1024]{3,2,1,0:T(8,128)(2,1)S(1)}, u32[]{:S(2)}, u32[]{:S(2)}) collective-permute-start(bf16[1,2,88,1024]{3,2,1,0:T(8,128)(2,1)S(1)} %fusion.111), channel_id=1, source_target_pairs={{0,8},{4,12},{8,0},{12,4},{16,24},{20,28},{24,16},{28,20},{1,9},{5... | collective-permute-start | bytes 1081352 | tf_op jit(solution)/shard_map/ppermute | solution.py:214
  456.2 35.2 %collective-permute-start.20 = (bf16[1,2,88,1024]{3,2,1,0:T(8,128)(2,1)S(1)}, bf16[1,2,88,1024]{3,2,1,0:T(8,128)(2,1)S(1)}, u32[]{:S(2)}, u32[]{:S(2)}) collective-permute-start(bf16[1,2,88,1024]{3,2,1,0:T(8,128)(2,1)S(1)} %fusion.114), channel_id=1, source_target_pairs={{0,16},{4,20},{8,24},{12,28},{16,0},{20,4},{24,8},{28,12},{1,17},{... | collective-permute-start | bytes 1081352 | tf_op jit(solution)/shard_map/ppermute | solution.py:214
  493.6 55.4 %reduce-scatter.9.cloned.1.call-start = ((), (), s32[]{:S(2)}) async-start(), calls=%async_computation.11 | async-start | bytes 1802240 | tf_op jit(solution)/shard_map/reduce_scatter | solution.py:250
  552.8 27.7 %all-to-all-start.1 = ((bf16[4,120,1024]{2,1,0:T(8,128)(2,1)}), bf16[4,120,1024]{2,1,0:T(8,128)(2,1)S(1)}, u32[]{:S(2)}, u32[]{:S(2)}) async-start(bf16[4,120,1024]{2,1,0:T(8,128)(2,1)} %fusion.106), calls=%async_computation.5 | async-start | bytes 1966080 | tf_op jit(solution)/shard_map/all_to_all | solution.py:320
  597.4 30.3 %collective-permute-start.27 = (bf16[2,224,1024]{2,1,0:T(8,128)(2,1)S(1)}, bf16[2,224,1024]{2,1,0:T(8,128)(2,1)S(1)}, u32[]{:S(2)}, u32[]{:S(2)}) collective-permute-start(bf16[2,224,1024]{2,1,0:T(8,128)(2,1)S(1)} %pad_maximum_fusion.9), channel_id=1, source_target_pairs={{0,16},{8,24},{16,0},{24,8},{1,17},{9,25},{17,1},{25,9},{2,18},{10... | collective-permute-start | bytes 2752520 | tf_op jit(solution)/shard_map/ppermute | solution.py:303
  605.2 22.5 %collective-permute-start.26 = (bf16[2,128,1024]{2,1,0:T(8,128)(2,1)S(1)}, bf16[2,128,1024]{2,1,0:T(8,128)(2,1)S(1)}, u32[]{:S(2)}, u32[]{:S(2)}) collective-permute-start(bf16[2,128,1024]{2,1,0:T(8,128)(2,1)S(1)} %fusion.119), channel_id=1, source_target_pairs={{0,16},{4,20},{8,24},{12,28},{16,0},{20,4},{24,8},{28,12},{1,17},{... | collective-permute-start | bytes 1572872 | tf_op jit(solution)/shard_map/ppermute | solution.py:214
  767.7 27.0 %collective-permute-start.34 = (bf16[352,1024]{1,0:T(8,128)(2,1)}, bf16[352,1024]{1,0:T(8,128)(2,1)}, u32[]{:S(2)}, u32[]{:S(2)}) collective-permute-start(bf16[352,1024]{1,0:T(8,128)(2,1)} %slice.204), channel_id=1, source_target_pairs={{0,4},{8,12},{16,20},{24,28},{1,5},{9,13},{17,21},{25,29},{2,6},{1... | collective-permute-start | bytes 2162696 | tf_op jit(solution)/shard_map/ppermute | solution.py:296
  800.5 27.7 %all-to-all-start.2 = ((bf16[4,120,1024]{2,1,0:T(8,128)(2,1)}), bf16[4,120,1024]{2,1,0:T(8,128)(2,1)S(1)}, u32[]{:S(2)}, u32[]{:S(2)}) async-start(bf16[4,120,1024]{2,1,0:T(8,128)(2,1)} %pad_maximum_fusion.7), calls=%async_computation.6 | async-start | bytes 1966080 | tf_op jit(solution)/shard_map/all_to_all | solution.py:359
  (102 other events, 1548.1 us)
Sparse Core Ops, SparseCore 0:
  11.6 88.7 all-gather.3
  103.9 115.3 all-gather.5
  419.2 17.6 reduce-scatter.6
  439.6 25.5 reduce-scatter.4
  493.7 20.5 reduce-scatter.10
  516.5 32.4 reduce-scatter.8

commit v2 on v0

v2 whole, which is shorter than its diff:
```python
import math

import jax
import jax.numpy as jnp
from jax import lax
from jax.experimental import pallas as pl
from jax.experimental.pallas import tpu as pltpu
from jax.sharding import PartitionSpec as P

D = 1024
FF = 2816
NS_STEPS = 5


EPS = 1e-06
NS_EPS = 1e-07
NS_A = 3.4445
NS_B = -4.775
NS_C = 2.0315
LR_MUON = 0.3
LR_GAIN = 0.1
MOMENT_DECAY = 0.5
BETA_ONE = 0.9
BETA_TWO = 0.95
ADAM_EPS = 1e-08
F32 = jnp.float32
B16 = jnp.bfloat16
ROWS_BY_ROWS = (((1,), (1,)), ((), ()))
TOKENS_OUT = (((0,), (0,)), ((), ()))


def rms_scale(series):
    return lax.rsqrt(jnp.mean(series * series, axis=-1, keepdims=True) + EPS)


def rms_back(series, factor, upstream):
    return factor * upstream - series * (factor * factor * factor) * jnp.mean(
        upstream * series, axis=-1, keepdims=True
    )


def decay_mask(segments, decay_rate):
    length = segments.shape[0]
    places = jnp.arange(length, dtype=jnp.int32)
    distance = places[:, None] - places[None, :]
    allowed = (segments[:, None] == segments[None, :]) & (distance >= 0)
    fading = jnp.exp(-decay_rate[:, None, None] * jnp.maximum(distance, 0).astype(F32)[None])
    return jnp.where(allowed[None], fading, 0.0)


def forward(tokens, segments, decay_rate, attn_full, ffn_full, gain_low):
    length, model_width = tokens.shape
    head_count = decay_rate.shape[0]
    head_size = model_width // head_count
    hidden = ffn_full[0].shape[1]
    gain_full = gain_low.astype(F32)
    inputs = tokens.astype(F32)
    first_scale = rms_scale(inputs)
    normed = (inputs * first_scale * gain_full[0]).astype(B16)
    projected = lax.dot_general(
        normed,
        attn_full[0].reshape(4 * model_width, model_width),
        ROWS_BY_ROWS,
        preferred_element_type=F32,
    )
    query_act = jax.nn.relu(projected[:, :model_width]).astype(B16)
    key_act = jax.nn.relu(projected[:, model_width : 2 * model_width]).astype(B16)
    value_act = projected[:, 2 * model_width : 3 * model_width].astype(B16)
    gate_pre = projected[:, 3 * model_width :]
    fading_mask = decay_mask(segments, decay_rate)
    query_heads = query_act.reshape(length, head_count, head_size)
    key_heads = key_act.reshape(length, head_count, head_size)
    value_heads = value_act.reshape(length, head_count, head_size)
    scores = jnp.einsum("the,she->hts", query_heads, key_heads, preferred_element_type=F32)
    weights_low = (scores * fading_mask).astype(B16)
    attended = jnp.einsum(
        "hts,she->the", weights_low, value_heads, preferred_element_type=F32
    ).reshape(length, model_width)
    out_scale = rms_scale(attended)
    normal_out = attended * out_scale * gain_full[2]
    gate_sig = jax.nn.sigmoid(gate_pre)
    gated_out = (normal_out * gate_sig).astype(B16)
    branch = lax.dot_general(gated_out, attn_full[1], ROWS_BY_ROWS, preferred_element_type=F32)
    middle = inputs + branch
    second_scale = rms_scale(middle)
    normed_two = (middle * second_scale * gain_full[1]).astype(B16)
    up_pair = lax.dot_general(
        normed_two,
        ffn_full[0].reshape(2 * hidden, model_width),
        ROWS_BY_ROWS,
        preferred_element_type=F32,
    )
    up_one = up_pair[:, :hidden]
    up_two = up_pair[:, hidden:]
    product = (up_one * up_two).astype(B16)
    stored = (
        inputs,
        first_scale,
        normed,
        query_act,
        key_act,
        value_act,
        gate_pre,
        fading_mask,
        weights_low,
        attended,
        out_scale,
        normal_out,
        gate_sig,
        gated_out,
        middle,
        second_scale,
        normed_two,
        up_one,
        up_two,
        product,
    )
    return stored


def backward(stored, cotangent, attn_full, ffn_full, gain_low):
    (
        inputs,
        first_scale,
        normed,
        query_act,
        key_act,
        value_act,
        gate_pre,
        fading_mask,
        weights_low,
        attended,
        out_scale,
        normal_out,
        gate_sig,
        gated_out,
        middle,
        second_scale,
        normed_two,
        up_one,
        up_two,
        product,
    ) = stored
    length, model_width = inputs.shape
    head_count = fading_mask.shape[0]
    head_size = model_width // head_count
    hidden = ffn_full[0].shape[1]
    gain_full = gain_low.astype(F32)
    grad_out = cotangent.astype(F32)
    grad_down = lax.dot_general(product, cotangent, TOKENS_OUT, preferred_element_type=F32).astype(B16)
    down = Halving(grad_down[None])
    down_out, cotangent = tied([down.payloads()], cotangent)
    down_in = down.swap(down_out)
    grad_product = lax.dot_general(cotangent, ffn_full[1], ROWS_BY_ROWS, preferred_element_type=F32)
    grad_pair = jnp.concatenate([grad_product * up_two, grad_product * up_one], axis=1).astype(B16)
    down_in, grad_pair = tied([down_in], grad_pair)
    down.accept(down_in)
    down_out, grad_pair = tied([down.payloads()], grad_pair)
    down_in = down.swap(down_out)
    grad_up = lax.dot_general(grad_pair, normed_two, TOKENS_OUT, preferred_element_type=F32).astype(B16)
    up = Halving(grad_up.reshape(2, hidden, model_width))
    up_out, grad_pair = tied([up.payloads()], grad_pair)
    up_in = up.swap(up_out)
    grad_normed_two = jnp.dot(
        grad_pair, ffn_full[0].reshape(2 * hidden, model_width), preferred_element_type=F32
    )
    gain_two = jnp.sum(grad_normed_two * middle * second_scale, axis=0)
    grad_middle = grad_out + rms_back(middle, second_scale, grad_normed_two * gain_full[1])
    middle_low = grad_middle.astype(B16)
    down_in, up_in, middle_low = tied([down_in, up_in], middle_low)
    down.accept(down_in)
    up.accept(up_in)
    down_out, up_out, middle_low = tied([down.payloads(), up.payloads()], middle_low)
    down_in, up_in = down.swap(down_out), up.swap(up_out)
    grad_outproj = lax.dot_general(middle_low, gated_out, TOKENS_OUT, preferred_element_type=F32).astype(B16)
    proj = Halving(grad_outproj[None])
    proj_out, middle_low = tied([proj.payloads()], middle_low)
    proj_in = proj.swap(proj_out)
    grad_gated = jnp.dot(middle_low, attn_full[1], preferred_element_type=F32)
    grad_normal = grad_gated * gate_sig
    grad_gate = grad_gated * normal_out * gate_sig * (1.0 - gate_sig)
    gain_three = jnp.sum(grad_normal * attended * out_scale, axis=0)
    grad_attended = (
        rms_back(attended, out_scale, grad_normal * gain_full[2])
        .astype(B16)
        .reshape(length, head_count, head_size)
    )
    query_heads = query_act.reshape(length, head_count, head_size)
    key_heads = key_act.reshape(length, head_count, head_size)
    value_heads = value_act.reshape(length, head_count, head_size)
    grad_weights = jnp.einsum(
        "the,she->hts", grad_attended, value_heads, preferred_element_type=F32
    )
    grad_values = jnp.einsum(
        "hts,the->she", weights_low, grad_attended, preferred_element_type=F32
    ).reshape(length, model_width)
    grad_scores = (grad_weights * fading_mask).astype(B16)
    grad_queries = jnp.einsum(
        "hts,she->the", grad_scores, key_heads, preferred_element_type=F32
    ).reshape(length, model_width)
    grad_keys = jnp.einsum(
        "hts,the->she", grad_scores, query_heads, preferred_element_type=F32
    ).reshape(length, model_width)
    grad_mixed = jnp.concatenate(
        [
            jnp.where(query_act > 0, grad_queries, 0.0),
            jnp.where(key_act > 0, grad_keys, 0.0),
            grad_values,
            grad_gate,
        ],
        axis=1,
    ).astype(B16)
    down_in, up_in, proj_in, grad_mixed = tied([down_in, up_in, proj_in], grad_mixed)
    down.accept(down_in)
    up.accept(up_in)
    proj.accept(proj_in)
    up_out, proj_out, grad_mixed = tied([up.payloads(), proj.payloads()], grad_mixed)
    up_in, proj_in = up.swap(up_out), proj.swap(proj_out)
    grad_inner = lax.dot_general(grad_mixed, normed, TOKENS_OUT, preferred_element_type=F32).astype(B16)
    inner = Halving(grad_inner.reshape(4, model_width, model_width))
    inner_out, grad_mixed = tied([inner.payloads()], grad_mixed)
    inner_in = inner.swap(inner_out)
    grad_normed = jnp.dot(
        grad_mixed, attn_full[0].reshape(4 * model_width, model_width), preferred_element_type=F32
    )
    gain_one = jnp.sum(grad_normed * inputs * first_scale, axis=0)
    grad_inputs = grad_middle + rms_back(inputs, first_scale, grad_normed * gain_full[0])
    grad_gain = jnp.stack([gain_one, gain_two, gain_three])
    up_in, proj_in, inner_in, grad_inputs = tied([up_in, proj_in, inner_in], grad_inputs)
    up.accept(up_in)
    proj.accept(proj_in)
    inner.accept(inner_in)
    return (grad_inputs, (down, up, proj, inner), grad_gain)


def ordered(*values):
    return lax.optimization_barrier(values)


def plane_bits():
    return lax.axis_size("dp").bit_length() - 1


def swap_bit(value, bit):
    count = lax.axis_size("dp")
    return lax.ppermute(value, "dp", [(i, i ^ (1 << bit)) for i in range(count)])


class Halving:
    def __init__(self, grad):
        count, rows, columns = grad.shape
        bits = plane_bits()
        self.chunk = rows // lax.axis_size("dp")
        blocks = grad.reshape((count,) + (2,) * bits + (self.chunk, columns))
        self.parts = [[(blocks, list(range(bits))[::-1])]]
        self.orders = [[0]]

    def choose(self, term, dims, bit, other):
        place = (lax.axis_index("dp") >> bit) & 1
        index = 1 - place if other else place
        return lax.dynamic_index_in_dim(term, index, 1 + dims.index(bit), keepdims=False)

    def payloads(self):
        if self.orders == [[]]:
            rest = list(range(1, plane_bits()))
            half = self.chunk // 2
            self.parts = [
                [(t[..., color * half : (color + 1) * half, :], dims) for t, dims in self.parts[0]]
                for color in range(2)
            ]
            self.orders = [rest, rest[::-1]]
        self.bits = [order[0] for order in self.orders]
        return [
            sum(self.choose(t, dims, bit, True).astype(F32) for t, dims in part).astype(B16)
            for part, bit in zip(self.parts, self.bits)
        ]

    def swap(self, payloads):
        return [swap_bit(value, bit) for value, bit in zip(payloads, self.bits)]

    def accept(self, arrived):
        for color, (part, bit) in enumerate(zip(self.parts, self.bits)):
            left = [b for b in part[0][1] if b != bit]
            self.parts[color] = [(self.choose(t, dims, bit, False), left) for t, dims in part]
            self.parts[color].append((arrived[color], left))
            self.orders[color] = self.orders[color][1:]

    def finish(self):
        while len(self.parts) == 1 or self.orders[0]:
            self.accept(self.swap(self.payloads()))
        return jnp.concatenate([sum(t.astype(F32) for t, _ in part).astype(B16) for part in self.parts], axis=1)


def tied(lists, *values):
    flat = ordered(*[v for part in lists for v in part], *values)
    out, at = [], 0
    for part in lists:
        out.append(list(flat[at : at + len(part)]))
        at += len(part)
    return (*out, *flat[at:])


def gain_sum(grad):
    rows, columns = grad.shape
    total = lax.axis_size("dp") * lax.axis_size("fsdp")
    blocks = jnp.transpose(grad.reshape(rows, total, columns // total), (1, 0, 2))
    return jnp.sum(lax.all_to_all(blocks, ("dp", "fsdp"), 0, 0, tiled=True), axis=0)


NS_ROWS = 256


def polynomial_kernel(gram_ref, rows_ref, out_ref, gram, rest_low, poly, poly_low, current):
    size = gram_ref.shape[0]
    count = rows_ref.shape[0]
    blocks = size // NS_ROWS
    parts = count // 2

    def block(i):
        return pl.ds(pl.multiple_of(i * NS_ROWS, NS_ROWS), NS_ROWS)

    def on_diagonal(i):
        row = lax.broadcasted_iota(jnp.int32, (NS_ROWS, size), 0) + i * NS_ROWS
        return row == lax.broadcasted_iota(jnp.int32, (NS_ROWS, size), 1)

    def trace_of(ref):
        def add(i, total):
            return total + jnp.sum(jnp.where(on_diagonal(i), ref[block(i), :], 0.0))

        return lax.fori_loop(0, blocks, add, jnp.float32(0.0))

    square = jnp.full((1, 1), trace_of(gram_ref), F32)
    norm = jnp.sqrt(square) + NS_EPS
    scale = 1.0 / norm

    def start(i, carry):
        gram[block(i), :] = gram_ref[block(i), :] * (scale * scale)
        return carry

    lax.fori_loop(0, blocks, start, 0)
    current[...] = rows_ref[...].astype(F32) * scale

    def step(iteration, trace):
        shift = trace / size
        factor = NS_A + NS_B * shift + NS_C * shift * shift

        def low_rest(i, carry):
            rest_low[block(i), :] = (gram[block(i), :] - jnp.where(on_diagonal(i), shift, 0.0)).astype(B16)
            return carry

        lax.fori_loop(0, blocks, low_rest, 0)

        def polynomial(i, carry):
            eye = on_diagonal(i)
            own = gram[block(i), :]
            rest = own - jnp.where(eye, shift, 0.0)
            squared = jnp.dot(rest_low[block(i), :], rest_low[...], preferred_element_type=F32)
            squared = squared + 2.0 * shift * rest + jnp.where(eye, shift * shift, 0.0)
            value = NS_B * own + NS_C * squared + jnp.where(eye, NS_A - factor, 0.0)
            poly[block(i), :] = value
            poly_low[block(i), :] = value.astype(B16)
            return carry

        lax.fori_loop(0, blocks, polynomial, 0)

        def apply(i, carry):
            where = pl.ds(pl.multiple_of(i * parts, parts), parts)
            value = current[where, :]
            current[where, :] = factor * value + jnp.dot(
                value.astype(B16), poly_low[...], preferred_element_type=F32
            )
            return carry

        lax.fori_loop(0, 2, apply, 0)

        def next_gram(i, total):
            eye = on_diagonal(i)
            rest = gram[block(i), :] - jnp.where(eye, shift, 0.0)
            own = poly[block(i), :]
            half_way = jnp.dot(rest_low[block(i), :], poly_low[...], preferred_element_type=F32)
            half_way = half_way + shift * own + factor * rest
            value = jnp.dot(half_way.astype(B16), poly_low[...], preferred_element_type=F32)
            value = value + (shift * factor) * own + factor * half_way
            value = value + jnp.where(eye, shift * factor * factor, 0.0)
            gram[block(i), :] = value
            return total + jnp.sum(jnp.where(eye, value, 0.0))

        steps = jnp.where(iteration + 1 < NS_STEPS, blocks, 0)
        return lax.fori_loop(0, steps, next_gram, jnp.float32(0.0))

    lax.fori_loop(0, NS_STEPS, step, trace_of(gram))
    out_ref[...] = current[...].astype(B16)


def gram_orthogonalize(rows, gram):
    size = gram.shape[0]
    whole = pltpu.VMEM((size, size), F32)
    low = pltpu.VMEM((size, size), B16)
    return pl.pallas_call(
        polynomial_kernel,
        out_shape=jax.ShapeDtypeStruct(rows.shape, B16),
        in_specs=[pl.BlockSpec(memory_space=pltpu.VMEM)] * 2,
        out_specs=pl.BlockSpec(memory_space=pltpu.VMEM),
        scratch_shapes=[whole, low, whole, low, pltpu.VMEM(rows.shape, F32)],
        compiler_params=pltpu.CompilerParams(vmem_limit_bytes=48 * 1024 * 1024),
        cost_estimate=pl.CostEstimate(flops=30 * size**3, transcendentals=0, bytes_accessed=8 * size * size),
    )(gram, rows)


def one_way(value, bit, lower):
    count = lax.axis_size("dp")
    start = 1 if lower else 0
    return lax.ppermute(
        value, "dp", [(i, i ^ (1 << bit)) for i in range(count) if (i & 1) == start]
    )


def swap_core(value, bit, core):
    count = lax.axis_size("dp")
    return lax.ppermute(value, "dp", [(i, i ^ (1 << bit)) for i in range(count) if (i & 1) == core])


def gather_plane(own, other, core):
    rest = list(range(1, plane_bits()))
    held = [own[None], other[None]]
    for step in range(len(rest)):
        for color in range(2):
            bit = rest[step] if color == 0 else rest[::-1][step]
            held[color] = jnp.concatenate([held[color], swap_core(held[color], bit, core)])
    return held


def gram_of(held):
    return sum(
        lax.dot_general(
            part.reshape(-1, part.shape[-1]),
            part.reshape(-1, part.shape[-1]),
            TOKENS_OUT,
            preferred_element_type=F32,
        )
        for part in held
    )


def to_owners(attn, ffn):
    lines = lax.axis_size("fsdp")
    attn_count, small, columns = attn.shape
    ffn_count, large, _ = ffn.shape
    at_one = min(lines, attn_count)
    spare = attn_count - at_one
    top = [ffn]
    if spare:
        top.append(jnp.pad(attn[at_one:], ((0, 0), (0, large - small), (0, 0))))
    if lines > ffn_count + spare:
        top.append(jnp.zeros((lines - ffn_count - spare, large, columns), ffn.dtype))
    low = attn[:at_one]
    if lines > at_one:
        low = jnp.pad(low, ((0, lines - at_one), (0, 0), (0, 0)))
    return jnp.concatenate(top), low


def exchange(top, low):
    large = top.shape[1]
    both = lax.all_to_all(
        jnp.concatenate([top, low], axis=1), "fsdp", split_axis=0, concat_axis=0, tiled=True
    )
    return both[:, :large], both[:, large:]


def from_owners(top, low, ffn_count, attn_count):
    at_one = min(top.shape[0], attn_count)
    spare = attn_count - at_one
    attn = low[:at_one]
    if spare:
        attn = jnp.concatenate([attn, top[ffn_count : ffn_count + spare, : low.shape[1]]])
    return attn, top[:ffn_count]


def owner_momentum(moment, grad):
    return (MOMENT_DECAY * moment.astype(F32) + (1.0 - MOMENT_DECAY) * grad.astype(F32)).astype(B16)


def on_device(
    tokens,
    segment_ids,
    decay_rate,
    cotangent,
    attn_master,
    ffn_master,
    gains,
    attn_moment,
    ffn_moment,
    gain_first,
    gain_second,
):
    attn_low = attn_master.astype(B16)
    ffn_low = ffn_master.astype(B16)
    gain_low = gains.astype(B16)
    in_full, proj_full, up_full, down_full, gain_whole = (
        lax.all_gather(value, ("dp", "fsdp"), axis=1, tiled=True)
        for value in (attn_low[:4], attn_low[4:], ffn_low[:2], ffn_low[2:], gain_low)
    )
    ffn_full = (up_full, down_full[0])
    top_moment, low_moment = exchange(*to_owners(attn_moment.astype(B16), ffn_moment.astype(B16)))
    top_moment, low_moment, in_full = ordered(top_moment, low_moment, in_full)
    attn_full = (in_full, proj_full[0])
    stored = forward(tokens, segment_ids[0], decay_rate, attn_full, ffn_full, gain_whole)
    x_grad, grads, grad_gain = backward(
        stored, cotangent, attn_full, ffn_full, gain_whole
    )
    down, up, proj, inner = grads
    lines = lax.axis_size("fsdp")
    attn_count, small, columns = attn_master.shape
    ffn_count, large, _ = ffn_master.shape
    block, little = lines * large, lines * small
    inner_out = inner.payloads()
    inner_out, middle, product = tied([inner_out], stored[-6], stored[-1])
    inner.accept(inner.swap(inner_out))
    down_sum = down.finish()
    up_sum = up.finish()
    proj_sum = proj.finish()
    out = (middle + jnp.dot(product, ffn_full[1], preferred_element_type=F32)).astype(B16)
    at_one = min(lines, attn_count)
    top_grad = [up_sum, down_sum]
    if attn_count > at_one:
        spread = jnp.pad(proj_sum.reshape(1, lines, small, columns), ((0, 0), (0, 0), (0, large - small), (0, 0)))
        top_grad.append(spread.reshape(1, block, columns))
    top_grad = jnp.concatenate(top_grad)
    if lines > top_grad.shape[0]:
        top_grad = jnp.pad(top_grad, ((0, lines - top_grad.shape[0]), (0, 0), (0, 0)))
    top_grad = lax.psum_scatter(top_grad, "fsdp", scatter_dimension=0, tiled=True)[0]
    at_core = lax.axis_index("dp") & 1
    big = owner_momentum(top_moment.reshape(block, columns), top_grad)
    big_other = one_way(big, 0, True)
    top_gram = gram_of(gather_plane(big, big_other, 0))
    low_grad = inner.finish()
    if attn_count == at_one:
        low_grad = jnp.concatenate([low_grad, proj_sum])
    if lines > low_grad.shape[0]:
        low_grad = jnp.pad(low_grad, ((0, lines - low_grad.shape[0]), (0, 0), (0, 0)))
    top_grad, low_grad = ordered(top_grad, low_grad)
    low_grad = lax.psum_scatter(low_grad, "fsdp", scatter_dimension=0, tiled=True)[0]
    low = owner_momentum(low_moment.reshape(little, columns), low_grad)
    low_other = one_way(low, 0, False)
    low_gram = gram_of(gather_plane(low, low_other, 1))
    gram = jnp.where(at_core == 0, top_gram, low_gram)
    fill = ((0, block - little), (0, 0))
    mine = jnp.concatenate(
        [
            jnp.where(at_core == 0, big, jnp.pad(low, fill)),
            jnp.where(at_core == 0, big_other, jnp.pad(low_other, fill)),
        ]
    )
    result = gram_orthogonalize(mine, gram)
    own, other = result[:block], result[block:]
    back_top = one_way(other, 0, False)
    back_low = one_way(other[:little], 0, True)
    top_orth = jnp.where(at_core == 0, own, back_top).reshape(lines, large, columns)
    low_orth = jnp.where(at_core == 0, back_low, own[:little]).reshape(lines, small, columns)
    attn_orth, ffn_orth = from_owners(*exchange(top_orth, low_orth), ffn_count, attn_count)
    attn_orth, ffn_orth = attn_orth.astype(F32), ffn_orth.astype(F32)
    attn_grad, ffn_grad = from_owners(
        *exchange(top_grad.reshape(lines, large, columns), low_grad.reshape(lines, small, columns)),
        ffn_count,
        attn_count,
    )
    attn_grad, ffn_grad = attn_grad.astype(F32), ffn_grad.astype(F32)
    attn_state = MOMENT_DECAY * attn_moment + (1.0 - MOMENT_DECAY) * attn_grad
    ffn_state = MOMENT_DECAY * ffn_moment + (1.0 - MOMENT_DECAY) * ffn_grad
    gain_grad = gain_sum(grad_gain)
    attn_new = attn_master - LR_MUON * attn_orth
    ffn_new = ffn_master - LR_MUON * math.sqrt(FF / D) * ffn_orth
    first_new = BETA_ONE * gain_first + (1.0 - BETA_ONE) * gain_grad
    second_new = BETA_TWO * gain_second + (1.0 - BETA_TWO) * gain_grad * gain_grad
    gains_new = gains - LR_GAIN * first_new / (jnp.sqrt(second_new) + ADAM_EPS)
    return (
        out,
        x_grad,
        attn_grad,
        ffn_grad,
        gain_grad,
        attn_state,
        ffn_state,
        attn_new,
        ffn_new,
        attn_new.astype(B16),
        ffn_new.astype(B16),
        gains_new,
        first_new,
        second_new,
    )


def solution(mesh):
    return jax.shard_map(
        on_device,
        mesh=mesh,
        in_specs=(
            P(("dp", "fsdp"), None),
            P(("dp", "fsdp"), None),
            P(),
            P(("dp", "fsdp"), None),
            P(None, ("dp", "fsdp"), None),
            P(None, ("dp", "fsdp"), None),
            P(None, ("dp", "fsdp")),
            P(None, ("dp", "fsdp"), None),
            P(None, ("dp", "fsdp"), None),
            P(None, ("dp", "fsdp")),
            P(None, ("dp", "fsdp")),
        ),
        out_specs=(
            P(("dp", "fsdp"), None),
            P(("dp", "fsdp"), None),
            P(None, ("dp", "fsdp"), None),
            P(None, ("dp", "fsdp"), None),
            P(None, ("dp", "fsdp")),
            P(None, ("dp", "fsdp"), None),
            P(None, ("dp", "fsdp"), None),
            P(None, ("dp", "fsdp"), None),
            P(None, ("dp", "fsdp"), None),
            P(None, ("dp", "fsdp"), None),
            P(None, ("dp", "fsdp"), None),
            P(None, ("dp", "fsdp")),
            P(None, ("dp", "fsdp")),
            P(None, ("dp", "fsdp")),
        ),
        check_vma=False,
    )
```

time: 2270 us -> 807 us (0.36)
  waiting for transfers between devices: 1760 us -> 283 us
  matrix products: 273 us -> 125 us
  Pallas kernels: 0 us -> 66.2 us
  starting transfers between devices: 6.19 us -> 59.2 us
  local copies, waits for them, and re-layouts: 40.4 us -> 92.2 us
    reduce_scatter x2, waiting for transfers between devices: 1140 us -> 34.9 us  [the longest x1 24.2 us: on_device(): lax.psum_scatter(low_grad, 'fsdp', scatter_dimension=0, tiled=True)[0]]
    psum x5 -> x0, waiting for transfers between devices: 400 us -> none  [newton_schulz(): lax.psum(local_gram.astype(jnp.bfloat16), 'dp').astype(jnp.float32)]
    dot_general x38 -> x12, matrix products: 204 us -> 76.1 us  [the longest x4 16.1 us: gram_of(): lax.dot_general(part.reshape(-1, part.shape[-1]), part.reshape(-1, part.s...]
    unnamed x11 -> x6, waiting for transfers between devices: 127 us -> 0.14 us
    ppermute x0 -> x32, waiting for transfers between devices: none -> 91 us  [the longest x20 63.3 us: swap_bit(): return lax.ppermute(value, 'dp', [(i, i ^ 1 << bit) for i in range(count)])]
    pallas_call x0 -> x1, Pallas kernels: none -> 66.2 us  [gram_orthogonalize(): pl.pallas_call(polynomial_kernel, out_shape=jax.ShapeDtypeStruct(rows.sha...]
    all_gather x2 -> x4, waiting for transfers between devices: 92.3 us -> 146 us  [on_device(): lax.all_gather(value, ('dp', 'fsdp'), axis=1, tiled=True)]
    ppermute x0 -> x32, starting transfers between devices: none -> 39.2 us  [the longest x20 17.5 us: swap_bit(): return lax.ppermute(value, 'dp', [(i, i ^ 1 << bit) for i in range(count)])]
  transfers between devices with their start and end apart: 11 -> 42, of which waited for: 10 -> 15; matrix products, arithmetic and copies ran while one was open for 5% -> 21% of each run, Pallas kernels for 0% -> 8%
where the time goes in v2:
time: 807 us; the launch traced here: 796 us
  waiting for transfers between devices  283 us (35%)
  matrix products  125 us (15%)
  local copies, waits for them, and re-layouts  92.2 us (11%)
  blocking collectives  88.4 us (11%)
  Pallas kernels  66.2 us (8%)
  other arithmetic  66.1 us (8%)
  starting transfers between devices  59.2 us (7%)
  between operations  16.2 us (2%)
    all_gather x4, waiting for transfers between devices, on_device(): lax.all_gather(value, ('dp', 'fsdp'), axis=1, tiled=True)  146 us
    all_gather x1, blocking collectives, on_device(): lax.all_gather(value, ('dp', 'fsdp'), axis=1, tiled=True)  88.4 us
    pallas_call x1, Pallas kernels, gram_orthogonalize(): pl.pallas_call(polynomial_kernel, out_shape=jax.ShapeDtypeStruct(rows.sha...  66.2 us
    ppermute x20, waiting for transfers between devices, swap_bit(): return lax.ppermute(value, 'dp', [(i, i ^ 1 << bit) for i in range(count)])  63.3 us
    unnamed x171, local copies, waits for them, and re-layouts  29.2 us
    ppermute x8, waiting for transfers between devices, swap_core(): lax.ppermute(value, 'dp', [(i, i ^ 1 << bit) for i in range(count) if i &...  26.3 us
    reduce_scatter x1, waiting for transfers between devices, on_device(): lax.psum_scatter(low_grad, 'fsdp', scatter_dimension=0, tiled=True)[0]  24.2 us
    convert_element_type x16, other arithmetic, payloads(): sum((self.choose(t, dims, bit, True).astype(F32) for t, dims in part))  18.2 us
  transfers between devices with their start and end apart: 42, of which 15 were waited for; matrix products, arithmetic and copies ran while one was open for 21% of the time, Pallas kernels for 8%

profile of v2, /device:TPU:0, one launch (start us, length us, event | category | flops | bytes accessed | tf_op | source)
XLA Modules:
  0.0 795.8 jit_solution(8094379103252482500)
XLA Ops:
  19.4 88.4 %all-gather = bf16[32,32,3]{1,2,0:T(4,128)(2,1)S(1)} all-gather(bf16[1,32,3]{1,2,0:T(4,128)(2,1)S(1)} %convert_bitcast_fusion.1), channel_id=1, replica_groups=mesh['dp'=8,'fsdp'=4] {'dp','fsdp'}, dimensions={0}, use_global_device_ids=true | all-gather | bytes 6336 | tf_op jit(solution)/shard_map/all_gather | solution.py:500
  111.8 7.1 fusion.95
  141.1 18.7 %all-gather.8.cloned.1.call-done = bf16[1,1024,1024]{2,1,0:T(8,128)(2,1)} async-done(((bf16[1,32,1024]{2,1,0:T(8,128)(2,1)}), bf16[1,1024,1024]{2,1,0:T(8,128)(2,1)}) %all-gather.8.cloned.1.call-update) | async-done | bytes 2097168 | tf_op jit(solution)/shard_map/all_gather | solution.py:500
  164.6 88.3 %all-gather.10.cloned.1.call-done = bf16[2,2816,1024]{2,1,0:T(8,128)(2,1)} async-done(((bf16[2,88,1024]{2,1,0:T(8,128)(2,1)}), bf16[2,2816,1024]{2,1,0:T(8,128)(2,1)}) %all-gather.10.cloned.1.call-update) | async-done | bytes 11534352 | tf_op jit(solution)/shard_map/all_gather | solution.py:500
  252.9 10.1 %fusion.110 = f32[512,5632]{1,0:T(8,128)S(1)} fusion(bf16[5632,1024]{1,0:T(8,128)(2,1)} %bitcast.332, f32[512,1024]{1,0:T(8,128)} %get-tuple-element.95, f32[1024]{0:T(1024)S(1)} %bitcast.327, f32[512]{0:T(512)S(1)} %get-tuple-element.164), kind=kOutput, calls=%fused_computation.227 | convolution fusion | flops 5907152896 | bytes 25171968 | tf_op jit(solution)/shard_map/dot_general | solution.py:87
  283.1 39.0 %all-gather.12.cloned.1.call-done = bf16[1,2816,1024]{2,1,0:T(8,128)(2,1)} async-done(((bf16[1,88,1024]{2,1,0:T(8,128)(2,1)}), bf16[1,2816,1024]{2,1,0:T(8,128)(2,1)}) %all-gather.12.cloned.1.call-update) | async-done | bytes 5767184 | tf_op jit(solution)/shard_map/all_gather | solution.py:500
  322.1 9.5 %multiply_convert_fusion.3 = (bf16[512,2816]{1,0:T(8,128)(2,1)S(1)}, bf16[512,2816]{1,0:T(8,128)(2,1)S(1)}) fusion(f32[512,5632]{1,0:T(8,128)} %copy-done.1, bf16[512,1024]{1,0:T(8,128)(2,1)} %param.14, bf16[1,2816,1024]{2,1,0:T(8,128)(2,1)} %all-gather.12.cloned.1.call-done), kind=kOutput, calls=%fused_computation.13 | convolution fusion | flops 2958557184 | bytes 24117248 | tf_op jit(solution)/shard_map/dot_general | solution.py:154
  341.4 9.3 %convolution_convert_fusion = bf16[5632,1024]{1,0:T(8,128)(2,1)} fusion(bf16[512,5632]{1,0:T(8,128)(2,1)S(1)} %pad_maximum_fusion, f32[512,1024]{1,0:T(8,128)S(1)} %copy-done.46, f32[1024]{0:T(1024)S(1)} %bitcast.328, f32[512]{0:T(512)S(1)} %get-tuple-element.164), kind=kOutput, calls=%fused_computation.3 | convolution fusion | flops 5912920064 | bytes 19404800 | tf_op jit(solution)/shard_map/dot_general | solution.py:160
  350.6 10.5 %constant_dynamic-slice_fusion.3 = (bf16[2,2,2,1,352,1024]{5,4,3,2,1,0:T(8,128)(2,1)}, bf16[2,2,2,1,352,1024]{5,4,3,2,1,0:T(8,128)(2,1)}) fusion(bf16[2,2,2,2,352,1024]{5,4,3,2,1,0:T(8,128)(2,1)} %bitcast.286, s32[]{:T(128)S(6)} %select_n.168, s32[]{:T(128)S(6)} %select_n.170), kind=kLoop, calls=%fused_computation.207 | loop fusion | bytes 23068680 | tf_op jit(solution)/shard_map/jit(dynamic_index_in_dim)/dynamic_slice | solution.py:261
  372.7 11.1 %multiply_reduce_fusion.1 = (f32[1024]{0:T(1024)S(1)}, f32[512]{0:T(512)S(1)}, f32[512,1024]{1,0:T(8,128)S(1)}) fusion(f32[512,1024]{1,0:T(8,128)S(1)} %copy-done.47, f32[512]{0:T(512)S(1)} %get-tuple-element.164, f32[1024]{0:T(1024)S(1)} %bitcast.329, bf16[512,5632]{1,0:T(8,128)(2,1)} %copy-done.19, bf16[5632,1024]{1,0:T(8,128)(2,1)} %bitcast.333), kind=kOutput, calls=%fused_computation.70 | convolution fusion | flops 5908724224 | bytes 21508096 | tf_op jit(solution)/shard_map/dot_general | solution.py:164
  442.2 24.6 %collective-permute-done.4 = bf16[1,176,1024]{2,1,0:T(8,128)(2,1)} collective-permute-done((bf16[1,176,1024]{2,1,0:T(8,128)(2,1)}, bf16[1,176,1024]{2,1,0:T(8,128)(2,1)}, u32[]{:S(2)}, u32[]{:S(2)}) %collective-permute-start.4) | collective-permute-done | bytes 360480 | tf_op jit(solution)/shard_map/ppermute | solution.py:246
  474.9 7.7 convolution_convert_fusion.1
  482.5 7.0 constant_dynamic-slice_fusion.1
  494.7 7.3 fusion.25
  507.0 7.5 collective-permute-done.11
  532.5 20.6 %collective-permute-done.18 = bf16[4,2,64,1024]{3,2,0,1:T(8,128)(2,1)S(1)} collective-permute-done((bf16[4,2,64,1024]{3,2,0,1:T(8,128)(2,1)S(1)}, bf16[4,2,64,1024]{3,2,0,1:T(8,128)(2,1)S(1)}, u32[]{:S(2)}, u32[]{:S(2)}) %collective-permute-start.18) | collective-permute-done | bytes 1048608 | tf_op jit(solution)/shard_map/ppermute | solution.py:246
  556.0 9.3 %collective-permute-done.19 = bf16[4,64,1024]{2,1,0:T(8,128)(2,1)S(1)} collective-permute-done((bf16[4,64,1024]{2,1,0:T(8,128)(2,1)S(1)}, bf16[4,64,1024]{2,1,0:T(8,128)(2,1)S(1)}, u32[]{:S(2)}, u32[]{:S(2)}) %collective-permute-start.19) | collective-permute-done | bytes 524320 | tf_op jit(solution)/shard_map/ppermute | solution.py:246
  567.8 10.7 %reduce-scatter.3.cloned.1.call-done = bf16[1,352,1024]{2,1,0:T(8,128)(2,1)} async-done(((bf16[4,352,1024]{2,1,0:T(8,128)(2,1)}), bf16[1,352,1024]{2,1,0:T(8,128)(2,1)}) %reduce-scatter.3.cloned.1.call-update) | async-done | bytes 720912 | tf_op jit(solution)/shard_map/reduce_scatter | solution.py:531
  584.1 24.2 %reduce-scatter.5.cloned.1.call-done = bf16[1,128,1024]{2,1,0:T(8,128)(2,1)} async-done(((bf16[4,128,1024]{2,1,0:T(8,128)(2,1)}), bf16[1,128,1024]{2,1,0:T(8,128)(2,1)}) %reduce-scatter.5.cloned.1.call-update) | async-done | bytes 262160 | tf_op jit(solution)/shard_map/reduce_scatter | solution.py:542
  628.5 17.6 %collective-permute-done.23 = bf16[1,352,1024]{2,1,0:T(8,128)(2,1)} collective-permute-done((bf16[1,352,1024]{2,1,0:T(8,128)(2,1)S(1)}, bf16[1,352,1024]{2,1,0:T(8,128)(2,1)}, u32[]{:S(2)}, u32[]{:S(2)}) %collective-permute-start.23) | collective-permute-done | bytes 720928 | tf_op jit(solution)/shard_map/ppermute | solution.py:420
  662.1 8.6 %collective-permute-done.24 = bf16[2,352,1024]{2,1,0:T(8,128)(2,1)S(1)} collective-permute-done((bf16[2,352,1024]{2,1,0:T(8,128)(2,1)S(1)}, bf16[2,352,1024]{2,1,0:T(8,128)(2,1)S(1)}, u32[]{:S(2)}, u32[]{:S(2)}) %collective-permute-start.24) | collective-permute-done | bytes 1441824 | tf_op jit(solution)/shard_map/ppermute | solution.py:420
  684.0 66.2 %shard_map.218 = bf16[704,1024]{1,0:T(8,128)(2,1)S(1)} custom-call(f32[1024,1024]{1,0:T(8,128)} %fusion.4.gram_ref, bf16[704,1024]{1,0:T(8,128)(2,1)S(1)} %pad_maximum_fusion.5.rows_ref), custom_call_target="tpu_custom_call" | custom-call | flops 32212254720 | bytes 8388608 | tf_op jit(solution)/shard_map/pallas_call | solution.py:399
  761.5 8.3 %add_convert_fusion.2 = bf16[512,1024]{1,0:T(8,128)(2,1)} fusion(f32[512,1024]{1,0:T(8,128)} %get-tuple-element.95, bf16[512,2816]{1,0:T(8,128)(2,1)} %copy-done.40, bf16[1,2816,1024]{2,1,0:T(8,128)(2,1)} %all-gather.12.cloned.1.call-done), kind=kOutput, calls=%fused_computation.71 | convolution fusion | flops 2953838592 | bytes 11796480 | tf_op jit(solution)/shard_map/dot_general | solution.py:522
  775.6 10.5 %all-to-all-done.3 = bf16[4,120,1024]{2,1,0:T(8,128)(2,1)S(1)} async-done(((bf16[4,120,1024]{2,1,0:T(8,128)(2,1)}), bf16[4,120,1024]{2,1,0:T(8,128)(2,1)S(1)}, u32[]{:S(2)}, u32[]{:S(2)}) %all-to-all-start.3) | async-done | bytes 983072 | tf_op jit(solution)/shard_map/all_to_all | solution.py:464
  (384 shorter events, 257.7 us)
Async XLA Ops:
  7.2 104.6 %all-gather.6.cloned.1.call-start = ((), (), s32[]{:S(2)}) async-start(), calls=%async_computation.6 | async-start | bytes 8650752 | tf_op jit(solution)/shard_map/all_gather | solution.py:500
  9.2 150.6 %all-gather.8.cloned.1.call-start = ((), (), s32[]{:S(2)}) async-start(), calls=%async_computation.7 | async-start | bytes 2162688 | tf_op jit(solution)/shard_map/all_gather | solution.py:500
  10.0 242.9 %all-gather.10.cloned.1.call-start = ((), (), s32[]{:S(2)}) async-start(), calls=%async_computation.8 | async-start | bytes 11894784 | tf_op jit(solution)/shard_map/all_gather | solution.py:500
  10.9 311.2 %all-gather.12.cloned.1.call-start = ((), (), s32[]{:S(2)}) async-start(), calls=%async_computation.9 | async-start | bytes 5947392 | tf_op jit(solution)/shard_map/all_gather | solution.py:500
  12.9 97.2 %all-to-all-start = ((bf16[4,120,1024]{2,1,0:T(8,128)(2,1)}), bf16[4,120,1024]{2,1,0:T(8,128)(2,1)S(1)}, u32[]{:S(2)}, u32[]{:S(2)}) async-start(bf16[4,120,1024]{2,1,0:T(8,128)(2,1)} %fusion.79), calls=%async_computation | async-start | bytes 1966080 | tf_op jit(solution)/shard_map/all_to_all | solution.py:464
  19.4 559.1 %reduce-scatter.3.cloned.1.call-start = ((), (), s32[]{:S(2)}) async-start(), calls=%async_computation.10 | async-start | bytes 3604480 | tf_op jit(solution)/shard_map/reduce_scatter | solution.py:531
  279.0 53.0 %collective-permute-start = (bf16[1,2,2,352,1024]{4,3,1,2,0:T(8,128)(2,1)}, bf16[1,2,2,352,1024]{4,3,1,2,0:T(8,128)(2,1)}, u32[]{:S(2)}, u32[]{:S(2)}) collective-permute-start(bf16[1,2,2,352,1024]{4,3,1,2,0:T(8,128)(2,1)} %bitcast.281), channel_id=1, source_target_pairs={{0,4},{4,0},{8,12},{12,8},{16,20},{20,16},{24,28},{28,24},{1,5},{5... | collective-permute-start | bytes 8650760 | tf_op jit(solution)/shard_map/ppermute | solution.py:246
  424.3 42.5 %collective-permute-start.6 = (bf16[2,2,176,1024]{3,2,0,1:T(8,128)(2,1)}, bf16[2,2,176,1024]{3,2,0,1:T(8,128)(2,1)}, u32[]{:S(2)}, u32[]{:S(2)}) collective-permute-start(bf16[2,2,176,1024]{3,2,0,1:T(8,128)(2,1)} %fusion.43), channel_id=1, source_target_pairs={{0,8},{4,12},{8,0},{12,4},{16,24},{20,28},{24,16},{28,20},{1,9},{5... | collective-permute-start | bytes 4325384 | tf_op jit(solution)/shard_map/ppermute | solution.py:246
  425.9 41.0 %collective-permute-start.7 = (bf16[2,2,176,1024]{3,2,0,1:T(8,128)(2,1)}, bf16[2,2,176,1024]{3,2,0,1:T(8,128)(2,1)}, u32[]{:S(2)}, u32[]{:S(2)}) collective-permute-start(bf16[2,2,176,1024]{3,2,0,1:T(8,128)(2,1)} %fusion.44), channel_id=1, source_target_pairs={{0,16},{4,20},{8,24},{12,28},{16,0},{20,4},{24,8},{28,12},{1,17},{... | collective-permute-start | bytes 4325384 | tf_op jit(solution)/shard_map/ppermute | solution.py:246
  431.5 35.3 %collective-permute-start.4 = (bf16[1,176,1024]{2,1,0:T(8,128)(2,1)}, bf16[1,176,1024]{2,1,0:T(8,128)(2,1)}, u32[]{:S(2)}, u32[]{:S(2)}) collective-permute-start(bf16[1,176,1024]{2,1,0:T(8,128)(2,1)} %fusion.88), channel_id=1, source_target_pairs={{0,16},{4,20},{8,24},{12,28},{16,0},{20,4},{24,8},{28,12},{1,17},{... | collective-permute-start | bytes 1081352 | tf_op jit(solution)/shard_map/ppermute | solution.py:246
  433.0 33.8 %collective-permute-start.5 = (bf16[1,176,1024]{2,1,0:T(8,128)(2,1)}, bf16[1,176,1024]{2,1,0:T(8,128)(2,1)}, u32[]{:S(2)}, u32[]{:S(2)}) collective-permute-start(bf16[1,176,1024]{2,1,0:T(8,128)(2,1)} %fusion.87), channel_id=1, source_target_pairs={{0,8},{4,12},{8,0},{12,4},{16,24},{20,28},{24,16},{28,20},{1,9},{5... | collective-permute-start | bytes 1081352 | tf_op jit(solution)/shard_map/ppermute | solution.py:246
  433.5 33.3 %collective-permute-start.8 = (bf16[1,2,2,128,1024]{4,3,2,1,0:T(8,128)(2,1)}, bf16[1,2,2,128,1024]{4,3,2,1,0:T(8,128)(2,1)}, u32[]{:S(2)}, u32[]{:S(2)}) collective-permute-start(bf16[1,2,2,128,1024]{4,3,2,1,0:T(8,128)(2,1)} %get-tuple-element.81), channel_id=1, source_target_pairs={{0,4},{4,0},{8,12},{12,8},{16,20},{20,16},{24,28},{28,24},{1,5},{5... | collective-permute-start | bytes 3145736 | tf_op jit(solution)/shard_map/ppermute | solution.py:246
  490.1 24.5 %collective-permute-start.13 = (bf16[4,2,2,128,1024]{4,3,0,1,2:T(8,128)(2,1)S(1)}, bf16[4,2,2,128,1024]{4,3,0,1,2:T(8,128)(2,1)S(1)}, u32[]{:S(2)}, u32[]{:S(2)}) collective-permute-start(bf16[4,2,2,128,1024]{4,3,0,1,2:T(8,128)(2,1)S(1)} %bitcast.305), channel_id=1, source_target_pairs={{0,4},{4,0},{8,12},{12,8},{16,20},{20,16},{24,28},{28,24},{1,5},{5... | collective-permute-start | bytes 12582920 | tf_op jit(solution)/shard_map/ppermute | solution.py:246
  490.6 23.9 %collective-permute-start.9 = (bf16[2,176,1024]{2,1,0:T(8,128)(2,1)S(1)}, bf16[2,176,1024]{2,1,0:T(8,128)(2,1)S(1)}, u32[]{:S(2)}, u32[]{:S(2)}) collective-permute-start(bf16[2,176,1024]{2,1,0:T(8,128)(2,1)S(1)} %copy-done.59), channel_id=1, source_target_pairs={{0,16},{4,20},{8,24},{12,28},{16,0},{20,4},{24,8},{28,12},{1,17},{... | collective-permute-start | bytes 2162696 | tf_op jit(solution)/shard_map/ppermute | solution.py:246
  523.2 85.1 %reduce-scatter.5.cloned.1.call-start = ((), (), s32[]{:S(2)}) async-start(), calls=%async_computation.11 | async-start | bytes 1310720 | tf_op jit(solution)/shard_map/reduce_scatter | solution.py:542
  531.0 23.9 %collective-permute-start.16 = (bf16[4,2,64,1024]{3,2,0,1:T(8,128)(2,1)S(1)}, bf16[4,2,64,1024]{3,2,0,1:T(8,128)(2,1)S(1)}, u32[]{:S(2)}, u32[]{:S(2)}) collective-permute-start(bf16[4,2,64,1024]{3,2,0,1:T(8,128)(2,1)S(1)} %fusion.56), channel_id=1, source_target_pairs={{0,8},{4,12},{8,0},{12,4},{16,24},{20,28},{24,16},{28,20},{1,9},{5... | collective-permute-start | bytes 3145736 | tf_op jit(solution)/shard_map/ppermute | solution.py:246
  580.7 30.4 %collective-permute-start.20 = (bf16[1,352,1024]{2,1,0:T(8,128)(2,1)}, bf16[1,352,1024]{2,1,0:T(8,128)(2,1)}, u32[]{:S(2)}, u32[]{:S(2)}) collective-permute-start(bf16[1,352,1024]{2,1,0:T(8,128)(2,1)} %fusion.55), channel_id=1, source_target_pairs={{0,8},{8,0},{16,24},{24,16},{1,9},{9,1},{17,25},{25,17},{2,10},{10... | collective-permute-start | bytes 2162696 | tf_op jit(solution)/shard_map/ppermute | solution.py:420
  613.8 38.7 %collective-permute-start.21 = (bf16[2,352,1024]{2,1,0:T(8,128)(2,1)}, bf16[2,352,1024]{2,1,0:T(8,128)(2,1)}, u32[]{:S(2)}, u32[]{:S(2)}) collective-permute-start(bf16[2,352,1024]{2,1,0:T(8,128)(2,1)} %pad_maximum_fusion.3), channel_id=1, source_target_pairs={{0,16},{8,24},{16,0},{24,8},{1,17},{9,25},{17,1},{25,9},{2,18},{10... | collective-permute-start | bytes 4325384 | tf_op jit(solution)/shard_map/ppermute | solution.py:420
  617.1 29.0 %collective-permute-start.23 = (bf16[1,352,1024]{2,1,0:T(8,128)(2,1)S(1)}, bf16[1,352,1024]{2,1,0:T(8,128)(2,1)}, u32[]{:S(2)}, u32[]{:S(2)}) collective-permute-start(bf16[1,352,1024]{2,1,0:T(8,128)(2,1)S(1)} %bitcast.307), channel_id=1, source_target_pairs={{0,16},{8,24},{16,0},{24,8},{1,17},{9,25},{17,1},{25,9},{2,18},{10... | collective-permute-start | bytes 2162696 | tf_op jit(solution)/shard_map/ppermute | solution.py:420
  621.4 57.9 %all-to-all-start.2 = ((f32[32,3,32]{2,1,0:T(4,128)}), f32[32,3,32]{2,1,0:T(4,128)S(1)}, u32[]{:S(2)}, u32[]{:S(2)}) async-start(f32[32,3,32]{2,1,0:T(4,128)} %maximum_bitcast_fusion), calls=%async_computation.4 | async-start | bytes 131072 | tf_op jit(solution)/shard_map/all_to_all | solution.py:307
  624.5 27.3 %collective-permute-start.27 = (bf16[128,1024]{1,0:T(8,128)(2,1)S(1)}, bf16[128,1024]{1,0:T(8,128)(2,1)S(1)}, u32[]{:S(2)}, u32[]{:S(2)}) collective-permute-start(bf16[128,1024]{1,0:T(8,128)(2,1)S(1)} %fusion.93), channel_id=1, source_target_pairs={{0,4},{8,12},{16,20},{24,28},{1,5},{9,13},{17,21},{25,29},{2,6},{1... | collective-permute-start | bytes 786440 | tf_op jit(solution)/shard_map/ppermute | solution.py:413
  627.8 30.9 %collective-permute-start.25 = (bf16[1,128,1024]{2,1,0:T(8,128)(2,1)S(1)}, bf16[1,128,1024]{2,1,0:T(8,128)(2,1)S(1)}, u32[]{:S(2)}, u32[]{:S(2)}) collective-permute-start(bf16[1,128,1024]{2,1,0:T(8,128)(2,1)S(1)} %fusion.90), channel_id=1, source_target_pairs={{4,12},{12,4},{20,28},{28,20},{5,13},{13,5},{21,29},{29,21},{6,14}... | collective-permute-start | bytes 786440 | tf_op jit(solution)/shard_map/ppermute | solution.py:420
  679.3 76.8 %all-to-all-start.1 = ((bf16[4,120,1024]{2,1,0:T(8,128)(2,1)}), bf16[4,120,1024]{2,1,0:T(8,128)(2,1)}, u32[]{:S(2)}, u32[]{:S(2)}) async-start(bf16[4,120,1024]{2,1,0:T(8,128)(2,1)} %pad_maximum_fusion.7), calls=%async_computation.3 | async-start | bytes 1966080 | tf_op jit(solution)/shard_map/all_to_all | solution.py:464
  756.2 30.0 %all-to-all-start.3 = ((bf16[4,120,1024]{2,1,0:T(8,128)(2,1)}), bf16[4,120,1024]{2,1,0:T(8,128)(2,1)S(1)}, u32[]{:S(2)}, u32[]{:S(2)}) async-start(bf16[4,120,1024]{2,1,0:T(8,128)(2,1)} %pad_maximum_fusion.8), calls=%async_computation.5 | async-start | bytes 1966080 | tf_op jit(solution)/shard_map/all_to_all | solution.py:464
  (101 other events, 1288.7 us)
Sparse Core Ops, SparseCore 0:
  11.6 89.6 all-gather.5
  104.8 54.9 all-gather.7
  163.3 89.5 all-gather.9
  256.2 65.8 all-gather.11
  523.3 55.1 reduce-scatter.2
  581.2 27.0 reduce-scatter.4

commit v3 on v2

--- a/solution.py
+++ b/solution.py
@@ -48,25 +48,24 @@
     return jnp.where(allowed[None], fading, 0.0)
 
 
-def forward(tokens, segments, decay_rate, attn_full, ffn_full, gain_low):
+def forward(tokens, segments, decay_rate, attn_full, up_gather, down_gather, gain_low):
     length, model_width = tokens.shape
     head_count = decay_rate.shape[0]
     head_size = model_width // head_count
-    hidden = ffn_full[0].shape[1]
     gain_full = gain_low.astype(F32)
     inputs = tokens.astype(F32)
     first_scale = rms_scale(inputs)
     normed = (inputs * first_scale * gain_full[0]).astype(B16)
     projected = lax.dot_general(
         normed,
-        attn_full[0].reshape(4 * model_width, model_width),
+        attn_full.reshape(5 * model_width, model_width),
         ROWS_BY_ROWS,
         preferred_element_type=F32,
     )
     query_act = jax.nn.relu(projected[:, :model_width]).astype(B16)
     key_act = jax.nn.relu(projected[:, model_width : 2 * model_width]).astype(B16)
     value_act = projected[:, 2 * model_width : 3 * model_width].astype(B16)
-    gate_pre = projected[:, 3 * model_width :]
+    gate_pre = projected[:, 3 * model_width : 4 * model_width]
     fading_mask = decay_mask(segments, decay_rate)
     query_heads = query_act.reshape(length, head_count, head_size)
     key_heads = key_act.reshape(length, head_count, head_size)
@@ -80,18 +79,17 @@
     normal_out = attended * out_scale * gain_full[2]
     gate_sig = jax.nn.sigmoid(gate_pre)
     gated_out = (normal_out * gate_sig).astype(B16)
-    branch = lax.dot_general(gated_out, attn_full[1], ROWS_BY_ROWS, preferred_element_type=F32)
+    down_gather.held, gated_out = tied([down_gather.held], gated_out)
+    down_gather.send()
+    branch = lax.dot_general(gated_out, attn_full[4], ROWS_BY_ROWS, preferred_element_type=F32)
     middle = inputs + branch
     second_scale = rms_scale(middle)
     normed_two = (middle * second_scale * gain_full[1]).astype(B16)
-    up_pair = lax.dot_general(
-        normed_two,
-        ffn_full[0].reshape(2 * hidden, model_width),
-        ROWS_BY_ROWS,
-        preferred_element_type=F32,
-    )
-    up_one = up_pair[:, :hidden]
-    up_two = up_pair[:, hidden:]
+    up_gather.pieces, normed_two = tied([up_gather.pieces], normed_two)
+    ffn_up = up_gather.join()
+    up_one, up_two = (
+        lax.dot_general(normed_two, matrix, ROWS_BY_ROWS, preferred_element_type=F32) for matrix in ffn_up
+    )
     product = (up_one * up_two).astype(B16)
     stored = (
         inputs,
@@ -115,10 +113,10 @@
         up_two,
         product,
     )
-    return stored
-
-
-def backward(stored, cotangent, attn_full, ffn_full, gain_low):
+    return stored, ffn_up
+
+
+def backward(stored, cotangent, attn_full, ffn_up, down_gather, gain_low):
     (
         inputs,
         first_scale,
@@ -144,39 +142,46 @@
     length, model_width = inputs.shape
     head_count = fading_mask.shape[0]
     head_size = model_width // head_count
-    hidden = ffn_full[0].shape[1]
+    hidden = product.shape[1]
     gain_full = gain_low.astype(F32)
     grad_out = cotangent.astype(F32)
-    grad_down = lax.dot_general(product, cotangent, TOKENS_OUT, preferred_element_type=F32).astype(B16)
-    down = Halving(grad_down[None])
-    down_out, cotangent = tied([down.payloads()], cotangent)
+    half = hidden // 2
+    down = Halving(
+        weight_grad(product[:, :half], cotangent), weight_grad(product[:, half:], cotangent)
+    )
+    down_out, down_gather.pieces, cotangent = tied([down.payloads(), down_gather.pieces], cotangent)
     down_in = down.swap(down_out)
-    grad_product = lax.dot_general(cotangent, ffn_full[1], ROWS_BY_ROWS, preferred_element_type=F32)
-    grad_pair = jnp.concatenate([grad_product * up_two, grad_product * up_one], axis=1).astype(B16)
-    down_in, grad_pair = tied([down_in], grad_pair)
+    ffn_down = down_gather.join()[0]
+    grad_product = lax.dot_general(cotangent, ffn_down, ROWS_BY_ROWS, preferred_element_type=F32)
+    grad_one = (grad_product * up_two).astype(B16)
+    grad_two = (grad_product * up_one).astype(B16)
+    send_one, send_two = weight_grad(grad_one[:, half:], normed_two), weight_grad(grad_two[:, half:], normed_two)
+    down_in, sends, grad_one, grad_two = tied([down_in, [send_one, send_two]], grad_one, grad_two)
     down.accept(down_in)
-    down_out, grad_pair = tied([down.payloads()], grad_pair)
+    one = Halving(weight_grad(grad_one[:, :half], normed_two), sends[0])
+    two = Halving(weight_grad(grad_two[:, :half], normed_two), sends[1])
+    one_in, two_in = one.swap(one.payloads()), two.swap(two.payloads())
+    down_out, grad_one, grad_two = tied([down.payloads()], grad_one, grad_two)
     down_in = down.swap(down_out)
-    grad_up = lax.dot_general(grad_pair, normed_two, TOKENS_OUT, preferred_element_type=F32).astype(B16)
-    up = Halving(grad_up.reshape(2, hidden, model_width))
-    up_out, grad_pair = tied([up.payloads()], grad_pair)
-    up_in = up.swap(up_out)
-    grad_normed_two = jnp.dot(
-        grad_pair, ffn_full[0].reshape(2 * hidden, model_width), preferred_element_type=F32
+    grad_normed_two = jnp.dot(grad_one, ffn_up[0], preferred_element_type=F32) + jnp.dot(
+        grad_two, ffn_up[1], preferred_element_type=F32
     )
     gain_two = jnp.sum(grad_normed_two * middle * second_scale, axis=0)
     grad_middle = grad_out + rms_back(middle, second_scale, grad_normed_two * gain_full[1])
     middle_low = grad_middle.astype(B16)
-    down_in, up_in, middle_low = tied([down_in, up_in], middle_low)
+    down_in, one_in, two_in, middle_low = tied([down_in, one_in, two_in], middle_low)
     down.accept(down_in)
-    up.accept(up_in)
-    down_out, up_out, middle_low = tied([down.payloads(), up.payloads()], middle_low)
-    down_in, up_in = down.swap(down_out), up.swap(up_out)
+    one.accept(one_in)
+    two.accept(two_in)
+    down_out, one_out, two_out, middle_low = tied(
+        [down.payloads(), one.payloads(), two.payloads()], middle_low
+    )
+    down_in, one_in, two_in = down.swap(down_out), one.swap(one_out), two.swap(two_out)
     grad_outproj = lax.dot_general(middle_low, gated_out, TOKENS_OUT, preferred_element_type=F32).astype(B16)
     proj = Halving(grad_outproj[None])
     proj_out, middle_low = tied([proj.payloads()], middle_low)
     proj_in = proj.swap(proj_out)
-    grad_gated = jnp.dot(middle_low, attn_full[1], preferred_element_type=F32)
+    grad_gated = jnp.dot(middle_low, attn_full[4], preferred_element_type=F32)
     grad_normal = grad_gated * gate_sig
     grad_gate = grad_gated * normal_out * gate_sig * (1.0 - gate_sig)
     gain_three = jnp.sum(grad_normal * attended * out_scale, axis=0)
@@ -210,27 +215,35 @@
         ],
         axis=1,
     ).astype(B16)
-    down_in, up_in, proj_in, grad_mixed = tied([down_in, up_in, proj_in], grad_mixed)
+    down_in, one_in, two_in, proj_in, grad_mixed = tied([down_in, one_in, two_in, proj_in], grad_mixed)
     down.accept(down_in)
-    up.accept(up_in)
+    one.accept(one_in)
+    two.accept(two_in)
     proj.accept(proj_in)
-    up_out, proj_out, grad_mixed = tied([up.payloads(), proj.payloads()], grad_mixed)
-    up_in, proj_in = up.swap(up_out), proj.swap(proj_out)
+    one_out, two_out, proj_out, grad_mixed = tied(
+        [one.payloads(), two.payloads(), proj.payloads()], grad_mixed
+    )
+    one_in, two_in, proj_in = one.swap(one_out), two.swap(two_out), proj.swap(proj_out)
     grad_inner = lax.dot_general(grad_mixed, normed, TOKENS_OUT, preferred_element_type=F32).astype(B16)
     inner = Halving(grad_inner.reshape(4, model_width, model_width))
     inner_out, grad_mixed = tied([inner.payloads()], grad_mixed)
     inner_in = inner.swap(inner_out)
     grad_normed = jnp.dot(
-        grad_mixed, attn_full[0].reshape(4 * model_width, model_width), preferred_element_type=F32
+        jnp.pad(grad_mixed, ((0, 0), (0, model_width))),
+        attn_full.reshape(5 * model_width, model_width),
+        preferred_element_type=F32,
     )
     gain_one = jnp.sum(grad_normed * inputs * first_scale, axis=0)
     grad_inputs = grad_middle + rms_back(inputs, first_scale, grad_normed * gain_full[0])
     grad_gain = jnp.stack([gain_one, gain_two, gain_three])
-    up_in, proj_in, inner_in, grad_inputs = tied([up_in, proj_in, inner_in], grad_inputs)
-    up.accept(up_in)
+    one_in, two_in, proj_in, inner_in, grad_inputs = tied(
+        [one_in, two_in, proj_in, inner_in], grad_inputs
+    )
+    one.accept(one_in)
+    two.accept(two_in)
     proj.accept(proj_in)
     inner.accept(inner_in)
-    return (grad_inputs, (down, up, proj, inner), grad_gain)
+    return (grad_inputs, (one, two, down, proj, inner), grad_gain, ffn_down)
 
 
 def ordered(*values):
@@ -246,18 +259,36 @@
     return lax.ppermute(value, "dp", [(i, i ^ (1 << bit)) for i in range(count)])
 
 
+def weight_grad(features, series):
+    return lax.dot_general(features, series, TOKENS_OUT, preferred_element_type=F32).astype(B16)
+
+
 class Halving:
-    def __init__(self, grad):
-        count, rows, columns = grad.shape
+    def __init__(self, grad, sent=None):
         bits = plane_bits()
-        self.chunk = rows // lax.axis_size("dp")
-        blocks = grad.reshape((count,) + (2,) * bits + (self.chunk, columns))
-        self.parts = [[(blocks, list(range(bits))[::-1])]]
+        self.fixed = sent is not None
+        if self.fixed:
+            rows, columns = grad.shape
+            self.chunk = 2 * rows // lax.axis_size("dp")
+            shape = (1,) + (2,) * (bits - 1) + (self.chunk, columns)
+            self.first = [sent.reshape(shape)]
+            self.parts = [[(grad.reshape(shape), list(range(1, bits))[::-1])]]
+        else:
+            count, rows, columns = grad.shape
+            self.chunk = rows // lax.axis_size("dp")
+            self.first = None
+            blocks = grad.reshape((count,) + (2,) * bits + (self.chunk, columns))
+            self.parts = [[(blocks, list(range(bits))[::-1])]]
         self.orders = [[0]]
 
     def choose(self, term, dims, bit, other):
-        place = (lax.axis_index("dp") >> bit) & 1
-        index = 1 - place if other else place
+        if bit not in dims:
+            return term
+        if self.fixed:
+            index = 1 if other else 0
+        else:
+            place = (lax.axis_index("dp") >> bit) & 1
+            index = 1 - place if other else place
         return lax.dynamic_index_in_dim(term, index, 1 + dims.index(bit), keepdims=False)
 
     def payloads(self):
@@ -270,6 +301,9 @@
             ]
             self.orders = [rest, rest[::-1]]
         self.bits = [order[0] for order in self.orders]
+        if self.first is not None:
+            first, self.first = self.first, None
+            return first
         return [
             sum(self.choose(t, dims, bit, True).astype(F32) for t, dims in part).astype(B16)
             for part, bit in zip(self.parts, self.bits)
@@ -298,6 +332,62 @@
         out.append(list(flat[at : at + len(part)]))
         at += len(part)
     return (*out, *flat[at:])
+
+
+def line_gather(value):
+    lines = lax.axis_size("fsdp")
+    above, below = [], []
+    from_above = from_below = value
+    for _ in range(lines - 1):
+        from_above = lax.ppermute(from_above, "fsdp", [(i, i - 1) for i in range(1, lines)])
+        from_below = lax.ppermute(from_below, "fsdp", [(i, i + 1) for i in range(lines - 1)])
+        above.append(from_above)
+        below.append(from_below)
+    every = jnp.stack(below[::-1] + [value] + above, axis=1)
+    return lax.dynamic_slice_in_dim(every, lines - 1 - lax.axis_index("fsdp"), lines, axis=1)
+
+
+class HiddenGather:
+    def __init__(self, line):
+        self.count, lines, _, self.columns = line.shape
+        rest = list(range(1, plane_bits()))
+        self.orders = (rest, rest[::-1])
+        self.held, self.have = [], []
+        for color, order in enumerate(self.orders):
+            held = line[:, : lines // 2] if color == 0 else line[:, lines // 2 :]
+            have = []
+            for bit in order[:-1]:
+                have = sorted(have + [bit], reverse=True)
+                held = jnp.stack([held, swap_bit(held, bit)], axis=1 + have.index(bit))
+            self.held.append(held)
+            self.have.append(have)
+
+    def send(self):
+        self.pieces = []
+        for held, order in zip(self.held, self.orders):
+            came = swap_bit(held, order[-1])
+            self.pieces += [held, came, swap_bit(held, 0), swap_bit(came, 0)]
+
+    def join(self):
+        out = []
+        for matrix in range(self.count):
+            sides = [[], []]
+            for color, (have, order) in enumerate(zip(self.have, self.orders)):
+                axis = sorted(have + order[-1:], reverse=True).index(order[-1])
+                held, came, other_held, other_came = (p[matrix] for p in self.pieces[4 * color : 4 * color + 4])
+                sides[0].append(jnp.stack([held, came], axis=axis))
+                sides[1].append(jnp.stack([other_held, other_came], axis=axis))
+            whole = jnp.stack([jnp.concatenate(side, axis=len(self.orders[0])) for side in sides])
+            out.append(whole.reshape(-1, self.columns))
+        return out
+
+
+def gain_gather(value):
+    rows, own = value.shape
+    total = lax.axis_size("dp") * lax.axis_size("fsdp")
+    copies = jnp.broadcast_to(value[None], (total, rows, own))
+    every = lax.all_to_all(copies, ("dp", "fsdp"), 0, 0, tiled=True)
+    return jnp.transpose(every, (1, 0, 2)).reshape(rows, total * own)
 
 
 def gain_sum(grad):
@@ -496,19 +586,20 @@
     attn_low = attn_master.astype(B16)
     ffn_low = ffn_master.astype(B16)
     gain_low = gains.astype(B16)
-    in_full, proj_full, up_full, down_full, gain_whole = (
-        lax.all_gather(value, ("dp", "fsdp"), axis=1, tiled=True)
-        for value in (attn_low[:4], attn_low[4:], ffn_low[:2], ffn_low[2:], gain_low)
-    )
-    ffn_full = (up_full, down_full[0])
+    attn_full = lax.all_gather(attn_low, ("dp", "fsdp"), axis=1, tiled=True)
+    up_line, down_low = ordered(line_gather(ffn_low[:2]), ffn_low[2:])
+    up_gather, down_gather = HiddenGather(up_line), HiddenGather(line_gather(down_low))
+    gain_whole = gain_gather(gain_low)
     top_moment, low_moment = exchange(*to_owners(attn_moment.astype(B16), ffn_moment.astype(B16)))
-    top_moment, low_moment, in_full = ordered(top_moment, low_moment, in_full)
-    attn_full = (in_full, proj_full[0])
-    stored = forward(tokens, segment_ids[0], decay_rate, attn_full, ffn_full, gain_whole)
-    x_grad, grads, grad_gain = backward(
-        stored, cotangent, attn_full, ffn_full, gain_whole
-    )
-    down, up, proj, inner = grads
+    up_gather.held, top_moment, low_moment, attn_full = tied(
+        [up_gather.held], top_moment, low_moment, attn_full
+    )
+    up_gather.send()
+    stored, ffn_up = forward(tokens, segment_ids[0], decay_rate, attn_full, up_gather, down_gather, gain_whole)
+    x_grad, grads, grad_gain, ffn_down = backward(
+        stored, cotangent, attn_full, ffn_up, down_gather, gain_whole
+    )
+    one, two, down, proj, inner = grads
     lines = lax.axis_size("fsdp")
     attn_count, small, columns = attn_master.shape
     ffn_count, large, _ = ffn_master.shape
@@ -516,12 +607,11 @@
     inner_out = inner.payloads()
     inner_out, middle, product = tied([inner_out], stored[-6], stored[-1])
     inner.accept(inner.swap(inner_out))
-    down_sum = down.finish()
-    up_sum = up.finish()
+    ffn_sums = [value.finish() for value in (one, two, down)]
     proj_sum = proj.finish()
-    out = (middle + jnp.dot(product, ffn_full[1], preferred_element_type=F32)).astype(B16)
+    out = (middle + jnp.dot(product, ffn_down, preferred_element_type=F32)).astype(B16)
     at_one = min(lines, attn_count)
-    top_grad = [up_sum, down_sum]
+    top_grad = ffn_sums
     if attn_count > at_one:
         spread = jnp.pad(proj_sum.reshape(1, lines, small, columns), ((0, 0), (0, 0), (0, large - small), (0, 0)))
         top_grad.append(spread.reshape(1, block, columns))

time: 807 us -> 741 us (0.918)
  blocking collectives: 88.4 us -> 0 us
  starting transfers between devices: 59.2 us -> 120 us
  waiting for transfers between devices: 283 us -> 251 us
  local copies, waits for them, and re-layouts: 92.2 us -> 66.7 us
  other arithmetic: 66.1 us -> 89.1 us
    all_gather x4 -> x1, waiting for transfers between devices: 146 us -> 0.01 us  [on_device(): attn_full = lax.all_gather(attn_low, ('dp', 'fsdp'), axis=1, tiled=True)]
    all_gather x1 -> x0, blocking collectives: 88.4 us -> none  [on_device(): lax.all_gather(value, ('dp', 'fsdp'), axis=1, tiled=True)]
    ppermute x0 -> x12, waiting for transfers between devices: none -> 61.5 us  [the longest x6 41.9 us: line_gather(): lax.ppermute(from_above, 'fsdp', [(i, i - 1) for i in range(1, lines)])]
    ppermute x20 -> x41, waiting for transfers between devices: 63.3 us -> 117 us  [swap_bit(): return lax.ppermute(value, 'dp', [(i, i ^ 1 << bit) for i in range(count)])]
    ppermute x0 -> x12, starting transfers between devices: none -> 42.6 us  [the longest x6 34.9 us: line_gather(): lax.ppermute(from_below, 'fsdp', [(i, i + 1) for i in range(lines - 1)])]
    ppermute x20 -> x41, starting transfers between devices: 17.5 us -> 33.5 us  [swap_bit(): return lax.ppermute(value, 'dp', [(i, i ^ 1 << bit) for i in range(count)])]
    another operation x1 -> x13, other arithmetic: 2.32 us -> 17.3 us  [the longest x4 7.74 us: __init__(): held = jnp.stack([held, swap_bit(held, bit)], axis=1 + have.index(bit))]
    dynamic_slice x2 -> x1, local copies, waits for them, and re-layouts: 17.5 us -> 3.37 us  [choose(): lax.dynamic_index_in_dim(term, index, 1 + dims.index(bit), keepdims=False)]
  transfers between devices with their start and end apart: 42 -> 73, of which waited for: 15 -> 30; matrix products, arithmetic and copies ran while one was open for 21% -> 26% of each run, Pallas kernels for 8% -> 9%
where the time goes in v3:
time: 741 us; the launch traced here: 735 us
  waiting for transfers between devices  251 us (34%)
  matrix products  126 us (17%)
  starting transfers between devices  120 us (16%)
  other arithmetic  89.1 us (12%)
  local copies, waits for them, and re-layouts  66.7 us (9%)
  Pallas kernels  66.2 us (9%)
  between operations  15.9 us (2%)
    ppermute x41, waiting for transfers between devices, swap_bit(): return lax.ppermute(value, 'dp', [(i, i ^ 1 << bit) for i in range(count)])  117 us
    pallas_call x1, Pallas kernels, gram_orthogonalize(): pl.pallas_call(polynomial_kernel, out_shape=jax.ShapeDtypeStruct(rows.sha...  66.2 us
    ppermute x6, waiting for transfers between devices, line_gather(): lax.ppermute(from_above, 'fsdp', [(i, i - 1) for i in range(1, lines)])  41.9 us
    ppermute x6, starting transfers between devices, line_gather(): lax.ppermute(from_below, 'fsdp', [(i, i + 1) for i in range(lines - 1)])  34.9 us
    ppermute x41, starting transfers between devices, swap_bit(): return lax.ppermute(value, 'dp', [(i, i ^ 1 << bit) for i in range(count)])  33.5 us
    ppermute x8, waiting for transfers between devices, swap_core(): lax.ppermute(value, 'dp', [(i, i ^ 1 << bit) for i in range(count) if i &...  26.5 us
    reduce_scatter x1, waiting for transfers between devices, on_device(): lax.psum_scatter(low_grad, 'fsdp', scatter_dimension=0, tiled=True)[0]  24.3 us
    dot_general x6, matrix products, weight_grad(): lax.dot_general(features, series, TOKENS_OUT, preferred_element_type=F32)  20.7 us
  transfers between devices with their start and end apart: 73, of which 30 were waited for; matrix products, arithmetic and copies ran while one was open for 26% of the time, Pallas kernels for 9%

profile of v3, /device:TPU:0, one launch (start us, length us, event | category | flops | bytes accessed | tf_op | source)
XLA Modules:
  0.0 735.0 jit_solution(8311680220270870108)
XLA Ops:
  18.4 7.1 collective-permute-done
  47.0 15.9 %collective-permute-done.4 = bf16[2,88,1024]{2,1,0:T(8,128)(2,1)S(1)} collective-permute-done((bf16[2,88,1024]{2,1,0:T(8,128)(2,1)S(1)}, bf16[2,88,1024]{2,1,0:T(8,128)(2,1)S(1)}, u32[]{:S(2)}, u32[]{:S(2)}) %collective-permute-start.4) | collective-permute-done | bytes 360480 | tf_op jit(solution)/shard_map/ppermute | solution.py:342
  66.4 7.5 %collective-permute-done.5 = bf16[2,88,1024]{2,1,0:T(8,128)(2,1)S(1)} collective-permute-done((bf16[2,88,1024]{2,1,0:T(8,128)(2,1)S(1)}, bf16[2,88,1024]{2,1,0:T(8,128)(2,1)S(1)}, u32[]{:S(2)}, u32[]{:S(2)}) %collective-permute-start.5) | collective-permute-done | bytes 360480 | tf_op jit(solution)/shard_map/ppermute | solution.py:342
  85.8 8.4 %collective-permute-start.15 = (bf16[1,88,1024]{2,1,0:T(8,128)(2,1)}, bf16[1,88,1024]{2,1,0:T(8,128)(2,1)}, u32[]{:S(2)}, u32[]{:S(2)}) collective-permute-start(bf16[1,88,1024]{2,1,0:T(8,128)(2,1)} %collective-permute-done.14), channel_id=1, source_target_pairs={{0,1},{1,2},{2,3},{4,5},{5,6},{6,7},{8,9},{9,10},{10,11},{12,13},{... | collective-permute-start | bytes 540680 | tf_op jit(solution)/shard_map/ppermute | solution.py:343
  102.6 6.9 collective-permute-start.16
  114.0 11.2 %collective-permute-done.18 = bf16[1,88,1024]{2,1,0:T(8,128)(2,1)S(1)} collective-permute-done((bf16[1,88,1024]{2,1,0:T(8,128)(2,1)}, bf16[1,88,1024]{2,1,0:T(8,128)(2,1)S(1)}, u32[]{:S(2)}, u32[]{:S(2)}) %collective-permute-start.18) | collective-permute-done | bytes 180256 | tf_op jit(solution)/shard_map/ppermute | solution.py:342
  135.3 7.3 collective-permute-done.19
  157.3 8.6 %fusion.105 = f32[512,5120]{1,0:T(8,128)S(1)} fusion(bf16[5120,1024]{1,0:T(8,128)(2,1)} %bitcast.430, bf16[512,1024]{1,0:T(8,128)(2,1)S(1)} %copy-done.19, f32[1024]{0:T(1024)S(1)} %mul.337, f32[512]{0:T(512)S(1)} %get-tuple-element.256), kind=kOutput, calls=%fused_computation.235 | convolution fusion | flops 5370806272 | bytes 22026240 | tf_op jit(solution)/shard_map/dot_general | solution.py:59
  195.7 13.2 %collective-permute-done.11 = bf16[2,2,2,88,1024]{4,3,2,1,0:T(8,128)(2,1)} collective-permute-done((bf16[2,2,2,88,1024]{4,3,2,1,0:T(8,128)(2,1)}, bf16[2,2,2,88,1024]{4,3,2,1,0:T(8,128)(2,1)}, u32[]{:S(2)}, u32[]{:S(2)}) %collective-permute-start.11) | collective-permute-done | bytes 1441824 | tf_op jit(solution)/shard_map/ppermute | solution.py:259
  213.5 12.1 %collective-permute-done.22 = bf16[1,2,2,88,1024]{4,3,2,0,1:T(8,128)(2,1)} collective-permute-done((bf16[1,2,2,88,1024]{4,3,2,0,1:T(8,128)(2,1)}, bf16[1,2,2,88,1024]{4,3,2,0,1:T(8,128)(2,1)}, u32[]{:S(2)}, u32[]{:S(2)}) %collective-permute-start.22) | collective-permute-done | bytes 720928 | tf_op jit(solution)/shard_map/ppermute | solution.py:259
  230.0 10.6 %collective-permute-done.25 = bf16[1,2,2,88,1024]{4,3,2,1,0:T(8,128)(2,1)} collective-permute-done((bf16[1,2,2,88,1024]{4,3,2,1,0:T(8,128)(2,1)S(1)}, bf16[1,2,2,88,1024]{4,3,2,1,0:T(8,128)(2,1)}, u32[]{:S(2)}, u32[]{:S(2)}) %collective-permute-start.25) | collective-permute-done | bytes 720928 | tf_op jit(solution)/shard_map/ppermute | solution.py:259
  282.1 8.4 %multiply_convert_fusion.2 = (bf16[512,2816]{1,0:T(8,128)(2,1)}, bf16[512,2816]{1,0:T(8,128)(2,1)}) fusion(f32[512,2816]{1,0:T(8,128)} %get-tuple-element.266, f32[512,2816]{1,0:T(8,128)} %copy-done.2, bf16[512,1024]{1,0:T(8,128)(2,1)} %param.14, bf16[2816,1024]{1,0:T(8,128)(2,1)S(1)} %bitcast.377), kind=kOutput, calls=%fused_computation.7 | convolution fusion | flops 2958557184 | bytes 24117248 | tf_op jit(solution)/shard_map/dot_general | solution.py:155
  368.9 21.1 %collective-permute-done.33 = bf16[1,176,1024]{2,1,0:T(8,128)(2,1)S(1)} collective-permute-done((bf16[1,176,1024]{2,1,0:T(8,128)(2,1)}, bf16[1,176,1024]{2,1,0:T(8,128)(2,1)S(1)}, u32[]{:S(2)}, u32[]{:S(2)}) %collective-permute-start.33) | collective-permute-done | bytes 360480 | tf_op jit(solution)/shard_map/ppermute | solution.py:259
  392.4 15.0 %collective-permute-done.37 = bf16[1,2,176,1024]{3,2,1,0:T(8,128)(2,1)S(1)} collective-permute-done((bf16[1,2,176,1024]{3,2,1,0:T(8,128)(2,1)S(1)}, bf16[1,2,176,1024]{3,2,1,0:T(8,128)(2,1)S(1)}, u32[]{:S(2)}, u32[]{:S(2)}) %collective-permute-start.37) | collective-permute-done | bytes 720928 | tf_op jit(solution)/shard_map/ppermute | solution.py:259
  430.8 10.1 %fusion.23 = (f32[1024]{0:T(1024)S(1)}, f32[512]{0:T(512)S(1)}, f32[512,1024]{1,0:T(8,128)S(1)}) fusion(bf16[512,1024]{1,0:T(8,128)(2,1)S(1)} %copy-done.20, f32[512]{0:T(512)S(1)} %copy-done.86, f32[1024]{0:T(1024)S(1)} %copy-done.82, bf16[5120,1024]{1,0:T(8,128)(2,1)} %bitcast.431, bf16[512,4096]{1,0:T(8,128)(2,1)} %copy-done.25), kind=kOutput, calls=%fused_computation.57 | convolution fusion | flops 5372377600 | bytes 17838080 | tf_op jit(solution)/shard_map/dot_general | solution.py:231
  474.0 20.7 %collective-permute-done.49 = bf16[4,2,64,1024]{3,2,0,1:T(8,128)(2,1)S(1)} collective-permute-done((bf16[4,2,64,1024]{3,2,0,1:T(8,128)(2,1)S(1)}, bf16[4,2,64,1024]{3,2,0,1:T(8,128)(2,1)S(1)}, u32[]{:S(2)}, u32[]{:S(2)}) %collective-permute-start.49) | collective-permute-done | bytes 1048608 | tf_op jit(solution)/shard_map/ppermute | solution.py:259
  498.6 7.6 %collective-permute-done.50 = bf16[4,64,1024]{2,1,0:T(8,128)(2,1)S(1)} collective-permute-done((bf16[4,64,1024]{2,1,0:T(8,128)(2,1)S(1)}, bf16[4,64,1024]{2,1,0:T(8,128)(2,1)S(1)}, u32[]{:S(2)}, u32[]{:S(2)}) %collective-permute-start.50) | collective-permute-done | bytes 524320 | tf_op jit(solution)/shard_map/ppermute | solution.py:259
  508.0 9.9 %reduce-scatter.3.cloned.1.call-done = bf16[1,352,1024]{2,1,0:T(8,128)(2,1)} async-done(((bf16[4,352,1024]{2,1,0:T(8,128)(2,1)}), bf16[1,352,1024]{2,1,0:T(8,128)(2,1)}) %reduce-scatter.3.cloned.1.call-update) | async-done | bytes 720912 | tf_op jit(solution)/shard_map/reduce_scatter | solution.py:621
  523.4 24.3 %reduce-scatter.5.cloned.1.call-done = bf16[1,128,1024]{2,1,0:T(8,128)(2,1)} async-done(((bf16[4,128,1024]{2,1,0:T(8,128)(2,1)}), bf16[1,128,1024]{2,1,0:T(8,128)(2,1)}) %reduce-scatter.5.cloned.1.call-update) | async-done | bytes 262160 | tf_op jit(solution)/shard_map/reduce_scatter | solution.py:632
  568.0 17.7 %collective-permute-done.56 = bf16[1,352,1024]{2,1,0:T(8,128)(2,1)} collective-permute-done((bf16[1,352,1024]{2,1,0:T(8,128)(2,1)S(1)}, bf16[1,352,1024]{2,1,0:T(8,128)(2,1)}, u32[]{:S(2)}, u32[]{:S(2)}) %collective-permute-start.56) | collective-permute-done | bytes 720928 | tf_op jit(solution)/shard_map/ppermute | solution.py:510
  601.5 8.8 %collective-permute-done.57 = bf16[2,352,1024]{2,1,0:T(8,128)(2,1)S(1)} collective-permute-done((bf16[2,352,1024]{2,1,0:T(8,128)(2,1)S(1)}, bf16[2,352,1024]{2,1,0:T(8,128)(2,1)S(1)}, u32[]{:S(2)}, u32[]{:S(2)}) %collective-permute-start.57) | collective-permute-done | bytes 1441824 | tf_op jit(solution)/shard_map/ppermute | solution.py:510
  623.8 66.2 %shard_map.218 = bf16[704,1024]{1,0:T(8,128)(2,1)S(1)} custom-call(f32[1024,1024]{1,0:T(8,128)} %fusion.2.gram_ref, bf16[704,1024]{1,0:T(8,128)(2,1)S(1)} %pad_maximum_fusion.10.rows_ref), custom_call_target="tpu_custom_call" | custom-call | flops 32212254720 | bytes 8388608 | tf_op jit(solution)/shard_map/pallas_call | solution.py:489
  701.1 8.3 %add_convert_fusion = bf16[512,1024]{1,0:T(8,128)(2,1)} fusion(f32[512,1024]{1,0:T(8,128)} %copy-done.8, bf16[512,2816]{1,0:T(8,128)(2,1)} %copy-done.41, bf16[2816,1024]{1,0:T(8,128)(2,1)} %bitcast.378), kind=kOutput, calls=%fused_computation.75 | convolution fusion | flops 2953838592 | bytes 11796480 | tf_op jit(solution)/shard_map/dot_general | solution.py:612
  715.2 10.5 %all-to-all-done.4 = bf16[4,120,1024]{2,1,0:T(8,128)(2,1)S(1)} async-done(((bf16[4,120,1024]{2,1,0:T(8,128)(2,1)}), bf16[4,120,1024]{2,1,0:T(8,128)(2,1)S(1)}, u32[]{:S(2)}, u32[]{:S(2)}) %all-to-all-start.4) | async-done | bytes 983072 | tf_op jit(solution)/shard_map/all_to_all | solution.py:554
  (506 shorter events, 381.8 us)
Async XLA Ops:
  7.2 150.1 %all-gather.2.cloned.1.call-start = ((), (), s32[]{:S(2)}) async-start(), calls=%async_computation.7 | async-start | bytes 10813440 | tf_op jit(solution)/shard_map/all_gather | solution.py:589
  31.3 62.9 %all-to-all-start.1 = ((bf16[32,3,32]{2,1,0:T(4,128)(2,1)}), bf16[32,3,32]{2,1,0:T(4,128)(2,1)S(1)}, u32[]{:S(2)}, u32[]{:S(2)}) async-start(bf16[32,3,32]{2,1,0:T(4,128)(2,1)} %broadcast_in_dim.20), calls=%async_computation.1 | async-start | bytes 65536 | tf_op jit(solution)/shard_map/all_to_all | solution.py:389
  94.2 51.1 %all-to-all-start = ((bf16[4,120,1024]{2,1,0:T(8,128)(2,1)}), bf16[4,120,1024]{2,1,0:T(8,128)(2,1)S(1)}, u32[]{:S(2)}, u32[]{:S(2)}) async-start(bf16[4,120,1024]{2,1,0:T(8,128)(2,1)} %fusion.74), calls=%async_computation | async-start | bytes 1966080 | tf_op jit(solution)/shard_map/all_to_all | solution.py:554
  97.7 420.1 %reduce-scatter.3.cloned.1.call-start = ((), (), s32[]{:S(2)}) async-start(), calls=%async_computation.8 | async-start | bytes 3604480 | tf_op jit(solution)/shard_map/reduce_scatter | solution.py:621
  111.2 37.2 %collective-permute-start.7 = (bf16[2,2,88,1024]{3,2,1,0:T(8,128)(2,1)}, bf16[2,2,88,1024]{3,2,1,0:T(8,128)(2,1)}, u32[]{:S(2)}, u32[]{:S(2)}) collective-permute-start(bf16[2,2,88,1024]{3,2,1,0:T(8,128)(2,1)} %get-tuple-element.247), channel_id=1, source_target_pairs={{0,16},{4,20},{8,24},{12,28},{16,0},{20,4},{24,8},{28,12},{1,17},{... | collective-permute-start | bytes 2162696 | tf_op jit(solution)/shard_map/ppermute | solution.py:259
  112.5 38.3 %collective-permute-start.6 = (bf16[2,2,88,1024]{3,2,1,0:T(8,128)(2,1)}, bf16[2,2,88,1024]{3,2,1,0:T(8,128)(2,1)}, u32[]{:S(2)}, u32[]{:S(2)}) collective-permute-start(bf16[2,2,88,1024]{3,2,1,0:T(8,128)(2,1)} %get-tuple-element.248), channel_id=1, source_target_pairs={{0,8},{4,12},{8,0},{12,4},{16,24},{20,28},{24,16},{28,20},{1,9},{5... | collective-permute-start | bytes 2162696 | tf_op jit(solution)/shard_map/ppermute | solution.py:259
  177.2 31.8 %collective-permute-start.11 = (bf16[2,2,2,88,1024]{4,3,2,1,0:T(8,128)(2,1)}, bf16[2,2,2,88,1024]{4,3,2,1,0:T(8,128)(2,1)}, u32[]{:S(2)}, u32[]{:S(2)}) collective-permute-start(bf16[2,2,2,88,1024]{4,3,2,1,0:T(8,128)(2,1)} %copy.117), channel_id=1, source_target_pairs={{0,8},{4,12},{8,0},{12,4},{16,24},{20,28},{24,16},{28,20},{1,9},{5... | collective-permute-start | bytes 4325384 | tf_op jit(solution)/shard_map/ppermute | solution.py:259
  178.6 34.8 %collective-permute-start.8 = (bf16[2,2,2,88,1024]{4,3,2,0,1:T(8,128)(2,1)}, bf16[2,2,2,88,1024]{4,3,2,0,1:T(8,128)(2,1)}, u32[]{:S(2)}, u32[]{:S(2)}) collective-permute-start(bf16[2,2,2,88,1024]{4,3,2,0,1:T(8,128)(2,1)} %pad_maximum_fusion.5), channel_id=1, source_target_pairs={{0,16},{4,20},{8,24},{12,28},{16,0},{20,4},{24,8},{28,12},{1,17},{... | collective-permute-start | bytes 4325384 | tf_op jit(solution)/shard_map/ppermute | solution.py:259
  193.8 31.8 %collective-permute-start.22 = (bf16[1,2,2,88,1024]{4,3,2,0,1:T(8,128)(2,1)}, bf16[1,2,2,88,1024]{4,3,2,0,1:T(8,128)(2,1)}, u32[]{:S(2)}, u32[]{:S(2)}) collective-permute-start(bf16[1,2,2,88,1024]{4,3,2,0,1:T(8,128)(2,1)} %pad_maximum_fusion.14), channel_id=1, source_target_pairs={{0,16},{4,20},{8,24},{12,28},{16,0},{20,4},{24,8},{28,12},{1,17},{... | collective-permute-start | bytes 2162696 | tf_op jit(solution)/shard_map/ppermute | solution.py:259
  195.2 45.3 %collective-permute-start.12 = (bf16[2,2,2,88,1024]{4,3,2,0,1:T(8,128)(2,1)}, bf16[2,2,2,88,1024]{4,3,2,0,1:T(8,128)(2,1)}, u32[]{:S(2)}, u32[]{:S(2)}) collective-permute-start(bf16[2,2,2,88,1024]{4,3,2,0,1:T(8,128)(2,1)} %pad_maximum_fusion.6), channel_id=1, source_target_pairs={{0,4},{4,0},{8,12},{12,8},{16,20},{20,16},{24,28},{28,24},{1,5},{5... | collective-permute-start | bytes 4325384 | tf_op jit(solution)/shard_map/ppermute | solution.py:259
  195.2 45.9 %collective-permute-start.9 = (bf16[2,2,2,88,1024]{4,3,2,0,1:T(8,128)(2,1)}, bf16[2,2,2,88,1024]{4,3,2,0,1:T(8,128)(2,1)}, u32[]{:S(2)}, u32[]{:S(2)}) collective-permute-start(bf16[2,2,2,88,1024]{4,3,2,0,1:T(8,128)(2,1)} %pad_maximum_fusion.5), channel_id=1, source_target_pairs={{0,4},{4,0},{8,12},{12,8},{16,20},{20,16},{24,28},{28,24},{1,5},{5... | collective-permute-start | bytes 4325384 | tf_op jit(solution)/shard_map/ppermute | solution.py:259
  209.0 32.2 %collective-permute-start.13 = (bf16[2,2,2,88,1024]{4,3,2,1,0:T(8,128)(2,1)}, bf16[2,2,2,88,1024]{4,3,2,1,0:T(8,128)(2,1)}, u32[]{:S(2)}, u32[]{:S(2)}) collective-permute-start(bf16[2,2,2,88,1024]{4,3,2,1,0:T(8,128)(2,1)} %collective-permute-done.11), channel_id=1, source_target_pairs={{0,4},{4,0},{8,12},{12,8},{16,20},{20,16},{24,28},{28,24},{1,5},{5... | collective-permute-start | bytes 4325384 | tf_op jit(solution)/shard_map/ppermute | solution.py:259
  240.6 30.7 %collective-permute-start.23 = (bf16[1,2,2,88,1024]{4,3,2,0,1:T(8,128)(2,1)}, bf16[1,2,2,88,1024]{4,3,2,0,1:T(8,128)(2,1)}, u32[]{:S(2)}, u32[]{:S(2)}) collective-permute-start(bf16[1,2,2,88,1024]{4,3,2,0,1:T(8,128)(2,1)} %pad_maximum_fusion.14), channel_id=1, source_target_pairs={{0,4},{4,0},{8,12},{12,8},{16,20},{20,16},{24,28},{28,24},{1,5},{5... | collective-permute-start | bytes 2162696 | tf_op jit(solution)/shard_map/ppermute | solution.py:259
  240.6 30.7 %collective-permute-start.26 = (bf16[1,2,2,88,1024]{4,3,2,1,0:T(8,128)(2,1)S(1)}, bf16[1,2,2,88,1024]{4,3,2,1,0:T(8,128)(2,1)}, u32[]{:S(2)}, u32[]{:S(2)}) collective-permute-start(bf16[1,2,2,88,1024]{4,3,2,1,0:T(8,128)(2,1)S(1)} %copy-done.40), channel_id=1, source_target_pairs={{0,4},{4,0},{8,12},{12,8},{16,20},{20,16},{24,28},{28,24},{1,5},{5... | collective-permute-start | bytes 2162696 | tf_op jit(solution)/shard_map/ppermute | solution.py:259
  241.1 30.2 %collective-permute-start.24 = (bf16[1,2,2,88,1024]{4,3,2,0,1:T(8,128)(2,1)}, bf16[1,2,2,88,1024]{4,3,2,0,1:T(8,128)(2,1)}, u32[]{:S(2)}, u32[]{:S(2)}) collective-permute-start(bf16[1,2,2,88,1024]{4,3,2,0,1:T(8,128)(2,1)} %collective-permute-done.22), channel_id=1, source_target_pairs={{0,4},{4,0},{8,12},{12,8},{16,20},{20,16},{24,28},{28,24},{1,5},{5... | collective-permute-start | bytes 2162696 | tf_op jit(solution)/shard_map/ppermute | solution.py:259
  241.2 30.1 %collective-permute-start.27 = (bf16[1,2,2,88,1024]{4,3,2,1,0:T(8,128)(2,1)}, bf16[1,2,2,88,1024]{4,3,2,1,0:T(8,128)(2,1)}, u32[]{:S(2)}, u32[]{:S(2)}) collective-permute-start(bf16[1,2,2,88,1024]{4,3,2,1,0:T(8,128)(2,1)} %collective-permute-done.25), channel_id=1, source_target_pairs={{0,4},{4,0},{8,12},{12,8},{16,20},{20,16},{24,28},{28,24},{1,5},{5... | collective-permute-start | bytes 2162696 | tf_op jit(solution)/shard_map/ppermute | solution.py:259
  362.5 45.4 %collective-permute-start.39 = (bf16[1,2,2,128,1024]{4,3,2,1,0:T(8,128)(2,1)}, bf16[1,2,2,128,1024]{4,3,2,1,0:T(8,128)(2,1)S(1)}, u32[]{:S(2)}, u32[]{:S(2)}) collective-permute-start(bf16[1,2,2,128,1024]{4,3,2,1,0:T(8,128)(2,1)} %get-tuple-element.145), channel_id=1, source_target_pairs={{0,4},{4,0},{8,12},{12,8},{16,20},{20,16},{24,28},{28,24},{1,5},{5... | collective-permute-start | bytes 3145736 | tf_op jit(solution)/shard_map/ppermute | solution.py:259
  362.6 29.8 %collective-permute-start.35 = (bf16[1,2,176,1024]{3,2,1,0:T(8,128)(2,1)}, bf16[1,2,176,1024]{3,2,1,0:T(8,128)(2,1)S(1)}, u32[]{:S(2)}, u32[]{:S(2)}) collective-permute-start(bf16[1,2,176,1024]{3,2,1,0:T(8,128)(2,1)} %fusion.77), channel_id=1, source_target_pairs={{0,8},{4,12},{8,0},{12,4},{16,24},{20,28},{24,16},{28,20},{1,9},{5... | collective-permute-start | bytes 2162696 | tf_op jit(solution)/shard_map/ppermute | solution.py:259
  462.7 85.0 %reduce-scatter.5.cloned.1.call-start = ((), (), s32[]{:S(2)}) async-start(), calls=%async_computation.9 | async-start | bytes 1310720 | tf_op jit(solution)/shard_map/reduce_scatter | solution.py:632
  520.1 30.5 %collective-permute-start.53 = (bf16[1,352,1024]{2,1,0:T(8,128)(2,1)}, bf16[1,352,1024]{2,1,0:T(8,128)(2,1)}, u32[]{:S(2)}, u32[]{:S(2)}) collective-permute-start(bf16[1,352,1024]{2,1,0:T(8,128)(2,1)} %fusion.48), channel_id=1, source_target_pairs={{0,8},{8,0},{16,24},{24,16},{1,9},{9,1},{17,25},{25,17},{2,10},{10... | collective-permute-start | bytes 2162696 | tf_op jit(solution)/shard_map/ppermute | solution.py:510
  553.2 38.9 %collective-permute-start.54 = (bf16[2,352,1024]{2,1,0:T(8,128)(2,1)}, bf16[2,352,1024]{2,1,0:T(8,128)(2,1)}, u32[]{:S(2)}, u32[]{:S(2)}) collective-permute-start(bf16[2,352,1024]{2,1,0:T(8,128)(2,1)} %pad_maximum_fusion.8), channel_id=1, source_target_pairs={{0,16},{8,24},{16,0},{24,8},{1,17},{9,25},{17,1},{25,9},{2,18},{10... | collective-permute-start | bytes 4325384 | tf_op jit(solution)/shard_map/ppermute | solution.py:510
  560.9 58.0 %all-to-all-start.3 = ((f32[32,3,32]{2,1,0:T(4,128)}), f32[32,3,32]{2,1,0:T(4,128)S(1)}, u32[]{:S(2)}, u32[]{:S(2)}) async-start(f32[32,3,32]{2,1,0:T(4,128)} %maximum_bitcast_fusion.6), calls=%async_computation.5 | async-start | bytes 131072 | tf_op jit(solution)/shard_map/all_to_all | solution.py:397
  567.3 31.1 %collective-permute-start.58 = (bf16[1,128,1024]{2,1,0:T(8,128)(2,1)S(1)}, bf16[1,128,1024]{2,1,0:T(8,128)(2,1)S(1)}, u32[]{:S(2)}, u32[]{:S(2)}) collective-permute-start(bf16[1,128,1024]{2,1,0:T(8,128)(2,1)S(1)} %fusion.100), channel_id=1, source_target_pairs={{4,12},{12,4},{20,28},{28,20},{5,13},{13,5},{21,29},{29,21},{6,14}... | collective-permute-start | bytes 786440 | tf_op jit(solution)/shard_map/ppermute | solution.py:510
  618.9 77.1 %all-to-all-start.2 = ((bf16[4,120,1024]{2,1,0:T(8,128)(2,1)}), bf16[4,120,1024]{2,1,0:T(8,128)(2,1)}, u32[]{:S(2)}, u32[]{:S(2)}) async-start(bf16[4,120,1024]{2,1,0:T(8,128)(2,1)} %pad_maximum_fusion.12), calls=%async_computation.4 | async-start | bytes 1966080 | tf_op jit(solution)/shard_map/all_to_all | solution.py:554
  (148 other events, 2172.8 us)
Sparse Core Ops, SparseCore 0:
  11.6 113.2 all-gather.1
  462.8 54.9 reduce-scatter.2
  520.7 27.0 reduce-scatter.4

commit v4 on v3

--- a/solution.py
+++ b/solution.py
@@ -48,7 +48,7 @@
     return jnp.where(allowed[None], fading, 0.0)
 
 
-def forward(tokens, segments, decay_rate, attn_full, up_gather, down_gather, gain_low):
+def forward(tokens, segments, decay_rate, attn_full, ffn_up, gain_low):
     length, model_width = tokens.shape
     head_count = decay_rate.shape[0]
     head_size = model_width // head_count
@@ -79,14 +79,10 @@
     normal_out = attended * out_scale * gain_full[2]
     gate_sig = jax.nn.sigmoid(gate_pre)
     gated_out = (normal_out * gate_sig).astype(B16)
-    down_gather.held, gated_out = tied([down_gather.held], gated_out)
-    down_gather.send()
     branch = lax.dot_general(gated_out, attn_full[4], ROWS_BY_ROWS, preferred_element_type=F32)
     middle = inputs + branch
     second_scale = rms_scale(middle)
     normed_two = (middle * second_scale * gain_full[1]).astype(B16)
-    up_gather.pieces, normed_two = tied([up_gather.pieces], normed_two)
-    ffn_up = up_gather.join()
     up_one, up_two = (
         lax.dot_general(normed_two, matrix, ROWS_BY_ROWS, preferred_element_type=F32) for matrix in ffn_up
     )
@@ -113,10 +109,10 @@
         up_two,
         product,
     )
-    return stored, ffn_up
-
-
-def backward(stored, cotangent, attn_full, ffn_up, down_gather, gain_low):
+    return stored
+
+
+def backward(stored, cotangent, attn_full, ffn_up, ffn_down, gain_low):
     (
         inputs,
         first_scale,
@@ -149,9 +145,8 @@
     down = Halving(
         weight_grad(product[:, :half], cotangent), weight_grad(product[:, half:], cotangent)
     )
-    down_out, down_gather.pieces, cotangent = tied([down.payloads(), down_gather.pieces], cotangent)
+    down_out, cotangent = tied([down.payloads()], cotangent)
     down_in = down.swap(down_out)
-    ffn_down = down_gather.join()[0]
     grad_product = lax.dot_general(cotangent, ffn_down, ROWS_BY_ROWS, preferred_element_type=F32)
     grad_one = (grad_product * up_two).astype(B16)
     grad_two = (grad_product * up_one).astype(B16)
@@ -188,8 +183,13 @@
     grad_attended = (
         rms_back(attended, out_scale, grad_normal * gain_full[2])
         .astype(B16)
-        .reshape(length, head_count, head_size)
-    )
+    )
+    down_in, proj_in, grad_attended = tied([down_in, proj_in], grad_attended)
+    down.accept(down_in)
+    proj.accept(proj_in)
+    proj_out, grad_attended = tied([proj.payloads()], grad_attended)
+    proj_in = proj.swap(proj_out)
+    grad_attended = grad_attended.reshape(length, head_count, head_size)
     query_heads = query_act.reshape(length, head_count, head_size)
     key_heads = key_act.reshape(length, head_count, head_size)
     value_heads = value_act.reshape(length, head_count, head_size)
@@ -215,18 +215,18 @@
         ],
         axis=1,
     ).astype(B16)
-    down_in, one_in, two_in, proj_in, grad_mixed = tied([down_in, one_in, two_in, proj_in], grad_mixed)
-    down.accept(down_in)
+    inner = Halving(weight_grad(grad_mixed, normed).reshape(4, model_width, model_width))
+    inner_out, grad_mixed = tied([inner.payloads()], grad_mixed)
+    inner_in = inner.swap(inner_out)
+    one_in, two_in, proj_in, inner_in, grad_mixed = tied([one_in, two_in, proj_in, inner_in], grad_mixed)
     one.accept(one_in)
     two.accept(two_in)
     proj.accept(proj_in)
-    one_out, two_out, proj_out, grad_mixed = tied(
-        [one.payloads(), two.payloads(), proj.payloads()], grad_mixed
+    inner.accept(inner_in)
+    one_out, two_out, proj_out, inner_out, grad_mixed = tied(
+        [one.payloads(), two.payloads(), proj.payloads(), inner.payloads()], grad_mixed
     )
     one_in, two_in, proj_in = one.swap(one_out), two.swap(two_out), proj.swap(proj_out)
-    grad_inner = lax.dot_general(grad_mixed, normed, TOKENS_OUT, preferred_element_type=F32).astype(B16)
-    inner = Halving(grad_inner.reshape(4, model_width, model_width))
-    inner_out, grad_mixed = tied([inner.payloads()], grad_mixed)
     inner_in = inner.swap(inner_out)
     grad_normed = jnp.dot(
         jnp.pad(grad_mixed, ((0, 0), (0, model_width))),
@@ -236,14 +236,12 @@
     gain_one = jnp.sum(grad_normed * inputs * first_scale, axis=0)
     grad_inputs = grad_middle + rms_back(inputs, first_scale, grad_normed * gain_full[0])
     grad_gain = jnp.stack([gain_one, gain_two, gain_three])
-    one_in, two_in, proj_in, inner_in, grad_inputs = tied(
-        [one_in, two_in, proj_in, inner_in], grad_inputs
-    )
+    one_in, two_in, proj_in, grad_inputs = tied([one_in, two_in, proj_in], grad_inputs)
     one.accept(one_in)
     two.accept(two_in)
     proj.accept(proj_in)
     inner.accept(inner_in)
-    return (grad_inputs, (one, two, down, proj, inner), grad_gain, ffn_down)
+    return (grad_inputs, (one, two, down, proj, inner), grad_gain)
 
 
 def ordered(*values):
@@ -335,51 +333,37 @@
 
 
 def line_gather(value):
-    lines = lax.axis_size("fsdp")
-    above, below = [], []
-    from_above = from_below = value
-    for _ in range(lines - 1):
-        from_above = lax.ppermute(from_above, "fsdp", [(i, i - 1) for i in range(1, lines)])
-        from_below = lax.ppermute(from_below, "fsdp", [(i, i + 1) for i in range(lines - 1)])
-        above.append(from_above)
-        below.append(from_below)
-    every = jnp.stack(below[::-1] + [value] + above, axis=1)
-    return lax.dynamic_slice_in_dim(every, lines - 1 - lax.axis_index("fsdp"), lines, axis=1)
-
-
-class HiddenGather:
-    def __init__(self, line):
-        self.count, lines, _, self.columns = line.shape
-        rest = list(range(1, plane_bits()))
-        self.orders = (rest, rest[::-1])
-        self.held, self.have = [], []
-        for color, order in enumerate(self.orders):
-            held = line[:, : lines // 2] if color == 0 else line[:, lines // 2 :]
-            have = []
-            for bit in order[:-1]:
-                have = sorted(have + [bit], reverse=True)
-                held = jnp.stack([held, swap_bit(held, bit)], axis=1 + have.index(bit))
-            self.held.append(held)
-            self.have.append(have)
-
-    def send(self):
-        self.pieces = []
-        for held, order in zip(self.held, self.orders):
-            came = swap_bit(held, order[-1])
-            self.pieces += [held, came, swap_bit(held, 0), swap_bit(came, 0)]
-
-    def join(self):
-        out = []
-        for matrix in range(self.count):
-            sides = [[], []]
-            for color, (have, order) in enumerate(zip(self.have, self.orders)):
-                axis = sorted(have + order[-1:], reverse=True).index(order[-1])
-                held, came, other_held, other_came = (p[matrix] for p in self.pieces[4 * color : 4 * color + 4])
-                sides[0].append(jnp.stack([held, came], axis=axis))
-                sides[1].append(jnp.stack([other_held, other_came], axis=axis))
-            whole = jnp.stack([jnp.concatenate(side, axis=len(self.orders[0])) for side in sides])
-            out.append(whole.reshape(-1, self.columns))
-        return out
+    copies = jnp.broadcast_to(value[None], (lax.axis_size("fsdp"), *value.shape))
+    return lax.all_to_all(copies, "fsdp", 0, 0, tiled=True)
+
+
+def hidden_gather(line):
+    lines, count, _, columns = line.shape
+    rest = list(range(1, plane_bits()))
+    sides = [[], []]
+    for color, order in enumerate((rest, rest[::-1])):
+        held = line[: lines // 2] if color == 0 else line[lines // 2 :]
+        have = []
+        for bit in order:
+            came = swap_bit(held, bit)
+            have = sorted(have + [bit], reverse=True)
+            axis = have.index(bit)
+            if bit == order[-1]:
+                sides[0].append((held, came, axis))
+                sides[1].append((swap_bit(held, 0), swap_bit(came, 0), axis))
+            else:
+                held = jnp.stack([held, came], axis=axis)
+    out = []
+    for matrix in range(count):
+        halves = [
+            jnp.concatenate(
+                [jnp.stack([a[..., matrix, :, :], b[..., matrix, :, :]], axis=axis) for a, b, axis in side],
+                axis=len(rest),
+            )
+            for side in sides
+        ]
+        out.append(jnp.stack(halves).reshape(-1, columns))
+    return out
 
 
 def gain_gather(value):
@@ -510,14 +494,16 @@
     return lax.ppermute(value, "dp", [(i, i ^ (1 << bit)) for i in range(count) if (i & 1) == core])
 
 
-def gather_plane(own, other, core):
+def gather_plane(own, other, core, late=None):
     rest = list(range(1, plane_bits()))
     held = [own[None], other[None]]
     for step in range(len(rest)):
+        if late is not None and step + 1 == len(rest):
+            held, late = tied([held], late)
         for color in range(2):
             bit = rest[step] if color == 0 else rest[::-1][step]
             held[color] = jnp.concatenate([held[color], swap_core(held[color], bit, core)])
-    return held
+    return held, late
 
 
 def gram_of(held):
@@ -588,25 +574,18 @@
     gain_low = gains.astype(B16)
     attn_full = lax.all_gather(attn_low, ("dp", "fsdp"), axis=1, tiled=True)
     up_line, down_low = ordered(line_gather(ffn_low[:2]), ffn_low[2:])
-    up_gather, down_gather = HiddenGather(up_line), HiddenGather(line_gather(down_low))
+    ffn_up, (ffn_down,) = hidden_gather(up_line), hidden_gather(line_gather(down_low))
     gain_whole = gain_gather(gain_low)
     top_moment, low_moment = exchange(*to_owners(attn_moment.astype(B16), ffn_moment.astype(B16)))
-    up_gather.held, top_moment, low_moment, attn_full = tied(
-        [up_gather.held], top_moment, low_moment, attn_full
-    )
-    up_gather.send()
-    stored, ffn_up = forward(tokens, segment_ids[0], decay_rate, attn_full, up_gather, down_gather, gain_whole)
-    x_grad, grads, grad_gain, ffn_down = backward(
-        stored, cotangent, attn_full, ffn_up, down_gather, gain_whole
-    )
+    top_moment, low_moment, attn_full = ordered(top_moment, low_moment, attn_full)
+    stored = forward(tokens, segment_ids[0], decay_rate, attn_full, ffn_up, gain_whole)
+    x_grad, grads, grad_gain = backward(stored, cotangent, attn_full, ffn_up, ffn_down, gain_whole)
     one, two, down, proj, inner = grads
     lines = lax.axis_size("fsdp")
     attn_count, small, columns = attn_master.shape
     ffn_count, large, _ = ffn_master.shape
     block, little = lines * large, lines * small
-    inner_out = inner.payloads()
-    inner_out, middle, product = tied([inner_out], stored[-6], stored[-1])
-    inner.accept(inner.swap(inner_out))
+    middle, product = stored[-6], stored[-1]
     ffn_sums = [value.finish() for value in (one, two, down)]
     proj_sum = proj.finish()
     out = (middle + jnp.dot(product, ffn_down, preferred_element_type=F32)).astype(B16)
@@ -619,10 +598,6 @@
     if lines > top_grad.shape[0]:
         top_grad = jnp.pad(top_grad, ((0, lines - top_grad.shape[0]), (0, 0), (0, 0)))
     top_grad = lax.psum_scatter(top_grad, "fsdp", scatter_dimension=0, tiled=True)[0]
-    at_core = lax.axis_index("dp") & 1
-    big = owner_momentum(top_moment.reshape(block, columns), top_grad)
-    big_other = one_way(big, 0, True)
-    top_gram = gram_of(gather_plane(big, big_other, 0))
     low_grad = inner.finish()
     if attn_count == at_one:
         low_grad = jnp.concatenate([low_grad, proj_sum])
@@ -630,9 +605,14 @@
         low_grad = jnp.pad(low_grad, ((0, lines - low_grad.shape[0]), (0, 0), (0, 0)))
     top_grad, low_grad = ordered(top_grad, low_grad)
     low_grad = lax.psum_scatter(low_grad, "fsdp", scatter_dimension=0, tiled=True)[0]
+    at_core = lax.axis_index("dp") & 1
+    big = owner_momentum(top_moment.reshape(block, columns), top_grad)
+    big_other = one_way(big, 0, True)
+    top_held, low_grad = gather_plane(big, big_other, 0, low_grad)
+    top_gram = gram_of(top_held)
     low = owner_momentum(low_moment.reshape(little, columns), low_grad)
     low_other = one_way(low, 0, False)
-    low_gram = gram_of(gather_plane(low, low_other, 1))
+    low_gram = gram_of(gather_plane(low, low_other, 1)[0])
     gram = jnp.where(at_core == 0, top_gram, low_gram)
     fill = ((0, block - little), (0, 0))
     mine = jnp.concatenate(

time: 741 us -> 697 us (0.941)
  starting transfers between devices: 120 us -> 89.7 us
  local copies, waits for them, and re-layouts: 66.7 us -> 52.7 us
    all_to_all x0 -> x2, waiting for transfers between devices: none -> 71.3 us  [line_gather(): return lax.all_to_all(copies, 'fsdp', 0, 0, tiled=True)]
    ppermute x12 -> x0, waiting for transfers between devices: 61.5 us -> none  [the longest x6 41.9 us: line_gather(): lax.ppermute(from_above, 'fsdp', [(i, i - 1) for i in range(1, lines)])]
    ppermute x12 -> x0, starting transfers between devices: 42.6 us -> none  [the longest x6 34.9 us: line_gather(): lax.ppermute(from_below, 'fsdp', [(i, i + 1) for i in range(lines - 1)])]
    ppermute x41, waiting for transfers between devices: 117 us -> 89.4 us  [swap_bit(): return lax.ppermute(value, 'dp', [(i, i ^ 1 << bit) for i in range(count)])]
    all_to_all x3, waiting for transfers between devices: 10.5 us -> 31.1 us  [exchange(): lax.all_to_all(jnp.concatenate([top, low], axis=1), 'fsdp', split_axis=0,...]
    reduce_scatter x1, waiting for transfers between devices: 24.3 us -> 9.97 us  [on_device(): lax.psum_scatter(low_grad, 'fsdp', scatter_dimension=0, tiled=True)[0]]
    all_to_all x0 -> x2, starting transfers between devices: none -> 10.7 us  [line_gather(): return lax.all_to_all(copies, 'fsdp', 0, 0, tiled=True)]
    reduce_scatter x1, waiting for transfers between devices: 9.86 us -> 18.5 us  [on_device(): lax.psum_scatter(top_grad, 'fsdp', scatter_dimension=0, tiled=True)[0]]
  transfers between devices with their start and end apart: 73 -> 63, of which waited for: 30 -> 27; matrix products, arithmetic and copies ran while one was open for 26% -> 27% of each run, Pallas kernels for 9% -> 10%
where the time goes in v4:
time: 697 us; the launch traced here: 692 us
  waiting for transfers between devices  252 us (36%)
  matrix products  125 us (18%)
  other arithmetic  90.5 us (13%)
  starting transfers between devices  89.7 us (13%)
  Pallas kernels  66.2 us (9%)
  local copies, waits for them, and re-layouts  52.7 us (8%)
  between operations  15.8 us (2%)
    ppermute x41, waiting for transfers between devices, swap_bit(): return lax.ppermute(value, 'dp', [(i, i ^ 1 << bit) for i in range(count)])  89.4 us
    all_to_all x2, waiting for transfers between devices, line_gather(): return lax.all_to_all(copies, 'fsdp', 0, 0, tiled=True)  71.3 us
    pallas_call x1, Pallas kernels, gram_orthogonalize(): pl.pallas_call(polynomial_kernel, out_shape=jax.ShapeDtypeStruct(rows.sha...  66.2 us
    all_to_all x3, waiting for transfers between devices, exchange(): lax.all_to_all(jnp.concatenate([top, low], axis=1), 'fsdp', split_axis=0,...  31.1 us
    ppermute x41, starting transfers between devices, swap_bit(): return lax.ppermute(value, 'dp', [(i, i ^ 1 << bit) for i in range(count)])  30.9 us
    dot_general x7, matrix products, weight_grad(): lax.dot_general(features, series, TOKENS_OUT, preferred_element_type=F32)  25.2 us
    ppermute x8, waiting for transfers between devices, swap_core(): lax.ppermute(value, 'dp', [(i, i ^ 1 << bit) for i in range(count) if i &...  21.3 us
    convert_element_type x17, other arithmetic, payloads(): sum((self.choose(t, dims, bit, True).astype(F32) for t, dims in part))  18.9 us
  transfers between devices with their start and end apart: 63, of which 27 were waited for; matrix products, arithmetic and copies ran while one was open for 27% of the time, Pallas kernels for 10%

profile of v4, /device:TPU:0, one launch (start us, length us, event | category | flops | bytes accessed | tf_op | source)
XLA Modules:
  0.0 691.8 jit_solution(10488398958810944899)
XLA Ops:
  11.7 6.3 all-to-all-start.2
  18.1 41.1 %all-to-all-done.2 = bf16[4,2,88,1024]{3,2,1,0:T(8,128)(2,1)S(1)} async-done(((bf16[4,2,88,1024]{3,2,1,0:T(8,128)(2,1)}), bf16[4,2,88,1024]{3,2,1,0:T(8,128)(2,1)S(1)}, u32[]{:S(2)}, u32[]{:S(2)}) %all-to-all-start.2) | async-done | bytes 1441824 | tf_op jit(solution)/shard_map/all_to_all | solution.py:337
  63.5 7.8 %all-to-all-done = bf16[32,3,32]{2,1,0:T(4,128)(2,1)S(1)} async-done(((bf16[32,3,32]{2,1,0:T(4,128)(2,1)}), bf16[32,3,32]{2,1,0:T(4,128)(2,1)S(1)}, u32[]{:S(2)}, u32[]{:S(2)}) %all-to-all-start) | async-done | bytes 6176 | tf_op jit(solution)/shard_map/all_to_all | solution.py:373
  80.6 30.3 %all-to-all-done.3 = bf16[4,1,88,1024]{3,2,1,0:T(8,128)(2,1)} async-done(((bf16[4,1,88,1024]{3,2,1,0:T(8,128)(2,1)}), bf16[4,1,88,1024]{3,2,1,0:T(8,128)(2,1)}, u32[]{:S(2)}, u32[]{:S(2)}) %all-to-all-start.3) | async-done | bytes 720928 | tf_op jit(solution)/shard_map/all_to_all | solution.py:337
  127.3 19.6 %all-to-all-done.1 = bf16[4,120,1024]{2,1,0:T(8,128)(2,1)S(1)} async-done(((bf16[4,120,1024]{2,1,0:T(8,128)(2,1)}), bf16[4,120,1024]{2,1,0:T(8,128)(2,1)S(1)}, u32[]{:S(2)}, u32[]{:S(2)}) %all-to-all-start.1) | async-done | bytes 983072 | tf_op jit(solution)/shard_map/all_to_all | solution.py:540
  148.8 9.0 %collective-permute-done.10 = bf16[2,1,88,1024]{3,2,0,1:T(8,128)(2,1)} collective-permute-done((bf16[2,1,88,1024]{3,2,0,1:T(8,128)(2,1)}, bf16[2,1,88,1024]{3,2,0,1:T(8,128)(2,1)}, u32[]{:S(2)}, u32[]{:S(2)}) %collective-permute-start.10) | collective-permute-done | bytes 360480 | tf_op jit(solution)/shard_map/ppermute | solution.py:257
  170.7 9.4 %collective-permute-done.11 = bf16[2,2,1,88,1024]{4,3,1,0,2:T(8,128)(2,1)} collective-permute-done((bf16[2,2,1,88,1024]{4,3,1,0,2:T(8,128)(2,1)}, bf16[2,2,1,88,1024]{4,3,1,0,2:T(8,128)(2,1)}, u32[]{:S(2)}, u32[]{:S(2)}) %collective-permute-start.11) | collective-permute-done | bytes 720928 | tf_op jit(solution)/shard_map/ppermute | solution.py:257
  194.4 8.4 %fusion.104 = f32[512,5120]{1,0:T(8,128)S(1)} fusion(bf16[5120,1024]{1,0:T(8,128)(2,1)} %bitcast.415, bf16[512,1024]{1,0:T(8,128)(2,1)S(1)} %copy-done.20, f32[1024]{0:T(1024)S(1)} %mul.333, f32[512]{0:T(512)S(1)} %get-tuple-element.229), kind=kOutput, calls=%fused_computation.238 | convolution fusion | flops 5370806272 | bytes 22026240 | tf_op jit(solution)/shard_map/dot_general | solution.py:59
  211.1 6.5 multiply_convert_fusion.1
  251.3 8.5 %multiply_convert_fusion.2 = (bf16[512,2816]{1,0:T(8,128)(2,1)}, bf16[512,2816]{1,0:T(8,128)(2,1)}) fusion(f32[512,2816]{1,0:T(8,128)} %get-tuple-element.239, f32[512,2816]{1,0:T(8,128)} %copy-done.2, bf16[512,1024]{1,0:T(8,128)(2,1)} %param.14, bf16[2816,1024]{1,0:T(8,128)(2,1)S(1)} %bitcast.355), kind=kOutput, calls=%fused_computation.7 | convolution fusion | flops 2958557184 | bytes 24117248 | tf_op jit(solution)/shard_map/dot_general | solution.py:150
  339.2 6.9 convolution_convert_fusion
  362.4 11.8 %collective-permute-done.21 = bf16[1,2,176,1024]{3,2,1,0:T(8,128)(2,1)S(1)} collective-permute-done((bf16[1,2,176,1024]{3,2,1,0:T(8,128)(2,1)}, bf16[1,2,176,1024]{3,2,1,0:T(8,128)(2,1)S(1)}, u32[]{:S(2)}, u32[]{:S(2)}) %collective-permute-start.21) | collective-permute-done | bytes 720928 | tf_op jit(solution)/shard_map/ppermute | solution.py:257
  378.2 11.5 %collective-permute-done.23 = bf16[1,2,176,1024]{3,2,1,0:T(8,128)(2,1)} collective-permute-done((bf16[1,2,176,1024]{3,2,1,0:T(8,128)(2,1)}, bf16[1,2,176,1024]{3,2,1,0:T(8,128)(2,1)}, u32[]{:S(2)}, u32[]{:S(2)}) %collective-permute-start.23) | collective-permute-done | bytes 720928 | tf_op jit(solution)/shard_map/ppermute | solution.py:257
  412.9 8.8 %fusion.19 = (f32[1024]{0:T(1024)S(1)}, f32[512]{0:T(512)S(1)}, f32[512,1024]{1,0:T(8,128)S(1)}) fusion(bf16[512,1024]{1,0:T(8,128)(2,1)S(1)} %copy-done.22, f32[512]{0:T(512)S(1)} %get-tuple-element.229, f32[1024]{0:T(1024)S(1)} %mul.333, bf16[5120,1024]{1,0:T(8,128)(2,1)} %bitcast.416, bf16[512,4096]{1,0:T(8,128)(2,1)S(1)} %copy-done.27), kind=kOutput, calls=%fused_computation.53 | convolution fusion | flops 5372377600 | bytes 17838080 | tf_op jit(solution)/shard_map/dot_general | solution.py:231
  439.2 19.5 %collective-permute-done.39 = bf16[4,2,64,1024]{3,2,0,1:T(8,128)(2,1)S(1)} collective-permute-done((bf16[4,2,64,1024]{3,2,0,1:T(8,128)(2,1)}, bf16[4,2,64,1024]{3,2,0,1:T(8,128)(2,1)S(1)}, u32[]{:S(2)}, u32[]{:S(2)}) %collective-permute-start.39) | collective-permute-done | bytes 1048608 | tf_op jit(solution)/shard_map/ppermute | solution.py:257
  464.3 6.6 collective-permute-done.40
  475.2 18.5 %reduce-scatter.3.cloned.1.call-done = bf16[1,352,1024]{2,1,0:T(8,128)(2,1)} async-done(((bf16[4,352,1024]{2,1,0:T(8,128)(2,1)}), bf16[1,352,1024]{2,1,0:T(8,128)(2,1)}) %reduce-scatter.3.cloned.1.call-update) | async-done | bytes 720912 | tf_op jit(solution)/shard_map/reduce_scatter | solution.py:600
  514.7 10.0 %reduce-scatter.5.cloned.1.call-done = bf16[1,128,1024]{2,1,0:T(8,128)(2,1)} async-done(((bf16[4,128,1024]{2,1,0:T(8,128)(2,1)}), bf16[1,128,1024]{2,1,0:T(8,128)(2,1)}) %reduce-scatter.5.cloned.1.call-update) | async-done | bytes 262160 | tf_op jit(solution)/shard_map/reduce_scatter | solution.py:607
  541.0 7.6 %collective-permute-done.45 = bf16[2,352,1024]{2,1,0:T(8,128)(2,1)S(1)} collective-permute-done((bf16[2,352,1024]{2,1,0:T(8,128)(2,1)}, bf16[2,352,1024]{2,1,0:T(8,128)(2,1)S(1)}, u32[]{:S(2)}, u32[]{:S(2)}) %collective-permute-start.45) | collective-permute-done | bytes 1441824 | tf_op jit(solution)/shard_map/ppermute | solution.py:494
  552.1 8.5 %collective-permute-done.44 = bf16[2,352,1024]{2,1,0:T(8,128)(2,1)S(1)} collective-permute-done((bf16[2,352,1024]{2,1,0:T(8,128)(2,1)}, bf16[2,352,1024]{2,1,0:T(8,128)(2,1)S(1)}, u32[]{:S(2)}, u32[]{:S(2)}) %collective-permute-start.44) | collective-permute-done | bytes 1441824 | tf_op jit(solution)/shard_map/ppermute | solution.py:494
  571.5 66.2 %shard_map.218 = bf16[704,1024]{1,0:T(8,128)(2,1)S(1)} custom-call(f32[1024,1024]{1,0:T(8,128)} %fusion.2.gram_ref, bf16[704,1024]{1,0:T(8,128)(2,1)S(1)} %pad_maximum_fusion.11.rows_ref), custom_call_target="tpu_custom_call" | custom-call | flops 32212254720 | bytes 8388608 | tf_op jit(solution)/shard_map/pallas_call | solution.py:473
  637.7 8.8 %collective-permute-start.51 = (bf16[352,1024]{1,0:T(8,128)(2,1)S(1)}, bf16[352,1024]{1,0:T(8,128)(2,1)S(1)}, u32[]{:S(2)}, u32[]{:S(2)}) collective-permute-start(bf16[352,1024]{1,0:T(8,128)(2,1)S(1)} %slice.418), channel_id=1, source_target_pairs={{0,4},{8,12},{16,20},{24,28},{1,5},{9,13},{17,21},{25,29},{2,6},{1... | collective-permute-start | bytes 2162696 | tf_op jit(solution)/shard_map/ppermute | solution.py:487
  657.0 7.7 %add_convert_fusion.2 = bf16[512,1024]{1,0:T(8,128)(2,1)} fusion(f32[512,1024]{1,0:T(8,128)S(1)} %copy-done.11, bf16[512,2816]{1,0:T(8,128)(2,1)} %copy-done.50, bf16[2816,1024]{1,0:T(8,128)(2,1)} %bitcast.356), kind=kOutput, calls=%fused_computation.80 | convolution fusion | flops 2953838592 | bytes 11796480 | tf_op jit(solution)/shard_map/dot_general | solution.py:591
  670.1 11.5 %all-to-all-done.6 = bf16[4,120,1024]{2,1,0:T(8,128)(2,1)S(1)} async-done(((bf16[4,120,1024]{2,1,0:T(8,128)(2,1)}), bf16[4,120,1024]{2,1,0:T(8,128)(2,1)S(1)}, u32[]{:S(2)}, u32[]{:S(2)}) %all-to-all-start.6) | async-done | bytes 983072 | tf_op jit(solution)/shard_map/all_to_all | solution.py:540
  (475 shorter events, 325.3 us)
Async XLA Ops:
  7.2 187.2 %all-gather.2.cloned.1.call-start = ((), (), s32[]{:S(2)}) async-start(), calls=%async_computation.9 | async-start | bytes 10813440 | tf_op jit(solution)/shard_map/all_gather | solution.py:575
  11.7 47.4 %all-to-all-start.2 = ((bf16[4,2,88,1024]{3,2,1,0:T(8,128)(2,1)}), bf16[4,2,88,1024]{3,2,1,0:T(8,128)(2,1)S(1)}, u32[]{:S(2)}, u32[]{:S(2)}) async-start(bf16[4,2,88,1024]{3,2,1,0:T(8,128)(2,1)} %broadcast_in_dim.34), calls=%async_computation.2 | async-start | bytes 2883584 | tf_op jit(solution)/shard_map/all_to_all | solution.py:337
  72.3 38.6 %all-to-all-start.3 = ((bf16[4,1,88,1024]{3,2,1,0:T(8,128)(2,1)}), bf16[4,1,88,1024]{3,2,1,0:T(8,128)(2,1)}, u32[]{:S(2)}, u32[]{:S(2)}) async-start(bf16[4,1,88,1024]{3,2,1,0:T(8,128)(2,1)} %broadcast_in_dim.36), calls=%async_computation.3 | async-start | bytes 1441792 | tf_op jit(solution)/shard_map/all_to_all | solution.py:337
  78.1 36.9 %collective-permute-start.2 = (bf16[2,2,88,1024]{3,2,0,1:T(8,128)(2,1)}, bf16[2,2,88,1024]{3,2,0,1:T(8,128)(2,1)}, u32[]{:S(2)}, u32[]{:S(2)}) collective-permute-start(bf16[2,2,88,1024]{3,2,0,1:T(8,128)(2,1)} %get-tuple-element.214), channel_id=1, source_target_pairs={{0,16},{4,20},{8,24},{12,28},{16,0},{20,4},{24,8},{28,12},{1,17},{... | collective-permute-start | bytes 2162696 | tf_op jit(solution)/shard_map/ppermute | solution.py:257
  78.8 39.5 %collective-permute-start = (bf16[2,2,88,1024]{3,2,0,1:T(8,128)(2,1)}, bf16[2,2,88,1024]{3,2,0,1:T(8,128)(2,1)}, u32[]{:S(2)}, u32[]{:S(2)}) collective-permute-start(bf16[2,2,88,1024]{3,2,0,1:T(8,128)(2,1)} %get-tuple-element.215), channel_id=1, source_target_pairs={{0,8},{4,12},{8,0},{12,4},{16,24},{20,28},{24,16},{28,20},{1,9},{5... | collective-permute-start | bytes 2162696 | tf_op jit(solution)/shard_map/ppermute | solution.py:257
  110.9 36.1 %all-to-all-start.1 = ((bf16[4,120,1024]{2,1,0:T(8,128)(2,1)}), bf16[4,120,1024]{2,1,0:T(8,128)(2,1)S(1)}, u32[]{:S(2)}, u32[]{:S(2)}) async-start(bf16[4,120,1024]{2,1,0:T(8,128)(2,1)} %fusion.68), calls=%async_computation.1 | async-start | bytes 1966080 | tf_op jit(solution)/shard_map/all_to_all | solution.py:540
  114.4 379.3 %reduce-scatter.3.cloned.1.call-start = ((), (), s32[]{:S(2)}) async-start(), calls=%async_computation.10 | async-start | bytes 3604480 | tf_op jit(solution)/shard_map/reduce_scatter | solution.py:600
  117.4 45.1 %collective-permute-start.3 = (bf16[2,2,2,88,1024]{4,3,1,0,2:T(8,128)(2,1)}, bf16[2,2,2,88,1024]{4,3,1,0,2:T(8,128)(2,1)}, u32[]{:S(2)}, u32[]{:S(2)}) collective-permute-start(bf16[2,2,2,88,1024]{4,3,1,0,2:T(8,128)(2,1)} %pad_maximum_fusion.6), channel_id=1, source_target_pairs={{0,8},{4,12},{8,0},{12,4},{16,24},{20,28},{24,16},{28,20},{1,9},{5... | collective-permute-start | bytes 4325384 | tf_op jit(solution)/shard_map/ppermute | solution.py:257
  120.7 43.2 %collective-permute-start.1 = (bf16[2,2,2,88,1024]{4,3,1,0,2:T(8,128)(2,1)}, bf16[2,2,2,88,1024]{4,3,1,0,2:T(8,128)(2,1)}, u32[]{:S(2)}, u32[]{:S(2)}) collective-permute-start(bf16[2,2,2,88,1024]{4,3,1,0,2:T(8,128)(2,1)} %pad_maximum_fusion.5), channel_id=1, source_target_pairs={{0,16},{4,20},{8,24},{12,28},{16,0},{20,4},{24,8},{28,12},{1,17},{... | collective-permute-start | bytes 4325384 | tf_op jit(solution)/shard_map/ppermute | solution.py:257
  122.7 44.5 %collective-permute-start.6 = (bf16[2,2,2,88,1024]{4,3,1,0,2:T(8,128)(2,1)}, bf16[2,2,2,88,1024]{4,3,1,0,2:T(8,128)(2,1)}, u32[]{:S(2)}, u32[]{:S(2)}) collective-permute-start(bf16[2,2,2,88,1024]{4,3,1,0,2:T(8,128)(2,1)} %pad_maximum_fusion.6), channel_id=1, source_target_pairs={{0,4},{4,0},{8,12},{12,8},{16,20},{20,16},{24,28},{28,24},{1,5},{5... | collective-permute-start | bytes 4325384 | tf_op jit(solution)/shard_map/ppermute | solution.py:257
  124.9 32.9 %collective-permute-start.10 = (bf16[2,1,88,1024]{3,2,0,1:T(8,128)(2,1)}, bf16[2,1,88,1024]{3,2,0,1:T(8,128)(2,1)}, u32[]{:S(2)}, u32[]{:S(2)}) collective-permute-start(bf16[2,1,88,1024]{3,2,0,1:T(8,128)(2,1)} %get-tuple-element.226), channel_id=1, source_target_pairs={{0,16},{4,20},{8,24},{12,28},{16,0},{20,4},{24,8},{28,12},{1,17},{... | collective-permute-start | bytes 1081352 | tf_op jit(solution)/shard_map/ppermute | solution.py:257
  170.5 72.2 %collective-permute-start.14 = (bf16[2,2,1,88,1024]{4,3,1,0,2:T(8,128)(2,1)}, bf16[2,2,1,88,1024]{4,3,1,0,2:T(8,128)(2,1)}, u32[]{:S(2)}, u32[]{:S(2)}) collective-permute-start(bf16[2,2,1,88,1024]{4,3,1,0,2:T(8,128)(2,1)} %get-tuple-element.223), channel_id=1, source_target_pairs={{0,4},{4,0},{8,12},{12,8},{16,20},{20,16},{24,28},{28,24},{1,5},{5... | collective-permute-start | bytes 2162696 | tf_op jit(solution)/shard_map/ppermute | solution.py:257
  180.1 62.6 %collective-permute-start.12 = (bf16[2,2,1,88,1024]{4,3,1,0,2:T(8,128)(2,1)}, bf16[2,2,1,88,1024]{4,3,1,0,2:T(8,128)(2,1)}, u32[]{:S(2)}, u32[]{:S(2)}) collective-permute-start(bf16[2,2,1,88,1024]{4,3,1,0,2:T(8,128)(2,1)} %get-tuple-element.221), channel_id=1, source_target_pairs={{0,4},{4,0},{8,12},{12,8},{16,20},{20,16},{24,28},{28,24},{1,5},{5... | collective-permute-start | bytes 2162696 | tf_op jit(solution)/shard_map/ppermute | solution.py:257
  185.8 56.9 %collective-permute-start.15 = (bf16[2,2,1,88,1024]{4,3,1,0,2:T(8,128)(2,1)}, bf16[2,2,1,88,1024]{4,3,1,0,2:T(8,128)(2,1)}, u32[]{:S(2)}, u32[]{:S(2)}) collective-permute-start(bf16[2,2,1,88,1024]{4,3,1,0,2:T(8,128)(2,1)} %collective-permute-done.11), channel_id=1, source_target_pairs={{0,4},{4,0},{8,12},{12,8},{16,20},{20,16},{24,28},{28,24},{1,5},{5... | collective-permute-start | bytes 2162696 | tf_op jit(solution)/shard_map/ppermute | solution.py:257
  185.8 56.9 %collective-permute-start.13 = (bf16[2,2,1,88,1024]{4,3,1,0,2:T(8,128)(2,1)}, bf16[2,2,1,88,1024]{4,3,1,0,2:T(8,128)(2,1)}, u32[]{:S(2)}, u32[]{:S(2)}) collective-permute-start(bf16[2,2,1,88,1024]{4,3,1,0,2:T(8,128)(2,1)} %collective-permute-done.9), channel_id=1, source_target_pairs={{0,4},{4,0},{8,12},{12,8},{16,20},{20,16},{24,28},{28,24},{1,5},{5... | collective-permute-start | bytes 2162696 | tf_op jit(solution)/shard_map/ppermute | solution.py:257
  354.5 40.0 %collective-permute-start.30 = (bf16[4,2,2,128,1024]{4,3,0,1,2:T(8,128)(2,1)}, bf16[4,2,2,128,1024]{4,3,0,1,2:T(8,128)(2,1)}, u32[]{:S(2)}, u32[]{:S(2)}) collective-permute-start(bf16[4,2,2,128,1024]{4,3,0,1,2:T(8,128)(2,1)} %bitcast.354), channel_id=1, source_target_pairs={{0,4},{4,0},{8,12},{12,8},{16,20},{20,16},{24,28},{28,24},{1,5},{5... | collective-permute-start | bytes 12582920 | tf_op jit(solution)/shard_map/ppermute | solution.py:257
  357.0 32.7 %collective-permute-start.23 = (bf16[1,2,176,1024]{3,2,1,0:T(8,128)(2,1)}, bf16[1,2,176,1024]{3,2,1,0:T(8,128)(2,1)}, u32[]{:S(2)}, u32[]{:S(2)}) collective-permute-start(bf16[1,2,176,1024]{3,2,1,0:T(8,128)(2,1)} %fusion.73), channel_id=1, source_target_pairs={{0,8},{4,12},{8,0},{12,4},{16,24},{20,28},{24,16},{28,20},{1,9},{5... | collective-permute-start | bytes 2162696 | tf_op jit(solution)/shard_map/ppermute | solution.py:257
  358.2 31.9 %collective-permute-start.24 = (bf16[1,2,176,1024]{3,2,1,0:T(8,128)(2,1)}, bf16[1,2,176,1024]{3,2,1,0:T(8,128)(2,1)}, u32[]{:S(2)}, u32[]{:S(2)}) collective-permute-start(bf16[1,2,176,1024]{3,2,1,0:T(8,128)(2,1)} %fusion.74), channel_id=1, source_target_pairs={{0,16},{4,20},{8,24},{12,28},{16,0},{20,4},{24,8},{28,12},{1,17},{... | collective-permute-start | bytes 2162696 | tf_op jit(solution)/shard_map/ppermute | solution.py:257
  436.4 88.3 %reduce-scatter.5.cloned.1.call-start = ((), (), s32[]{:S(2)}) async-start(), calls=%async_computation.11 | async-start | bytes 1310720 | tf_op jit(solution)/shard_map/reduce_scatter | solution.py:607
  504.1 63.7 %all-to-all-start.5 = ((f32[32,3,32]{2,1,0:T(4,128)}), f32[32,3,32]{2,1,0:T(4,128)S(1)}, u32[]{:S(2)}, u32[]{:S(2)}) async-start(f32[32,3,32]{2,1,0:T(4,128)} %maximum_bitcast_fusion.6), calls=%async_computation.7 | async-start | bytes 131072 | tf_op jit(solution)/shard_map/all_to_all | solution.py:381
  531.1 29.5 %collective-permute-start.44 = (bf16[2,352,1024]{2,1,0:T(8,128)(2,1)}, bf16[2,352,1024]{2,1,0:T(8,128)(2,1)S(1)}, u32[]{:S(2)}, u32[]{:S(2)}) collective-permute-start(bf16[2,352,1024]{2,1,0:T(8,128)(2,1)} %pad_maximum_fusion.9), channel_id=1, source_target_pairs={{0,16},{8,24},{16,0},{24,8},{1,17},{9,25},{17,1},{25,9},{2,18},{10... | collective-permute-start | bytes 4325384 | tf_op jit(solution)/shard_map/ppermute | solution.py:494
  538.4 25.7 %collective-permute-start.50 = (bf16[2,128,1024]{2,1,0:T(8,128)(2,1)S(1)}, bf16[2,128,1024]{2,1,0:T(8,128)(2,1)S(1)}, u32[]{:S(2)}, u32[]{:S(2)}) collective-permute-start(bf16[2,128,1024]{2,1,0:T(8,128)(2,1)S(1)} %pad_maximum_fusion.18), channel_id=1, source_target_pairs={{4,12},{12,4},{20,28},{28,20},{5,13},{13,5},{21,29},{29,21},{6,14}... | collective-permute-start | bytes 1572872 | tf_op jit(solution)/shard_map/ppermute | solution.py:494
  567.8 83.4 %all-to-all-start.4 = ((bf16[4,120,1024]{2,1,0:T(8,128)(2,1)}), bf16[4,120,1024]{2,1,0:T(8,128)(2,1)S(1)}, u32[]{:S(2)}, u32[]{:S(2)}) async-start(bf16[4,120,1024]{2,1,0:T(8,128)(2,1)} %pad_maximum_fusion.13), calls=%async_computation.6 | async-start | bytes 1966080 | tf_op jit(solution)/shard_map/all_to_all | solution.py:540
  652.2 29.4 %all-to-all-start.6 = ((bf16[4,120,1024]{2,1,0:T(8,128)(2,1)}), bf16[4,120,1024]{2,1,0:T(8,128)(2,1)S(1)}, u32[]{:S(2)}, u32[]{:S(2)}) async-start(bf16[4,120,1024]{2,1,0:T(8,128)(2,1)} %pad_maximum_fusion.14), calls=%async_computation.8 | async-start | bytes 1966080 | tf_op jit(solution)/shard_map/all_to_all | solution.py:540
  (142 other events, 1361.4 us)
Sparse Core Ops, SparseCore 0:
  11.6 129.7 all-gather.1
  436.5 57.1 reduce-scatter.2
  496.5 28.0 reduce-scatter.4

commit v5 on v4

--- a/solution.py
+++ b/solution.py
@@ -48,7 +48,7 @@
     return jnp.where(allowed[None], fading, 0.0)
 
 
-def forward(tokens, segments, decay_rate, attn_full, ffn_up, gain_low):
+def forward(tokens, segments, decay_rate, attn_full, ffn_up, gain_low, moments):
     length, model_width = tokens.shape
     head_count = decay_rate.shape[0]
     head_size = model_width // head_count
@@ -83,6 +83,7 @@
     middle = inputs + branch
     second_scale = rms_scale(middle)
     normed_two = (middle * second_scale * gain_full[1]).astype(B16)
+    moments, normed_two = tied([moments], normed_two)
     up_one, up_two = (
         lax.dot_general(normed_two, matrix, ROWS_BY_ROWS, preferred_element_type=F32) for matrix in ffn_up
     )
@@ -109,10 +110,10 @@
         up_two,
         product,
     )
-    return stored
-
-
-def backward(stored, cotangent, attn_full, ffn_up, ffn_down, gain_low):
+    return stored, moments
+
+
+def backward(stored, cotangent, attn_full, ffn_up, down_gather, gain_low):
     (
         inputs,
         first_scale,
@@ -145,8 +146,9 @@
     down = Halving(
         weight_grad(product[:, :half], cotangent), weight_grad(product[:, half:], cotangent)
     )
-    down_out, cotangent = tied([down.payloads()], cotangent)
+    down_out, down_gather.pieces, cotangent = tied([down.payloads(), down_gather.pieces], cotangent)
     down_in = down.swap(down_out)
+    (ffn_down,) = down_gather.join()
     grad_product = lax.dot_general(cotangent, ffn_down, ROWS_BY_ROWS, preferred_element_type=F32)
     grad_one = (grad_product * up_two).astype(B16)
     grad_two = (grad_product * up_one).astype(B16)
@@ -241,7 +243,7 @@
     two.accept(two_in)
     proj.accept(proj_in)
     inner.accept(inner_in)
-    return (grad_inputs, (one, two, down, proj, inner), grad_gain)
+    return (grad_inputs, (one, two, down, proj, inner), grad_gain, ffn_down)
 
 
 def ordered(*values):
@@ -337,33 +339,40 @@
     return lax.all_to_all(copies, "fsdp", 0, 0, tiled=True)
 
 
-def hidden_gather(line):
-    lines, count, _, columns = line.shape
-    rest = list(range(1, plane_bits()))
-    sides = [[], []]
-    for color, order in enumerate((rest, rest[::-1])):
-        held = line[: lines // 2] if color == 0 else line[lines // 2 :]
-        have = []
-        for bit in order:
-            came = swap_bit(held, bit)
-            have = sorted(have + [bit], reverse=True)
-            axis = have.index(bit)
-            if bit == order[-1]:
-                sides[0].append((held, came, axis))
-                sides[1].append((swap_bit(held, 0), swap_bit(came, 0), axis))
-            else:
-                held = jnp.stack([held, came], axis=axis)
-    out = []
-    for matrix in range(count):
-        halves = [
-            jnp.concatenate(
-                [jnp.stack([a[..., matrix, :, :], b[..., matrix, :, :]], axis=axis) for a, b, axis in side],
-                axis=len(rest),
-            )
-            for side in sides
-        ]
-        out.append(jnp.stack(halves).reshape(-1, columns))
-    return out
+class HiddenGather:
+    def __init__(self, line):
+        lines, self.count, _, self.columns = line.shape
+        rest = list(range(1, plane_bits()))
+        self.orders = (rest, rest[::-1])
+        self.held, self.axes = [], []
+        for color, order in enumerate(self.orders):
+            held = line[: lines // 2] if color == 0 else line[lines // 2 :]
+            for step, bit in enumerate(order):
+                axis = sorted(order[: step + 1], reverse=True).index(bit)
+                if step + 1 < len(order):
+                    held = jnp.stack([held, swap_bit(held, bit)], axis=axis)
+            self.held.append(held)
+            self.axes.append(axis)
+
+    def send(self):
+        self.pieces = []
+        for held, order in zip(self.held, self.orders):
+            came = swap_bit(held, order[-1])
+            self.pieces += [held, came, swap_bit(held, 0), swap_bit(came, 0)]
+
+    def join(self):
+        out = []
+        for matrix in range(self.count):
+            sides = []
+            for side in range(2):
+                halves = []
+                for color, axis in enumerate(self.axes):
+                    first = 4 * color + 2 * side
+                    pair = [p[..., matrix, :, :] for p in self.pieces[first : first + 2]]
+                    halves.append(jnp.stack(pair, axis=axis))
+                sides.append(jnp.concatenate(halves, axis=len(self.orders[0])))
+            out.append(jnp.stack(sides).reshape(-1, self.columns))
+        return out
 
 
 def gain_gather(value):
@@ -573,13 +582,20 @@
     ffn_low = ffn_master.astype(B16)
     gain_low = gains.astype(B16)
     attn_full = lax.all_gather(attn_low, ("dp", "fsdp"), axis=1, tiled=True)
-    up_line, down_low = ordered(line_gather(ffn_low[:2]), ffn_low[2:])
-    ffn_up, (ffn_down,) = hidden_gather(up_line), hidden_gather(line_gather(down_low))
-    gain_whole = gain_gather(gain_low)
-    top_moment, low_moment = exchange(*to_owners(attn_moment.astype(B16), ffn_moment.astype(B16)))
-    top_moment, low_moment, attn_full = ordered(top_moment, low_moment, attn_full)
-    stored = forward(tokens, segment_ids[0], decay_rate, attn_full, ffn_up, gain_whole)
-    x_grad, grads, grad_gain = backward(stored, cotangent, attn_full, ffn_up, ffn_down, gain_whole)
+    gain_whole, up_low = ordered(gain_gather(gain_low), ffn_low[:2])
+    up_gather = HiddenGather(line_gather(up_low))
+    up_gather.held, down_low = tied([up_gather.held], ffn_low[2:])
+    up_gather.send()
+    down_gather = HiddenGather(line_gather(down_low))
+    down_gather.send()
+    ffn_up = up_gather.join()
+    *moments, attn_full = ordered(*to_owners(attn_moment.astype(B16), ffn_moment.astype(B16)), attn_full)
+    moments = exchange(*moments)
+    stored, moments = forward(tokens, segment_ids[0], decay_rate, attn_full, ffn_up, gain_whole, moments)
+    top_moment, low_moment = moments
+    x_grad, grads, grad_gain, ffn_down = backward(
+        stored, cotangent, attn_full, ffn_up, down_gather, gain_whole
+    )
     one, two, down, proj, inner = grads
     lines = lax.axis_size("fsdp")
     attn_count, small, columns = attn_master.shape

time: 697 us -> 731 us (1.049)
  blocking collectives: 0 us -> 54.4 us
  waiting for transfers between devices: 252 us -> 211 us
  matrix products: 125 us -> 139 us
    all_to_all x2 -> x1, waiting for transfers between devices: 71.3 us -> 12 us  [line_gather(): return lax.all_to_all(copies, 'fsdp', 0, 0, tiled=True)]
    all_to_all x0 -> x1, blocking collectives: none -> 54.4 us  [line_gather(): return lax.all_to_all(copies, 'fsdp', 0, 0, tiled=True)]
    ppermute x41, waiting for transfers between devices: 89.4 us -> 128 us  [swap_bit(): return lax.ppermute(value, 'dp', [(i, i ^ 1 << bit) for i in range(count)])]
    all_to_all x3, waiting for transfers between devices: 31.1 us -> 15 us  [exchange(): lax.all_to_all(jnp.concatenate([top, low], axis=1), 'fsdp', split_axis=0,...]
    dot_general x1, matrix products: 8.49 us -> 18.8 us  [backward(): lax.dot_general(cotangent, ffn_down, ROWS_BY_ROWS, preferred_element_type...]
    another operation x14 -> x12, other arithmetic: 23.9 us -> 15 us  [the longest x7 10.2 us: join(): out.append(jnp.stack(sides).reshape(-1, self.columns))]
    unnamed x202 -> x192, local copies, waits for them, and re-layouts: 15 us -> 15.8 us
  transfers between devices with their start and end apart: 63 -> 62, of which waited for: 27 -> 31; matrix products, arithmetic and copies ran while one was open for 27% -> 28% of each run, Pallas kernels for 10% -> 9%
where the time goes in v5:
time: 731 us; the launch traced here: 721 us
  waiting for transfers between devices  211 us (29%)
  matrix products  139 us (19%)
  starting transfers between devices  89.3 us (12%)
  other arithmetic  88.3 us (12%)
  Pallas kernels  66.1 us (9%)
  local copies, waits for them, and re-layouts  57.3 us (8%)
  blocking collectives  54.4 us (7%)
  between operations  16 us (2%)
    ppermute x41, waiting for transfers between devices, swap_bit(): return lax.ppermute(value, 'dp', [(i, i ^ 1 << bit) for i in range(count)])  128 us
    pallas_call x1, Pallas kernels, gram_orthogonalize(): pl.pallas_call(polynomial_kernel, out_shape=jax.ShapeDtypeStruct(rows.sha...  66.1 us
    all_to_all x1, blocking collectives, line_gather(): return lax.all_to_all(copies, 'fsdp', 0, 0, tiled=True)  54.4 us
    ppermute x41, starting transfers between devices, swap_bit(): return lax.ppermute(value, 'dp', [(i, i ^ 1 << bit) for i in range(count)])  31.8 us
    dot_general x7, matrix products, weight_grad(): lax.dot_general(features, series, TOKENS_OUT, preferred_element_type=F32)  25.2 us
    ppermute x8, waiting for transfers between devices, swap_core(): lax.ppermute(value, 'dp', [(i, i ^ 1 << bit) for i in range(count) if i &...  21.5 us
    convert_element_type x17, other arithmetic, payloads(): sum((self.choose(t, dims, bit, True).astype(F32) for t, dims in part))  18.9 us
    dot_general x1, matrix products, backward(): lax.dot_general(cotangent, ffn_down, ROWS_BY_ROWS, preferred_element_type...  18.8 us
  transfers between devices with their start and end apart: 62, of which 31 were waited for; matrix products, arithmetic and copies ran while one was open for 28% of the time, Pallas kernels for 9%

profile of v5, /device:TPU:0, one launch (start us, length us, event | category | flops | bytes accessed | tf_op | source)
XLA Modules:
  0.0 721.5 jit_solution(1595120484223183707)
XLA Ops:
  10.4 7.3 %all-to-all-start = ((bf16[32,3,32]{2,1,0:T(4,128)(2,1)}), bf16[32,3,32]{2,1,0:T(4,128)(2,1)S(1)}, u32[]{:S(2)}, u32[]{:S(2)}) async-start(bf16[32,3,32]{2,1,0:T(4,128)(2,1)} %broadcast_in_dim.30), calls=%async_computation | async-start | bytes 65536 | tf_op jit(solution)/shard_map/all_to_all | solution.py:382
  25.3 54.4 %all_to_all.35 = bf16[4,2,88,1024]{3,2,1,0:T(8,128)(2,1)S(1)} all-to-all(bf16[4,2,88,1024]{3,2,1,0:T(8,128)(2,1)S(1)} %broadcast_in_dim.34), channel_id=1, replica_groups=mesh['dp'=8,'fsdp'=4] {'fsdp'}, dimensions={0} | all-to-all | bytes 2883584 | tf_op jit(solution)/shard_map/all_to_all | solution.py:339
  83.3 30.3 %collective-permute-done = bf16[2,2,88,1024]{3,2,0,1:T(8,128)(2,1)S(1)} collective-permute-done((bf16[2,2,88,1024]{3,2,0,1:T(8,128)(2,1)S(1)}, bf16[2,2,88,1024]{3,2,0,1:T(8,128)(2,1)S(1)}, u32[]{:S(2)}, u32[]{:S(2)}) %collective-permute-start) | collective-permute-done | bytes 720928 | tf_op jit(solution)/shard_map/ppermute | solution.py:259
  131.6 12.0 %all-to-all-done.3 = bf16[4,1,88,1024]{3,2,1,0:T(8,128)(2,1)} async-done(((bf16[4,1,88,1024]{3,2,1,0:T(8,128)(2,1)}), bf16[4,1,88,1024]{3,2,1,0:T(8,128)(2,1)}, u32[]{:S(2)}, u32[]{:S(2)}) %all-to-all-start.3) | async-done | bytes 720928 | tf_op jit(solution)/shard_map/all_to_all | solution.py:339
  145.7 11.0 %collective-permute-done.3 = bf16[2,2,2,88,1024]{4,3,1,0,2:T(8,128)(2,1)} collective-permute-done((bf16[2,2,2,88,1024]{4,3,1,0,2:T(8,128)(2,1)S(1)}, bf16[2,2,2,88,1024]{4,3,1,0,2:T(8,128)(2,1)}, u32[]{:S(2)}, u32[]{:S(2)}) %collective-permute-start.3) | collective-permute-done | bytes 1441824 | tf_op jit(solution)/shard_map/ppermute | solution.py:259
  175.4 9.9 %collective-permute-done.9 = bf16[2,2,1,88,1024]{4,3,1,0,2:T(8,128)(2,1)} collective-permute-done((bf16[2,2,1,88,1024]{4,3,1,0,2:T(8,128)(2,1)}, bf16[2,2,1,88,1024]{4,3,1,0,2:T(8,128)(2,1)}, u32[]{:S(2)}, u32[]{:S(2)}) %collective-permute-start.9) | collective-permute-done | bytes 720928 | tf_op jit(solution)/shard_map/ppermute | solution.py:259
  196.5 8.4 %fusion.93 = f32[512,5120]{1,0:T(8,128)S(1)} fusion(bf16[5120,1024]{1,0:T(8,128)(2,1)} %bitcast.431, bf16[512,1024]{1,0:T(8,128)(2,1)S(1)} %copy-done.20, f32[1024]{0:T(1024)S(1)} %bitcast.426, f32[512]{0:T(512)S(1)} %get-tuple-element.255), kind=kOutput, calls=%fused_computation.223 | convolution fusion | flops 5370806272 | bytes 22026240 | tf_op jit(solution)/shard_map/dot_general | solution.py:59
  221.0 6.5 multiply_convert_fusion.1
  249.2 6.3 fusion.118
  272.6 18.8 %multiply_convert_fusion.2 = (bf16[512,2816]{1,0:T(8,128)(2,1)}, bf16[512,2816]{1,0:T(8,128)(2,1)}) fusion(f32[512,2816]{1,0:T(8,128)} %get-tuple-element.265, f32[512,2816]{1,0:T(8,128)} %copy-done.2, bf16[512,1024]{1,0:T(8,128)(2,1)} %param.14, bf16[2816,1024]{1,0:T(8,128)(2,1)S(1)} %bitcast.357), kind=kOutput, calls=%fused_computation.7 | convolution fusion | flops 2958557184 | bytes 24117248 | tf_op jit(solution)/shard_map/dot_general | solution.py:152
  371.1 6.9 convolution_convert_fusion
  394.3 11.8 %collective-permute-done.21 = bf16[1,2,176,1024]{3,2,1,0:T(8,128)(2,1)S(1)} collective-permute-done((bf16[1,2,176,1024]{3,2,1,0:T(8,128)(2,1)}, bf16[1,2,176,1024]{3,2,1,0:T(8,128)(2,1)S(1)}, u32[]{:S(2)}, u32[]{:S(2)}) %collective-permute-start.21) | collective-permute-done | bytes 720928 | tf_op jit(solution)/shard_map/ppermute | solution.py:259
  409.7 11.9 %collective-permute-done.23 = bf16[1,2,176,1024]{3,2,1,0:T(8,128)(2,1)} collective-permute-done((bf16[1,2,176,1024]{3,2,1,0:T(8,128)(2,1)}, bf16[1,2,176,1024]{3,2,1,0:T(8,128)(2,1)}, u32[]{:S(2)}, u32[]{:S(2)}) %collective-permute-start.23) | collective-permute-done | bytes 720928 | tf_op jit(solution)/shard_map/ppermute | solution.py:259
  444.4 8.8 %fusion.19 = (f32[1024]{0:T(1024)S(1)}, f32[512]{0:T(512)S(1)}, f32[512,1024]{1,0:T(8,128)S(1)}) fusion(bf16[512,1024]{1,0:T(8,128)(2,1)S(1)} %copy-done.22, f32[512]{0:T(512)S(1)} %get-tuple-element.255, f32[1024]{0:T(1024)S(1)} %bitcast.428, bf16[5120,1024]{1,0:T(8,128)(2,1)} %bitcast.432, bf16[512,4096]{1,0:T(8,128)(2,1)S(1)} %copy-done.27), kind=kOutput, calls=%fused_computation.53 | convolution fusion | flops 5372377600 | bytes 17838080 | tf_op jit(solution)/shard_map/dot_general | solution.py:233
  471.0 19.5 %collective-permute-done.39 = bf16[4,2,64,1024]{3,2,0,1:T(8,128)(2,1)S(1)} collective-permute-done((bf16[4,2,64,1024]{3,2,0,1:T(8,128)(2,1)}, bf16[4,2,64,1024]{3,2,0,1:T(8,128)(2,1)S(1)}, u32[]{:S(2)}, u32[]{:S(2)}) %collective-permute-start.39) | collective-permute-done | bytes 1048608 | tf_op jit(solution)/shard_map/ppermute | solution.py:259
  496.1 6.5 collective-permute-done.40
  507.0 16.5 %reduce-scatter.3.cloned.1.call-done = bf16[1,352,1024]{2,1,0:T(8,128)(2,1)} async-done(((bf16[4,352,1024]{2,1,0:T(8,128)(2,1)}), bf16[1,352,1024]{2,1,0:T(8,128)(2,1)}) %reduce-scatter.3.cloned.1.call-update) | async-done | bytes 720912 | tf_op jit(solution)/shard_map/reduce_scatter | solution.py:616
  544.5 10.0 %reduce-scatter.5.cloned.1.call-done = bf16[1,128,1024]{2,1,0:T(8,128)(2,1)} async-done(((bf16[4,128,1024]{2,1,0:T(8,128)(2,1)}), bf16[1,128,1024]{2,1,0:T(8,128)(2,1)}) %reduce-scatter.5.cloned.1.call-update) | async-done | bytes 262160 | tf_op jit(solution)/shard_map/reduce_scatter | solution.py:623
  570.6 7.7 %collective-permute-done.45 = bf16[2,352,1024]{2,1,0:T(8,128)(2,1)S(1)} collective-permute-done((bf16[2,352,1024]{2,1,0:T(8,128)(2,1)}, bf16[2,352,1024]{2,1,0:T(8,128)(2,1)S(1)}, u32[]{:S(2)}, u32[]{:S(2)}) %collective-permute-start.45) | collective-permute-done | bytes 1441824 | tf_op jit(solution)/shard_map/ppermute | solution.py:503
  581.9 8.6 %collective-permute-done.44 = bf16[2,352,1024]{2,1,0:T(8,128)(2,1)S(1)} collective-permute-done((bf16[2,352,1024]{2,1,0:T(8,128)(2,1)}, bf16[2,352,1024]{2,1,0:T(8,128)(2,1)S(1)}, u32[]{:S(2)}, u32[]{:S(2)}) %collective-permute-start.44) | collective-permute-done | bytes 1441824 | tf_op jit(solution)/shard_map/ppermute | solution.py:503
  601.4 66.1 %shard_map.218 = bf16[704,1024]{1,0:T(8,128)(2,1)S(1)} custom-call(f32[1024,1024]{1,0:T(8,128)} %fusion.2.gram_ref, bf16[704,1024]{1,0:T(8,128)(2,1)S(1)} %pad_maximum_fusion.11.rows_ref), custom_call_target="tpu_custom_call" | custom-call | flops 32212254720 | bytes 8388608 | tf_op jit(solution)/shard_map/pallas_call | solution.py:482
  667.6 8.3 %collective-permute-start.51 = (bf16[352,1024]{1,0:T(8,128)(2,1)S(1)}, bf16[352,1024]{1,0:T(8,128)(2,1)S(1)}, u32[]{:S(2)}, u32[]{:S(2)}) collective-permute-start(bf16[352,1024]{1,0:T(8,128)(2,1)S(1)} %slice.407), channel_id=1, source_target_pairs={{0,4},{8,12},{16,20},{24,28},{1,5},{9,13},{17,21},{25,29},{2,6},{1... | collective-permute-start | bytes 2162696 | tf_op jit(solution)/shard_map/ppermute | solution.py:496
  686.4 7.7 %add_convert_fusion.2 = bf16[512,1024]{1,0:T(8,128)(2,1)} fusion(f32[512,1024]{1,0:T(8,128)S(1)} %copy-done.11, bf16[512,2816]{1,0:T(8,128)(2,1)} %copy-done.48, bf16[2816,1024]{1,0:T(8,128)(2,1)} %bitcast.358), kind=kOutput, calls=%fused_computation.80 | convolution fusion | flops 2953838592 | bytes 11796480 | tf_op jit(solution)/shard_map/dot_general | solution.py:607
  699.5 11.5 %all-to-all-done.6 = bf16[4,120,1024]{2,1,0:T(8,128)(2,1)S(1)} async-done(((bf16[4,120,1024]{2,1,0:T(8,128)(2,1)}), bf16[4,120,1024]{2,1,0:T(8,128)(2,1)S(1)}, u32[]{:S(2)}, u32[]{:S(2)}) %all-to-all-start.6) | async-done | bytes 983072 | tf_op jit(solution)/shard_map/all_to_all | solution.py:549
  (463 shorter events, 338.6 us)
Async XLA Ops:
  7.2 189.3 %all-gather.2.cloned.1.call-start = ((), (), s32[]{:S(2)}) async-start(), calls=%async_computation.9 | async-start | bytes 10813440 | tf_op jit(solution)/shard_map/all_gather | solution.py:584
  79.9 33.6 %collective-permute-start = (bf16[2,2,88,1024]{3,2,0,1:T(8,128)(2,1)S(1)}, bf16[2,2,88,1024]{3,2,0,1:T(8,128)(2,1)S(1)}, u32[]{:S(2)}, u32[]{:S(2)}) collective-permute-start(bf16[2,2,88,1024]{3,2,0,1:T(8,128)(2,1)S(1)} %copy.200), channel_id=1, source_target_pairs={{0,8},{4,12},{8,0},{12,4},{16,24},{20,28},{24,16},{28,20},{1,9},{5... | collective-permute-start | bytes 2162696 | tf_op jit(solution)/shard_map/ppermute | solution.py:259
  81.4 34.0 %collective-permute-start.1 = (bf16[2,2,88,1024]{3,2,0,1:T(8,128)(2,1)S(1)}, bf16[2,2,88,1024]{3,2,0,1:T(8,128)(2,1)S(1)}, u32[]{:S(2)}, u32[]{:S(2)}) collective-permute-start(bf16[2,2,88,1024]{3,2,0,1:T(8,128)(2,1)S(1)} %copy.199), channel_id=1, source_target_pairs={{0,16},{4,20},{8,24},{12,28},{16,0},{20,4},{24,8},{28,12},{1,17},{... | collective-permute-start | bytes 2162696 | tf_op jit(solution)/shard_map/ppermute | solution.py:259
  116.5 27.1 %all-to-all-start.3 = ((bf16[4,1,88,1024]{3,2,1,0:T(8,128)(2,1)}), bf16[4,1,88,1024]{3,2,1,0:T(8,128)(2,1)}, u32[]{:S(2)}, u32[]{:S(2)}) async-start(bf16[4,1,88,1024]{3,2,1,0:T(8,128)(2,1)} %broadcast_in_dim.36), calls=%async_computation.3 | async-start | bytes 1441792 | tf_op jit(solution)/shard_map/all_to_all | solution.py:339
  122.1 34.6 %collective-permute-start.3 = (bf16[2,2,2,88,1024]{4,3,1,0,2:T(8,128)(2,1)S(1)}, bf16[2,2,2,88,1024]{4,3,1,0,2:T(8,128)(2,1)}, u32[]{:S(2)}, u32[]{:S(2)}) collective-permute-start(bf16[2,2,2,88,1024]{4,3,1,0,2:T(8,128)(2,1)S(1)} %pad_maximum_fusion.6), channel_id=1, source_target_pairs={{0,8},{4,12},{8,0},{12,4},{16,24},{20,28},{24,16},{28,20},{1,9},{5... | collective-permute-start | bytes 4325384 | tf_op jit(solution)/shard_map/ppermute | solution.py:259
  127.7 32.3 %collective-permute-start.2 = (bf16[2,2,2,88,1024]{4,3,1,0,2:T(8,128)(2,1)S(1)}, bf16[2,2,2,88,1024]{4,3,1,0,2:T(8,128)(2,1)}, u32[]{:S(2)}, u32[]{:S(2)}) collective-permute-start(bf16[2,2,2,88,1024]{4,3,1,0,2:T(8,128)(2,1)S(1)} %pad_maximum_fusion.5), channel_id=1, source_target_pairs={{0,16},{4,20},{8,24},{12,28},{16,0},{20,4},{24,8},{28,12},{1,17},{... | collective-permute-start | bytes 4325384 | tf_op jit(solution)/shard_map/ppermute | solution.py:259
  129.8 41.2 %collective-permute-start.6 = (bf16[2,2,2,88,1024]{4,3,1,0,2:T(8,128)(2,1)S(1)}, bf16[2,2,2,88,1024]{4,3,1,0,2:T(8,128)(2,1)}, u32[]{:S(2)}, u32[]{:S(2)}) collective-permute-start(bf16[2,2,2,88,1024]{4,3,1,0,2:T(8,128)(2,1)S(1)} %pad_maximum_fusion.6), channel_id=1, source_target_pairs={{0,4},{4,0},{8,12},{12,8},{16,20},{20,16},{24,28},{28,24},{1,5},{5... | collective-permute-start | bytes 4325384 | tf_op jit(solution)/shard_map/ppermute | solution.py:259
  129.8 44.0 %collective-permute-start.4 = (bf16[2,2,2,88,1024]{4,3,1,0,2:T(8,128)(2,1)S(1)}, bf16[2,2,2,88,1024]{4,3,1,0,2:T(8,128)(2,1)}, u32[]{:S(2)}, u32[]{:S(2)}) collective-permute-start(bf16[2,2,2,88,1024]{4,3,1,0,2:T(8,128)(2,1)S(1)} %pad_maximum_fusion.5), channel_id=1, source_target_pairs={{0,4},{4,0},{8,12},{12,8},{16,20},{20,16},{24,28},{28,24},{1,5},{5... | collective-permute-start | bytes 4325384 | tf_op jit(solution)/shard_map/ppermute | solution.py:259
  156.7 30.5 %collective-permute-start.7 = (bf16[2,2,2,88,1024]{4,3,1,0,2:T(8,128)(2,1)}, bf16[2,2,2,88,1024]{4,3,1,0,2:T(8,128)(2,1)S(1)}, u32[]{:S(2)}, u32[]{:S(2)}) collective-permute-start(bf16[2,2,2,88,1024]{4,3,1,0,2:T(8,128)(2,1)} %collective-permute-done.3), channel_id=1, source_target_pairs={{0,4},{4,0},{8,12},{12,8},{16,20},{20,16},{24,28},{28,24},{1,5},{5... | collective-permute-start | bytes 4325384 | tf_op jit(solution)/shard_map/ppermute | solution.py:259
  175.3 88.6 %collective-permute-start.10 = (bf16[2,2,1,88,1024]{4,3,1,0,2:T(8,128)(2,1)}, bf16[2,2,1,88,1024]{4,3,1,0,2:T(8,128)(2,1)}, u32[]{:S(2)}, u32[]{:S(2)}) collective-permute-start(bf16[2,2,1,88,1024]{4,3,1,0,2:T(8,128)(2,1)} %pad_maximum_fusion.16), channel_id=1, source_target_pairs={{0,4},{4,0},{8,12},{12,8},{16,20},{20,16},{24,28},{28,24},{1,5},{5... | collective-permute-start | bytes 2162696 | tf_op jit(solution)/shard_map/ppermute | solution.py:259
  185.3 78.7 %collective-permute-start.14 = (bf16[2,2,1,88,1024]{4,3,1,0,2:T(8,128)(2,1)}, bf16[2,2,1,88,1024]{4,3,1,0,2:T(8,128)(2,1)}, u32[]{:S(2)}, u32[]{:S(2)}) collective-permute-start(bf16[2,2,1,88,1024]{4,3,1,0,2:T(8,128)(2,1)} %pad_maximum_fusion.17), channel_id=1, source_target_pairs={{0,4},{4,0},{8,12},{12,8},{16,20},{20,16},{24,28},{28,24},{1,5},{5... | collective-permute-start | bytes 2162696 | tf_op jit(solution)/shard_map/ppermute | solution.py:259
  187.1 76.8 %collective-permute-start.11 = (bf16[2,2,1,88,1024]{4,3,1,0,2:T(8,128)(2,1)}, bf16[2,2,1,88,1024]{4,3,1,0,2:T(8,128)(2,1)}, u32[]{:S(2)}, u32[]{:S(2)}) collective-permute-start(bf16[2,2,1,88,1024]{4,3,1,0,2:T(8,128)(2,1)} %collective-permute-done.9), channel_id=1, source_target_pairs={{0,4},{4,0},{8,12},{12,8},{16,20},{20,16},{24,28},{28,24},{1,5},{5... | collective-permute-start | bytes 2162696 | tf_op jit(solution)/shard_map/ppermute | solution.py:259
  187.2 76.8 %collective-permute-start.15 = (bf16[2,2,1,88,1024]{4,3,1,0,2:T(8,128)(2,1)}, bf16[2,2,1,88,1024]{4,3,1,0,2:T(8,128)(2,1)}, u32[]{:S(2)}, u32[]{:S(2)}) collective-permute-start(bf16[2,2,1,88,1024]{4,3,1,0,2:T(8,128)(2,1)} %collective-permute-done.13), channel_id=1, source_target_pairs={{0,4},{4,0},{8,12},{12,8},{16,20},{20,16},{24,28},{28,24},{1,5},{5... | collective-permute-start | bytes 2162696 | tf_op jit(solution)/shard_map/ppermute | solution.py:259
  215.4 29.9 %all-to-all-start.1 = ((bf16[4,120,1024]{2,1,0:T(8,128)(2,1)}), bf16[4,120,1024]{2,1,0:T(8,128)(2,1)}, u32[]{:S(2)}, u32[]{:S(2)}) async-start(bf16[4,120,1024]{2,1,0:T(8,128)(2,1)} %pad_maximum_fusion.13), calls=%async_computation.1 | async-start | bytes 1966080 | tf_op jit(solution)/shard_map/all_to_all | solution.py:549
  220.7 302.8 %reduce-scatter.3.cloned.1.call-start = ((), (), s32[]{:S(2)}) async-start(), calls=%async_computation.10 | async-start | bytes 3604480 | tf_op jit(solution)/shard_map/reduce_scatter | solution.py:616
  264.0 35.8 %collective-permute-start.16 = (bf16[1,2,2,352,1024]{4,3,2,1,0:T(8,128)(2,1)}, bf16[1,2,2,352,1024]{4,3,2,1,0:T(8,128)(2,1)}, u32[]{:S(2)}, u32[]{:S(2)}) collective-permute-start(bf16[1,2,2,352,1024]{4,3,2,1,0:T(8,128)(2,1)} %bitcast.42), channel_id=1, source_target_pairs={{0,4},{4,0},{8,12},{12,8},{16,20},{20,16},{24,28},{28,24},{1,5},{5... | collective-permute-start | bytes 8650760 | tf_op jit(solution)/shard_map/ppermute | solution.py:259
  386.3 40.1 %collective-permute-start.30 = (bf16[4,2,2,128,1024]{4,3,0,1,2:T(8,128)(2,1)}, bf16[4,2,2,128,1024]{4,3,0,1,2:T(8,128)(2,1)}, u32[]{:S(2)}, u32[]{:S(2)}) collective-permute-start(bf16[4,2,2,128,1024]{4,3,0,1,2:T(8,128)(2,1)} %bitcast.354), channel_id=1, source_target_pairs={{0,4},{4,0},{8,12},{12,8},{16,20},{20,16},{24,28},{28,24},{1,5},{5... | collective-permute-start | bytes 12582920 | tf_op jit(solution)/shard_map/ppermute | solution.py:259
  388.5 33.1 %collective-permute-start.23 = (bf16[1,2,176,1024]{3,2,1,0:T(8,128)(2,1)}, bf16[1,2,176,1024]{3,2,1,0:T(8,128)(2,1)}, u32[]{:S(2)}, u32[]{:S(2)}) collective-permute-start(bf16[1,2,176,1024]{3,2,1,0:T(8,128)(2,1)} %fusion.70), channel_id=1, source_target_pairs={{0,8},{4,12},{8,0},{12,4},{16,24},{20,28},{24,16},{28,20},{1,9},{5... | collective-permute-start | bytes 2162696 | tf_op jit(solution)/shard_map/ppermute | solution.py:259
  390.0 32.1 %collective-permute-start.24 = (bf16[1,2,176,1024]{3,2,1,0:T(8,128)(2,1)}, bf16[1,2,176,1024]{3,2,1,0:T(8,128)(2,1)}, u32[]{:S(2)}, u32[]{:S(2)}) collective-permute-start(bf16[1,2,176,1024]{3,2,1,0:T(8,128)(2,1)} %fusion.71), channel_id=1, source_target_pairs={{0,16},{4,20},{8,24},{12,28},{16,0},{20,4},{24,8},{28,12},{1,17},{... | collective-permute-start | bytes 2162696 | tf_op jit(solution)/shard_map/ppermute | solution.py:259
  468.2 86.2 %reduce-scatter.5.cloned.1.call-start = ((), (), s32[]{:S(2)}) async-start(), calls=%async_computation.11 | async-start | bytes 1310720 | tf_op jit(solution)/shard_map/reduce_scatter | solution.py:623
  533.9 63.7 %all-to-all-start.5 = ((f32[32,3,32]{2,1,0:T(4,128)}), f32[32,3,32]{2,1,0:T(4,128)S(1)}, u32[]{:S(2)}, u32[]{:S(2)}) async-start(f32[32,3,32]{2,1,0:T(4,128)} %maximum_bitcast_fusion.6), calls=%async_computation.7 | async-start | bytes 131072 | tf_op jit(solution)/shard_map/all_to_all | solution.py:390
  560.9 29.5 %collective-permute-start.44 = (bf16[2,352,1024]{2,1,0:T(8,128)(2,1)}, bf16[2,352,1024]{2,1,0:T(8,128)(2,1)S(1)}, u32[]{:S(2)}, u32[]{:S(2)}) collective-permute-start(bf16[2,352,1024]{2,1,0:T(8,128)(2,1)} %pad_maximum_fusion.9), channel_id=1, source_target_pairs={{0,16},{8,24},{16,0},{24,8},{1,17},{9,25},{17,1},{25,9},{2,18},{10... | collective-permute-start | bytes 4325384 | tf_op jit(solution)/shard_map/ppermute | solution.py:503
  597.6 83.0 %all-to-all-start.4 = ((bf16[4,120,1024]{2,1,0:T(8,128)(2,1)}), bf16[4,120,1024]{2,1,0:T(8,128)(2,1)S(1)}, u32[]{:S(2)}, u32[]{:S(2)}) async-start(bf16[4,120,1024]{2,1,0:T(8,128)(2,1)} %pad_maximum_fusion.14), calls=%async_computation.6 | async-start | bytes 1966080 | tf_op jit(solution)/shard_map/all_to_all | solution.py:549
  681.6 29.4 %all-to-all-start.6 = ((bf16[4,120,1024]{2,1,0:T(8,128)(2,1)}), bf16[4,120,1024]{2,1,0:T(8,128)(2,1)S(1)}, u32[]{:S(2)}, u32[]{:S(2)}) async-start(bf16[4,120,1024]{2,1,0:T(8,128)(2,1)} %pad_maximum_fusion.15), calls=%async_computation.8 | async-start | bytes 1966080 | tf_op jit(solution)/shard_map/all_to_all | solution.py:549
  (135 other events, 1467.4 us)
Sparse Core Ops, SparseCore 0:
  11.6 125.2 all-gather.1
  468.4 55.0 reduce-scatter.2
  526.4 28.0 reduce-scatter.4

commit v6 on v5

--- a/solution.py
+++ b/solution.py
@@ -1,3 +1,4 @@
+import itertools
 import math
 
 import jax
@@ -48,7 +49,7 @@
     return jnp.where(allowed[None], fading, 0.0)
 
 
-def forward(tokens, segments, decay_rate, attn_full, ffn_up, gain_low, moments):
+def forward(tokens, segments, decay_rate, attn_full, up_gather, down_line, gain_low, moments):
     length, model_width = tokens.shape
     head_count = decay_rate.shape[0]
     head_size = model_width // head_count
@@ -79,11 +80,18 @@
     normal_out = attended * out_scale * gain_full[2]
     gate_sig = jax.nn.sigmoid(gate_pre)
     gated_out = (normal_out * gate_sig).astype(B16)
+    up_gather.came, moments, down_line, gated_out = tied([up_gather.came, moments], down_line, gated_out)
+    up_gather.cores()
+    down_gather = Gather(down_line)
+    moments = exchange(*moments)
     branch = lax.dot_general(gated_out, attn_full[4], ROWS_BY_ROWS, preferred_element_type=F32)
     middle = inputs + branch
     second_scale = rms_scale(middle)
     normed_two = (middle * second_scale * gain_full[1]).astype(B16)
-    moments, normed_two = tied([moments], normed_two)
+    up_gather.pieces, down_gather.held, normed_two = tied([up_gather.pieces, down_gather.held], normed_two)
+    ffn_up = up_gather.join()
+    down_gather.cross()
+    down_gather.cores()
     up_one, up_two = (
         lax.dot_general(normed_two, matrix, ROWS_BY_ROWS, preferred_element_type=F32) for matrix in ffn_up
     )
@@ -110,10 +118,10 @@
         up_two,
         product,
     )
-    return stored, moments
-
-
-def backward(stored, cotangent, attn_full, ffn_up, down_gather, gain_low):
+    return stored, down_gather, moments, ffn_up
+
+
+def backward(stored, cotangent, attn_full, ffn_up, down_gather, moments, gain_low):
     (
         inputs,
         first_scale,
@@ -146,7 +154,9 @@
     down = Halving(
         weight_grad(product[:, :half], cotangent), weight_grad(product[:, half:], cotangent)
     )
-    down_out, down_gather.pieces, cotangent = tied([down.payloads(), down_gather.pieces], cotangent)
+    down_out, down_gather.pieces, moments, cotangent = tied(
+        [down.payloads(), down_gather.pieces, moments], cotangent
+    )
     down_in = down.swap(down_out)
     (ffn_down,) = down_gather.join()
     grad_product = lax.dot_general(cotangent, ffn_down, ROWS_BY_ROWS, preferred_element_type=F32)
@@ -243,7 +253,7 @@
     two.accept(two_in)
     proj.accept(proj_in)
     inner.accept(inner_in)
-    return (grad_inputs, (one, two, down, proj, inner), grad_gain, ffn_down)
+    return (grad_inputs, (one, two, down, proj, inner), grad_gain, ffn_down, moments)
 
 
 def ordered(*values):
@@ -339,7 +349,7 @@
     return lax.all_to_all(copies, "fsdp", 0, 0, tiled=True)
 
 
-class HiddenGather:
+class Gather:
     def __init__(self, line):
         lines, self.count, _, self.columns = line.shape
         rest = list(range(1, plane_bits()))
@@ -354,11 +364,29 @@
             self.held.append(held)
             self.axes.append(axis)
 
-    def send(self):
+    def cross(self):
+        self.came = [swap_bit(held, order[-1]) for held, order in zip(self.held, self.orders)]
+
+    def cores(self):
         self.pieces = []
-        for held, order in zip(self.held, self.orders):
-            came = swap_bit(held, order[-1])
+        for held, came in zip(self.held, self.came):
             self.pieces += [held, came, swap_bit(held, 0), swap_bit(came, 0)]
+
+    def natural(self):
+        half, _, own, _ = self.held[0].shape[-4:]
+        planes = lax.axis_size("dp")
+        whole = jnp.zeros((self.count, planes, 2 * half, own, self.columns), self.held[0].dtype)
+        for number in range(4):
+            for color, order in enumerate(self.orders):
+                piece = self.pieces[4 * color + number]
+                bits = sorted(order[:-1], reverse=True)
+                base = (1 << order[-1]) * (number % 2) + number // 2
+                for index in itertools.product(range(2), repeat=len(bits)):
+                    place = base + sum(value << bit for value, bit in zip(index, bits))
+                    block = jnp.swapaxes(piece[index], 0, 1)[:, None]
+                    where = (0, lax.axis_index("dp") ^ place, color * half, 0, 0)
+                    whole = lax.dynamic_update_slice(whole, block, where)
+        return whole.reshape(self.count, -1, self.columns)
 
     def join(self):
         out = []
@@ -581,20 +609,21 @@
     attn_low = attn_master.astype(B16)
     ffn_low = ffn_master.astype(B16)
     gain_low = gains.astype(B16)
-    attn_full = lax.all_gather(attn_low, ("dp", "fsdp"), axis=1, tiled=True)
-    gain_whole, up_low = ordered(gain_gather(gain_low), ffn_low[:2])
-    up_gather = HiddenGather(line_gather(up_low))
-    up_gather.held, down_low = tied([up_gather.held], ffn_low[2:])
-    up_gather.send()
-    down_gather = HiddenGather(line_gather(down_low))
-    down_gather.send()
-    ffn_up = up_gather.join()
-    *moments, attn_full = ordered(*to_owners(attn_moment.astype(B16), ffn_moment.astype(B16)), attn_full)
-    moments = exchange(*moments)
-    stored, moments = forward(tokens, segment_ids[0], decay_rate, attn_full, ffn_up, gain_whole, moments)
-    top_moment, low_moment = moments
-    x_grad, grads, grad_gain, ffn_down = backward(
-        stored, cotangent, attn_full, ffn_up, down_gather, gain_whole
+    gain_whole, attn_low = ordered(gain_gather(gain_low), attn_low)
+    attn_gather = Gather(line_gather(attn_low))
+    attn_gather.held, up_low = tied([attn_gather.held], ffn_low[:2])
+    attn_gather.cross()
+    attn_gather.cores()
+    up_gather = Gather(line_gather(up_low))
+    attn_full = attn_gather.natural()
+    moments = to_owners(attn_moment.astype(B16), ffn_moment.astype(B16))
+    up_gather.held, moments, down_low, attn_full = tied([up_gather.held, moments], ffn_low[2:], attn_full)
+    up_gather.cross()
+    stored, down_gather, moments, ffn_up = forward(
+        tokens, segment_ids[0], decay_rate, attn_full, up_gather, line_gather(down_low), gain_whole, moments
+    )
+    x_grad, grads, grad_gain, ffn_down, (top_moment, low_moment) = backward(
+        stored, cotangent, attn_full, ffn_up, down_gather, moments, gain_whole
     )
     one, two, down, proj, inner = grads
     lines = lax.axis_size("fsdp")

time: 731 us -> 715 us (0.978)
  waiting for transfers between devices: 211 us -> 169 us
  local copies, waits for them, and re-layouts: 57.3 us -> 97.9 us
  blocking collectives: 54.4 us -> 34.1 us
  starting transfers between devices: 89.3 us -> 97.4 us
    dynamic_update_slice x0 -> x16, local copies, waits for them, and re-layouts: none -> 29.6 us  [natural(): whole = lax.dynamic_update_slice(whole, block, where)]
    ppermute x41 -> x49, waiting for transfers between devices: 128 us -> 100 us  [swap_bit(): return lax.ppermute(value, 'dp', [(i, i ^ 1 << bit) for i in range(count)])]
    all_to_all x1, blocking collectives: 54.4 us -> 34.1 us  [line_gather(): return lax.all_to_all(copies, 'fsdp', 0, 0, tiled=True)]
    all_to_all x1 -> x2, waiting for transfers between devices: 12 us -> 0.01 us  [line_gather(): return lax.all_to_all(copies, 'fsdp', 0, 0, tiled=True)]
    dot_general x1, matrix products: 18.8 us -> 9.82 us  [backward(): lax.dot_general(cotangent, ffn_down, ROWS_BY_ROWS, preferred_element_type...]
    ppermute x41 -> x49, starting transfers between devices: 31.8 us -> 36.1 us  [swap_bit(): return lax.ppermute(value, 'dp', [(i, i ^ 1 << bit) for i in range(count)])]
    unnamed x192 -> x198, local copies, waits for them, and re-layouts: 15.8 us -> 11.6 us
  transfers between devices with their start and end apart: 62 -> 70, of which waited for: 31 -> 24; matrix products, arithmetic and copies ran while one was open for 28% -> 33% of each run, Pallas kernels for 9% -> 9%
where the time goes in v6:
time: 715 us; the launch traced here: 708 us
  waiting for transfers between devices  169 us (24%)
  matrix products  135 us (19%)
  local copies, waits for them, and re-layouts  97.9 us (14%)
  starting transfers between devices  97.4 us (14%)
  other arithmetic  92.1 us (13%)
  Pallas kernels  66.2 us (9%)
  blocking collectives  34.1 us (5%)
  between operations  16.2 us (2%)
    ppermute x49, waiting for transfers between devices, swap_bit(): return lax.ppermute(value, 'dp', [(i, i ^ 1 << bit) for i in range(count)])  100 us
    pallas_call x1, Pallas kernels, gram_orthogonalize(): pl.pallas_call(polynomial_kernel, out_shape=jax.ShapeDtypeStruct(rows.sha...  66.2 us
    ppermute x49, starting transfers between devices, swap_bit(): return lax.ppermute(value, 'dp', [(i, i ^ 1 << bit) for i in range(count)])  36.1 us
    all_to_all x1, blocking collectives, line_gather(): return lax.all_to_all(copies, 'fsdp', 0, 0, tiled=True)  34.1 us
    dynamic_update_slice x16, local copies, waits for them, and re-layouts, natural(): whole = lax.dynamic_update_slice(whole, block, where)  29.6 us
    dot_general x7, matrix products, weight_grad(): lax.dot_general(features, series, TOKENS_OUT, preferred_element_type=F32)  26.9 us
    ppermute x8, waiting for transfers between devices, swap_core(): lax.ppermute(value, 'dp', [(i, i ^ 1 << bit) for i in range(count) if i &...  21.2 us
    convert_element_type x17, other arithmetic, payloads(): sum((self.choose(t, dims, bit, True).astype(F32) for t, dims in part))  20.7 us
  transfers between devices with their start and end apart: 70, of which 24 were waited for; matrix products, arithmetic and copies ran while one was open for 33% of the time, Pallas kernels for 9%

profile of v6, /device:TPU:0, one launch (start us, length us, event | category | flops | bytes accessed | tf_op | source)
XLA Modules:
  0.0 707.7 jit_solution(8940311069706282812)
XLA Ops:
  8.5 7.3 %all-to-all-start = ((bf16[32,3,32]{2,1,0:T(4,128)(2,1)}), bf16[32,3,32]{2,1,0:T(4,128)(2,1)S(1)}, u32[]{:S(2)}, u32[]{:S(2)}) async-start(bf16[32,3,32]{2,1,0:T(4,128)(2,1)} %broadcast_in_dim.115), calls=%async_computation | async-start | bytes 65536 | tf_op jit(solution)/shard_map/all_to_all | solution.py:410
  23.4 34.1 %all_to_all.40 = bf16[4,5,32,1024]{3,2,1,0:T(8,128)(2,1)S(1)} all-to-all(bf16[4,5,32,1024]{3,2,1,0:T(8,128)(2,1)S(1)} %broadcast_in_dim.116), channel_id=1, replica_groups=mesh['dp'=8,'fsdp'=4] {'fsdp'}, dimensions={0} | all-to-all | bytes 2621440 | tf_op jit(solution)/shard_map/all_to_all | solution.py:349
  62.5 11.0 %collective-permute-done = bf16[2,5,32,1024]{3,2,0,1:T(8,128)(2,1)S(1)} collective-permute-done((bf16[2,5,32,1024]{3,2,0,1:T(8,128)(2,1)S(1)}, bf16[2,5,32,1024]{3,2,0,1:T(8,128)(2,1)S(1)}, u32[]{:S(2)}, u32[]{:S(2)}) %collective-permute-start) | collective-permute-done | bytes 655392 | tf_op jit(solution)/shard_map/ppermute | solution.py:269
  94.4 9.7 %collective-permute-done.4 = bf16[2,2,5,32,1024]{4,3,1,2,0:T(8,128)(2,1)} collective-permute-done((bf16[2,2,5,32,1024]{4,3,1,2,0:T(8,128)(2,1)}, bf16[2,2,5,32,1024]{4,3,1,2,0:T(8,128)(2,1)}, u32[]{:S(2)}, u32[]{:S(2)}) %collective-permute-start.4) | collective-permute-done | bytes 1310752 | tf_op jit(solution)/shard_map/ppermute | solution.py:269
  130.4 8.4 %collective-permute-done.2 = bf16[2,2,88,1024]{3,2,0,1:T(8,128)(2,1)S(1)} collective-permute-done((bf16[2,2,88,1024]{3,2,0,1:T(8,128)(2,1)S(1)}, bf16[2,2,88,1024]{3,2,0,1:T(8,128)(2,1)S(1)}, u32[]{:S(2)}, u32[]{:S(2)}) %collective-permute-start.2) | collective-permute-done | bytes 720928 | tf_op jit(solution)/shard_map/ppermute | solution.py:269
  148.9 8.4 %fusion.105 = f32[512,5120]{1,0:T(8,128)S(1)} fusion(bf16[5120,1024]{1,0:T(8,128)(2,1)} %bitcast.76, bf16[512,1024]{1,0:T(8,128)(2,1)S(1)} %copy-done.24, f32[1024]{0:T(1024)S(1)} %bitcast.588, f32[512]{0:T(512)S(1)} %get-tuple-element.299), kind=kOutput, calls=%fused_computation.253 | convolution fusion | flops 5370806272 | bytes 22026240 | tf_op jit(solution)/shard_map/dot_general | solution.py:60
  163.7 8.3 %multiply_convert_fusion.1 = bf16[16,512,512]{2,1,0:T(8,128)(2,1)} fusion(bf16[512,16,64]{0,2,1:T(8,128)(2,1)S(1)} %bitcast.525, bf16[512,16,64]{0,2,1:T(8,128)(2,1)} %bitcast.537, f32[512,512]{1,0:T(8,128)} %maximum_convert_fusion, f32[16]{0:T(128)S(1)} %neg.7, pred[512,512]{1,0:T(8,128)(4,1)S(1)} %copy-done.79), kind=kOutput, calls=%fused_computation.1 | convolution fusion | flops 553648128 | bytes 11796544 | tf_op jit(solution)/shard_map/the,she->hts/dot_general | solution.py:74
  173.6 7.7 %fusion.29 = (f32[512]{0:T(512)S(1)}, f32[16,64,512]{2,1,0:T(8,128)}) fusion(bf16[512,16,64]{0,2,1:T(8,128)(2,1)S(1)} %bitcast.539, bf16[16,512,512]{2,1,0:T(8,128)(2,1)} %multiply_convert_fusion.1), kind=kOutput, calls=%fused_computation.68 | convolution fusion | flops 537918976 | bytes 11536384 | tf_op jit(solution)/shard_map/hts,she->the/dot_general | solution.py:76
  258.8 9.8 %multiply_convert_fusion.2 = (bf16[512,2816]{1,0:T(8,128)(2,1)}, bf16[512,2816]{1,0:T(8,128)(2,1)}) fusion(f32[512,2816]{1,0:T(8,128)} %get-tuple-element.309, f32[512,2816]{1,0:T(8,128)S(1)} %bitcast.521, bf16[512,1024]{1,0:T(8,128)(2,1)} %param.14, bf16[2816,1024]{1,0:T(8,128)(2,1)S(1)} %bitcast.514), kind=kOutput, calls=%fused_computation.7 | convolution fusion | flops 2958557184 | bytes 24117248 | tf_op jit(solution)/shard_map/dot_general | solution.py:162
  345.2 8.8 %convolution_convert_fusion = bf16[4096,1024]{1,0:T(8,128)(2,1)} fusion(bf16[512,1024]{1,0:T(8,128)(2,1)S(1)} %copy-done.26, f32[1024]{0:T(1024)S(1)} %bitcast.589, f32[512]{0:T(512)S(1)} %get-tuple-element.299, bf16[512,1024]{1,0:T(8,128)(2,1)S(1)} %copy-done.71, bf16[512,1024]{1,0:T(8,128)(2,1)S(1)} %copy-done.33, ...), kind=kOutput, calls=%fused_computation.3 | convolution fusion | flops 4318035968 | bytes 13637632 | tf_op jit(solution)/shard_map/dot_general | solution.py:273
  356.3 7.0 constant_dynamic-slice_fusion
  373.9 11.9 %collective-permute-done.29 = bf16[1,2,176,1024]{3,2,1,0:T(8,128)(2,1)} collective-permute-done((bf16[1,2,176,1024]{3,2,1,0:T(8,128)(2,1)}, bf16[1,2,176,1024]{3,2,1,0:T(8,128)(2,1)}, u32[]{:S(2)}, u32[]{:S(2)}) %collective-permute-start.29) | collective-permute-done | bytes 720928 | tf_op jit(solution)/shard_map/ppermute | solution.py:269
  390.0 11.3 %collective-permute-done.31 = bf16[1,2,176,1024]{3,2,1,0:T(8,128)(2,1)} collective-permute-done((bf16[1,2,176,1024]{3,2,1,0:T(8,128)(2,1)}, bf16[1,2,176,1024]{3,2,1,0:T(8,128)(2,1)}, u32[]{:S(2)}, u32[]{:S(2)}) %collective-permute-start.31) | collective-permute-done | bytes 720928 | tf_op jit(solution)/shard_map/ppermute | solution.py:269
  425.8 8.8 %fusion.19 = (f32[1024]{0:T(1024)S(1)}, f32[512]{0:T(512)S(1)}, f32[512,1024]{1,0:T(8,128)S(1)}) fusion(bf16[512,1024]{1,0:T(8,128)(2,1)S(1)} %copy-done.26, f32[512]{0:T(512)S(1)} %get-tuple-element.299, f32[1024]{0:T(1024)S(1)} %bitcast.590, bf16[5120,1024]{1,0:T(8,128)(2,1)} %bitcast.76, bf16[512,4096]{1,0:T(8,128)(2,1)S(1)} %copy-done.30), kind=kOutput, calls=%fused_computation.53 | convolution fusion | flops 5372377600 | bytes 17838080 | tf_op jit(solution)/shard_map/dot_general | solution.py:243
  453.1 20.1 %collective-permute-done.47 = bf16[4,2,64,1024]{3,2,0,1:T(8,128)(2,1)S(1)} collective-permute-done((bf16[4,2,64,1024]{3,2,0,1:T(8,128)(2,1)}, bf16[4,2,64,1024]{3,2,0,1:T(8,128)(2,1)S(1)}, u32[]{:S(2)}, u32[]{:S(2)}) %collective-permute-start.47) | collective-permute-done | bytes 1048608 | tf_op jit(solution)/shard_map/ppermute | solution.py:269
  478.2 6.8 collective-permute-done.48
  489.2 18.5 %reduce-scatter.3.cloned.1.call-done = bf16[1,352,1024]{2,1,0:T(8,128)(2,1)} async-done(((bf16[4,352,1024]{2,1,0:T(8,128)(2,1)}), bf16[1,352,1024]{2,1,0:T(8,128)(2,1)}) %reduce-scatter.3.cloned.1.call-update) | async-done | bytes 720912 | tf_op jit(solution)/shard_map/reduce_scatter | solution.py:645
  528.6 10.0 %reduce-scatter.5.cloned.1.call-done = bf16[1,128,1024]{2,1,0:T(8,128)(2,1)} async-done(((bf16[4,128,1024]{2,1,0:T(8,128)(2,1)}), bf16[1,128,1024]{2,1,0:T(8,128)(2,1)}) %reduce-scatter.5.cloned.1.call-update) | async-done | bytes 262160 | tf_op jit(solution)/shard_map/reduce_scatter | solution.py:652
  555.0 7.6 %collective-permute-done.53 = bf16[2,352,1024]{2,1,0:T(8,128)(2,1)S(1)} collective-permute-done((bf16[2,352,1024]{2,1,0:T(8,128)(2,1)}, bf16[2,352,1024]{2,1,0:T(8,128)(2,1)S(1)}, u32[]{:S(2)}, u32[]{:S(2)}) %collective-permute-start.53) | collective-permute-done | bytes 1441824 | tf_op jit(solution)/shard_map/ppermute | solution.py:531
  566.1 8.5 %collective-permute-done.52 = bf16[2,352,1024]{2,1,0:T(8,128)(2,1)S(1)} collective-permute-done((bf16[2,352,1024]{2,1,0:T(8,128)(2,1)}, bf16[2,352,1024]{2,1,0:T(8,128)(2,1)S(1)}, u32[]{:S(2)}, u32[]{:S(2)}) %collective-permute-start.52) | collective-permute-done | bytes 1441824 | tf_op jit(solution)/shard_map/ppermute | solution.py:531
  585.4 66.2 %shard_map.218 = bf16[704,1024]{1,0:T(8,128)(2,1)S(1)} custom-call(f32[1024,1024]{1,0:T(8,128)} %fusion.2.gram_ref, bf16[704,1024]{1,0:T(8,128)(2,1)S(1)} %pad_maximum_fusion.11.rows_ref), custom_call_target="tpu_custom_call" | custom-call | flops 32212254720 | bytes 8388608 | tf_op jit(solution)/shard_map/pallas_call | solution.py:510
  651.7 8.5 %collective-permute-start.59 = (bf16[352,1024]{1,0:T(8,128)(2,1)S(1)}, bf16[352,1024]{1,0:T(8,128)(2,1)S(1)}, u32[]{:S(2)}, u32[]{:S(2)}) collective-permute-start(bf16[352,1024]{1,0:T(8,128)(2,1)S(1)} %slice.481), channel_id=1, source_target_pairs={{0,4},{8,12},{16,20},{24,28},{1,5},{9,13},{17,21},{25,29},{2,6},{1... | collective-permute-start | bytes 2162696 | tf_op jit(solution)/shard_map/ppermute | solution.py:524
  669.7 7.7 %add_convert_fusion.2 = bf16[512,1024]{1,0:T(8,128)(2,1)} fusion(f32[512,1024]{1,0:T(8,128)S(1)} %copy-done.12, bf16[512,2816]{1,0:T(8,128)(2,1)} %copy-done.51, bf16[2816,1024]{1,0:T(8,128)(2,1)} %bitcast.515), kind=kOutput, calls=%fused_computation.80 | convolution fusion | flops 2953838592 | bytes 11796480 | tf_op jit(solution)/shard_map/dot_general | solution.py:636
  683.7 10.6 %all-to-all-done.7 = bf16[4,120,1024]{2,1,0:T(8,128)(2,1)} async-done(((bf16[4,120,1024]{2,1,0:T(8,128)(2,1)}), bf16[4,120,1024]{2,1,0:T(8,128)(2,1)}, u32[]{:S(2)}, u32[]{:S(2)}) %all-to-all-start.7) | async-done | bytes 983072 | tf_op jit(solution)/shard_map/all_to_all | solution.py:577
  (508 shorter events, 374.5 us)
Async XLA Ops:
  74.8 29.3 %collective-permute-start.4 = (bf16[2,2,5,32,1024]{4,3,1,2,0:T(8,128)(2,1)}, bf16[2,2,5,32,1024]{4,3,1,2,0:T(8,128)(2,1)}, u32[]{:S(2)}, u32[]{:S(2)}) collective-permute-start(bf16[2,2,5,32,1024]{4,3,1,2,0:T(8,128)(2,1)} %pad_maximum_fusion.12), channel_id=1, source_target_pairs={{0,16},{4,20},{8,24},{12,28},{16,0},{20,4},{24,8},{28,12},{1,17},{... | collective-permute-start | bytes 3932168 | tf_op jit(solution)/shard_map/ppermute | solution.py:269
  76.8 29.3 %collective-permute-start.5 = (bf16[2,2,5,32,1024]{4,3,1,2,0:T(8,128)(2,1)S(1)}, bf16[2,2,5,32,1024]{4,3,1,2,0:T(8,128)(2,1)}, u32[]{:S(2)}, u32[]{:S(2)}) collective-permute-start(bf16[2,2,5,32,1024]{4,3,1,2,0:T(8,128)(2,1)S(1)} %pad_maximum_fusion.13), channel_id=1, source_target_pairs={{0,8},{4,12},{8,0},{12,4},{16,24},{20,28},{24,16},{28,20},{1,9},{5... | collective-permute-start | bytes 3932168 | tf_op jit(solution)/shard_map/ppermute | solution.py:269
  77.9 34.7 %collective-permute-start.6 = (bf16[2,2,5,32,1024]{4,3,1,2,0:T(8,128)(2,1)}, bf16[2,2,5,32,1024]{4,3,1,2,0:T(8,128)(2,1)}, u32[]{:S(2)}, u32[]{:S(2)}) collective-permute-start(bf16[2,2,5,32,1024]{4,3,1,2,0:T(8,128)(2,1)} %pad_maximum_fusion.12), channel_id=1, source_target_pairs={{0,4},{4,0},{8,12},{12,8},{16,20},{20,16},{24,28},{28,24},{1,5},{5... | collective-permute-start | bytes 3932168 | tf_op jit(solution)/shard_map/ppermute | solution.py:269
  78.0 38.6 %collective-permute-start.7 = (bf16[2,2,5,32,1024]{4,3,1,2,0:T(8,128)(2,1)S(1)}, bf16[2,2,5,32,1024]{4,3,1,2,0:T(8,128)(2,1)}, u32[]{:S(2)}, u32[]{:S(2)}) collective-permute-start(bf16[2,2,5,32,1024]{4,3,1,2,0:T(8,128)(2,1)S(1)} %pad_maximum_fusion.13), channel_id=1, source_target_pairs={{0,4},{4,0},{8,12},{12,8},{16,20},{20,16},{24,28},{28,24},{1,5},{5... | collective-permute-start | bytes 3932168 | tf_op jit(solution)/shard_map/ppermute | solution.py:269
  79.7 40.8 %all-to-all-start.2 = ((bf16[4,2,88,1024]{3,2,1,0:T(8,128)(2,1)}), bf16[4,2,88,1024]{3,2,1,0:T(8,128)(2,1)S(1)}, u32[]{:S(2)}, u32[]{:S(2)}) async-start(bf16[4,2,88,1024]{3,2,1,0:T(8,128)(2,1)} %broadcast_in_dim.117), calls=%async_computation.2 | async-start | bytes 2883584 | tf_op jit(solution)/shard_map/all_to_all | solution.py:349
  141.3 45.2 %collective-permute-start.10 = (bf16[2,2,2,88,1024]{4,3,1,0,2:T(8,128)(2,1)}, bf16[2,2,2,88,1024]{4,3,1,0,2:T(8,128)(2,1)}, u32[]{:S(2)}, u32[]{:S(2)}) collective-permute-start(bf16[2,2,2,88,1024]{4,3,1,0,2:T(8,128)(2,1)} %pad_maximum_fusion.5), channel_id=1, source_target_pairs={{0,16},{4,20},{8,24},{12,28},{16,0},{20,4},{24,8},{28,12},{1,17},{... | collective-permute-start | bytes 4325384 | tf_op jit(solution)/shard_map/ppermute | solution.py:269
  142.3 69.9 %collective-permute-start.12 = (bf16[2,2,2,88,1024]{4,3,1,0,2:T(8,128)(2,1)}, bf16[2,2,2,88,1024]{4,3,1,0,2:T(8,128)(2,1)}, u32[]{:S(2)}, u32[]{:S(2)}) collective-permute-start(bf16[2,2,2,88,1024]{4,3,1,0,2:T(8,128)(2,1)} %pad_maximum_fusion.5), channel_id=1, source_target_pairs={{0,4},{4,0},{8,12},{12,8},{16,20},{20,16},{24,28},{28,24},{1,5},{5... | collective-permute-start | bytes 4325384 | tf_op jit(solution)/shard_map/ppermute | solution.py:269
  142.3 44.2 %collective-permute-start.11 = (bf16[2,2,2,88,1024]{4,3,1,0,2:T(8,128)(2,1)}, bf16[2,2,2,88,1024]{4,3,1,0,2:T(8,128)(2,1)}, u32[]{:S(2)}, u32[]{:S(2)}) collective-permute-start(bf16[2,2,2,88,1024]{4,3,1,0,2:T(8,128)(2,1)} %pad_maximum_fusion.6), channel_id=1, source_target_pairs={{0,8},{4,12},{8,0},{12,4},{16,24},{20,28},{24,16},{28,20},{1,9},{5... | collective-permute-start | bytes 4325384 | tf_op jit(solution)/shard_map/ppermute | solution.py:269
  143.0 69.1 %collective-permute-start.14 = (bf16[2,2,2,88,1024]{4,3,1,0,2:T(8,128)(2,1)}, bf16[2,2,2,88,1024]{4,3,1,0,2:T(8,128)(2,1)}, u32[]{:S(2)}, u32[]{:S(2)}) collective-permute-start(bf16[2,2,2,88,1024]{4,3,1,0,2:T(8,128)(2,1)} %pad_maximum_fusion.6), channel_id=1, source_target_pairs={{0,4},{4,0},{8,12},{12,8},{16,20},{20,16},{24,28},{28,24},{1,5},{5... | collective-permute-start | bytes 4325384 | tf_op jit(solution)/shard_map/ppermute | solution.py:269
  144.2 42.3 %all-to-all-start.3 = ((bf16[4,1,88,1024]{3,2,1,0:T(8,128)(2,1)}), bf16[4,1,88,1024]{3,2,1,0:T(8,128)(2,1)}, u32[]{:S(2)}, u32[]{:S(2)}) async-start(bf16[4,1,88,1024]{3,2,1,0:T(8,128)(2,1)} %broadcast_in_dim.136), calls=%async_computation.3 | async-start | bytes 1441792 | tf_op jit(solution)/shard_map/all_to_all | solution.py:349
  186.5 25.7 %collective-permute-start.13 = (bf16[2,2,2,88,1024]{4,3,1,0,2:T(8,128)(2,1)}, bf16[2,2,2,88,1024]{4,3,1,0,2:T(8,128)(2,1)}, u32[]{:S(2)}, u32[]{:S(2)}) collective-permute-start(bf16[2,2,2,88,1024]{4,3,1,0,2:T(8,128)(2,1)} %collective-permute-done.10), channel_id=1, source_target_pairs={{0,4},{4,0},{8,12},{12,8},{16,20},{20,16},{24,28},{28,24},{1,5},{5... | collective-permute-start | bytes 4325384 | tf_op jit(solution)/shard_map/ppermute | solution.py:269
  196.1 48.0 %all-to-all-start.4 = ((bf16[4,120,1024]{2,1,0:T(8,128)(2,1)}), bf16[4,120,1024]{2,1,0:T(8,128)(2,1)}, u32[]{:S(2)}, u32[]{:S(2)}) async-start(bf16[4,120,1024]{2,1,0:T(8,128)(2,1)} %pad_maximum_fusion.15), calls=%async_computation.4 | async-start | bytes 1966080 | tf_op jit(solution)/shard_map/all_to_all | solution.py:577
  201.3 306.4 %reduce-scatter.3.cloned.1.call-start = ((), (), s32[]{:S(2)}) async-start(), calls=%async_computation.10 | async-start | bytes 3604480 | tf_op jit(solution)/shard_map/reduce_scatter | solution.py:645
  213.3 34.6 %collective-permute-start.19 = (bf16[2,2,1,88,1024]{4,3,1,0,2:T(8,128)(2,1)}, bf16[2,2,1,88,1024]{4,3,1,0,2:T(8,128)(2,1)}, u32[]{:S(2)}, u32[]{:S(2)}) collective-permute-start(bf16[2,2,1,88,1024]{4,3,1,0,2:T(8,128)(2,1)} %pad_maximum_fusion.18), channel_id=1, source_target_pairs={{0,4},{4,0},{8,12},{12,8},{16,20},{20,16},{24,28},{28,24},{1,5},{5... | collective-permute-start | bytes 2162696 | tf_op jit(solution)/shard_map/ppermute | solution.py:269
  214.3 33.7 %collective-permute-start.22 = (bf16[2,2,1,88,1024]{4,3,1,0,2:T(8,128)(2,1)}, bf16[2,2,1,88,1024]{4,3,1,0,2:T(8,128)(2,1)}, u32[]{:S(2)}, u32[]{:S(2)}) collective-permute-start(bf16[2,2,1,88,1024]{4,3,1,0,2:T(8,128)(2,1)} %pad_maximum_fusion.19), channel_id=1, source_target_pairs={{0,4},{4,0},{8,12},{12,8},{16,20},{20,16},{24,28},{28,24},{1,5},{5... | collective-permute-start | bytes 2162696 | tf_op jit(solution)/shard_map/ppermute | solution.py:269
  248.0 27.5 %collective-permute-start.24 = (bf16[1,2,2,352,1024]{4,3,2,1,0:T(8,128)(2,1)}, bf16[1,2,2,352,1024]{4,3,2,1,0:T(8,128)(2,1)}, u32[]{:S(2)}, u32[]{:S(2)}) collective-permute-start(bf16[1,2,2,352,1024]{4,3,2,1,0:T(8,128)(2,1)} %bitcast.594), channel_id=1, source_target_pairs={{0,4},{4,0},{8,12},{12,8},{16,20},{20,16},{24,28},{28,24},{1,5},{5... | collective-permute-start | bytes 8650760 | tf_op jit(solution)/shard_map/ppermute | solution.py:269
  365.9 40.8 %collective-permute-start.38 = (bf16[4,2,2,128,1024]{4,3,0,1,2:T(8,128)(2,1)}, bf16[4,2,2,128,1024]{4,3,0,1,2:T(8,128)(2,1)}, u32[]{:S(2)}, u32[]{:S(2)}) collective-permute-start(bf16[4,2,2,128,1024]{4,3,0,1,2:T(8,128)(2,1)} %bitcast.509), channel_id=1, source_target_pairs={{0,4},{4,0},{8,12},{12,8},{16,20},{20,16},{24,28},{28,24},{1,5},{5... | collective-permute-start | bytes 12582920 | tf_op jit(solution)/shard_map/ppermute | solution.py:269
  368.8 32.4 %collective-permute-start.31 = (bf16[1,2,176,1024]{3,2,1,0:T(8,128)(2,1)}, bf16[1,2,176,1024]{3,2,1,0:T(8,128)(2,1)}, u32[]{:S(2)}, u32[]{:S(2)}) collective-permute-start(bf16[1,2,176,1024]{3,2,1,0:T(8,128)(2,1)} %fusion.70), channel_id=1, source_target_pairs={{0,8},{4,12},{8,0},{12,4},{16,24},{20,28},{24,16},{28,20},{1,9},{5... | collective-permute-start | bytes 2162696 | tf_op jit(solution)/shard_map/ppermute | solution.py:269
  369.7 32.7 %collective-permute-start.32 = (bf16[1,2,176,1024]{3,2,1,0:T(8,128)(2,1)}, bf16[1,2,176,1024]{3,2,1,0:T(8,128)(2,1)}, u32[]{:S(2)}, u32[]{:S(2)}) collective-permute-start(bf16[1,2,176,1024]{3,2,1,0:T(8,128)(2,1)} %fusion.71), channel_id=1, source_target_pairs={{0,16},{4,20},{8,24},{12,28},{16,0},{20,4},{24,8},{28,12},{1,17},{... | collective-permute-start | bytes 2162696 | tf_op jit(solution)/shard_map/ppermute | solution.py:269
  451.0 87.7 %reduce-scatter.5.cloned.1.call-start = ((), (), s32[]{:S(2)}) async-start(), calls=%async_computation.11 | async-start | bytes 1310720 | tf_op jit(solution)/shard_map/reduce_scatter | solution.py:652
  518.1 63.6 %all-to-all-start.6 = ((f32[32,3,32]{2,1,0:T(4,128)}), f32[32,3,32]{2,1,0:T(4,128)S(1)}, u32[]{:S(2)}, u32[]{:S(2)}) async-start(f32[32,3,32]{2,1,0:T(4,128)} %maximum_bitcast_fusion.6), calls=%async_computation.8 | async-start | bytes 131072 | tf_op jit(solution)/shard_map/all_to_all | solution.py:418
  545.1 29.5 %collective-permute-start.52 = (bf16[2,352,1024]{2,1,0:T(8,128)(2,1)}, bf16[2,352,1024]{2,1,0:T(8,128)(2,1)S(1)}, u32[]{:S(2)}, u32[]{:S(2)}) collective-permute-start(bf16[2,352,1024]{2,1,0:T(8,128)(2,1)} %pad_maximum_fusion.9), channel_id=1, source_target_pairs={{0,16},{8,24},{16,0},{24,8},{1,17},{9,25},{17,1},{25,9},{2,18},{10... | collective-permute-start | bytes 4325384 | tf_op jit(solution)/shard_map/ppermute | solution.py:531
  581.7 83.1 %all-to-all-start.5 = ((bf16[4,120,1024]{2,1,0:T(8,128)(2,1)}), bf16[4,120,1024]{2,1,0:T(8,128)(2,1)S(1)}, u32[]{:S(2)}, u32[]{:S(2)}) async-start(bf16[4,120,1024]{2,1,0:T(8,128)(2,1)} %pad_maximum_fusion.16), calls=%async_computation.7 | async-start | bytes 1966080 | tf_op jit(solution)/shard_map/all_to_all | solution.py:577
  664.8 29.5 %all-to-all-start.7 = ((bf16[4,120,1024]{2,1,0:T(8,128)(2,1)}), bf16[4,120,1024]{2,1,0:T(8,128)(2,1)}, u32[]{:S(2)}, u32[]{:S(2)}) async-start(bf16[4,120,1024]{2,1,0:T(8,128)(2,1)} %pad_maximum_fusion.17), calls=%async_computation.9 | async-start | bytes 1966080 | tf_op jit(solution)/shard_map/all_to_all | solution.py:577
  (146 other events, 1620.4 us)
Sparse Core Ops, SparseCore 0:
  451.1 56.5 reduce-scatter.2
  510.5 28.0 reduce-scatter.4

commit v7 on v6

--- a/solution.py
+++ b/solution.py
@@ -49,7 +49,7 @@
     return jnp.where(allowed[None], fading, 0.0)
 
 
-def forward(tokens, segments, decay_rate, attn_full, up_gather, down_line, gain_low, moments):
+def forward(tokens, segments, decay_rate, attn_full, up_gathers, down_line, gain_low, moments):
     length, model_width = tokens.shape
     head_count = decay_rate.shape[0]
     head_size = model_width // head_count
@@ -80,16 +80,22 @@
     normal_out = attended * out_scale * gain_full[2]
     gate_sig = jax.nn.sigmoid(gate_pre)
     gated_out = (normal_out * gate_sig).astype(B16)
-    up_gather.came, moments, down_line, gated_out = tied([up_gather.came, moments], down_line, gated_out)
-    up_gather.cores()
+    one_gather, two_gather = up_gathers
+    one_gather.came, two_gather.came, moments, down_line, gated_out = tied(
+        [one_gather.came, two_gather.came, moments], down_line, gated_out
+    )
+    one_gather.cores()
+    two_gather.cores()
     down_gather = Gather(down_line)
     moments = exchange(*moments)
     branch = lax.dot_general(gated_out, attn_full[4], ROWS_BY_ROWS, preferred_element_type=F32)
     middle = inputs + branch
     second_scale = rms_scale(middle)
     normed_two = (middle * second_scale * gain_full[1]).astype(B16)
-    up_gather.pieces, down_gather.held, normed_two = tied([up_gather.pieces, down_gather.held], normed_two)
-    ffn_up = up_gather.join()
+    one_gather.pieces, two_gather.pieces, down_gather.held, normed_two = tied(
+        [one_gather.pieces, two_gather.pieces, down_gather.held], normed_two
+    )
+    ffn_up = one_gather.join() + two_gather.join()
     down_gather.cross()
     down_gather.cores()
     up_one, up_two = (
@@ -346,21 +352,21 @@
 
 def line_gather(value):
     copies = jnp.broadcast_to(value[None], (lax.axis_size("fsdp"), *value.shape))
-    return lax.all_to_all(copies, "fsdp", 0, 0, tiled=True)
+    return jnp.swapaxes(lax.all_to_all(copies, "fsdp", 0, 0, tiled=True), 0, 1)
 
 
 class Gather:
     def __init__(self, line):
-        lines, self.count, _, self.columns = line.shape
+        self.count, lines, _, self.columns = line.shape
         rest = list(range(1, plane_bits()))
         self.orders = (rest, rest[::-1])
         self.held, self.axes = [], []
         for color, order in enumerate(self.orders):
-            held = line[: lines // 2] if color == 0 else line[lines // 2 :]
+            held = line[:, : lines // 2] if color == 0 else line[:, lines // 2 :]
             for step, bit in enumerate(order):
                 axis = sorted(order[: step + 1], reverse=True).index(bit)
                 if step + 1 < len(order):
-                    held = jnp.stack([held, swap_bit(held, bit)], axis=axis)
+                    held = jnp.stack([held, swap_bit(held, bit)], axis=1 + axis)
             self.held.append(held)
             self.axes.append(axis)
 
@@ -373,7 +379,7 @@
             self.pieces += [held, came, swap_bit(held, 0), swap_bit(came, 0)]
 
     def natural(self):
-        half, _, own, _ = self.held[0].shape[-4:]
+        half, own, _ = self.held[0].shape[-3:]
         planes = lax.axis_size("dp")
         whole = jnp.zeros((self.count, planes, 2 * half, own, self.columns), self.held[0].dtype)
         for number in range(4):
@@ -383,7 +389,7 @@
                 base = (1 << order[-1]) * (number % 2) + number // 2
                 for index in itertools.product(range(2), repeat=len(bits)):
                     place = base + sum(value << bit for value, bit in zip(index, bits))
-                    block = jnp.swapaxes(piece[index], 0, 1)[:, None]
+                    block = piece[(slice(None), *index)][:, None]
                     where = (0, lax.axis_index("dp") ^ place, color * half, 0, 0)
                     whole = lax.dynamic_update_slice(whole, block, where)
         return whole.reshape(self.count, -1, self.columns)
@@ -396,7 +402,7 @@
                 halves = []
                 for color, axis in enumerate(self.axes):
                     first = 4 * color + 2 * side
-                    pair = [p[..., matrix, :, :] for p in self.pieces[first : first + 2]]
+                    pair = [p[matrix] for p in self.pieces[first : first + 2]]
                     halves.append(jnp.stack(pair, axis=axis))
                 sides.append(jnp.concatenate(halves, axis=len(self.orders[0])))
             out.append(jnp.stack(sides).reshape(-1, self.columns))
@@ -609,18 +615,30 @@
     attn_low = attn_master.astype(B16)
     ffn_low = ffn_master.astype(B16)
     gain_low = gains.astype(B16)
-    gain_whole, attn_low = ordered(gain_gather(gain_low), attn_low)
-    attn_gather = Gather(line_gather(attn_low))
+    attn_line, gain_low = ordered(line_gather(attn_low), gain_low)
+    gain_whole = gain_gather(gain_low)
+    attn_gather = Gather(attn_line)
     attn_gather.held, up_low = tied([attn_gather.held], ffn_low[:2])
     attn_gather.cross()
     attn_gather.cores()
-    up_gather = Gather(line_gather(up_low))
+    up_line = line_gather(up_low)
+    one_gather, two_gather = Gather(up_line[:1]), Gather(up_line[1:])
     attn_full = attn_gather.natural()
     moments = to_owners(attn_moment.astype(B16), ffn_moment.astype(B16))
-    up_gather.held, moments, down_low, attn_full = tied([up_gather.held, moments], ffn_low[2:], attn_full)
-    up_gather.cross()
+    one_gather.held, two_gather.held, moments, down_low, attn_full = tied(
+        [one_gather.held, two_gather.held, moments], ffn_low[2:], attn_full
+    )
+    one_gather.cross()
+    two_gather.cross()
     stored, down_gather, moments, ffn_up = forward(
-        tokens, segment_ids[0], decay_rate, attn_full, up_gather, line_gather(down_low), gain_whole, moments
+        tokens,
+        segment_ids[0],
+        decay_rate,
+        attn_full,
+        (one_gather, two_gather),
+        line_gather(down_low),
+        gain_whole,
+        moments,
     )
     x_grad, grads, grad_gain, ffn_down, (top_moment, low_moment) = backward(
         stored, cotangent, attn_full, ffn_up, down_gather, moments, gain_whole

time: 715 us -> 699 us (0.978)
  blocking collectives: 34.1 us -> 0 us
  waiting for transfers between devices: 169 us -> 194 us
  local copies, waits for them, and re-layouts: 97.9 us -> 86.4 us
  starting transfers between devices: 97.4 us -> 105 us
    all_to_all x2 -> x3, waiting for transfers between devices: 0.01 us -> 34.4 us  [line_gather(): return jnp.swapaxes(lax.all_to_all(copies, 'fsdp', 0, 0, tiled=True), 0, 1)]
    all_to_all x1 -> x0, blocking collectives: 34.1 us -> none  [line_gather(): return lax.all_to_all(copies, 'fsdp', 0, 0, tiled=True)]
    another operation x13 -> x3, local copies, waits for them, and re-layouts: 13.9 us -> 3.92 us  [__init__(): held = jnp.stack([held, swap_bit(held, bit)], axis=1 + axis)]
    all_to_all x2 -> x3, starting transfers between devices: 8.28 us -> 14.6 us  [line_gather(): return jnp.swapaxes(lax.all_to_all(copies, 'fsdp', 0, 0, tiled=True), 0, 1)]
    ppermute x49 -> x57, starting transfers between devices: 36.1 us -> 41.3 us  [swap_bit(): return lax.ppermute(value, 'dp', [(i, i ^ 1 << bit) for i in range(count)])]
    unnamed x198 -> x218, local copies, waits for them, and re-layouts: 11.6 us -> 16.2 us
    ppermute x49 -> x57, waiting for transfers between devices: 100 us -> 96 us  [swap_bit(): return lax.ppermute(value, 'dp', [(i, i ^ 1 << bit) for i in range(count)])]
  transfers between devices with their start and end apart: 70 -> 79, of which waited for: 24 -> 32; matrix products, arithmetic and copies ran while one was open for 33% -> 32% of each run, Pallas kernels for 9% -> 10%
where the time goes in v7:
time: 699 us; the launch traced here: 692 us
  waiting for transfers between devices  194 us (28%)
  matrix products  128 us (18%)
  starting transfers between devices  105 us (15%)
  other arithmetic  95.9 us (14%)
  local copies, waits for them, and re-layouts  86.4 us (12%)
  Pallas kernels  66.1 us (9%)
  between operations  16.2 us (2%)
    ppermute x57, waiting for transfers between devices, swap_bit(): return lax.ppermute(value, 'dp', [(i, i ^ 1 << bit) for i in range(count)])  96 us
    pallas_call x1, Pallas kernels, gram_orthogonalize(): pl.pallas_call(polynomial_kernel, out_shape=jax.ShapeDtypeStruct(rows.sha...  66.1 us
    ppermute x57, starting transfers between devices, swap_bit(): return lax.ppermute(value, 'dp', [(i, i ^ 1 << bit) for i in range(count)])  41.3 us
    all_to_all x3, waiting for transfers between devices, line_gather(): return jnp.swapaxes(lax.all_to_all(copies, 'fsdp', 0, 0, tiled=True), 0, 1)  34.4 us
    dynamic_update_slice x16, local copies, waits for them, and re-layouts, natural(): whole = lax.dynamic_update_slice(whole, block, where)  29.6 us
    dot_general x7, matrix products, weight_grad(): lax.dot_general(features, series, TOKENS_OUT, preferred_element_type=F32)  26.9 us
    ppermute x8, waiting for transfers between devices, swap_core(): lax.ppermute(value, 'dp', [(i, i ^ 1 << bit) for i in range(count) if i &...  21.3 us
    convert_element_type x17, other arithmetic, payloads(): sum((self.choose(t, dims, bit, True).astype(F32) for t, dims in part))  18.9 us
  transfers between devices with their start and end apart: 79, of which 32 were waited for; matrix products, arithmetic and copies ran while one was open for 32% of the time, Pallas kernels for 10%

profile of v7, /device:TPU:0, one launch (start us, length us, event | category | flops | bytes accessed | tf_op | source)
XLA Modules:
  0.0 691.6 jit_solution(162889231900014045)
XLA Ops:
  9.6 6.3 all-to-all-start
  16.3 31.0 %all-to-all-done = bf16[4,5,32,1024]{3,2,1,0:T(8,128)(2,1)S(1)} async-done(((bf16[4,5,32,1024]{3,2,1,0:T(8,128)(2,1)}), bf16[4,5,32,1024]{3,2,1,0:T(8,128)(2,1)S(1)}, u32[]{:S(2)}, u32[]{:S(2)}) %all-to-all-start) | async-done | bytes 1310752 | tf_op jit(solution)/shard_map/all_to_all | solution.py:355
  80.6 5.3 broadcast_in_dim.37
  91.6 7.1 %collective-permute-done.6 = bf16[5,2,2,32,1024]{4,3,2,0,1:T(8,128)(2,1)} collective-permute-done((bf16[5,2,2,32,1024]{4,3,2,0,1:T(8,128)(2,1)}, bf16[5,2,2,32,1024]{4,3,2,0,1:T(8,128)(2,1)}, u32[]{:S(2)}, u32[]{:S(2)}) %collective-permute-start.6) | collective-permute-done | bytes 1310752 | tf_op jit(solution)/shard_map/ppermute | solution.py:275
  154.8 8.4 %fusion.99 = f32[512,5120]{1,0:T(8,128)S(1)} fusion(bf16[5120,1024]{1,0:T(8,128)(2,1)} %bitcast.29, bf16[512,1024]{1,0:T(8,128)(2,1)S(1)} %copy-done.24, f32[1024]{0:T(1024)S(1)} %mul.333, f32[512]{0:T(512)S(1)} %copy-done.92), kind=kOutput, calls=%fused_computation.235 | convolution fusion | flops 5370806272 | bytes 22026240 | tf_op jit(solution)/shard_map/dot_general | solution.py:60
  171.6 6.5 multiply_convert_fusion.1
  249.3 9.8 %multiply_convert_fusion.2 = (bf16[512,2816]{1,0:T(8,128)(2,1)}, bf16[512,2816]{1,0:T(8,128)(2,1)}) fusion(f32[512,2816]{1,0:T(8,128)} %get-tuple-element.317, f32[512,2816]{1,0:T(8,128)S(1)} %bitcast.374, bf16[512,1024]{1,0:T(8,128)(2,1)} %param.14, bf16[2816,1024]{1,0:T(8,128)(2,1)S(1)} %bitcast.367), kind=kOutput, calls=%fused_computation.7 | convolution fusion | flops 2958557184 | bytes 24117248 | tf_op jit(solution)/shard_map/dot_general | solution.py:168
  301.4 5.3 multiply_reduce_fusion
  318.0 5.3 multiply_convert_fusion
  338.2 6.9 convolution_convert_fusion
  361.5 11.8 %collective-permute-done.37 = bf16[1,2,176,1024]{3,2,1,0:T(8,128)(2,1)S(1)} collective-permute-done((bf16[1,2,176,1024]{3,2,1,0:T(8,128)(2,1)}, bf16[1,2,176,1024]{3,2,1,0:T(8,128)(2,1)S(1)}, u32[]{:S(2)}, u32[]{:S(2)}) %collective-permute-start.37) | collective-permute-done | bytes 720928 | tf_op jit(solution)/shard_map/ppermute | solution.py:275
  378.1 10.7 %collective-permute-done.39 = bf16[1,2,176,1024]{3,2,1,0:T(8,128)(2,1)} collective-permute-done((bf16[1,2,176,1024]{3,2,1,0:T(8,128)(2,1)}, bf16[1,2,176,1024]{3,2,1,0:T(8,128)(2,1)}, u32[]{:S(2)}, u32[]{:S(2)}) %collective-permute-start.39) | collective-permute-done | bytes 720928 | tf_op jit(solution)/shard_map/ppermute | solution.py:275
  412.8 8.8 %fusion.19 = (f32[1024]{0:T(1024)S(1)}, f32[512]{0:T(512)S(1)}, f32[512,1024]{1,0:T(8,128)S(1)}) fusion(bf16[512,1024]{1,0:T(8,128)(2,1)S(1)} %copy-done.25, f32[512]{0:T(512)S(1)} %copy-done.93, f32[1024]{0:T(1024)S(1)} %copy-done.89, bf16[5120,1024]{1,0:T(8,128)(2,1)} %bitcast.29, bf16[512,4096]{1,0:T(8,128)(2,1)S(1)} %copy-done.30), kind=kOutput, calls=%fused_computation.53 | convolution fusion | flops 5372377600 | bytes 17838080 | tf_op jit(solution)/shard_map/dot_general | solution.py:249
  421.6 5.3 collective-permute-done.51
  438.7 20.0 %collective-permute-done.55 = bf16[4,2,64,1024]{3,2,0,1:T(8,128)(2,1)S(1)} collective-permute-done((bf16[4,2,64,1024]{3,2,0,1:T(8,128)(2,1)}, bf16[4,2,64,1024]{3,2,0,1:T(8,128)(2,1)S(1)}, u32[]{:S(2)}, u32[]{:S(2)}) %collective-permute-start.55) | collective-permute-done | bytes 1048608 | tf_op jit(solution)/shard_map/ppermute | solution.py:275
  463.8 7.2 %collective-permute-done.56 = bf16[4,64,1024]{2,1,0:T(8,128)(2,1)S(1)} collective-permute-done((bf16[4,64,1024]{2,1,0:T(8,128)(2,1)S(1)}, bf16[4,64,1024]{2,1,0:T(8,128)(2,1)S(1)}, u32[]{:S(2)}, u32[]{:S(2)}) %collective-permute-start.56) | collective-permute-done | bytes 524320 | tf_op jit(solution)/shard_map/ppermute | solution.py:275
  475.1 18.4 %reduce-scatter.3.cloned.1.call-done = bf16[1,352,1024]{2,1,0:T(8,128)(2,1)} async-done(((bf16[4,352,1024]{2,1,0:T(8,128)(2,1)}), bf16[1,352,1024]{2,1,0:T(8,128)(2,1)}) %reduce-scatter.3.cloned.1.call-update) | async-done | bytes 720912 | tf_op jit(solution)/shard_map/reduce_scatter | solution.py:663
  514.5 10.0 %reduce-scatter.5.cloned.1.call-done = bf16[1,128,1024]{2,1,0:T(8,128)(2,1)} async-done(((bf16[4,128,1024]{2,1,0:T(8,128)(2,1)}), bf16[1,128,1024]{2,1,0:T(8,128)(2,1)}) %reduce-scatter.5.cloned.1.call-update) | async-done | bytes 262160 | tf_op jit(solution)/shard_map/reduce_scatter | solution.py:670
  540.9 7.5 %collective-permute-done.61 = bf16[2,352,1024]{2,1,0:T(8,128)(2,1)S(1)} collective-permute-done((bf16[2,352,1024]{2,1,0:T(8,128)(2,1)}, bf16[2,352,1024]{2,1,0:T(8,128)(2,1)S(1)}, u32[]{:S(2)}, u32[]{:S(2)}) %collective-permute-start.61) | collective-permute-done | bytes 1441824 | tf_op jit(solution)/shard_map/ppermute | solution.py:537
  551.9 8.6 %collective-permute-done.60 = bf16[2,352,1024]{2,1,0:T(8,128)(2,1)S(1)} collective-permute-done((bf16[2,352,1024]{2,1,0:T(8,128)(2,1)}, bf16[2,352,1024]{2,1,0:T(8,128)(2,1)S(1)}, u32[]{:S(2)}, u32[]{:S(2)}) %collective-permute-start.60) | collective-permute-done | bytes 1441824 | tf_op jit(solution)/shard_map/ppermute | solution.py:537
  571.3 66.1 %shard_map.218 = bf16[704,1024]{1,0:T(8,128)(2,1)S(1)} custom-call(f32[1024,1024]{1,0:T(8,128)} %fusion.2.gram_ref, bf16[704,1024]{1,0:T(8,128)(2,1)S(1)} %pad_maximum_fusion.9.rows_ref), custom_call_target="tpu_custom_call" | custom-call | flops 32212254720 | bytes 8388608 | tf_op jit(solution)/shard_map/pallas_call | solution.py:516
  637.5 8.5 %collective-permute-start.67 = (bf16[352,1024]{1,0:T(8,128)(2,1)S(1)}, bf16[352,1024]{1,0:T(8,128)(2,1)S(1)}, u32[]{:S(2)}, u32[]{:S(2)}) collective-permute-start(bf16[352,1024]{1,0:T(8,128)(2,1)S(1)} %slice.432), channel_id=1, source_target_pairs={{0,4},{8,12},{16,20},{24,28},{1,5},{9,13},{17,21},{25,29},{2,6},{1... | collective-permute-start | bytes 2162696 | tf_op jit(solution)/shard_map/ppermute | solution.py:530
  656.4 7.7 %add_convert_fusion.2 = bf16[512,1024]{1,0:T(8,128)(2,1)} fusion(f32[512,1024]{1,0:T(8,128)S(1)} %copy-done.12, bf16[512,2816]{1,0:T(8,128)(2,1)} %copy-done.51, bf16[2816,1024]{1,0:T(8,128)(2,1)} %bitcast.368), kind=kOutput, calls=%fused_computation.80 | convolution fusion | flops 2953838592 | bytes 11796480 | tf_op jit(solution)/shard_map/dot_general | solution.py:654
  669.5 11.5 %all-to-all-done.7 = bf16[4,120,1024]{2,1,0:T(8,128)(2,1)S(1)} async-done(((bf16[4,120,1024]{2,1,0:T(8,128)(2,1)}), bf16[4,120,1024]{2,1,0:T(8,128)(2,1)S(1)}, u32[]{:S(2)}, u32[]{:S(2)}) %all-to-all-start.7) | async-done | bytes 983072 | tf_op jit(solution)/shard_map/all_to_all | solution.py:583
  (542 shorter events, 381.2 us)
Async XLA Ops:
  9.6 37.7 %all-to-all-start = ((bf16[4,5,32,1024]{3,2,1,0:T(8,128)(2,1)}), bf16[4,5,32,1024]{3,2,1,0:T(8,128)(2,1)S(1)}, u32[]{:S(2)}, u32[]{:S(2)}) async-start(bf16[4,5,32,1024]{3,2,1,0:T(8,128)(2,1)} %broadcast_in_dim.34), calls=%async_computation | async-start | bytes 2621440 | tf_op jit(solution)/shard_map/all_to_all | solution.py:355
  69.8 28.9 %collective-permute-start.6 = (bf16[5,2,2,32,1024]{4,3,2,0,1:T(8,128)(2,1)}, bf16[5,2,2,32,1024]{4,3,2,0,1:T(8,128)(2,1)}, u32[]{:S(2)}, u32[]{:S(2)}) collective-permute-start(bf16[5,2,2,32,1024]{4,3,2,0,1:T(8,128)(2,1)} %pad_maximum_fusion.10), channel_id=1, source_target_pairs={{0,16},{4,20},{8,24},{12,28},{16,0},{20,4},{24,8},{28,12},{1,17},{... | collective-permute-start | bytes 3932168 | tf_op jit(solution)/shard_map/ppermute | solution.py:275
  74.2 33.6 %collective-permute-start.8 = (bf16[5,2,2,32,1024]{4,3,2,0,1:T(8,128)(2,1)}, bf16[5,2,2,32,1024]{4,3,2,0,1:T(8,128)(2,1)}, u32[]{:S(2)}, u32[]{:S(2)}) collective-permute-start(bf16[5,2,2,32,1024]{4,3,2,0,1:T(8,128)(2,1)} %pad_maximum_fusion.10), channel_id=1, source_target_pairs={{0,4},{4,0},{8,12},{12,8},{16,20},{20,16},{24,28},{28,24},{1,5},{5... | collective-permute-start | bytes 3932168 | tf_op jit(solution)/shard_map/ppermute | solution.py:275
  74.2 43.0 %collective-permute-start.9 = (bf16[5,2,2,32,1024]{4,3,2,1,0:T(8,128)(2,1)S(1)}, bf16[5,2,2,32,1024]{4,3,2,1,0:T(8,128)(2,1)}, u32[]{:S(2)}, u32[]{:S(2)}) collective-permute-start(bf16[5,2,2,32,1024]{4,3,2,1,0:T(8,128)(2,1)S(1)} %pad_maximum_fusion.11), channel_id=1, source_target_pairs={{0,4},{4,0},{8,12},{12,8},{16,20},{20,16},{24,28},{28,24},{1,5},{5... | collective-permute-start | bytes 3932168 | tf_op jit(solution)/shard_map/ppermute | solution.py:275
  77.0 38.1 %all-to-all-start.1 = ((bf16[4,2,88,1024]{3,2,1,0:T(8,128)(2,1)}), bf16[4,2,88,1024]{3,2,1,0:T(8,128)(2,1)S(1)}, u32[]{:S(2)}, u32[]{:S(2)}) async-start(bf16[4,2,88,1024]{3,2,1,0:T(8,128)(2,1)} %broadcast_in_dim.35), calls=%async_computation.1 | async-start | bytes 2883584 | tf_op jit(solution)/shard_map/all_to_all | solution.py:355
  98.7 38.3 %collective-permute-start.10 = (bf16[5,2,2,32,1024]{4,3,2,0,1:T(8,128)(2,1)}, bf16[5,2,2,32,1024]{4,3,2,0,1:T(8,128)(2,1)}, u32[]{:S(2)}, u32[]{:S(2)}) collective-permute-start(bf16[5,2,2,32,1024]{4,3,2,0,1:T(8,128)(2,1)} %collective-permute-done.6), channel_id=1, source_target_pairs={{0,4},{4,0},{8,12},{12,8},{16,20},{20,16},{24,28},{28,24},{1,5},{5... | collective-permute-start | bytes 3932168 | tf_op jit(solution)/shard_map/ppermute | solution.py:275
  99.9 41.2 %collective-permute-start.11 = (bf16[5,2,2,32,1024]{4,3,2,1,0:T(8,128)(2,1)}, bf16[5,2,2,32,1024]{4,3,2,1,0:T(8,128)(2,1)}, u32[]{:S(2)}, u32[]{:S(2)}) collective-permute-start(bf16[5,2,2,32,1024]{4,3,2,1,0:T(8,128)(2,1)} %collective-permute-done.7), channel_id=1, source_target_pairs={{0,4},{4,0},{8,12},{12,8},{16,20},{20,16},{24,28},{28,24},{1,5},{5... | collective-permute-start | bytes 3932168 | tf_op jit(solution)/shard_map/ppermute | solution.py:275
  145.1 42.3 %collective-permute-start.12 = (bf16[1,2,2,88,1024]{4,3,2,0,1:T(8,128)(2,1)}, bf16[1,2,2,88,1024]{4,3,2,0,1:T(8,128)(2,1)}, u32[]{:S(2)}, u32[]{:S(2)}) collective-permute-start(bf16[1,2,2,88,1024]{4,3,2,0,1:T(8,128)(2,1)} %pad_maximum_fusion.16), channel_id=1, source_target_pairs={{0,16},{4,20},{8,24},{12,28},{16,0},{20,4},{24,8},{28,12},{1,17},{... | collective-permute-start | bytes 2162696 | tf_op jit(solution)/shard_map/ppermute | solution.py:275
  145.6 55.3 %collective-permute-start.16 = (bf16[1,2,2,88,1024]{4,3,2,0,1:T(8,128)(2,1)}, bf16[1,2,2,88,1024]{4,3,2,0,1:T(8,128)(2,1)}, u32[]{:S(2)}, u32[]{:S(2)}) collective-permute-start(bf16[1,2,2,88,1024]{4,3,2,0,1:T(8,128)(2,1)} %pad_maximum_fusion.16), channel_id=1, source_target_pairs={{0,4},{4,0},{8,12},{12,8},{16,20},{20,16},{24,28},{28,24},{1,5},{5... | collective-permute-start | bytes 2162696 | tf_op jit(solution)/shard_map/ppermute | solution.py:275
  145.6 41.8 %collective-permute-start.13 = (bf16[1,2,2,88,1024]{4,3,2,1,0:T(8,128)(2,1)}, bf16[1,2,2,88,1024]{4,3,2,1,0:T(8,128)(2,1)}, u32[]{:S(2)}, u32[]{:S(2)}) collective-permute-start(bf16[1,2,2,88,1024]{4,3,2,1,0:T(8,128)(2,1)} %pad_maximum_fusion.17), channel_id=1, source_target_pairs={{0,8},{4,12},{8,0},{12,4},{16,24},{20,28},{24,16},{28,20},{1,9},{5... | collective-permute-start | bytes 2162696 | tf_op jit(solution)/shard_map/ppermute | solution.py:275
  146.2 41.7 %collective-permute-start.14 = (bf16[1,2,2,88,1024]{4,3,2,0,1:T(8,128)(2,1)}, bf16[1,2,2,88,1024]{4,3,2,0,1:T(8,128)(2,1)}, u32[]{:S(2)}, u32[]{:S(2)}) collective-permute-start(bf16[1,2,2,88,1024]{4,3,2,0,1:T(8,128)(2,1)} %pad_maximum_fusion.18), channel_id=1, source_target_pairs={{0,16},{4,20},{8,24},{12,28},{16,0},{20,4},{24,8},{28,12},{1,17},{... | collective-permute-start | bytes 2162696 | tf_op jit(solution)/shard_map/ppermute | solution.py:275
  147.7 40.2 %collective-permute-start.15 = (bf16[1,2,2,88,1024]{4,3,2,1,0:T(8,128)(2,1)}, bf16[1,2,2,88,1024]{4,3,2,1,0:T(8,128)(2,1)}, u32[]{:S(2)}, u32[]{:S(2)}) collective-permute-start(bf16[1,2,2,88,1024]{4,3,2,1,0:T(8,128)(2,1)} %pad_maximum_fusion.19), channel_id=1, source_target_pairs={{0,8},{4,12},{8,0},{12,4},{16,24},{20,28},{24,16},{28,20},{1,9},{5... | collective-permute-start | bytes 2162696 | tf_op jit(solution)/shard_map/ppermute | solution.py:275
  150.1 37.8 %all-to-all-start.2 = ((bf16[4,1,88,1024]{3,2,1,0:T(8,128)(2,1)}), bf16[4,1,88,1024]{3,2,1,0:T(8,128)(2,1)}, u32[]{:S(2)}, u32[]{:S(2)}) async-start(bf16[4,1,88,1024]{3,2,1,0:T(8,128)(2,1)} %broadcast_in_dim.39), calls=%async_computation.2 | async-start | bytes 1441792 | tf_op jit(solution)/shard_map/all_to_all | solution.py:355
  192.2 45.6 %all-to-all-start.4 = ((bf16[4,120,1024]{2,1,0:T(8,128)(2,1)}), bf16[4,120,1024]{2,1,0:T(8,128)(2,1)S(1)}, u32[]{:S(2)}, u32[]{:S(2)}) async-start(bf16[4,120,1024]{2,1,0:T(8,128)(2,1)} %pad_maximum_fusion.13), calls=%async_computation.4 | async-start | bytes 1966080 | tf_op jit(solution)/shard_map/all_to_all | solution.py:583
  197.3 296.3 %reduce-scatter.3.cloned.1.call-start = ((), (), s32[]{:S(2)}) async-start(), calls=%async_computation.10 | async-start | bytes 3604480 | tf_op jit(solution)/shard_map/reduce_scatter | solution.py:663
  237.9 29.6 %collective-permute-start.32 = (bf16[1,2,2,352,1024]{4,3,2,1,0:T(8,128)(2,1)}, bf16[1,2,2,352,1024]{4,3,2,1,0:T(8,128)(2,1)}, u32[]{:S(2)}, u32[]{:S(2)}) collective-permute-start(bf16[1,2,2,352,1024]{4,3,2,1,0:T(8,128)(2,1)} %bitcast.437), channel_id=1, source_target_pairs={{0,4},{4,0},{8,12},{12,8},{16,20},{20,16},{24,28},{28,24},{1,5},{5... | collective-permute-start | bytes 8650760 | tf_op jit(solution)/shard_map/ppermute | solution.py:275
  353.5 41.0 %collective-permute-start.46 = (bf16[4,2,2,128,1024]{4,3,0,1,2:T(8,128)(2,1)}, bf16[4,2,2,128,1024]{4,3,0,1,2:T(8,128)(2,1)}, u32[]{:S(2)}, u32[]{:S(2)}) collective-permute-start(bf16[4,2,2,128,1024]{4,3,0,1,2:T(8,128)(2,1)} %bitcast.364), channel_id=1, source_target_pairs={{0,4},{4,0},{8,12},{12,8},{16,20},{20,16},{24,28},{28,24},{1,5},{5... | collective-permute-start | bytes 12582920 | tf_op jit(solution)/shard_map/ppermute | solution.py:275
  357.0 31.8 %collective-permute-start.39 = (bf16[1,2,176,1024]{3,2,1,0:T(8,128)(2,1)}, bf16[1,2,176,1024]{3,2,1,0:T(8,128)(2,1)}, u32[]{:S(2)}, u32[]{:S(2)}) collective-permute-start(bf16[1,2,176,1024]{3,2,1,0:T(8,128)(2,1)} %fusion.70), channel_id=1, source_target_pairs={{0,8},{4,12},{8,0},{12,4},{16,24},{20,28},{24,16},{28,20},{1,9},{5... | collective-permute-start | bytes 2162696 | tf_op jit(solution)/shard_map/ppermute | solution.py:275
  357.6 32.6 %collective-permute-start.40 = (bf16[1,2,176,1024]{3,2,1,0:T(8,128)(2,1)}, bf16[1,2,176,1024]{3,2,1,0:T(8,128)(2,1)}, u32[]{:S(2)}, u32[]{:S(2)}) collective-permute-start(bf16[1,2,176,1024]{3,2,1,0:T(8,128)(2,1)} %fusion.71), channel_id=1, source_target_pairs={{0,16},{4,20},{8,24},{12,28},{16,0},{20,4},{24,8},{28,12},{1,17},{... | collective-permute-start | bytes 2162696 | tf_op jit(solution)/shard_map/ppermute | solution.py:275
  436.4 88.1 %reduce-scatter.5.cloned.1.call-start = ((), (), s32[]{:S(2)}) async-start(), calls=%async_computation.11 | async-start | bytes 1310720 | tf_op jit(solution)/shard_map/reduce_scatter | solution.py:670
  504.0 63.7 %all-to-all-start.6 = ((f32[32,3,32]{2,1,0:T(4,128)}), f32[32,3,32]{2,1,0:T(4,128)S(1)}, u32[]{:S(2)}, u32[]{:S(2)}) async-start(f32[32,3,32]{2,1,0:T(4,128)} %maximum_bitcast_fusion.6), calls=%async_computation.8 | async-start | bytes 131072 | tf_op jit(solution)/shard_map/all_to_all | solution.py:424
  530.9 29.5 %collective-permute-start.60 = (bf16[2,352,1024]{2,1,0:T(8,128)(2,1)}, bf16[2,352,1024]{2,1,0:T(8,128)(2,1)S(1)}, u32[]{:S(2)}, u32[]{:S(2)}) collective-permute-start(bf16[2,352,1024]{2,1,0:T(8,128)(2,1)} %pad_maximum_fusion.7), channel_id=1, source_target_pairs={{0,16},{8,24},{16,0},{24,8},{1,17},{9,25},{17,1},{25,9},{2,18},{10... | collective-permute-start | bytes 4325384 | tf_op jit(solution)/shard_map/ppermute | solution.py:537
  567.6 83.1 %all-to-all-start.5 = ((bf16[4,120,1024]{2,1,0:T(8,128)(2,1)}), bf16[4,120,1024]{2,1,0:T(8,128)(2,1)S(1)}, u32[]{:S(2)}, u32[]{:S(2)}) async-start(bf16[4,120,1024]{2,1,0:T(8,128)(2,1)} %pad_maximum_fusion.14), calls=%async_computation.7 | async-start | bytes 1966080 | tf_op jit(solution)/shard_map/all_to_all | solution.py:583
  651.6 29.4 %all-to-all-start.7 = ((bf16[4,120,1024]{2,1,0:T(8,128)(2,1)}), bf16[4,120,1024]{2,1,0:T(8,128)(2,1)S(1)}, u32[]{:S(2)}, u32[]{:S(2)}) async-start(bf16[4,120,1024]{2,1,0:T(8,128)(2,1)} %pad_maximum_fusion.15), calls=%async_computation.9 | async-start | bytes 1966080 | tf_op jit(solution)/shard_map/all_to_all | solution.py:583
  (168 other events, 1844.2 us)
Sparse Core Ops, SparseCore 0:
  436.5 56.9 reduce-scatter.2
  496.4 28.0 reduce-scatter.4

commit v8 on v7

--- a/solution.py
+++ b/solution.py
@@ -49,7 +49,7 @@
     return jnp.where(allowed[None], fading, 0.0)
 
 
-def forward(tokens, segments, decay_rate, attn_full, up_gathers, down_line, gain_low, moments):
+def forward(tokens, segments, decay_rate, attn_full, up_gathers, down_low, gain_low, moments):
     length, model_width = tokens.shape
     head_count = decay_rate.shape[0]
     head_size = model_width // head_count
@@ -67,6 +67,13 @@
     key_act = jax.nn.relu(projected[:, model_width : 2 * model_width]).astype(B16)
     value_act = projected[:, 2 * model_width : 3 * model_width].astype(B16)
     gate_pre = projected[:, 3 * model_width : 4 * model_width]
+    one_gather, two_gather = up_gathers
+    one_gather.held, two_gather.held, moments, down_low, query_act, key_act = tied(
+        [one_gather.held, two_gather.held, moments], down_low, query_act, key_act
+    )
+    one_gather.cross()
+    two_gather.cross()
+    down_line = line_gather(down_low)
     fading_mask = decay_mask(segments, decay_rate)
     query_heads = query_act.reshape(length, head_count, head_size)
     key_heads = key_act.reshape(length, head_count, head_size)
@@ -80,7 +87,6 @@
     normal_out = attended * out_scale * gain_full[2]
     gate_sig = jax.nn.sigmoid(gate_pre)
     gated_out = (normal_out * gate_sig).astype(B16)
-    one_gather, two_gather = up_gathers
     one_gather.came, two_gather.came, moments, down_line, gated_out = tied(
         [one_gather.came, two_gather.came, moments], down_line, gated_out
     )
@@ -424,14 +430,12 @@
     return jnp.sum(lax.all_to_all(blocks, ("dp", "fsdp"), 0, 0, tiled=True), axis=0)
 
 
-NS_ROWS = 256
+NS_ROWS = 1024
 
 
 def polynomial_kernel(gram_ref, rows_ref, out_ref, gram, rest_low, poly, poly_low, current):
     size = gram_ref.shape[0]
-    count = rows_ref.shape[0]
     blocks = size // NS_ROWS
-    parts = count // 2
 
     def block(i):
         return pl.ds(pl.multiple_of(i * NS_ROWS, NS_ROWS), NS_ROWS)
@@ -480,15 +484,8 @@
 
         lax.fori_loop(0, blocks, polynomial, 0)
 
-        def apply(i, carry):
-            where = pl.ds(pl.multiple_of(i * parts, parts), parts)
-            value = current[where, :]
-            current[where, :] = factor * value + jnp.dot(
-                value.astype(B16), poly_low[...], preferred_element_type=F32
-            )
-            return carry
-
-        lax.fori_loop(0, 2, apply, 0)
+        value = current[...]
+        current[...] = factor * value + jnp.dot(value.astype(B16), poly_low[...], preferred_element_type=F32)
 
         def next_gram(i, total):
             eye = on_diagonal(i)
@@ -622,21 +619,18 @@
     attn_gather.cross()
     attn_gather.cores()
     up_line = line_gather(up_low)
+    last, up_line = tied([attn_gather.pieces[3::4]], up_line)
+    attn_gather.pieces[3::4] = last
     one_gather, two_gather = Gather(up_line[:1]), Gather(up_line[1:])
     attn_full = attn_gather.natural()
     moments = to_owners(attn_moment.astype(B16), ffn_moment.astype(B16))
-    one_gather.held, two_gather.held, moments, down_low, attn_full = tied(
-        [one_gather.held, two_gather.held, moments], ffn_low[2:], attn_full
-    )
-    one_gather.cross()
-    two_gather.cross()
     stored, down_gather, moments, ffn_up = forward(
         tokens,
         segment_ids[0],
         decay_rate,
         attn_full,
         (one_gather, two_gather),
-        line_gather(down_low),
+        ffn_low[2:],
         gain_whole,
         moments,
     )
@@ -666,8 +660,8 @@
         low_grad = jnp.concatenate([low_grad, proj_sum])
     if lines > low_grad.shape[0]:
         low_grad = jnp.pad(low_grad, ((0, lines - low_grad.shape[0]), (0, 0), (0, 0)))
-    top_grad, low_grad = ordered(top_grad, low_grad)
-    low_grad = lax.psum_scatter(low_grad, "fsdp", scatter_dimension=0, tiled=True)[0]
+    low_parts = lax.all_to_all(low_grad, "fsdp", split_axis=0, concat_axis=0, tiled=True)
+    low_grad = jnp.sum(low_parts.astype(F32), axis=0).astype(B16)
     at_core = lax.axis_index("dp") & 1
     big = owner_momentum(top_moment.reshape(block, columns), top_grad)
     big_other = one_way(big, 0, True)

time: 699 us -> 684 us (0.979)
  Pallas kernels: 66.1 us -> 48.1 us
  waiting for transfers between devices: 194 us -> 187 us
    pallas_call x1, Pallas kernels: 66.1 us -> 48.1 us  [gram_orthogonalize(): pl.pallas_call(polynomial_kernel, out_shape=jax.ShapeDtypeStruct(rows.sha...]
    reduce_scatter x1 -> x0, waiting for transfers between devices: 10 us -> none  [on_device(): lax.psum_scatter(low_grad, 'fsdp', scatter_dimension=0, tiled=True)[0]]
    unnamed x218 -> x210, local copies, waits for them, and re-layouts: 16.2 us -> 13.6 us
  transfers between devices with their start and end apart: 79 -> 79, of which waited for: 32 -> 29; matrix products, arithmetic and copies ran while one was open for 32% -> 33% of each run, Pallas kernels for 10% -> 7%
where the time goes in v8:
time: 684 us; the launch traced here: 674 us
  waiting for transfers between devices  187 us (27%)
  matrix products  127 us (19%)
  starting transfers between devices  105 us (15%)
  other arithmetic  102 us (15%)
  local copies, waits for them, and re-layouts  88.3 us (13%)
  Pallas kernels  48.1 us (7%)
  between operations  16.5 us (2%)
    ppermute x57, waiting for transfers between devices, swap_bit(): return lax.ppermute(value, 'dp', [(i, i ^ 1 << bit) for i in range(count)])  100 us
    pallas_call x1, Pallas kernels, gram_orthogonalize(): pl.pallas_call(polynomial_kernel, out_shape=jax.ShapeDtypeStruct(rows.sha...  48.1 us
    ppermute x57, starting transfers between devices, swap_bit(): return lax.ppermute(value, 'dp', [(i, i ^ 1 << bit) for i in range(count)])  40.9 us
    all_to_all x3, waiting for transfers between devices, line_gather(): return jnp.swapaxes(lax.all_to_all(copies, 'fsdp', 0, 0, tiled=True), 0, 1)  31 us
    dynamic_update_slice x16, local copies, waits for them, and re-layouts, natural(): whole = lax.dynamic_update_slice(whole, block, where)  29.3 us
    dot_general x7, matrix products, weight_grad(): lax.dot_general(features, series, TOKENS_OUT, preferred_element_type=F32)  26.3 us
    reduce_scatter x1, waiting for transfers between devices, on_device(): lax.psum_scatter(top_grad, 'fsdp', scatter_dimension=0, tiled=True)[0]  22.4 us
    convert_element_type x17, other arithmetic, payloads(): sum((self.choose(t, dims, bit, True).astype(F32) for t, dims in part))  20 us
  transfers between devices with their start and end apart: 79, of which 29 were waited for; matrix products, arithmetic and copies ran while one was open for 33% of the time, Pallas kernels for 7%

profile of v8, /device:TPU:0, one launch (start us, length us, event | category | flops | bytes accessed | tf_op | source)
XLA Modules:
  0.0 674.2 jit_solution(11990205073397990135)
XLA Ops:
  9.6 6.3 all-to-all-start
  16.3 31.0 %all-to-all-done = bf16[4,5,32,1024]{3,2,1,0:T(8,128)(2,1)S(1)} async-done(((bf16[4,5,32,1024]{3,2,1,0:T(8,128)(2,1)}), bf16[4,5,32,1024]{3,2,1,0:T(8,128)(2,1)S(1)}, u32[]{:S(2)}, u32[]{:S(2)}) %all-to-all-start) | async-done | bytes 1310752 | tf_op jit(solution)/shard_map/all_to_all | solution.py:361
  59.8 5.2 collective-permute-done
  77.6 5.2 broadcast_in_dim.35
  88.6 10.1 %collective-permute-done.2 = bf16[5,2,2,32,1024]{4,3,2,0,1:T(8,128)(2,1)} collective-permute-done((bf16[5,2,2,32,1024]{4,3,2,0,1:T(8,128)(2,1)}, bf16[5,2,2,32,1024]{4,3,2,0,1:T(8,128)(2,1)}, u32[]{:S(2)}, u32[]{:S(2)}) %collective-permute-start.2) | collective-permute-done | bytes 1310752 | tf_op jit(solution)/shard_map/ppermute | solution.py:281
  132.4 8.4 %fusion.92 = f32[512,5120]{1,0:T(8,128)S(1)} fusion(bf16[5120,1024]{1,0:T(8,128)(2,1)} %bitcast.26, bf16[512,1024]{1,0:T(8,128)(2,1)S(1)} %copy-done.26, f32[1024]{0:T(1024)S(1)} %mul.335, f32[512]{0:T(512)S(1)} %get-tuple-element.311), kind=kOutput, calls=%fused_computation.231 | convolution fusion | flops 5370806272 | bytes 22026240 | tf_op jit(solution)/shard_map/dot_general | solution.py:60
  166.0 6.5 multiply_convert_fusion.1
  182.2 6.2 collective-permute-done.14
  251.4 9.8 %multiply_convert_fusion.2 = (bf16[512,2816]{1,0:T(8,128)(2,1)}, bf16[512,2816]{1,0:T(8,128)(2,1)}) fusion(f32[512,2816]{1,0:T(8,128)} %get-tuple-element.321, f32[512,2816]{1,0:T(8,128)S(1)} %bitcast.375, bf16[512,1024]{1,0:T(8,128)(2,1)} %param.14, bf16[2816,1024]{1,0:T(8,128)(2,1)S(1)} %bitcast.368), kind=kOutput, calls=%fused_computation.7 | convolution fusion | flops 2958557184 | bytes 24117248 | tf_op jit(solution)/shard_map/dot_general | solution.py:174
  321.2 5.3 multiply_convert_fusion
  342.5 6.4 convolution_convert_fusion
  362.6 12.3 %collective-permute-done.37 = bf16[1,2,176,1024]{3,2,1,0:T(8,128)(2,1)S(1)} collective-permute-done((bf16[1,2,176,1024]{3,2,1,0:T(8,128)(2,1)}, bf16[1,2,176,1024]{3,2,1,0:T(8,128)(2,1)S(1)}, u32[]{:S(2)}, u32[]{:S(2)}) %collective-permute-start.37) | collective-permute-done | bytes 720928 | tf_op jit(solution)/shard_map/ppermute | solution.py:281
  379.4 11.1 %collective-permute-done.39 = bf16[1,2,176,1024]{3,2,1,0:T(8,128)(2,1)} collective-permute-done((bf16[1,2,176,1024]{3,2,1,0:T(8,128)(2,1)}, bf16[1,2,176,1024]{3,2,1,0:T(8,128)(2,1)}, u32[]{:S(2)}, u32[]{:S(2)}) %collective-permute-start.39) | collective-permute-done | bytes 720928 | tf_op jit(solution)/shard_map/ppermute | solution.py:281
  415.4 8.8 %fusion.19 = (f32[1024]{0:T(1024)S(1)}, f32[512]{0:T(512)S(1)}, f32[512,1024]{1,0:T(8,128)S(1)}) fusion(bf16[512,1024]{1,0:T(8,128)(2,1)S(1)} %copy-done.27, f32[512]{0:T(512)S(1)} %get-tuple-element.311, f32[1024]{0:T(1024)S(1)} %mul.335, bf16[5120,1024]{1,0:T(8,128)(2,1)} %bitcast.26, bf16[512,4096]{1,0:T(8,128)(2,1)S(1)} %copy-done.33), kind=kOutput, calls=%fused_computation.53 | convolution fusion | flops 5372377600 | bytes 17838080 | tf_op jit(solution)/shard_map/dot_general | solution.py:255
  424.2 6.3 collective-permute-done.51
  441.8 20.9 %collective-permute-done.58 = bf16[4,2,64,1024]{3,2,0,1:T(8,128)(2,1)S(1)} collective-permute-done((bf16[4,2,64,1024]{3,2,0,1:T(8,128)(2,1)}, bf16[4,2,64,1024]{3,2,0,1:T(8,128)(2,1)S(1)}, u32[]{:S(2)}, u32[]{:S(2)}) %collective-permute-start.58) | collective-permute-done | bytes 1048608 | tf_op jit(solution)/shard_map/ppermute | solution.py:281
  467.3 7.6 %collective-permute-done.59 = bf16[4,64,1024]{2,1,0:T(8,128)(2,1)S(1)} collective-permute-done((bf16[4,64,1024]{2,1,0:T(8,128)(2,1)S(1)}, bf16[4,64,1024]{2,1,0:T(8,128)(2,1)S(1)}, u32[]{:S(2)}, u32[]{:S(2)}) %collective-permute-start.59) | collective-permute-done | bytes 524320 | tf_op jit(solution)/shard_map/ppermute | solution.py:281
  484.0 22.4 %reduce-scatter.2.cloned.1.call-done = bf16[1,352,1024]{2,1,0:T(8,128)(2,1)} async-done(((bf16[4,352,1024]{2,1,0:T(8,128)(2,1)}), bf16[1,352,1024]{2,1,0:T(8,128)(2,1)}) %reduce-scatter.2.cloned.1.call-update) | async-done | bytes 720912 | tf_op jit(solution)/shard_map/reduce_scatter | solution.py:657
  542.6 7.2 %collective-permute-done.61 = bf16[2,352,1024]{2,1,0:T(8,128)(2,1)S(1)} collective-permute-done((bf16[2,352,1024]{2,1,0:T(8,128)(2,1)S(1)}, bf16[2,352,1024]{2,1,0:T(8,128)(2,1)S(1)}, u32[]{:S(2)}, u32[]{:S(2)}) %collective-permute-start.61) | collective-permute-done | bytes 1441824 | tf_op jit(solution)/shard_map/ppermute | solution.py:534
  553.3 8.7 %collective-permute-done.60 = bf16[2,352,1024]{2,1,0:T(8,128)(2,1)S(1)} collective-permute-done((bf16[2,352,1024]{2,1,0:T(8,128)(2,1)S(1)}, bf16[2,352,1024]{2,1,0:T(8,128)(2,1)S(1)}, u32[]{:S(2)}, u32[]{:S(2)}) %collective-permute-start.60) | collective-permute-done | bytes 1441824 | tf_op jit(solution)/shard_map/ppermute | solution.py:534
  569.8 5.5 all-to-all-start.6
  575.4 48.1 %shard_map.218 = bf16[704,1024]{1,0:T(8,128)(2,1)S(1)} custom-call(f32[1024,1024]{1,0:T(8,128)} %fusion.2.gram_ref, bf16[704,1024]{1,0:T(8,128)(2,1)S(1)} %pad_maximum_fusion.9.rows_ref), custom_call_target="tpu_custom_call" | custom-call | flops 32212254720 | bytes 8388608 | tf_op jit(solution)/shard_map/pallas_call | solution.py:513
  638.8 7.7 %add_convert_fusion.2 = bf16[512,1024]{1,0:T(8,128)(2,1)} fusion(f32[512,1024]{1,0:T(8,128)S(1)} %copy-done.12, bf16[512,2816]{1,0:T(8,128)(2,1)} %copy-done.54, bf16[2816,1024]{1,0:T(8,128)(2,1)} %bitcast.369), kind=kOutput, calls=%fused_computation.76 | convolution fusion | flops 2953838592 | bytes 11796480 | tf_op jit(solution)/shard_map/dot_general | solution.py:648
  651.9 11.4 %all-to-all-done.8 = bf16[4,120,1024]{2,1,0:T(8,128)(2,1)S(1)} async-done(((bf16[4,120,1024]{2,1,0:T(8,128)(2,1)}), bf16[4,120,1024]{2,1,0:T(8,128)(2,1)S(1)}, u32[]{:S(2)}, u32[]{:S(2)}) %all-to-all-start.8) | async-done | bytes 983072 | tf_op jit(solution)/shard_map/all_to_all | solution.py:580
  (536 shorter events, 379.4 us)
Async XLA Ops:
  9.6 37.7 %all-to-all-start = ((bf16[4,5,32,1024]{3,2,1,0:T(8,128)(2,1)}), bf16[4,5,32,1024]{3,2,1,0:T(8,128)(2,1)S(1)}, u32[]{:S(2)}, u32[]{:S(2)}) async-start(bf16[4,5,32,1024]{3,2,1,0:T(8,128)(2,1)} %broadcast_in_dim.32), calls=%async_computation | async-start | bytes 2621440 | tf_op jit(solution)/shard_map/all_to_all | solution.py:361
  72.3 35.4 %collective-permute-start.10 = (bf16[5,2,2,32,1024]{4,3,2,0,1:T(8,128)(2,1)}, bf16[5,2,2,32,1024]{4,3,2,0,1:T(8,128)(2,1)}, u32[]{:S(2)}, u32[]{:S(2)}) collective-permute-start(bf16[5,2,2,32,1024]{4,3,2,0,1:T(8,128)(2,1)} %pad_maximum_fusion.10), channel_id=1, source_target_pairs={{0,4},{4,0},{8,12},{12,8},{16,20},{20,16},{24,28},{28,24},{1,5},{5... | collective-permute-start | bytes 3932168 | tf_op jit(solution)/shard_map/ppermute | solution.py:281
  72.3 39.3 %collective-permute-start.11 = (bf16[5,2,2,32,1024]{4,3,2,1,0:T(8,128)(2,1)S(1)}, bf16[5,2,2,32,1024]{4,3,2,1,0:T(8,128)(2,1)}, u32[]{:S(2)}, u32[]{:S(2)}) collective-permute-start(bf16[5,2,2,32,1024]{4,3,2,1,0:T(8,128)(2,1)S(1)} %pad_maximum_fusion.11), channel_id=1, source_target_pairs={{0,4},{4,0},{8,12},{12,8},{16,20},{20,16},{24,28},{28,24},{1,5},{5... | collective-permute-start | bytes 3932168 | tf_op jit(solution)/shard_map/ppermute | solution.py:281
  74.1 41.4 %all-to-all-start.1 = ((bf16[4,2,88,1024]{3,2,1,0:T(8,128)(2,1)}), bf16[4,2,88,1024]{3,2,1,0:T(8,128)(2,1)S(1)}, u32[]{:S(2)}, u32[]{:S(2)}) async-start(bf16[4,2,88,1024]{3,2,1,0:T(8,128)(2,1)} %broadcast_in_dim.33), calls=%async_computation.1 | async-start | bytes 2883584 | tf_op jit(solution)/shard_map/all_to_all | solution.py:361
  117.2 30.0 %collective-permute-start.6 = (bf16[1,2,88,1024]{3,2,1,0:T(8,128)(2,1)}, bf16[1,2,88,1024]{3,2,1,0:T(8,128)(2,1)}, u32[]{:S(2)}, u32[]{:S(2)}) collective-permute-start(bf16[1,2,88,1024]{3,2,1,0:T(8,128)(2,1)} %get-tuple-element.297), channel_id=1, source_target_pairs={{0,8},{4,12},{8,0},{12,4},{16,24},{20,28},{24,16},{28,20},{1,9},{5... | collective-permute-start | bytes 1081352 | tf_op jit(solution)/shard_map/ppermute | solution.py:281
  117.7 31.7 %collective-permute-start.7 = (bf16[1,2,88,1024]{3,2,1,0:T(8,128)(2,1)}, bf16[1,2,88,1024]{3,2,1,0:T(8,128)(2,1)}, u32[]{:S(2)}, u32[]{:S(2)}) collective-permute-start(bf16[1,2,88,1024]{3,2,1,0:T(8,128)(2,1)} %get-tuple-element.296), channel_id=1, source_target_pairs={{0,16},{4,20},{8,24},{12,28},{16,0},{20,4},{24,8},{28,12},{1,17},{... | collective-permute-start | bytes 1081352 | tf_op jit(solution)/shard_map/ppermute | solution.py:281
  118.6 32.8 %collective-permute-start.8 = (bf16[1,2,88,1024]{3,2,1,0:T(8,128)(2,1)}, bf16[1,2,88,1024]{3,2,1,0:T(8,128)(2,1)}, u32[]{:S(2)}, u32[]{:S(2)}) collective-permute-start(bf16[1,2,88,1024]{3,2,1,0:T(8,128)(2,1)} %get-tuple-element.295), channel_id=1, source_target_pairs={{0,8},{4,12},{8,0},{12,4},{16,24},{20,28},{24,16},{28,20},{1,9},{5... | collective-permute-start | bytes 1081352 | tf_op jit(solution)/shard_map/ppermute | solution.py:281
  120.2 33.2 %collective-permute-start.9 = (bf16[1,2,88,1024]{3,2,1,0:T(8,128)(2,1)}, bf16[1,2,88,1024]{3,2,1,0:T(8,128)(2,1)}, u32[]{:S(2)}, u32[]{:S(2)}) collective-permute-start(bf16[1,2,88,1024]{3,2,1,0:T(8,128)(2,1)} %get-tuple-element.294), channel_id=1, source_target_pairs={{0,16},{4,20},{8,24},{12,28},{16,0},{20,4},{24,8},{28,12},{1,17},{... | collective-permute-start | bytes 1081352 | tf_op jit(solution)/shard_map/ppermute | solution.py:281
  156.3 46.1 %collective-permute-start.16 = (bf16[1,2,2,88,1024]{4,3,2,0,1:T(8,128)(2,1)}, bf16[1,2,2,88,1024]{4,3,2,0,1:T(8,128)(2,1)}, u32[]{:S(2)}, u32[]{:S(2)}) collective-permute-start(bf16[1,2,2,88,1024]{4,3,2,0,1:T(8,128)(2,1)} %pad_maximum_fusion.16), channel_id=1, source_target_pairs={{0,4},{4,0},{8,12},{12,8},{16,20},{20,16},{24,28},{28,24},{1,5},{5... | collective-permute-start | bytes 2162696 | tf_op jit(solution)/shard_map/ppermute | solution.py:281
  156.7 31.7 %collective-permute-start.14 = (bf16[1,2,2,88,1024]{4,3,2,0,1:T(8,128)(2,1)}, bf16[1,2,2,88,1024]{4,3,2,0,1:T(8,128)(2,1)}, u32[]{:S(2)}, u32[]{:S(2)}) collective-permute-start(bf16[1,2,2,88,1024]{4,3,2,0,1:T(8,128)(2,1)} %pad_maximum_fusion.18), channel_id=1, source_target_pairs={{0,16},{4,20},{8,24},{12,28},{16,0},{20,4},{24,8},{28,12},{1,17},{... | collective-permute-start | bytes 2162696 | tf_op jit(solution)/shard_map/ppermute | solution.py:281
  157.7 32.9 %collective-permute-start.15 = (bf16[1,2,2,88,1024]{4,3,2,1,0:T(8,128)(2,1)}, bf16[1,2,2,88,1024]{4,3,2,1,0:T(8,128)(2,1)}, u32[]{:S(2)}, u32[]{:S(2)}) collective-permute-start(bf16[1,2,2,88,1024]{4,3,2,1,0:T(8,128)(2,1)} %pad_maximum_fusion.19), channel_id=1, source_target_pairs={{0,8},{4,12},{8,0},{12,4},{16,24},{20,28},{24,16},{28,20},{1,9},{5... | collective-permute-start | bytes 2162696 | tf_op jit(solution)/shard_map/ppermute | solution.py:281
  160.2 30.4 %all-to-all-start.3 = ((bf16[4,1,88,1024]{3,2,1,0:T(8,128)(2,1)}), bf16[4,1,88,1024]{3,2,1,0:T(8,128)(2,1)}, u32[]{:S(2)}, u32[]{:S(2)}) async-start(bf16[4,1,88,1024]{3,2,1,0:T(8,128)(2,1)} %broadcast_in_dim.38), calls=%async_computation.3 | async-start | bytes 1441792 | tf_op jit(solution)/shard_map/all_to_all | solution.py:361
  195.2 43.8 %all-to-all-start.4 = ((bf16[4,120,1024]{2,1,0:T(8,128)(2,1)}), bf16[4,120,1024]{2,1,0:T(8,128)(2,1)S(1)}, u32[]{:S(2)}, u32[]{:S(2)}) async-start(bf16[4,120,1024]{2,1,0:T(8,128)(2,1)} %pad_maximum_fusion.13), calls=%async_computation.4 | async-start | bytes 1966080 | tf_op jit(solution)/shard_map/all_to_all | solution.py:580
  198.8 307.6 %reduce-scatter.2.cloned.1.call-start = ((), (), s32[]{:S(2)}) async-start(), calls=%async_computation.10 | async-start | bytes 3604480 | tf_op jit(solution)/shard_map/reduce_scatter | solution.py:657
  210.0 30.0 %collective-permute-start.27 = (bf16[1,2,2,88,1024]{4,3,2,0,1:T(8,128)(2,1)}, bf16[1,2,2,88,1024]{4,3,2,0,1:T(8,128)(2,1)}, u32[]{:S(2)}, u32[]{:S(2)}) collective-permute-start(bf16[1,2,2,88,1024]{4,3,2,0,1:T(8,128)(2,1)} %pad_maximum_fusion.20), channel_id=1, source_target_pairs={{0,4},{4,0},{8,12},{12,8},{16,20},{20,16},{24,28},{28,24},{1,5},{5... | collective-permute-start | bytes 2162696 | tf_op jit(solution)/shard_map/ppermute | solution.py:281
  240.0 29.6 %collective-permute-start.32 = (bf16[1,2,2,352,1024]{4,3,2,1,0:T(8,128)(2,1)}, bf16[1,2,2,352,1024]{4,3,2,1,0:T(8,128)(2,1)}, u32[]{:S(2)}, u32[]{:S(2)}) collective-permute-start(bf16[1,2,2,352,1024]{4,3,2,1,0:T(8,128)(2,1)} %bitcast.430), channel_id=1, source_target_pairs={{0,4},{4,0},{8,12},{12,8},{16,20},{20,16},{24,28},{28,24},{1,5},{5... | collective-permute-start | bytes 8650760 | tf_op jit(solution)/shard_map/ppermute | solution.py:281
  355.7 41.1 %collective-permute-start.46 = (bf16[4,2,2,128,1024]{4,3,2,1,0:T(8,128)(2,1)}, bf16[4,2,2,128,1024]{4,3,2,1,0:T(8,128)(2,1)}, u32[]{:S(2)}, u32[]{:S(2)}) collective-permute-start(bf16[4,2,2,128,1024]{4,3,2,1,0:T(8,128)(2,1)} %get-tuple-element.211), channel_id=1, source_target_pairs={{0,4},{4,0},{8,12},{12,8},{16,20},{20,16},{24,28},{28,24},{1,5},{5... | collective-permute-start | bytes 12582920 | tf_op jit(solution)/shard_map/ppermute | solution.py:281
  358.3 32.2 %collective-permute-start.39 = (bf16[1,2,176,1024]{3,2,1,0:T(8,128)(2,1)}, bf16[1,2,176,1024]{3,2,1,0:T(8,128)(2,1)}, u32[]{:S(2)}, u32[]{:S(2)}) collective-permute-start(bf16[1,2,176,1024]{3,2,1,0:T(8,128)(2,1)} %fusion.65), channel_id=1, source_target_pairs={{0,8},{4,12},{8,0},{12,4},{16,24},{20,28},{24,16},{28,20},{1,9},{5... | collective-permute-start | bytes 2162696 | tf_op jit(solution)/shard_map/ppermute | solution.py:281
  358.8 33.2 %collective-permute-start.40 = (bf16[1,2,176,1024]{3,2,1,0:T(8,128)(2,1)}, bf16[1,2,176,1024]{3,2,1,0:T(8,128)(2,1)}, u32[]{:S(2)}, u32[]{:S(2)}) collective-permute-start(bf16[1,2,176,1024]{3,2,1,0:T(8,128)(2,1)} %fusion.66), channel_id=1, source_target_pairs={{0,16},{4,20},{8,24},{12,28},{16,0},{20,4},{24,8},{28,12},{1,17},{... | collective-permute-start | bytes 2162696 | tf_op jit(solution)/shard_map/ppermute | solution.py:281
  479.0 38.8 %all-to-all-start.5 = ((bf16[4,128,1024]{2,1,0:T(8,128)(2,1)}), bf16[4,128,1024]{2,1,0:T(8,128)(2,1)S(1)}, u32[]{:S(2)}, u32[]{:S(2)}) async-start(bf16[4,128,1024]{2,1,0:T(8,128)(2,1)} %pad_maximum_fusion.12), calls=%async_computation.6 | async-start | bytes 2097152 | tf_op jit(solution)/shard_map/all_to_all | solution.py:663
  517.8 51.4 %all-to-all-start.7 = ((f32[32,3,32]{2,1,0:T(4,128)}), f32[32,3,32]{2,1,0:T(4,128)S(1)}, u32[]{:S(2)}, u32[]{:S(2)}) async-start(f32[32,3,32]{2,1,0:T(4,128)} %maximum_bitcast_fusion.6), calls=%async_computation.8 | async-start | bytes 131072 | tf_op jit(solution)/shard_map/all_to_all | solution.py:430
  532.7 29.3 %collective-permute-start.60 = (bf16[2,352,1024]{2,1,0:T(8,128)(2,1)S(1)}, bf16[2,352,1024]{2,1,0:T(8,128)(2,1)S(1)}, u32[]{:S(2)}, u32[]{:S(2)}) collective-permute-start(bf16[2,352,1024]{2,1,0:T(8,128)(2,1)S(1)} %pad_maximum_fusion.7), channel_id=1, source_target_pairs={{0,16},{8,24},{16,0},{24,8},{1,17},{9,25},{17,1},{25,9},{2,18},{10... | collective-permute-start | bytes 4325384 | tf_op jit(solution)/shard_map/ppermute | solution.py:534
  569.8 62.8 %all-to-all-start.6 = ((bf16[4,120,1024]{2,1,0:T(8,128)(2,1)}), bf16[4,120,1024]{2,1,0:T(8,128)(2,1)S(1)}, u32[]{:S(2)}, u32[]{:S(2)}) async-start(bf16[4,120,1024]{2,1,0:T(8,128)(2,1)} %pad_maximum_fusion.14), calls=%async_computation.7 | async-start | bytes 1966080 | tf_op jit(solution)/shard_map/all_to_all | solution.py:580
  633.6 29.7 %all-to-all-start.8 = ((bf16[4,120,1024]{2,1,0:T(8,128)(2,1)}), bf16[4,120,1024]{2,1,0:T(8,128)(2,1)S(1)}, u32[]{:S(2)}, u32[]{:S(2)}) async-start(bf16[4,120,1024]{2,1,0:T(8,128)(2,1)} %pad_maximum_fusion.15), calls=%async_computation.9 | async-start | bytes 1966080 | tf_op jit(solution)/shard_map/all_to_all | solution.py:580
  (164 other events, 1701.0 us)
Sparse Core Ops, SparseCore 0:
  440.1 66.1 reduce-scatter.1

commit v9 on v8

--- a/solution.py
+++ b/solution.py
@@ -208,11 +208,15 @@
         rms_back(attended, out_scale, grad_normal * gain_full[2])
         .astype(B16)
     )
-    down_in, proj_in, grad_attended = tied([down_in, proj_in], grad_attended)
+    down_in, one_in, two_in, proj_in, grad_attended = tied([down_in, one_in, two_in, proj_in], grad_attended)
     down.accept(down_in)
+    one.accept(one_in)
+    two.accept(two_in)
     proj.accept(proj_in)
-    proj_out, grad_attended = tied([proj.payloads()], grad_attended)
-    proj_in = proj.swap(proj_out)
+    one_out, two_out, proj_out, grad_attended = tied(
+        [one.payloads(), two.payloads(), proj.payloads()], grad_attended
+    )
+    one_in, two_in, proj_in = one.swap(one_out), two.swap(two_out), proj.swap(proj_out)
     grad_attended = grad_attended.reshape(length, head_count, head_size)
     query_heads = query_act.reshape(length, head_count, head_size)
     key_heads = key_act.reshape(length, head_count, head_size)
@@ -239,18 +243,19 @@
         ],
         axis=1,
     ).astype(B16)
+    one_in, two_in, proj_in, grad_mixed = tied([one_in, two_in, proj_in], grad_mixed)
+    one.accept(one_in)
+    two.accept(two_in)
+    proj.accept(proj_in)
+    proj_out, grad_mixed = tied([proj.payloads()], grad_mixed)
+    proj_in = proj.swap(proj_out)
     inner = Halving(weight_grad(grad_mixed, normed).reshape(4, model_width, model_width))
     inner_out, grad_mixed = tied([inner.payloads()], grad_mixed)
     inner_in = inner.swap(inner_out)
-    one_in, two_in, proj_in, inner_in, grad_mixed = tied([one_in, two_in, proj_in, inner_in], grad_mixed)
-    one.accept(one_in)
-    two.accept(two_in)
+    proj_in, inner_in, grad_mixed = tied([proj_in, inner_in], grad_mixed)
     proj.accept(proj_in)
     inner.accept(inner_in)
-    one_out, two_out, proj_out, inner_out, grad_mixed = tied(
-        [one.payloads(), two.payloads(), proj.payloads(), inner.payloads()], grad_mixed
-    )
-    one_in, two_in, proj_in = one.swap(one_out), two.swap(two_out), proj.swap(proj_out)
+    inner_out, grad_mixed = tied([inner.payloads()], grad_mixed)
     inner_in = inner.swap(inner_out)
     grad_normed = jnp.dot(
         jnp.pad(grad_mixed, ((0, 0), (0, model_width))),
@@ -260,10 +265,6 @@
     gain_one = jnp.sum(grad_normed * inputs * first_scale, axis=0)
     grad_inputs = grad_middle + rms_back(inputs, first_scale, grad_normed * gain_full[0])
     grad_gain = jnp.stack([gain_one, gain_two, gain_three])
-    one_in, two_in, proj_in, grad_inputs = tied([one_in, two_in, proj_in], grad_inputs)
-    one.accept(one_in)
-    two.accept(two_in)
-    proj.accept(proj_in)
     inner.accept(inner_in)
     return (grad_inputs, (one, two, down, proj, inner), grad_gain, ffn_down, moments)
 

time: 684 us -> 677 us (0.990)
  waiting for transfers between devices: 187 us -> 172 us
  other arithmetic: 102 us -> 109 us
  transfers between devices with their start and end apart: 79 -> 79, of which waited for: 29 -> 23; matrix products, arithmetic and copies ran while one was open for 33% -> 38% of each run, Pallas kernels for 7% -> 7%
where the time goes in v9:
time: 677 us; the launch traced here: 667 us
  waiting for transfers between devices  172 us (25%)
  matrix products  130 us (19%)
  other arithmetic  109 us (16%)
  starting transfers between devices  109 us (16%)
  local copies, waits for them, and re-layouts  82.7 us (12%)
  Pallas kernels  48.1 us (7%)
  between operations  16.7 us (2%)
    ppermute x57, waiting for transfers between devices, swap_bit(): return lax.ppermute(value, 'dp', [(i, i ^ 1 << bit) for i in range(count)])  93.7 us
    pallas_call x1, Pallas kernels, gram_orthogonalize(): pl.pallas_call(polynomial_kernel, out_shape=jax.ShapeDtypeStruct(rows.sha...  48.1 us
    ppermute x57, starting transfers between devices, swap_bit(): return lax.ppermute(value, 'dp', [(i, i ^ 1 << bit) for i in range(count)])  41.2 us
    all_to_all x3, waiting for transfers between devices, line_gather(): return jnp.swapaxes(lax.all_to_all(copies, 'fsdp', 0, 0, tiled=True), 0, 1)  31.1 us
    dynamic_update_slice x16, local copies, waits for them, and re-layouts, natural(): whole = lax.dynamic_update_slice(whole, block, where)  29.3 us
    dot_general x7, matrix products, weight_grad(): lax.dot_general(features, series, TOKENS_OUT, preferred_element_type=F32)  25.2 us
    convert_element_type x17, other arithmetic, payloads(): sum((self.choose(t, dims, bit, True).astype(F32) for t, dims in part))  20.2 us
    ppermute x8, starting transfers between devices, swap_core(): lax.ppermute(value, 'dp', [(i, i ^ 1 << bit) for i in range(count) if i &...  16.7 us
  transfers between devices with their start and end apart: 79, of which 23 were waited for; matrix products, arithmetic and copies ran while one was open for 38% of the time, Pallas kernels for 7%

profile of v9, /device:TPU:0, one launch (start us, length us, event | category | flops | bytes accessed | tf_op | source)
XLA Modules:
  0.0 667.3 jit_solution(7311233751398910921)
XLA Ops:
  9.6 6.3 all-to-all-start
  16.3 31.0 %all-to-all-done = bf16[4,5,32,1024]{3,2,1,0:T(8,128)(2,1)S(1)} async-done(((bf16[4,5,32,1024]{3,2,1,0:T(8,128)(2,1)}), bf16[4,5,32,1024]{3,2,1,0:T(8,128)(2,1)S(1)}, u32[]{:S(2)}, u32[]{:S(2)}) %all-to-all-start) | async-done | bytes 1310752 | tf_op jit(solution)/shard_map/all_to_all | solution.py:362
  59.8 5.2 collective-permute-done
  77.6 5.2 broadcast_in_dim.35
  88.6 10.1 %collective-permute-done.2 = bf16[5,2,2,32,1024]{4,3,2,0,1:T(8,128)(2,1)} collective-permute-done((bf16[5,2,2,32,1024]{4,3,2,0,1:T(8,128)(2,1)}, bf16[5,2,2,32,1024]{4,3,2,0,1:T(8,128)(2,1)}, u32[]{:S(2)}, u32[]{:S(2)}) %collective-permute-start.2) | collective-permute-done | bytes 1310752 | tf_op jit(solution)/shard_map/ppermute | solution.py:282
  132.3 8.4 %fusion.92 = f32[512,5120]{1,0:T(8,128)S(1)} fusion(bf16[5120,1024]{1,0:T(8,128)(2,1)} %bitcast.26, bf16[512,1024]{1,0:T(8,128)(2,1)S(1)} %copy-done.26, f32[1024]{0:T(1024)S(1)} %mul.335, f32[512]{0:T(512)S(1)} %get-tuple-element.315), kind=kOutput, calls=%fused_computation.231 | convolution fusion | flops 5370806272 | bytes 22026240 | tf_op jit(solution)/shard_map/dot_general | solution.py:60
  166.0 6.5 multiply_convert_fusion.1
  182.2 6.2 collective-permute-done.14
  251.5 9.8 %multiply_convert_fusion.2 = (bf16[512,2816]{1,0:T(8,128)(2,1)}, bf16[512,2816]{1,0:T(8,128)(2,1)}) fusion(f32[512,2816]{1,0:T(8,128)} %get-tuple-element.325, f32[512,2816]{1,0:T(8,128)S(1)} %bitcast.373, bf16[512,1024]{1,0:T(8,128)(2,1)} %param.14, bf16[2816,1024]{1,0:T(8,128)(2,1)S(1)} %bitcast.366), kind=kOutput, calls=%fused_computation.7 | convolution fusion | flops 2958557184 | bytes 24117248 | tf_op jit(solution)/shard_map/dot_general | solution.py:174
  282.1 5.7 multiply_reduce_fusion.1
  314.8 11.0 %collective-permute-done.39 = bf16[1,2,176,1024]{3,2,1,0:T(8,128)(2,1)S(1)} collective-permute-done((bf16[1,2,176,1024]{3,2,1,0:T(8,128)(2,1)S(1)}, bf16[1,2,176,1024]{3,2,1,0:T(8,128)(2,1)S(1)}, u32[]{:S(2)}, u32[]{:S(2)}) %collective-permute-start.39) | collective-permute-done | bytes 720928 | tf_op jit(solution)/shard_map/ppermute | solution.py:282
  325.8 13.0 %collective-permute-done.41 = bf16[1,2,176,1024]{3,2,1,0:T(8,128)(2,1)S(1)} collective-permute-done((bf16[1,2,176,1024]{3,2,1,0:T(8,128)(2,1)S(1)}, bf16[1,2,176,1024]{3,2,1,0:T(8,128)(2,1)S(1)}, u32[]{:S(2)}, u32[]{:S(2)}) %collective-permute-start.41) | collective-permute-done | bytes 720928 | tf_op jit(solution)/shard_map/ppermute | solution.py:282
  348.9 5.7 multiply_convert_fusion
  372.9 10.3 %collective-permute-done.48 = bf16[1,2,64,1024]{3,2,1,0:T(8,128)(2,1)} collective-permute-done((bf16[1,2,64,1024]{3,2,1,0:T(8,128)(2,1)}, bf16[1,2,64,1024]{3,2,1,0:T(8,128)(2,1)}, u32[]{:S(2)}, u32[]{:S(2)}) %collective-permute-start.48) | collective-permute-done | bytes 262176 | tf_op jit(solution)/shard_map/ppermute | solution.py:282
  384.4 5.2 collective-permute-done.49
  425.9 21.9 %collective-permute-done.58 = bf16[4,2,64,1024]{3,2,0,1:T(8,128)(2,1)S(1)} collective-permute-done((bf16[4,2,64,1024]{3,2,0,1:T(8,128)(2,1)S(1)}, bf16[4,2,64,1024]{3,2,0,1:T(8,128)(2,1)S(1)}, u32[]{:S(2)}, u32[]{:S(2)}) %collective-permute-start.58) | collective-permute-done | bytes 1048608 | tf_op jit(solution)/shard_map/ppermute | solution.py:282
  455.5 16.7 %reduce-scatter.2.cloned.1.call-done = bf16[1,352,1024]{2,1,0:T(8,128)(2,1)} async-done(((bf16[4,352,1024]{2,1,0:T(8,128)(2,1)}), bf16[1,352,1024]{2,1,0:T(8,128)(2,1)}) %reduce-scatter.2.cloned.1.call-update) | async-done | bytes 720912 | tf_op jit(solution)/shard_map/reduce_scatter | solution.py:658
  492.6 11.4 %fusion.19 = (f32[1024]{0:T(1024)}, f32[512]{0:T(512)}, f32[512,1024]{1,0:T(8,128)}) fusion(bf16[512,1024]{1,0:T(8,128)(2,1)S(1)} %copy-done.28, f32[512]{0:T(512)S(1)} %copy-done.100, f32[1024]{0:T(1024)S(1)} %copy-done.95, bf16[5120,1024]{1,0:T(8,128)(2,1)} %bitcast.26, bf16[512,4096]{1,0:T(8,128)(2,1)} %copy-done.35), kind=kOutput, calls=%fused_computation.53 | convolution fusion | flops 5372377600 | bytes 17838080 | tf_op jit(solution)/shard_map/dot_general | solution.py:260
  532.3 8.2 %collective-permute-done.61 = bf16[2,352,1024]{2,1,0:T(8,128)(2,1)S(1)} collective-permute-done((bf16[2,352,1024]{2,1,0:T(8,128)(2,1)S(1)}, bf16[2,352,1024]{2,1,0:T(8,128)(2,1)S(1)}, u32[]{:S(2)}, u32[]{:S(2)}) %collective-permute-start.61) | collective-permute-done | bytes 1441824 | tf_op jit(solution)/shard_map/ppermute | solution.py:535
  544.0 7.8 %collective-permute-done.60 = bf16[2,352,1024]{2,1,0:T(8,128)(2,1)S(1)} collective-permute-done((bf16[2,352,1024]{2,1,0:T(8,128)(2,1)S(1)}, bf16[2,352,1024]{2,1,0:T(8,128)(2,1)S(1)}, u32[]{:S(2)}, u32[]{:S(2)}) %collective-permute-start.60) | collective-permute-done | bytes 1441824 | tf_op jit(solution)/shard_map/ppermute | solution.py:535
  563.9 48.1 %shard_map.218 = bf16[704,1024]{1,0:T(8,128)(2,1)S(1)} custom-call(f32[1024,1024]{1,0:T(8,128)} %fusion.2.gram_ref, bf16[704,1024]{1,0:T(8,128)(2,1)S(1)} %pad_maximum_fusion.9.rows_ref), custom_call_target="tpu_custom_call" | custom-call | flops 32212254720 | bytes 8388608 | tf_op jit(solution)/shard_map/pallas_call | solution.py:514
  612.1 9.1 %collective-permute-start.67 = (bf16[352,1024]{1,0:T(8,128)(2,1)S(1)}, bf16[352,1024]{1,0:T(8,128)(2,1)S(1)}, u32[]{:S(2)}, u32[]{:S(2)}) collective-permute-start(bf16[352,1024]{1,0:T(8,128)(2,1)S(1)} %slice.425), channel_id=1, source_target_pairs={{0,4},{8,12},{16,20},{24,28},{1,5},{9,13},{17,21},{25,29},{2,6},{1... | collective-permute-start | bytes 2162696 | tf_op jit(solution)/shard_map/ppermute | solution.py:528
  631.9 7.8 %add_convert_fusion.2 = bf16[512,1024]{1,0:T(8,128)(2,1)} fusion(f32[512,1024]{1,0:T(8,128)S(1)} %copy-done.11, bf16[512,2816]{1,0:T(8,128)(2,1)} %copy-done.52, bf16[2816,1024]{1,0:T(8,128)(2,1)} %bitcast.367), kind=kOutput, calls=%fused_computation.76 | convolution fusion | flops 2953838592 | bytes 11796480 | tf_op jit(solution)/shard_map/dot_general | solution.py:649
  647.2 9.2 %all-to-all-done.8 = bf16[4,120,1024]{2,1,0:T(8,128)(2,1)S(1)} async-done(((bf16[4,120,1024]{2,1,0:T(8,128)(2,1)}), bf16[4,120,1024]{2,1,0:T(8,128)(2,1)S(1)}, u32[]{:S(2)}, u32[]{:S(2)}) %all-to-all-start.8) | async-done | bytes 983072 | tf_op jit(solution)/shard_map/all_to_all | solution.py:581
  (557 shorter events, 370.7 us)
Async XLA Ops:
  9.6 37.7 %all-to-all-start = ((bf16[4,5,32,1024]{3,2,1,0:T(8,128)(2,1)}), bf16[4,5,32,1024]{3,2,1,0:T(8,128)(2,1)S(1)}, u32[]{:S(2)}, u32[]{:S(2)}) async-start(bf16[4,5,32,1024]{3,2,1,0:T(8,128)(2,1)} %broadcast_in_dim.32), calls=%async_computation | async-start | bytes 2621440 | tf_op jit(solution)/shard_map/all_to_all | solution.py:362
  69.8 28.9 %collective-permute-start.2 = (bf16[5,2,2,32,1024]{4,3,2,0,1:T(8,128)(2,1)}, bf16[5,2,2,32,1024]{4,3,2,0,1:T(8,128)(2,1)}, u32[]{:S(2)}, u32[]{:S(2)}) collective-permute-start(bf16[5,2,2,32,1024]{4,3,2,0,1:T(8,128)(2,1)} %pad_maximum_fusion.10), channel_id=1, source_target_pairs={{0,16},{4,20},{8,24},{12,28},{16,0},{20,4},{24,8},{28,12},{1,17},{... | collective-permute-start | bytes 3932168 | tf_op jit(solution)/shard_map/ppermute | solution.py:282
  72.3 35.4 %collective-permute-start.10 = (bf16[5,2,2,32,1024]{4,3,2,0,1:T(8,128)(2,1)}, bf16[5,2,2,32,1024]{4,3,2,0,1:T(8,128)(2,1)}, u32[]{:S(2)}, u32[]{:S(2)}) collective-permute-start(bf16[5,2,2,32,1024]{4,3,2,0,1:T(8,128)(2,1)} %pad_maximum_fusion.10), channel_id=1, source_target_pairs={{0,4},{4,0},{8,12},{12,8},{16,20},{20,16},{24,28},{28,24},{1,5},{5... | collective-permute-start | bytes 3932168 | tf_op jit(solution)/shard_map/ppermute | solution.py:282
  72.3 39.3 %collective-permute-start.11 = (bf16[5,2,2,32,1024]{4,3,2,1,0:T(8,128)(2,1)S(1)}, bf16[5,2,2,32,1024]{4,3,2,1,0:T(8,128)(2,1)}, u32[]{:S(2)}, u32[]{:S(2)}) collective-permute-start(bf16[5,2,2,32,1024]{4,3,2,1,0:T(8,128)(2,1)S(1)} %pad_maximum_fusion.11), channel_id=1, source_target_pairs={{0,4},{4,0},{8,12},{12,8},{16,20},{20,16},{24,28},{28,24},{1,5},{5... | collective-permute-start | bytes 3932168 | tf_op jit(solution)/shard_map/ppermute | solution.py:282
  74.1 41.4 %all-to-all-start.1 = ((bf16[4,2,88,1024]{3,2,1,0:T(8,128)(2,1)}), bf16[4,2,88,1024]{3,2,1,0:T(8,128)(2,1)S(1)}, u32[]{:S(2)}, u32[]{:S(2)}) async-start(bf16[4,2,88,1024]{3,2,1,0:T(8,128)(2,1)} %broadcast_in_dim.33), calls=%async_computation.1 | async-start | bytes 2883584 | tf_op jit(solution)/shard_map/all_to_all | solution.py:362
  117.2 30.0 %collective-permute-start.6 = (bf16[1,2,88,1024]{3,2,1,0:T(8,128)(2,1)}, bf16[1,2,88,1024]{3,2,1,0:T(8,128)(2,1)}, u32[]{:S(2)}, u32[]{:S(2)}) collective-permute-start(bf16[1,2,88,1024]{3,2,1,0:T(8,128)(2,1)} %get-tuple-element.301), channel_id=1, source_target_pairs={{0,8},{4,12},{8,0},{12,4},{16,24},{20,28},{24,16},{28,20},{1,9},{5... | collective-permute-start | bytes 1081352 | tf_op jit(solution)/shard_map/ppermute | solution.py:282
  117.6 31.7 %collective-permute-start.7 = (bf16[1,2,88,1024]{3,2,1,0:T(8,128)(2,1)}, bf16[1,2,88,1024]{3,2,1,0:T(8,128)(2,1)}, u32[]{:S(2)}, u32[]{:S(2)}) collective-permute-start(bf16[1,2,88,1024]{3,2,1,0:T(8,128)(2,1)} %get-tuple-element.300), channel_id=1, source_target_pairs={{0,16},{4,20},{8,24},{12,28},{16,0},{20,4},{24,8},{28,12},{1,17},{... | collective-permute-start | bytes 1081352 | tf_op jit(solution)/shard_map/ppermute | solution.py:282
  118.6 32.7 %collective-permute-start.8 = (bf16[1,2,88,1024]{3,2,1,0:T(8,128)(2,1)}, bf16[1,2,88,1024]{3,2,1,0:T(8,128)(2,1)}, u32[]{:S(2)}, u32[]{:S(2)}) collective-permute-start(bf16[1,2,88,1024]{3,2,1,0:T(8,128)(2,1)} %get-tuple-element.299), channel_id=1, source_target_pairs={{0,8},{4,12},{8,0},{12,4},{16,24},{20,28},{24,16},{28,20},{1,9},{5... | collective-permute-start | bytes 1081352 | tf_op jit(solution)/shard_map/ppermute | solution.py:282
  120.3 33.0 %collective-permute-start.9 = (bf16[1,2,88,1024]{3,2,1,0:T(8,128)(2,1)}, bf16[1,2,88,1024]{3,2,1,0:T(8,128)(2,1)}, u32[]{:S(2)}, u32[]{:S(2)}) collective-permute-start(bf16[1,2,88,1024]{3,2,1,0:T(8,128)(2,1)} %get-tuple-element.298), channel_id=1, source_target_pairs={{0,16},{4,20},{8,24},{12,28},{16,0},{20,4},{24,8},{28,12},{1,17},{... | collective-permute-start | bytes 1081352 | tf_op jit(solution)/shard_map/ppermute | solution.py:282
  156.3 46.1 %collective-permute-start.16 = (bf16[1,2,2,88,1024]{4,3,2,0,1:T(8,128)(2,1)}, bf16[1,2,2,88,1024]{4,3,2,0,1:T(8,128)(2,1)}, u32[]{:S(2)}, u32[]{:S(2)}) collective-permute-start(bf16[1,2,2,88,1024]{4,3,2,0,1:T(8,128)(2,1)} %pad_maximum_fusion.16), channel_id=1, source_target_pairs={{0,4},{4,0},{8,12},{12,8},{16,20},{20,16},{24,28},{28,24},{1,5},{5... | collective-permute-start | bytes 2162696 | tf_op jit(solution)/shard_map/ppermute | solution.py:282
  156.7 31.7 %collective-permute-start.14 = (bf16[1,2,2,88,1024]{4,3,2,0,1:T(8,128)(2,1)}, bf16[1,2,2,88,1024]{4,3,2,0,1:T(8,128)(2,1)}, u32[]{:S(2)}, u32[]{:S(2)}) collective-permute-start(bf16[1,2,2,88,1024]{4,3,2,0,1:T(8,128)(2,1)} %pad_maximum_fusion.18), channel_id=1, source_target_pairs={{0,16},{4,20},{8,24},{12,28},{16,0},{20,4},{24,8},{28,12},{1,17},{... | collective-permute-start | bytes 2162696 | tf_op jit(solution)/shard_map/ppermute | solution.py:282
  157.7 32.9 %collective-permute-start.15 = (bf16[1,2,2,88,1024]{4,3,2,1,0:T(8,128)(2,1)}, bf16[1,2,2,88,1024]{4,3,2,1,0:T(8,128)(2,1)}, u32[]{:S(2)}, u32[]{:S(2)}) collective-permute-start(bf16[1,2,2,88,1024]{4,3,2,1,0:T(8,128)(2,1)} %pad_maximum_fusion.19), channel_id=1, source_target_pairs={{0,8},{4,12},{8,0},{12,4},{16,24},{20,28},{24,16},{28,20},{1,9},{5... | collective-permute-start | bytes 2162696 | tf_op jit(solution)/shard_map/ppermute | solution.py:282
  160.2 30.4 %all-to-all-start.3 = ((bf16[4,1,88,1024]{3,2,1,0:T(8,128)(2,1)}), bf16[4,1,88,1024]{3,2,1,0:T(8,128)(2,1)}, u32[]{:S(2)}, u32[]{:S(2)}) async-start(bf16[4,1,88,1024]{3,2,1,0:T(8,128)(2,1)} %broadcast_in_dim.38), calls=%async_computation.3 | async-start | bytes 1441792 | tf_op jit(solution)/shard_map/all_to_all | solution.py:362
  195.3 43.7 %all-to-all-start.4 = ((bf16[4,120,1024]{2,1,0:T(8,128)(2,1)}), bf16[4,120,1024]{2,1,0:T(8,128)(2,1)S(1)}, u32[]{:S(2)}, u32[]{:S(2)}) async-start(bf16[4,120,1024]{2,1,0:T(8,128)(2,1)} %pad_maximum_fusion.13), calls=%async_computation.4 | async-start | bytes 1966080 | tf_op jit(solution)/shard_map/all_to_all | solution.py:581
  198.8 273.4 %reduce-scatter.2.cloned.1.call-start = ((), (), s32[]{:S(2)}) async-start(), calls=%async_computation.10 | async-start | bytes 3604480 | tf_op jit(solution)/shard_map/reduce_scatter | solution.py:658
  210.0 30.0 %collective-permute-start.27 = (bf16[1,2,2,88,1024]{4,3,2,0,1:T(8,128)(2,1)}, bf16[1,2,2,88,1024]{4,3,2,0,1:T(8,128)(2,1)}, u32[]{:S(2)}, u32[]{:S(2)}) collective-permute-start(bf16[1,2,2,88,1024]{4,3,2,0,1:T(8,128)(2,1)} %pad_maximum_fusion.20), channel_id=1, source_target_pairs={{0,4},{4,0},{8,12},{12,8},{16,20},{20,16},{24,28},{28,24},{1,5},{5... | collective-permute-start | bytes 2162696 | tf_op jit(solution)/shard_map/ppermute | solution.py:282
  240.0 29.7 %collective-permute-start.32 = (bf16[1,2,2,352,1024]{4,3,2,1,0:T(8,128)(2,1)}, bf16[1,2,2,352,1024]{4,3,2,1,0:T(8,128)(2,1)}, u32[]{:S(2)}, u32[]{:S(2)}) collective-permute-start(bf16[1,2,2,352,1024]{4,3,2,1,0:T(8,128)(2,1)} %bitcast.429), channel_id=1, source_target_pairs={{0,4},{4,0},{8,12},{12,8},{16,20},{20,16},{24,28},{28,24},{1,5},{5... | collective-permute-start | bytes 8650760 | tf_op jit(solution)/shard_map/ppermute | solution.py:282
  303.7 35.1 %collective-permute-start.43 = (bf16[1,2,2,128,1024]{4,3,2,1,0:T(8,128)(2,1)S(1)}, bf16[1,2,2,128,1024]{4,3,2,1,0:T(8,128)(2,1)S(1)}, u32[]{:S(2)}, u32[]{:S(2)}) collective-permute-start(bf16[1,2,2,128,1024]{4,3,2,1,0:T(8,128)(2,1)S(1)} %get-tuple-element.205), channel_id=1, source_target_pairs={{0,4},{4,0},{8,12},{12,8},{16,20},{20,16},{24,28},{28,24},{1,5},{5... | collective-permute-start | bytes 3145736 | tf_op jit(solution)/shard_map/ppermute | solution.py:282
  360.6 29.0 %collective-permute-start.44 = (bf16[1,176,1024]{2,1,0:T(8,128)(2,1)}, bf16[1,176,1024]{2,1,0:T(8,128)(2,1)}, u32[]{:S(2)}, u32[]{:S(2)}) collective-permute-start(bf16[1,176,1024]{2,1,0:T(8,128)(2,1)} %get-tuple-element.213), channel_id=1, source_target_pairs={{0,16},{4,20},{8,24},{12,28},{16,0},{20,4},{24,8},{28,12},{1,17},{... | collective-permute-start | bytes 1081352 | tf_op jit(solution)/shard_map/ppermute | solution.py:282
  479.6 29.8 %all-to-all-start.5 = ((bf16[4,128,1024]{2,1,0:T(8,128)(2,1)}), bf16[4,128,1024]{2,1,0:T(8,128)(2,1)S(1)}, u32[]{:S(2)}, u32[]{:S(2)}) async-start(bf16[4,128,1024]{2,1,0:T(8,128)(2,1)} %pad_maximum_fusion.12), calls=%async_computation.6 | async-start | bytes 2097152 | tf_op jit(solution)/shard_map/all_to_all | solution.py:664
  509.4 49.6 %all-to-all-start.7 = ((f32[32,3,32]{2,1,0:T(4,128)}), f32[32,3,32]{2,1,0:T(4,128)}, u32[]{:S(2)}, u32[]{:S(2)}) async-start(f32[32,3,32]{2,1,0:T(4,128)} %maximum_bitcast_fusion.6), calls=%async_computation.8 | async-start | bytes 131072 | tf_op jit(solution)/shard_map/all_to_all | solution.py:431
  522.6 29.3 %collective-permute-start.60 = (bf16[2,352,1024]{2,1,0:T(8,128)(2,1)S(1)}, bf16[2,352,1024]{2,1,0:T(8,128)(2,1)S(1)}, u32[]{:S(2)}, u32[]{:S(2)}) collective-permute-start(bf16[2,352,1024]{2,1,0:T(8,128)(2,1)S(1)} %pad_maximum_fusion.7), channel_id=1, source_target_pairs={{0,16},{8,24},{16,0},{24,8},{1,17},{9,25},{17,1},{25,9},{2,18},{10... | collective-permute-start | bytes 4325384 | tf_op jit(solution)/shard_map/ppermute | solution.py:535
  559.1 66.7 %all-to-all-start.6 = ((bf16[4,120,1024]{2,1,0:T(8,128)(2,1)}), bf16[4,120,1024]{2,1,0:T(8,128)(2,1)S(1)}, u32[]{:S(2)}, u32[]{:S(2)}) async-start(bf16[4,120,1024]{2,1,0:T(8,128)(2,1)} %pad_maximum_fusion.14), calls=%async_computation.7 | async-start | bytes 1966080 | tf_op jit(solution)/shard_map/all_to_all | solution.py:581
  626.7 29.7 %all-to-all-start.8 = ((bf16[4,120,1024]{2,1,0:T(8,128)(2,1)}), bf16[4,120,1024]{2,1,0:T(8,128)(2,1)S(1)}, u32[]{:S(2)}, u32[]{:S(2)}) async-start(bf16[4,120,1024]{2,1,0:T(8,128)(2,1)} %pad_maximum_fusion.15), calls=%async_computation.9 | async-start | bytes 1966080 | tf_op jit(solution)/shard_map/all_to_all | solution.py:581
  (175 other events, 2628.9 us)
Sparse Core Ops, SparseCore 0:
  415.2 56.9 reduce-scatter.1

commit v10 on v9

--- a/solution.py
+++ b/solution.py
@@ -666,7 +666,7 @@
     at_core = lax.axis_index("dp") & 1
     big = owner_momentum(top_moment.reshape(block, columns), top_grad)
     big_other = one_way(big, 0, True)
-    top_held, low_grad = gather_plane(big, big_other, 0, low_grad)
+    top_held, _ = gather_plane(big, big_other, 0)
     top_gram = gram_of(top_held)
     low = owner_momentum(low_moment.reshape(little, columns), low_grad)
     low_other = one_way(low, 0, False)

time: 677 us -> 692 us (1.022)
  waiting for transfers between devices: 172 us -> 186 us
    all_to_all x1, waiting for transfers between devices: 3.17 us -> 27.6 us  [on_device(): lax.all_to_all(low_grad, 'fsdp', split_axis=0, concat_axis=0, tiled=True)]
    reduce_scatter x1, waiting for transfers between devices: 16.7 us -> 0.01 us  [on_device(): lax.psum_scatter(top_grad, 'fsdp', scatter_dimension=0, tiled=True)[0]]
    ppermute x57, waiting for transfers between devices: 93.7 us -> 105 us  [swap_bit(): return lax.ppermute(value, 'dp', [(i, i ^ 1 << bit) for i in range(count)])]
  transfers between devices with their start and end apart: 79 -> 79, of which waited for: 23 -> 24; matrix products, arithmetic and copies ran while one was open for 38% -> 37% of each run, Pallas kernels for 7% -> 7%
where the time goes in v10:
time: 692 us; the launch traced here: 682 us
  waiting for transfers between devices  186 us (27%)
  matrix products  134 us (19%)
  starting transfers between devices  110 us (16%)
  other arithmetic  103 us (15%)
  local copies, waits for them, and re-layouts  84.2 us (12%)
  Pallas kernels  48.1 us (7%)
  between operations  16.6 us (2%)
    ppermute x57, waiting for transfers between devices, swap_bit(): return lax.ppermute(value, 'dp', [(i, i ^ 1 << bit) for i in range(count)])  105 us
    pallas_call x1, Pallas kernels, gram_orthogonalize(): pl.pallas_call(polynomial_kernel, out_shape=jax.ShapeDtypeStruct(rows.sha...  48.1 us
    ppermute x57, starting transfers between devices, swap_bit(): return lax.ppermute(value, 'dp', [(i, i ^ 1 << bit) for i in range(count)])  41.3 us
    all_to_all x3, waiting for transfers between devices, line_gather(): return jnp.swapaxes(lax.all_to_all(copies, 'fsdp', 0, 0, tiled=True), 0, 1)  31.1 us
    dynamic_update_slice x16, local copies, waits for them, and re-layouts, natural(): whole = lax.dynamic_update_slice(whole, block, where)  29.4 us
    all_to_all x1, waiting for transfers between devices, on_device(): lax.all_to_all(low_grad, 'fsdp', split_axis=0, concat_axis=0, tiled=True)  27.6 us
    dot_general x7, matrix products, weight_grad(): lax.dot_general(features, series, TOKENS_OUT, preferred_element_type=F32)  25.2 us
    ppermute x8, starting transfers between devices, swap_core(): lax.ppermute(value, 'dp', [(i, i ^ 1 << bit) for i in range(count) if i &...  17.6 us
  transfers between devices with their start and end apart: 79, of which 24 were waited for; matrix products, arithmetic and copies ran while one was open for 37% of the time, Pallas kernels for 7%

profile of v10, /device:TPU:0, one launch (start us, length us, event | category | flops | bytes accessed | tf_op | source)
XLA Modules:
  0.0 682.3 jit_solution(9532226552417451214)
XLA Ops:
  9.6 6.3 all-to-all-start
  16.3 31.0 %all-to-all-done = bf16[4,5,32,1024]{3,2,1,0:T(8,128)(2,1)S(1)} async-done(((bf16[4,5,32,1024]{3,2,1,0:T(8,128)(2,1)}), bf16[4,5,32,1024]{3,2,1,0:T(8,128)(2,1)S(1)}, u32[]{:S(2)}, u32[]{:S(2)}) %all-to-all-start) | async-done | bytes 1310752 | tf_op jit(solution)/shard_map/all_to_all | solution.py:362
  59.8 5.2 collective-permute-done
  77.6 5.2 broadcast_in_dim.33
  88.6 10.0 %collective-permute-done.2 = bf16[5,2,2,32,1024]{4,3,2,0,1:T(8,128)(2,1)} collective-permute-done((bf16[5,2,2,32,1024]{4,3,2,0,1:T(8,128)(2,1)}, bf16[5,2,2,32,1024]{4,3,2,0,1:T(8,128)(2,1)}, u32[]{:S(2)}, u32[]{:S(2)}) %collective-permute-start.2) | collective-permute-done | bytes 1310752 | tf_op jit(solution)/shard_map/ppermute | solution.py:282
  132.4 8.4 %fusion.99 = f32[512,5120]{1,0:T(8,128)S(1)} fusion(bf16[5120,1024]{1,0:T(8,128)(2,1)} %bitcast.26, bf16[512,1024]{1,0:T(8,128)(2,1)S(1)} %copy-done.23, f32[1024]{0:T(1024)S(1)} %mul.337, f32[512]{0:T(512)S(1)} %get-tuple-element.311), kind=kOutput, calls=%fused_computation.239 | convolution fusion | flops 5370806272 | bytes 22026240 | tf_op jit(solution)/shard_map/dot_general | solution.py:60
  166.0 6.5 multiply_convert_fusion.1
  182.3 6.3 collective-permute-done.14
  252.2 9.8 %multiply_convert_fusion.2 = (bf16[512,2816]{1,0:T(8,128)(2,1)}, bf16[512,2816]{1,0:T(8,128)(2,1)}) fusion(f32[512,2816]{1,0:T(8,128)} %get-tuple-element.321, f32[512,2816]{1,0:T(8,128)S(1)} %bitcast.384, bf16[512,1024]{1,0:T(8,128)(2,1)} %param.14, bf16[2816,1024]{1,0:T(8,128)(2,1)S(1)} %bitcast.377), kind=kOutput, calls=%fused_computation.7 | convolution fusion | flops 2958557184 | bytes 24117248 | tf_op jit(solution)/shard_map/dot_general | solution.py:174
  315.5 11.0 %collective-permute-done.39 = bf16[1,2,176,1024]{3,2,1,0:T(8,128)(2,1)S(1)} collective-permute-done((bf16[1,2,176,1024]{3,2,1,0:T(8,128)(2,1)S(1)}, bf16[1,2,176,1024]{3,2,1,0:T(8,128)(2,1)S(1)}, u32[]{:S(2)}, u32[]{:S(2)}) %collective-permute-start.39) | collective-permute-done | bytes 720928 | tf_op jit(solution)/shard_map/ppermute | solution.py:282
  326.5 13.1 %collective-permute-done.41 = bf16[1,2,176,1024]{3,2,1,0:T(8,128)(2,1)S(1)} collective-permute-done((bf16[1,2,176,1024]{3,2,1,0:T(8,128)(2,1)S(1)}, bf16[1,2,176,1024]{3,2,1,0:T(8,128)(2,1)S(1)}, u32[]{:S(2)}, u32[]{:S(2)}) %collective-permute-start.41) | collective-permute-done | bytes 720928 | tf_op jit(solution)/shard_map/ppermute | solution.py:282
  349.7 5.7 multiply_convert_fusion
  373.6 10.4 %collective-permute-done.48 = bf16[1,2,64,1024]{3,2,1,0:T(8,128)(2,1)} collective-permute-done((bf16[1,2,64,1024]{3,2,1,0:T(8,128)(2,1)}, bf16[1,2,64,1024]{3,2,1,0:T(8,128)(2,1)}, u32[]{:S(2)}, u32[]{:S(2)}) %collective-permute-start.48) | collective-permute-done | bytes 262176 | tf_op jit(solution)/shard_map/ppermute | solution.py:282
  424.6 21.9 %collective-permute-done.55 = bf16[4,2,64,1024]{3,2,0,1:T(8,128)(2,1)S(1)} collective-permute-done((bf16[4,2,64,1024]{3,2,0,1:T(8,128)(2,1)S(1)}, bf16[4,2,64,1024]{3,2,0,1:T(8,128)(2,1)S(1)}, u32[]{:S(2)}, u32[]{:S(2)}) %collective-permute-start.55) | collective-permute-done | bytes 1048608 | tf_op jit(solution)/shard_map/ppermute | solution.py:282
  449.4 9.5 %collective-permute-done.56 = bf16[4,64,1024]{2,1,0:T(8,128)(2,1)S(1)} collective-permute-done((bf16[4,64,1024]{2,1,0:T(8,128)(2,1)S(1)}, bf16[4,64,1024]{2,1,0:T(8,128)(2,1)S(1)}, u32[]{:S(2)}, u32[]{:S(2)}) %collective-permute-start.56) | collective-permute-done | bytes 524320 | tf_op jit(solution)/shard_map/ppermute | solution.py:282
  466.9 27.6 %all-to-all-done.5 = bf16[4,128,1024]{2,1,0:T(8,128)(2,1)} async-done(((bf16[4,128,1024]{2,1,0:T(8,128)(2,1)}), bf16[4,128,1024]{2,1,0:T(8,128)(2,1)}, u32[]{:S(2)}, u32[]{:S(2)}) %all-to-all-start.5) | async-done | bytes 1048608 | tf_op jit(solution)/shard_map/all_to_all | solution.py:664
  524.2 10.9 %fusion.23 = (f32[1024]{0:T(1024)S(1)}, f32[512]{0:T(512)S(1)}, f32[512,1024]{1,0:T(8,128)}) fusion(bf16[512,1024]{1,0:T(8,128)(2,1)S(1)} %copy-done.25, f32[512]{0:T(512)S(1)} %get-tuple-element.311, f32[1024]{0:T(1024)S(1)} %mul.337, bf16[5120,1024]{1,0:T(8,128)(2,1)} %bitcast.26, bf16[512,4096]{1,0:T(8,128)(2,1)} %copy-done.31), kind=kOutput, calls=%fused_computation.57 | convolution fusion | flops 5372377600 | bytes 17838080 | tf_op jit(solution)/shard_map/dot_general | solution.py:260
  536.6 7.4 %all-to-all-start.7 = ((f32[32,3,32]{2,1,0:T(4,128)}), f32[32,3,32]{2,1,0:T(4,128)S(1)}, u32[]{:S(2)}, u32[]{:S(2)}) async-start(f32[32,3,32]{2,1,0:T(4,128)} %maximum_bitcast_fusion.6), calls=%async_computation.8 | async-start | bytes 131072 | tf_op jit(solution)/shard_map/all_to_all | solution.py:431
  554.2 6.2 fusion.3
  560.4 11.4 %collective-permute-done.61 = bf16[2,352,1024]{2,1,0:T(8,128)(2,1)S(1)} collective-permute-done((bf16[2,352,1024]{2,1,0:T(8,128)(2,1)S(1)}, bf16[2,352,1024]{2,1,0:T(8,128)(2,1)S(1)}, u32[]{:S(2)}, u32[]{:S(2)}) %collective-permute-start.61) | collective-permute-done | bytes 1441824 | tf_op jit(solution)/shard_map/ppermute | solution.py:535
  585.4 48.1 %shard_map.218 = bf16[704,1024]{1,0:T(8,128)(2,1)S(1)} custom-call(f32[1024,1024]{1,0:T(8,128)} %fusion.2.gram_ref, bf16[704,1024]{1,0:T(8,128)(2,1)S(1)} %pad_maximum_fusion.9.rows_ref), custom_call_target="tpu_custom_call" | custom-call | flops 32212254720 | bytes 8388608 | tf_op jit(solution)/shard_map/pallas_call | solution.py:514
  639.6 5.4 all-to-all-start.8
  645.0 7.8 %add_convert_fusion.2 = bf16[512,1024]{1,0:T(8,128)(2,1)} fusion(f32[512,1024]{1,0:T(8,128)S(1)} %copy-done.11, bf16[512,2816]{1,0:T(8,128)(2,1)} %copy-done.46, bf16[2816,1024]{1,0:T(8,128)(2,1)} %bitcast.378), kind=kOutput, calls=%fused_computation.80 | convolution fusion | flops 2953838592 | bytes 11796480 | tf_op jit(solution)/shard_map/dot_general | solution.py:649
  661.2 8.4 %all-to-all-done.8 = bf16[4,120,1024]{2,1,0:T(8,128)(2,1)} async-done(((bf16[4,120,1024]{2,1,0:T(8,128)(2,1)}), bf16[4,120,1024]{2,1,0:T(8,128)(2,1)}, u32[]{:S(2)}, u32[]{:S(2)}) %all-to-all-start.8) | async-done | bytes 983072 | tf_op jit(solution)/shard_map/all_to_all | solution.py:581
  (540 shorter events, 372.3 us)
Async XLA Ops:
  9.6 37.7 %all-to-all-start = ((bf16[4,5,32,1024]{3,2,1,0:T(8,128)(2,1)}), bf16[4,5,32,1024]{3,2,1,0:T(8,128)(2,1)S(1)}, u32[]{:S(2)}, u32[]{:S(2)}) async-start(bf16[4,5,32,1024]{3,2,1,0:T(8,128)(2,1)} %broadcast_in_dim.26), calls=%async_computation | async-start | bytes 2621440 | tf_op jit(solution)/shard_map/all_to_all | solution.py:362
  72.3 35.4 %collective-permute-start.10 = (bf16[5,2,2,32,1024]{4,3,2,0,1:T(8,128)(2,1)}, bf16[5,2,2,32,1024]{4,3,2,0,1:T(8,128)(2,1)}, u32[]{:S(2)}, u32[]{:S(2)}) collective-permute-start(bf16[5,2,2,32,1024]{4,3,2,0,1:T(8,128)(2,1)} %pad_maximum_fusion.10), channel_id=1, source_target_pairs={{0,4},{4,0},{8,12},{12,8},{16,20},{20,16},{24,28},{28,24},{1,5},{5... | collective-permute-start | bytes 3932168 | tf_op jit(solution)/shard_map/ppermute | solution.py:282
  72.3 39.3 %collective-permute-start.11 = (bf16[5,2,2,32,1024]{4,3,2,1,0:T(8,128)(2,1)S(1)}, bf16[5,2,2,32,1024]{4,3,2,1,0:T(8,128)(2,1)}, u32[]{:S(2)}, u32[]{:S(2)}) collective-permute-start(bf16[5,2,2,32,1024]{4,3,2,1,0:T(8,128)(2,1)S(1)} %pad_maximum_fusion.11), channel_id=1, source_target_pairs={{0,4},{4,0},{8,12},{12,8},{16,20},{20,16},{24,28},{28,24},{1,5},{5... | collective-permute-start | bytes 3932168 | tf_op jit(solution)/shard_map/ppermute | solution.py:282
  74.1 41.4 %all-to-all-start.1 = ((bf16[4,2,88,1024]{3,2,1,0:T(8,128)(2,1)}), bf16[4,2,88,1024]{3,2,1,0:T(8,128)(2,1)S(1)}, u32[]{:S(2)}, u32[]{:S(2)}) async-start(bf16[4,2,88,1024]{3,2,1,0:T(8,128)(2,1)} %broadcast_in_dim.31), calls=%async_computation.1 | async-start | bytes 2883584 | tf_op jit(solution)/shard_map/all_to_all | solution.py:362
  117.2 30.1 %collective-permute-start.6 = (bf16[1,2,88,1024]{3,2,1,0:T(8,128)(2,1)}, bf16[1,2,88,1024]{3,2,1,0:T(8,128)(2,1)}, u32[]{:S(2)}, u32[]{:S(2)}) collective-permute-start(bf16[1,2,88,1024]{3,2,1,0:T(8,128)(2,1)} %get-tuple-element.297), channel_id=1, source_target_pairs={{0,8},{4,12},{8,0},{12,4},{16,24},{20,28},{24,16},{28,20},{1,9},{5... | collective-permute-start | bytes 1081352 | tf_op jit(solution)/shard_map/ppermute | solution.py:282
  117.8 31.6 %collective-permute-start.7 = (bf16[1,2,88,1024]{3,2,1,0:T(8,128)(2,1)}, bf16[1,2,88,1024]{3,2,1,0:T(8,128)(2,1)}, u32[]{:S(2)}, u32[]{:S(2)}) collective-permute-start(bf16[1,2,88,1024]{3,2,1,0:T(8,128)(2,1)} %get-tuple-element.296), channel_id=1, source_target_pairs={{0,16},{4,20},{8,24},{12,28},{16,0},{20,4},{24,8},{28,12},{1,17},{... | collective-permute-start | bytes 1081352 | tf_op jit(solution)/shard_map/ppermute | solution.py:282
  118.8 32.6 %collective-permute-start.8 = (bf16[1,2,88,1024]{3,2,1,0:T(8,128)(2,1)}, bf16[1,2,88,1024]{3,2,1,0:T(8,128)(2,1)}, u32[]{:S(2)}, u32[]{:S(2)}) collective-permute-start(bf16[1,2,88,1024]{3,2,1,0:T(8,128)(2,1)} %get-tuple-element.295), channel_id=1, source_target_pairs={{0,8},{4,12},{8,0},{12,4},{16,24},{20,28},{24,16},{28,20},{1,9},{5... | collective-permute-start | bytes 1081352 | tf_op jit(solution)/shard_map/ppermute | solution.py:282
  120.3 33.1 %collective-permute-start.9 = (bf16[1,2,88,1024]{3,2,1,0:T(8,128)(2,1)}, bf16[1,2,88,1024]{3,2,1,0:T(8,128)(2,1)}, u32[]{:S(2)}, u32[]{:S(2)}) collective-permute-start(bf16[1,2,88,1024]{3,2,1,0:T(8,128)(2,1)} %get-tuple-element.294), channel_id=1, source_target_pairs={{0,16},{4,20},{8,24},{12,28},{16,0},{20,4},{24,8},{28,12},{1,17},{... | collective-permute-start | bytes 1081352 | tf_op jit(solution)/shard_map/ppermute | solution.py:282
  156.4 46.1 %collective-permute-start.16 = (bf16[1,2,2,88,1024]{4,3,2,0,1:T(8,128)(2,1)}, bf16[1,2,2,88,1024]{4,3,2,0,1:T(8,128)(2,1)}, u32[]{:S(2)}, u32[]{:S(2)}) collective-permute-start(bf16[1,2,2,88,1024]{4,3,2,0,1:T(8,128)(2,1)} %pad_maximum_fusion.16), channel_id=1, source_target_pairs={{0,4},{4,0},{8,12},{12,8},{16,20},{20,16},{24,28},{28,24},{1,5},{5... | collective-permute-start | bytes 2162696 | tf_op jit(solution)/shard_map/ppermute | solution.py:282
  156.9 31.7 %collective-permute-start.14 = (bf16[1,2,2,88,1024]{4,3,2,0,1:T(8,128)(2,1)}, bf16[1,2,2,88,1024]{4,3,2,0,1:T(8,128)(2,1)}, u32[]{:S(2)}, u32[]{:S(2)}) collective-permute-start(bf16[1,2,2,88,1024]{4,3,2,0,1:T(8,128)(2,1)} %pad_maximum_fusion.18), channel_id=1, source_target_pairs={{0,16},{4,20},{8,24},{12,28},{16,0},{20,4},{24,8},{28,12},{1,17},{... | collective-permute-start | bytes 2162696 | tf_op jit(solution)/shard_map/ppermute | solution.py:282
  157.8 32.9 %collective-permute-start.15 = (bf16[1,2,2,88,1024]{4,3,2,1,0:T(8,128)(2,1)}, bf16[1,2,2,88,1024]{4,3,2,1,0:T(8,128)(2,1)}, u32[]{:S(2)}, u32[]{:S(2)}) collective-permute-start(bf16[1,2,2,88,1024]{4,3,2,1,0:T(8,128)(2,1)} %pad_maximum_fusion.19), channel_id=1, source_target_pairs={{0,8},{4,12},{8,0},{12,4},{16,24},{20,28},{24,16},{28,20},{1,9},{5... | collective-permute-start | bytes 2162696 | tf_op jit(solution)/shard_map/ppermute | solution.py:282
  160.3 30.4 %all-to-all-start.3 = ((bf16[4,1,88,1024]{3,2,1,0:T(8,128)(2,1)}), bf16[4,1,88,1024]{3,2,1,0:T(8,128)(2,1)}, u32[]{:S(2)}, u32[]{:S(2)}) async-start(bf16[4,1,88,1024]{3,2,1,0:T(8,128)(2,1)} %broadcast_in_dim.35), calls=%async_computation.3 | async-start | bytes 1441792 | tf_op jit(solution)/shard_map/all_to_all | solution.py:362
  195.3 43.8 %all-to-all-start.4 = ((bf16[4,120,1024]{2,1,0:T(8,128)(2,1)}), bf16[4,120,1024]{2,1,0:T(8,128)(2,1)S(1)}, u32[]{:S(2)}, u32[]{:S(2)}) async-start(bf16[4,120,1024]{2,1,0:T(8,128)(2,1)} %pad_maximum_fusion.13), calls=%async_computation.4 | async-start | bytes 1966080 | tf_op jit(solution)/shard_map/all_to_all | solution.py:581
  198.8 297.9 %reduce-scatter.2.cloned.1.call-start = ((), (), s32[]{:S(2)}) async-start(), calls=%async_computation.10 | async-start | bytes 3604480 | tf_op jit(solution)/shard_map/reduce_scatter | solution.py:658
  210.1 30.6 %collective-permute-start.27 = (bf16[1,2,2,88,1024]{4,3,2,0,1:T(8,128)(2,1)}, bf16[1,2,2,88,1024]{4,3,2,0,1:T(8,128)(2,1)}, u32[]{:S(2)}, u32[]{:S(2)}) collective-permute-start(bf16[1,2,2,88,1024]{4,3,2,0,1:T(8,128)(2,1)} %pad_maximum_fusion.20), channel_id=1, source_target_pairs={{0,4},{4,0},{8,12},{12,8},{16,20},{20,16},{24,28},{28,24},{1,5},{5... | collective-permute-start | bytes 2162696 | tf_op jit(solution)/shard_map/ppermute | solution.py:282
  240.8 29.7 %collective-permute-start.32 = (bf16[1,2,2,352,1024]{4,3,2,1,0:T(8,128)(2,1)}, bf16[1,2,2,352,1024]{4,3,2,1,0:T(8,128)(2,1)}, u32[]{:S(2)}, u32[]{:S(2)}) collective-permute-start(bf16[1,2,2,352,1024]{4,3,2,1,0:T(8,128)(2,1)} %bitcast.441), channel_id=1, source_target_pairs={{0,4},{4,0},{8,12},{12,8},{16,20},{20,16},{24,28},{28,24},{1,5},{5... | collective-permute-start | bytes 8650760 | tf_op jit(solution)/shard_map/ppermute | solution.py:282
  304.4 35.2 %collective-permute-start.43 = (bf16[1,2,2,128,1024]{4,3,2,1,0:T(8,128)(2,1)S(1)}, bf16[1,2,2,128,1024]{4,3,2,1,0:T(8,128)(2,1)S(1)}, u32[]{:S(2)}, u32[]{:S(2)}) collective-permute-start(bf16[1,2,2,128,1024]{4,3,2,1,0:T(8,128)(2,1)S(1)} %get-tuple-element.202), channel_id=1, source_target_pairs={{0,4},{4,0},{8,12},{12,8},{16,20},{20,16},{24,28},{28,24},{1,5},{5... | collective-permute-start | bytes 3145736 | tf_op jit(solution)/shard_map/ppermute | solution.py:282
  461.6 32.9 %all-to-all-start.5 = ((bf16[4,128,1024]{2,1,0:T(8,128)(2,1)}), bf16[4,128,1024]{2,1,0:T(8,128)(2,1)}, u32[]{:S(2)}, u32[]{:S(2)}) async-start(bf16[4,128,1024]{2,1,0:T(8,128)(2,1)} %pad_maximum_fusion.12), calls=%async_computation.6 | async-start | bytes 2097152 | tf_op jit(solution)/shard_map/all_to_all | solution.py:664
  512.6 37.4 %collective-permute-start.63 = (bf16[2,128,1024]{2,1,0:T(8,128)(2,1)}, bf16[2,128,1024]{2,1,0:T(8,128)(2,1)}, u32[]{:S(2)}, u32[]{:S(2)}) collective-permute-start(bf16[2,128,1024]{2,1,0:T(8,128)(2,1)} %pad_maximum_fusion.22), channel_id=1, source_target_pairs={{4,20},{12,28},{20,4},{28,12},{5,21},{13,29},{21,5},{29,13},{6,22}... | collective-permute-start | bytes 1572872 | tf_op jit(solution)/shard_map/ppermute | solution.py:535
  514.1 29.9 %collective-permute-start.60 = (bf16[1,352,1024]{2,1,0:T(8,128)(2,1)S(1)}, bf16[1,352,1024]{2,1,0:T(8,128)(2,1)}, u32[]{:S(2)}, u32[]{:S(2)}) collective-permute-start(bf16[1,352,1024]{2,1,0:T(8,128)(2,1)S(1)} %bitcast.420), channel_id=1, source_target_pairs={{0,16},{8,24},{16,0},{24,8},{1,17},{9,25},{17,1},{25,9},{2,18},{10... | collective-permute-start | bytes 2162696 | tf_op jit(solution)/shard_map/ppermute | solution.py:535
  520.8 33.4 %collective-permute-start.58 = (bf16[2,352,1024]{2,1,0:T(8,128)(2,1)}, bf16[2,352,1024]{2,1,0:T(8,128)(2,1)}, u32[]{:S(2)}, u32[]{:S(2)}) collective-permute-start(bf16[2,352,1024]{2,1,0:T(8,128)(2,1)} %pad_maximum_fusion.7), channel_id=1, source_target_pairs={{0,16},{8,24},{16,0},{24,8},{1,17},{9,25},{17,1},{25,9},{2,18},{10... | collective-permute-start | bytes 4325384 | tf_op jit(solution)/shard_map/ppermute | solution.py:535
  536.6 43.7 %all-to-all-start.7 = ((f32[32,3,32]{2,1,0:T(4,128)}), f32[32,3,32]{2,1,0:T(4,128)S(1)}, u32[]{:S(2)}, u32[]{:S(2)}) async-start(f32[32,3,32]{2,1,0:T(4,128)} %maximum_bitcast_fusion.6), calls=%async_computation.8 | async-start | bytes 131072 | tf_op jit(solution)/shard_map/all_to_all | solution.py:431
  580.3 59.2 %all-to-all-start.6 = ((bf16[4,120,1024]{2,1,0:T(8,128)(2,1)}), bf16[4,120,1024]{2,1,0:T(8,128)(2,1)}, u32[]{:S(2)}, u32[]{:S(2)}) async-start(bf16[4,120,1024]{2,1,0:T(8,128)(2,1)} %pad_maximum_fusion.14), calls=%async_computation.7 | async-start | bytes 1966080 | tf_op jit(solution)/shard_map/all_to_all | solution.py:581
  639.6 30.1 %all-to-all-start.8 = ((bf16[4,120,1024]{2,1,0:T(8,128)(2,1)}), bf16[4,120,1024]{2,1,0:T(8,128)(2,1)}, u32[]{:S(2)}, u32[]{:S(2)}) async-start(bf16[4,120,1024]{2,1,0:T(8,128)(2,1)} %pad_maximum_fusion.15), calls=%async_computation.9 | async-start | bytes 1966080 | tf_op jit(solution)/shard_map/all_to_all | solution.py:581
  (165 other events, 1967.1 us)
Sparse Core Ops, SparseCore 0:
  416.0 59.5 reduce-scatter.1
